TPU v7x, 32 devices: a whole 2x2x4 slice. The times are simulated.
32 devices in a mesh: dp: 8 (over y, x, core), seq: 4 (over z).
Axes of the slice: x: 2, y: 2, z: 4, core: 2. Of those that a mesh axis runs over, the one named last changes fastest.
Arguments:
- inputs: bfloat16 [8, 1024, 1024], P('dp', 'seq'), may hold values from -6 to 6
- positions: int32 [8, 1024], P('dp', 'seq'), may hold values from 0 to 8191
- attn_gain: bfloat16 [1024], P(('dp', 'seq')), may hold values from 0.5 to 1.5
- qkv_weight: bfloat16 [1024, 3072], P(('dp', 'seq')), may hold values from -0.1875 to 0.1875
- attn_out_weight: bfloat16 [1024, 1024], P(('dp', 'seq')), may hold values from -3.5 to 3.5
- mlp_gain: bfloat16 [1024], P(('dp', 'seq')), may hold values from 0.5 to 1.5
- up_weight: bfloat16 [1024, 5248], P(('dp', 'seq')), may hold values from -0.1875 to 0.1875
- down_weight: bfloat16 [1024, 2624], P(('dp', 'seq')), may hold values from -0.125 to 0.125
- cotangent: bfloat16 [8, 1024, 1024], P('dp', 'seq'), may hold values from -6 to 6
Outputs:
- output: bfloat16 [8, 1024, 1024], P('dp', 'seq')
- input_grad: bfloat16 [8, 1024, 1024], P('dp', 'seq')
- attn_gain_grad: float32 [1024], P(('dp', 'seq'))
- qkv_grad: float32 [1024, 3072], P(('dp', 'seq'))
- attn_out_grad: float32 [1024, 1024], P(('dp', 'seq'))
- mlp_gain_grad: float32 [1024], P(('dp', 'seq'))
- up_grad: float32 [1024, 5248], P(('dp', 'seq'))
- down_grad: float32 [1024, 2624], P(('dp', 'seq'))
All inputs are finite; a program needn't handle non-finite values.
Results may differ from a plain program's by a relative error of at most 0.019.
Values may be sent and summed in bfloat16 or wider, within the bound.
No kernel may reach another device: no remote copies, remote signals or barrier semaphores. Data moves between devices by JAX's collectives and lax.ppermute only.
A program may use at most 192 MiB of HBM per device.

v0:
```python
import jax
import jax.numpy as jnp
from jax import lax
from jax.sharding import PartitionSpec as P

HEADS = 16
HEAD_DIM = 64
FF = 2624


norm_eps = 1e-05
rope_base = 160000.0
inv_root_two = 0.7071067811865476
inv_root_tau = 0.3989422804014327


def for_sending(array):
    return jax.tree.map(lambda a: a.astype(jnp.bfloat16) if a.dtype == jnp.float32 else a, array)


def normalize(values):
    centre = jnp.mean(values, axis=-1, keepdims=True)
    centred = values - centre
    spread = lax.rsqrt(jnp.mean(centred * centred, axis=-1, keepdims=True) + norm_eps)
    return (centred * spread, spread)


def norm_back(grad_in, normed, spread, gain):
    scaled = grad_in * gain
    gain_term = jnp.sum(grad_in * normed, axis=0)
    centred = (
        scaled
        - jnp.mean(scaled, axis=-1, keepdims=True)
        - normed * jnp.mean(scaled * normed, axis=-1, keepdims=True)
    )
    return (spread * centred, gain_term)


def rope_tables(seq_pos):
    exponent = jnp.arange(0, HEAD_DIM, 2).astype(jnp.float32) / HEAD_DIM
    frequency = rope_base ** (-exponent)
    angles = seq_pos.astype(jnp.float32)[:, None] * frequency[None, :]
    angles = jnp.concatenate([angles, angles], axis=-1)[:, None, :]
    return (jnp.cos(angles), jnp.sin(angles))


def rotate(values, cos_table, sin_table):
    half_dim = values.shape[-1] // 2
    turned = jnp.concatenate([-values[..., half_dim:], values[..., :half_dim]], axis=-1)
    return values * cos_table + turned * sin_table


def rotate_back(grads, cos_table, sin_table):
    half_dim = grads.shape[-1] // 2
    weighted = grads * sin_table
    turned = jnp.concatenate([weighted[..., half_dim:], -weighted[..., :half_dim]], axis=-1)
    return grads * cos_table + turned


def gelu_parts(inner_act):
    normal_cdf = 0.5 * (1.0 + jax.scipy.special.erf(inner_act * inv_root_two))
    slope = normal_cdf + inner_act * jnp.exp(-0.5 * inner_act * inner_act) * inv_root_tau
    return (inner_act * normal_cdf, slope)


def project_heads(attn_in, w_qkv, cos_table, sin_table):
    token_count, model_width = attn_in.shape
    mixed_rows = jnp.dot(attn_in, w_qkv, preferred_element_type=jnp.float32)
    shaped = (token_count, HEADS, HEAD_DIM)
    queries = rotate(mixed_rows[:, :model_width].reshape(shaped), cos_table, sin_table)
    key_rows = rotate(
        mixed_rows[:, model_width : 2 * model_width].reshape(shaped), cos_table, sin_table
    )
    queries = queries.reshape(token_count, model_width).astype(jnp.bfloat16)
    key_rows = key_rows.reshape(token_count, model_width).astype(jnp.bfloat16)
    values = mixed_rows[:, 2 * model_width :].astype(jnp.bfloat16)
    return (queries, key_rows, values)


def attend_forward(q_heads, k_heads, v_heads):
    seq_len, columns = q_heads.shape
    head_count = columns // HEAD_DIM
    block_rows = min(512, seq_len)
    block_count = seq_len // block_rows
    score_scale = HEAD_DIM ** (-0.5)
    k_all = k_heads.reshape(seq_len, head_count, HEAD_DIM)
    v_all = v_heads.reshape(seq_len, head_count, HEAD_DIM)

    def one_block(q_block):
        scores = (
            jnp.einsum("qhd,khd->hqk", q_block, k_all, preferred_element_type=jnp.float32)
            * score_scale
        )
        row_peak = jnp.max(scores, axis=-1, keepdims=True)
        exp_scores = jnp.exp(scores - row_peak)
        totals = jnp.sum(exp_scores, axis=-1, keepdims=True)
        prob_rows = (exp_scores / totals).astype(jnp.bfloat16)
        attended = jnp.einsum("hqk,khd->qhd", prob_rows, v_all, preferred_element_type=jnp.float32)
        return (attended.astype(jnp.bfloat16), row_peak[..., 0] + jnp.log(totals[..., 0]))

    attended, log_totals = lax.map(
        one_block, q_heads.reshape(block_count, block_rows, head_count, HEAD_DIM)
    )
    return (attended.reshape(seq_len, columns), log_totals)


def attend_backward(q_heads, k_heads, v_heads, d_heads, log_totals):
    seq_len, columns = q_heads.shape
    head_count = columns // HEAD_DIM
    block_rows = min(512, seq_len)
    block_count = seq_len // block_rows
    score_scale = HEAD_DIM ** (-0.5)
    k_all = k_heads.reshape(seq_len, head_count, HEAD_DIM)
    v_all = v_heads.reshape(seq_len, head_count, HEAD_DIM)
    q_blocks = q_heads.reshape(block_count, block_rows, head_count, HEAD_DIM)
    d_blocks = d_heads.reshape(block_count, block_rows, head_count, HEAD_DIM)

    def one_block(carry, item):
        key_acc, value_acc = carry
        q_block, d_block, lse_block = item
        scores = (
            jnp.einsum("qhd,khd->hqk", q_block, k_all, preferred_element_type=jnp.float32)
            * score_scale
        )
        prob_rows = jnp.exp(scores - lse_block[..., None])
        value_acc = value_acc + jnp.einsum(
            "hqk,qhd->khd",
            prob_rows.astype(jnp.bfloat16),
            d_block,
            preferred_element_type=jnp.float32,
        )
        d_probs = jnp.einsum("qhd,khd->hqk", d_block, v_all, preferred_element_type=jnp.float32)
        d_scores = (
            prob_rows * (d_probs - jnp.sum(prob_rows * d_probs, axis=-1, keepdims=True))
        ).astype(jnp.bfloat16)
        d_query = (
            jnp.einsum("hqk,khd->qhd", d_scores, k_all, preferred_element_type=jnp.float32)
            * score_scale
        )
        key_acc = (
            key_acc
            + jnp.einsum("hqk,qhd->khd", d_scores, q_block, preferred_element_type=jnp.float32)
            * score_scale
        )
        return ((key_acc, value_acc), d_query.astype(jnp.bfloat16))

    empty_acc = jnp.zeros((seq_len, head_count, HEAD_DIM), jnp.float32)
    (key_acc, value_acc), d_query = lax.scan(
        one_block, (empty_acc, empty_acc), (q_blocks, d_blocks, log_totals)
    )
    d_q = d_query.reshape(seq_len, columns)
    d_k = key_acc.astype(jnp.bfloat16).reshape(seq_len, columns)
    d_v = value_acc.astype(jnp.bfloat16).reshape(seq_len, columns)
    return (d_q, d_k, d_v)


def add_sources(received):
    return tuple((jnp.sum(piece, axis=0) for piece in received))


def per_device(
    inputs,
    positions,
    attn_gain,
    qkv_weight,
    attn_out_weight,
    mlp_gain,
    up_weight,
    down_weight,
    cotangent,
):
    layer = (
        lax.all_gather(attn_gain, ("dp", "seq"), axis=0, tiled=True),
        lax.all_gather(qkv_weight, ("dp", "seq"), axis=0, tiled=True),
        lax.all_gather(attn_out_weight, ("dp", "seq"), axis=0, tiled=True),
        lax.all_gather(mlp_gain, ("dp", "seq"), axis=0, tiled=True),
        lax.all_gather(up_weight, ("dp", "seq"), axis=0, tiled=True),
        lax.all_gather(down_weight, ("dp", "seq"), axis=0, tiled=True),
    )
    gain_one, w_qkv, w_out, gain_two, w_up, w_down = layer
    token_count = inputs.shape[1]
    resid_in = inputs[0].astype(jnp.float32)
    cos_table, sin_table = rope_tables(positions[0])
    normed_one, spread_one = normalize(resid_in)
    attn_in = (normed_one * gain_one.astype(jnp.float32)).astype(jnp.bfloat16)
    queries, key_rows, values = project_heads(attn_in, w_qkv, cos_table, sin_table)
    q_heads, k_heads, v_heads = (
        lax.all_to_all(queries, "seq", split_axis=1, concat_axis=0, tiled=True),
        lax.all_to_all(key_rows, "seq", split_axis=1, concat_axis=0, tiled=True),
        lax.all_to_all(values, "seq", split_axis=1, concat_axis=0, tiled=True),
    )
    attended_heads, log_totals = attend_forward(q_heads, k_heads, v_heads)
    attended = lax.all_to_all(attended_heads, "seq", split_axis=0, concat_axis=1, tiled=True)
    resid = resid_in + jnp.dot(attended, w_out, preferred_element_type=jnp.float32)
    normed_two, spread_two = normalize(resid)
    mlp_in = (normed_two * gain_two.astype(jnp.float32)).astype(jnp.bfloat16)
    up_rows = jnp.dot(mlp_in, w_up, preferred_element_type=jnp.float32)
    inner_act = up_rows[:, :FF]
    gate_act = up_rows[:, FF:]
    gelu_val, gelu_slope = gelu_parts(inner_act)
    hidden = (gelu_val * gate_act).astype(jnp.bfloat16)
    output = resid + jnp.einsum("tf,df->td", hidden, w_down, preferred_element_type=jnp.float32)
    layer_back = (
        lax.all_gather(attn_gain, ("dp", "seq"), axis=0, tiled=True),
        lax.all_gather(qkv_weight, ("dp", "seq"), axis=0, tiled=True),
        lax.all_gather(attn_out_weight, ("dp", "seq"), axis=0, tiled=True),
        lax.all_gather(mlp_gain, ("dp", "seq"), axis=0, tiled=True),
        lax.all_gather(up_weight, ("dp", "seq"), axis=0, tiled=True),
        lax.all_gather(down_weight, ("dp", "seq"), axis=0, tiled=True),
    )
    gain_one, w_qkv, w_out, gain_two, w_up, w_down = layer_back
    d_out = cotangent[0]
    down_grad = jnp.einsum("td,tf->df", d_out, hidden, preferred_element_type=jnp.float32)
    d_hidden = jnp.dot(d_out, w_down, preferred_element_type=jnp.float32)
    d_up = jnp.concatenate([d_hidden * gate_act * gelu_slope, d_hidden * gelu_val], axis=1).astype(
        jnp.bfloat16
    )
    up_grad = jnp.einsum("tk,tn->kn", mlp_in, d_up, preferred_element_type=jnp.float32)
    d_mlp_in = jnp.einsum("tn,kn->tk", d_up, w_up, preferred_element_type=jnp.float32)
    d_norm_two, gain_two_grad = norm_back(
        d_mlp_in, normed_two, spread_two, gain_two.astype(jnp.float32)
    )
    d_resid = d_out.astype(jnp.float32) + d_norm_two
    d_resid_low = d_resid.astype(jnp.bfloat16)
    out_grad = jnp.einsum("tk,tn->kn", attended, d_resid_low, preferred_element_type=jnp.float32)
    d_attended = jnp.einsum(
        "tn,kn->tk", d_resid_low, w_out, preferred_element_type=jnp.float32
    ).astype(jnp.bfloat16)
    d_heads = lax.all_to_all(d_attended, "seq", split_axis=1, concat_axis=0, tiled=True)
    queries, key_rows, values = project_heads(attn_in, w_qkv, cos_table, sin_table)
    head_inputs = (
        lax.all_to_all(queries, "seq", split_axis=1, concat_axis=0, tiled=True),
        lax.all_to_all(key_rows, "seq", split_axis=1, concat_axis=0, tiled=True),
        lax.all_to_all(values, "seq", split_axis=1, concat_axis=0, tiled=True),
    )
    d_q, d_k, d_v = attend_backward(
        head_inputs[0], head_inputs[1], head_inputs[2], d_heads, log_totals
    )
    dq_rows, dk_rows, dv_rows = (
        lax.all_to_all(d_q, "seq", split_axis=0, concat_axis=1, tiled=True),
        lax.all_to_all(d_k, "seq", split_axis=0, concat_axis=1, tiled=True),
        lax.all_to_all(d_v, "seq", split_axis=0, concat_axis=1, tiled=True),
    )
    shaped = (token_count, HEADS, HEAD_DIM)
    dq_pre = rotate_back(dq_rows.astype(jnp.float32).reshape(shaped), cos_table, sin_table).reshape(
        token_count, -1
    )
    dk_pre = rotate_back(dk_rows.astype(jnp.float32).reshape(shaped), cos_table, sin_table).reshape(
        token_count, -1
    )
    d_mixed = jnp.concatenate(
        [dq_pre.astype(jnp.bfloat16), dk_pre.astype(jnp.bfloat16), dv_rows], axis=1
    )
    qkv_grad = jnp.einsum("tk,tn->kn", attn_in, d_mixed, preferred_element_type=jnp.float32)
    d_attn_in = jnp.einsum("tn,kn->tk", d_mixed, w_qkv, preferred_element_type=jnp.float32)
    d_norm_one, gain_one_grad = norm_back(
        d_attn_in, normed_one, spread_one, gain_one.astype(jnp.float32)
    )
    input_grad = (d_resid + d_norm_one).astype(jnp.bfloat16)
    all_sent = (
        lax.all_to_all(
            gain_one_grad[None].astype(jnp.bfloat16), "dp", split_axis=1, concat_axis=0, tiled=True
        ).astype(jnp.float32),
        lax.all_to_all(
            qkv_grad[None].astype(jnp.bfloat16), "dp", split_axis=1, concat_axis=0, tiled=True
        ).astype(jnp.float32),
        lax.all_to_all(
            out_grad[None].astype(jnp.bfloat16), "dp", split_axis=1, concat_axis=0, tiled=True
        ).astype(jnp.float32),
        lax.all_to_all(
            gain_two_grad[None].astype(jnp.bfloat16), "dp", split_axis=1, concat_axis=0, tiled=True
        ).astype(jnp.float32),
        lax.all_to_all(
            up_grad[None].astype(jnp.bfloat16), "dp", split_axis=1, concat_axis=0, tiled=True
        ).astype(jnp.float32),
        lax.all_to_all(
            down_grad[None].astype(jnp.bfloat16), "dp", split_axis=1, concat_axis=0, tiled=True
        ).astype(jnp.float32),
    )
    grads = jax.tree.map(
        lambda part: part.astype(jnp.float32),
        lax.psum_scatter(
            for_sending(add_sources(all_sent)), "seq", scatter_dimension=0, tiled=True
        ),
    )
    return (
        output.astype(jnp.bfloat16)[None],
        input_grad[None],
        grads[0],
        grads[1],
        grads[2],
        grads[3],
        grads[4],
        grads[5],
    )


def solution(mesh):
    return jax.shard_map(
        per_device,
        mesh=mesh,
        in_specs=(
            P("dp", "seq", None),
            P("dp", "seq"),
            P(("dp", "seq")),
            P(("dp", "seq"), None),
            P(("dp", "seq"), None),
            P(("dp", "seq")),
            P(("dp", "seq"), None),
            P(("dp", "seq"), None),
            P("dp", "seq", None),
        ),
        out_specs=(
            P("dp", "seq", None),
            P("dp", "seq", None),
            P(("dp", "seq")),
            P(("dp", "seq"), None),
            P(("dp", "seq"), None),
            P(("dp", "seq")),
            P(("dp", "seq"), None),
            P(("dp", "seq"), None),
        ),
        check_vma=False,
    )
```

profile of v0, /device:TPU:1, one launch (start us, length us, event | category | flops | bytes accessed | tf_op | source)
XLA Modules:
  0.0 986.1 jit_solution(249041889575331969)
XLA Ops:
  11.7 41.5 %all-reduce.4 = (bf16[1024]{0:T(1024)(128)(2,1)S(1)}, bf16[1024]{0:T(1024)(128)(2,1)S(1)}) all-reduce(bf16[1024]{0:T(1024)(128)(2,1)S(1)} %dynamic-update-slice, bf16[1024]{0:T(1024)(128)(2,1)S(1)} %dynamic-update-slice.1), channel_id=1, replica_groups=mesh['dp'=8,'seq'=4] {'dp','seq'}, use_global_device_ids=true, to_apply=%add | all-reduce | flops 2048 | bytes 8192
  58.2 24.9 %all-gather.5.cloned.1.call-done = bf16[1024,3072]{1,0:T(8,128)(2,1)} async-done(((bf16[32,3072]{1,0:T(8,128)(2,1)}), bf16[1024,3072]{1,0:T(8,128)(2,1)}) %all-gather.5.cloned.1.call-update) | async-done | bytes 6291472 | tf_op jit(solution)/shard_map/all_gather | solution.py:174
  114.5 14.3 %all-to-all-done = bf16[256,4,256]{0,2,1:T(8,128)(2,1)} async-done(((bf16[256,4,256]{0,2,1:T(8,128)(2,1)}), bf16[256,4,256]{0,2,1:T(8,128)(2,1)}, u32[]{:S(2)}, u32[]{:S(2)}) %all-to-all-start) | async-done | bytes 524320 | tf_op jit(solution)/shard_map/all_to_all | solution.py:188
  133.8 17.2 %all-to-all-done.1 = bf16[256,4,256]{2,0,1:T(8,128)(2,1)} async-done(((bf16[256,4,256]{2,0,1:T(8,128)(2,1)}), bf16[256,4,256]{2,0,1:T(8,128)(2,1)}, u32[]{:S(2)}, u32[]{:S(2)}) %all-to-all-start.1) | async-done | bytes 524320 | tf_op jit(solution)/shard_map/all_to_all | solution.py:189
  158.4 13.7 %all-to-all-done.2 = bf16[256,4,256]{2,0,1:T(8,128)(2,1)S(1)} async-done(((bf16[256,4,256]{2,0,1:T(8,128)(2,1)}), bf16[256,4,256]{2,0,1:T(8,128)(2,1)S(1)}, u32[]{:S(2)}, u32[]{:S(2)}) %all-to-all-start.2) | async-done | bytes 524320 | tf_op jit(solution)/shard_map/all_to_all | solution.py:190
  172.7 10.7 %while.27 = (s32[]{:T(128)}, bf16[2,512,4,64]{1,3,2,0:T(8,128)(2,1)S(1)}, f32[2,4,512]{2,1,0:T(4,128)S(1)}, bf16[2,512,4,64]{1,3,2,0:T(8,128)(2,1)S(1)}, bf16[10...) while((s32[]{:T(128)}, bf16[2,512,4,64]{1,3,2,0:T(8,128)(2,1)S(1)}, ...), condition=%wide.region_5.6_spmd, body=%wide.region_2.5_spmd.sunk | while | flops 555874304 | bytes 26804320 | solution.py:101
  189.2 21.9 %all-to-all-done.3 = bf16[4,256,256]{1,2,0:T(8,128)(2,1)S(1)} async-done(((bf16[4,256,256]{1,2,0:T(8,128)(2,1)}), bf16[4,256,256]{1,2,0:T(8,128)(2,1)S(1)}, u32[]{:S(2)}, u32[]{:S(2)}) %all-to-all-start.3) | async-done | bytes 524320 | tf_op jit(solution)/shard_map/all_to_all | solution.py:193
  214.1 38.0 %all-gather.9.cloned.1.call-done = bf16[1024,5248]{1,0:T(8,128)(2,1)} async-done(((bf16[32,5248]{1,0:T(8,128)(2,1)}), bf16[1024,5248]{1,0:T(8,128)(2,1)}) %all-gather.9.cloned.1.call-update) | async-done | bytes 10747920 | tf_op jit(solution)/shard_map/all_gather | solution.py:177
  252.0 8.9 fusion.87
  260.9 58.5 %all-gather.11.cloned.1.call-done = bf16[1024,2624]{1,0:T(8,128)(2,1)} async-done(((bf16[32,2624]{1,0:T(8,128)(2,1)}), bf16[1024,2624]{1,0:T(8,128)(2,1)}) %all-gather.11.cloned.1.call-update) | async-done | bytes 5373968 | tf_op jit(solution)/shard_map/all_gather | solution.py:178
  319.4 7.8 fusion.48
  344.9 14.4 %all-to-all-done.4 = bf16[256,4,256]{0,2,1:T(8,128)(2,1)} async-done(((bf16[256,4,256]{0,2,1:T(8,128)(2,1)}), bf16[256,4,256]{0,2,1:T(8,128)(2,1)}, u32[]{:S(2)}, u32[]{:S(2)}) %all-to-all-start.4) | async-done | bytes 524320 | tf_op jit(solution)/shard_map/all_to_all | solution.py:229
  366.9 34.1 %while.28 = (s32[]{:T(128)}, f32[1024,4,64]{0,2,1:T(8,128)S(1)}, f32[1024,4,64]{0,2,1:T(8,128)S(1)}, bf16[2,512,4,64]{1,3,2,0:T(8,128)(2,1)}, bf16[2,512,4,64]{1...) while((s32[]{:T(128)}, f32[1024,4,64]{0,2,1:T(8,128)S(1)}, ...), condition=%wide.region_12.13_spmd.clone, body=%wide.region_10.12_spmd.clone.sunk | while | flops 1368913920 | bytes 164422032 | solution.py:148
  411.0 9.6 all-to-all-done.7
  427.2 10.8 %all-to-all-done.5 = bf16[4,256,256]{1,2,0:T(8,128)(2,1)S(1)} async-done(((bf16[4,256,256]{1,2,0:T(8,128)(2,1)}), bf16[4,256,256]{1,2,0:T(8,128)(2,1)S(1)}, u32[]{:S(2)}, u32[]{:S(2)}) %all-to-all-start.5) | async-done | bytes 524320 | tf_op jit(solution)/shard_map/all_to_all | solution.py:240
  448.2 14.2 %reduce.20 = bf16[1024,1024]{1,0:T(8,128)(2,1)} reduce(bf16[1024,1,1024]{2,1,0:T(2,128)(2,1)} %bitcast.259, bf16[]{:T(256)} %broadcast.177), dimensions={1}, to_apply=%bitcast.213.reduce_sub_computation | reduce | bytes 4194306
  479.6 26.8 %copy.163 = bf16[1,1024,2624]{2,0,1:T(2,128)(2,1)} copy(bf16[1,1024,2624]{1,2,0:T(8,128)(2,1)} %fusion.42) | data formatting | bytes 10747904 | tf_op jit(solution)/shard_map/convert_element_type | solution.py:277
  506.4 34.3 %reduce.22 = bf16[1024,2624]{1,0:T(8,128)(2,1)} reduce(bf16[1024,1,2624]{2,1,0:T(2,128)(2,1)} %bitcast.254, bf16[]{:T(256)} %broadcast.177), dimensions={1}, to_apply=%bitcast.173.reduce_sub_computation | reduce | bytes 10747906
  540.8 10.1 %reshape.307 = bf16[8,2,167936]{2,1,0:T(2,128)(2,1)} reshape(bf16[1024,2624]{1,0:T(8,128)(2,1)} %reduce.22) | data formatting | bytes 10747904
  561.0 57.7 %copy.186 = bf16[1,1024,3072]{2,0,1:T(2,128)(2,1)} copy(bf16[1,1024,3072]{2,1,0:T(8,128)(2,1)S(1)} %convert_bitcast_fusion) | data formatting | bytes 12582912 | tf_op jit(solution)/shard_map/convert_element_type | solution.py:265
  618.7 37.8 %reduce.19 = bf16[1024,3072]{1,0:T(8,128)(2,1)} reduce(bf16[1024,1,3072]{2,1,0:T(2,128)(2,1)} %bitcast.253, bf16[]{:T(256)} %broadcast.177), dimensions={1}, to_apply=%bitcast.212.reduce_sub_computation | reduce | bytes 12582914
  656.6 9.4 reshape.309
  676.0 18.5 %copy.185 = bf16[1,1024,5248]{2,0,1:T(2,128)(2,1)} copy(bf16[1,1024,5248]{2,1,0:T(8,128)(2,1)S(1)} %fusion.41) | data formatting | bytes 21495808 | tf_op jit(solution)/shard_map/convert_element_type | solution.py:274
  694.5 66.9 %reduce.21 = bf16[1024,5248]{1,0:T(8,128)(2,1)} reduce(bf16[1024,1,5248]{2,1,0:T(2,128)(2,1)} %bitcast.250, bf16[]{:T(256)} %broadcast.177), dimensions={1}, to_apply=%bitcast.211.reduce_sub_computation | reduce | bytes 21495810
  761.4 11.3 %reshape.313 = bf16[8,2,335872]{2,1,0:T(2,128)(2,1)} reshape(bf16[1024,5248]{1,0:T(8,128)(2,1)} %reduce.21) | data formatting | bytes 21495808
  792.1 11.9 %reshape.308 = bf16[1024,1,2624]{2,1,0:T(2,128)(2,1)} reshape(bf16[8,2,167936]{2,1,0:T(2,128)(2,1)} %all-to-all-done.13) | data formatting | bytes 10747904
  815.7 11.0 %reshape.310 = bf16[1024,1,3072]{2,1,0:T(2,128)(2,1)} reshape(bf16[8,2,196608]{2,1,0:T(2,128)(2,1)} %all-to-all-done.9) | data formatting | bytes 12582912
  826.8 9.7 copy.171
  841.8 52.0 %all-to-all-done.12 = bf16[8,2,335872]{2,1,0:T(2,128)(2,1)} async-done(((bf16[8,2,335872]{2,1,0:T(2,128)(2,1)}), bf16[8,2,335872]{2,1,0:T(2,128)(2,1)}, u32[]{:S(2)}, u32[]{:S(2)}) %all-to-all-start.12) | async-done | bytes 10747936 | tf_op jit(solution)/shard_map/all_to_all | solution.py:273
  893.8 15.9 %reshape.314 = bf16[1024,1,5248]{2,1,0:T(2,128)(2,1)} reshape(bf16[8,2,335872]{2,1,0:T(2,128)(2,1)} %all-to-all-done.12) | data formatting | bytes 21495808
  909.7 15.0 %copy.173 = bf16[1,1024,5248]{2,1,0:T(8,128)(2,1)} copy(bf16[1,1024,5248]{2,0,1:T(2,128)(2,1)} %bitcast.251) | data formatting | bytes 21495808
  960.1 10.4 %all-reduce.5 = (bf16[128]{0:T(256)(128)(2,1)S(1)}, bf16[128]{0:T(256)(128)(2,1)S(1)}) all-reduce(bf16[128]{0:T(256)(128)(2,1)S(1)} %reduce_sum.189, bf16[128]{0:T(256)(128)(2,1)S(1)} %reduce_sum.193), channel_id=2, replica_groups=mesh['dp'=8,'seq'=4] {'seq'}, use_global_device_ids=true, to_apply=%region_17.18.clone | all-reduce | flops 256 | bytes 1024
  (266 shorter events, 275.7 us)
Async XLA Ops:
  7.2 75.9 %all-gather.5.cloned.1.call-start = ((), (), s32[]{:S(2)}) async-start(), calls=%async_computation.18 | async-start | bytes 6488064 | tf_op jit(solution)/shard_map/all_gather | solution.py:174
  7.9 181.3 %all-gather.7.cloned.1.call-start = ((), (), s32[]{:S(2)}) async-start(), calls=%async_computation.19 | async-start | bytes 2162688 | tf_op jit(solution)/shard_map/all_gather | solution.py:175
  8.6 243.4 %all-gather.9.cloned.1.call-start = ((), (), s32[]{:S(2)}) async-start(), calls=%async_computation.20 | async-start | bytes 11083776 | tf_op jit(solution)/shard_map/all_gather | solution.py:177
  9.4 310.0 %all-gather.11.cloned.1.call-start = ((), (), s32[]{:S(2)}) async-start(), calls=%async_computation.21 | async-start | bytes 5677056 | tf_op jit(solution)/shard_map/all_gather | solution.py:178
  108.4 20.3 %all-to-all-start = ((bf16[256,4,256]{0,2,1:T(8,128)(2,1)}), bf16[256,4,256]{0,2,1:T(8,128)(2,1)}, u32[]{:S(2)}, u32[]{:S(2)}) async-start(bf16[256,4,256]{0,2,1:T(8,128)(2,1)} %bitcast.274), calls=%async_computation | async-start | bytes 1048576 | tf_op jit(solution)/shard_map/all_to_all | solution.py:188
  128.8 22.2 %all-to-all-start.1 = ((bf16[256,4,256]{2,0,1:T(8,128)(2,1)}), bf16[256,4,256]{2,0,1:T(8,128)(2,1)}, u32[]{:S(2)}, u32[]{:S(2)}) async-start(bf16[256,4,256]{2,0,1:T(8,128)(2,1)} %bitcast.273), calls=%async_computation.1 | async-start | bytes 1048576 | tf_op jit(solution)/shard_map/all_to_all | solution.py:189
  151.0 21.0 %all-to-all-start.2 = ((bf16[256,4,256]{2,0,1:T(8,128)(2,1)}), bf16[256,4,256]{2,0,1:T(8,128)(2,1)S(1)}, u32[]{:S(2)}, u32[]{:S(2)}) async-start(bf16[256,4,256]{2,0,1:T(8,128)(2,1)} %bitcast.209), calls=%async_computation.2 | async-start | bytes 1048576 | tf_op jit(solution)/shard_map/all_to_all | solution.py:190
  185.1 26.0 %all-to-all-start.3 = ((bf16[4,256,256]{1,2,0:T(8,128)(2,1)}), bf16[4,256,256]{1,2,0:T(8,128)(2,1)S(1)}, u32[]{:S(2)}, u32[]{:S(2)}) async-start(bf16[4,256,256]{1,2,0:T(8,128)(2,1)} %copy.147), calls=%async_computation.3 | async-start | bytes 1048576 | tf_op jit(solution)/shard_map/all_to_all | solution.py:193
  189.2 145.4 %copy-start.27 = (f32[1024]{0:T(1024)}, f32[1024]{0:T(1024)S(1)}, u32[]{:S(2)}) copy-start(f32[1024]{0:T(1024)S(1)} %convert_element_type.229) | copy-start | bytes 12292
  211.1 49.8 %copy-start.14 = (bf16[4,256,256]{1,2,0:T(8,128)(2,1)}, bf16[4,256,256]{1,2,0:T(8,128)(2,1)S(1)}, u32[]{:S(2)}) copy-start(bf16[4,256,256]{1,2,0:T(8,128)(2,1)S(1)} %all-to-all-done.3) | copy-start | bytes 1572868
  213.7 120.8 %copy-start.3 = (f32[256,1024]{1,0:T(8,128)}, f32[256,1024]{1,0:T(8,128)S(1)}, u32[]{:S(2)}) copy-start(f32[256,1024]{1,0:T(8,128)S(1)} %get-tuple-element.292) | copy-start | bytes 3145732
  213.8 120.8 %copy-start.31 = (f32[256]{0:T(256)}, f32[256]{0:T(256)S(1)}, u32[]{:S(2)}) copy-start(f32[256]{0:T(256)S(1)} %broadcast_multiply_fusion.7) | copy-start | bytes 3076
  214.0 120.6 %copy-start.33 = (f32[256]{0:T(256)}, f32[256]{0:T(256)S(1)}, u32[]{:S(2)}) copy-start(f32[256]{0:T(256)S(1)} %add_rsqrt_fusion) | copy-start | bytes 3076
  214.0 105.4 %copy-start.18 = (bf16[1,256,1024]{2,1,0:T(8,128)(2,1)S(1)}, bf16[1,256,1024]{2,1,0:T(8,128)(2,1)}, u32[]{:S(2)}) copy-start(bf16[1,256,1024]{2,1,0:T(8,128)(2,1)} %param.21) | copy-start | bytes 1572868
  340.6 18.8 %all-to-all-start.4 = ((bf16[256,4,256]{0,2,1:T(8,128)(2,1)}), bf16[256,4,256]{0,2,1:T(8,128)(2,1)}, u32[]{:S(2)}, u32[]{:S(2)}) async-start(bf16[256,4,256]{0,2,1:T(8,128)(2,1)} %bitcast.19), calls=%async_computation.4 | async-start | bytes 1048576 | tf_op jit(solution)/shard_map/all_to_all | solution.py:229
  401.5 40.2 %copy-start.10 = (f32[256,1024]{1,0:T(8,128)S(1)}, f32[256,1024]{1,0:T(8,128)}, u32[]{:S(2)}) copy-start(f32[256,1024]{1,0:T(8,128)} %copy-done.9) | copy-start | bytes 3145732
  401.5 40.2 %copy-start.15 = (bf16[4,256,256]{1,2,0:T(8,128)(2,1)S(1)}, bf16[4,256,256]{1,2,0:T(8,128)(2,1)}, u32[]{:S(2)}) copy-start(bf16[4,256,256]{1,2,0:T(8,128)(2,1)} %copy-done.14) | copy-start | bytes 1572868
  402.4 18.2 %all-to-all-start.7 = ((bf16[4,256,256]{1,2,0:T(8,128)(2,1)}), bf16[4,256,256]{1,2,0:T(8,128)(2,1)}, u32[]{:S(2)}, u32[]{:S(2)}) async-start(bf16[4,256,256]{1,2,0:T(8,128)(2,1)} %copy.157), calls=%async_computation.7 | async-start | bytes 1048576 | tf_op jit(solution)/shard_map/all_to_all | solution.py:242
  420.6 17.4 %all-to-all-start.5 = ((bf16[4,256,256]{1,2,0:T(8,128)(2,1)}), bf16[4,256,256]{1,2,0:T(8,128)(2,1)S(1)}, u32[]{:S(2)}, u32[]{:S(2)}) async-start(bf16[4,256,256]{1,2,0:T(8,128)(2,1)} %copy.155), calls=%async_computation.5 | async-start | bytes 1048576 | tf_op jit(solution)/shard_map/all_to_all | solution.py:240
  438.0 30.7 %all-to-all-start.6 = ((bf16[4,256,256]{1,2,0:T(8,128)(2,1)}), bf16[4,256,256]{1,2,0:T(8,128)(2,1)S(1)}, u32[]{:S(2)}, u32[]{:S(2)}) async-start(bf16[4,256,256]{1,2,0:T(8,128)(2,1)} %copy.156), calls=%async_computation.6 | async-start | bytes 1048576 | tf_op jit(solution)/shard_map/all_to_all | solution.py:241
  468.7 82.2 %all-to-all-start.10 = ((bf16[8,2,65536]{2,1,0:T(2,128)(2,1)}), bf16[8,2,65536]{2,1,0:T(2,128)(2,1)}, u32[]{:S(2)}, u32[]{:S(2)}) async-start(bf16[8,2,65536]{2,1,0:T(2,128)(2,1)} %reshape.311), calls=%async_computation.11 | async-start | bytes 4194304 | tf_op jit(solution)/shard_map/all_to_all | solution.py:267
  550.8 115.1 %all-to-all-start.13 = ((bf16[8,2,167936]{2,1,0:T(2,128)(2,1)}), bf16[8,2,167936]{2,1,0:T(2,128)(2,1)}, u32[]{:S(2)}, u32[]{:S(2)}) async-start(bf16[8,2,167936]{2,1,0:T(2,128)(2,1)} %reshape.307), calls=%async_computation.16 | async-start | bytes 10747904 | tf_op jit(solution)/shard_map/all_to_all | solution.py:276
  557.5 61.2 %copy-start.20 = (bf16[256,1024]{0,1:T(8,128)(2,1)}, bf16[256,1024]{0,1:T(8,128)(2,1)S(1)}, u32[]{:S(2)}) copy-start(bf16[256,1024]{0,1:T(8,128)(2,1)S(1)} %get-tuple-element.283) | copy-start | bytes 1572868
  557.5 61.2 %copy-start.22 = (bf16[256,1024]{0,1:T(8,128)(2,1)}, bf16[256,1024]{0,1:T(8,128)(2,1)S(1)}, u32[]{:S(2)}) copy-start(bf16[256,1024]{0,1:T(8,128)(2,1)S(1)} %get-tuple-element.284) | copy-start | bytes 1572868
  666.0 106.8 %all-to-all-start.9 = ((bf16[8,2,196608]{2,1,0:T(2,128)(2,1)}), bf16[8,2,196608]{2,1,0:T(2,128)(2,1)}, u32[]{:S(2)}, u32[]{:S(2)}) async-start(bf16[8,2,196608]{2,1,0:T(2,128)(2,1)} %reshape.309), calls=%async_computation.9 | async-start | bytes 12582912 | tf_op jit(solution)/shard_map/all_to_all | solution.py:264
  772.7 121.1 %all-to-all-start.12 = ((bf16[8,2,335872]{2,1,0:T(2,128)(2,1)}), bf16[8,2,335872]{2,1,0:T(2,128)(2,1)}, u32[]{:S(2)}, u32[]{:S(2)}) async-start(bf16[8,2,335872]{2,1,0:T(2,128)(2,1)} %reshape.313), calls=%async_computation.14 | async-start | bytes 21495808 | tf_op jit(solution)/shard_map/all_to_all | solution.py:273
  777.9 193.7 %reduce-scatter.9.cloned.1.call-start = ((), (), s32[]{:S(2)}) async-start(), calls=%async_computation.23 | async-start | bytes 327680 | tf_op jit(solution)/shard_map/reduce_scatter | solution.py:282
  791.8 181.4 %reduce-scatter.13.cloned.1.call-start = ((), (), s32[]{:S(2)}) async-start(), calls=%async_computation.25 | async-start | bytes 860160
  815.7 159.7 %reduce-scatter.7.cloned.1.call-start = ((), (), s32[]{:S(2)}) async-start(), calls=%async_computation.22 | async-start | bytes 983040 | tf_op jit(solution)/shard_map/reduce_scatter | solution.py:282
  841.5 135.7 %reduce-scatter.11.cloned.1.call-start = ((), (), s32[]{:S(2)}) async-start(), calls=%async_computation.24 | async-start | bytes 1679360 | tf_op jit(solution)/shard_map/reduce_scatter | solution.py:282
  933.7 12.3 %all-to-all-start.11 = ((bf16[1,8,128]{2,0,1:T(2,128)(2,1)}), bf16[1,8,128]{2,0,1:T(2,128)(2,1)S(1)}, u32[]{:S(2)}, u32[]{:S(2)}) async-start(bf16[1,8,128]{2,0,1:T(2,128)(2,1)} %copy.161), calls=%async_computation.13 | async-start | bytes 8192 | tf_op jit(solution)/shard_map/all_to_all | solution.py:270
  951.9 8.2 all-to-all-start.8
  (39 other events, 330.9 us)
Sparse Core Ops, SparseCore 0:
  10.9 72.1 all-gather.4
  86.0 61.7 all-gather.6
  150.6 101.3 all-gather.8
  254.7 64.6 all-gather.10
  791.9 19.2 reduce-scatter.8
  815.8 21.3 reduce-scatter.12
  841.6 23.1 reduce-scatter.6
  931.9 33.9 reduce-scatter.10
where the time goes:
time: 999 us; the launch traced here: 986 us
  local copies, waits for them, and re-layouts  282 us (28%)
  waiting for transfers between devices  281 us (28%)
  other arithmetic  204 us (20%)
  matrix products  86.5 us (9%)
  starting transfers between devices  64.6 us (6%)
  blocking collectives  51.9 us (5%)
  between operations  15.9 us (2%)
    unnamed x6, other arithmetic  153 us
    unnamed x87, local copies, waits for them, and re-layouts  128 us
    all_gather x1, waiting for transfers between devices, per_device(): lax.all_gather(down_weight, ('dp', 'seq'), axis=0, tiled=True)  58.5 us
    convert_element_type x1, local copies, waits for them, and re-layouts, per_device(): qkv_grad[None].astype(jnp.bfloat16)  57.7 us
    all_to_all x1, waiting for transfers between devices, per_device(): lax.all_to_all(up_grad[None].astype(jnp.bfloat16), 'dp', split_axis=1, co...  52 us
    unnamed x2, blocking collectives  51.9 us
    all_gather x1, waiting for transfers between devices, per_device(): lax.all_gather(up_weight, ('dp', 'seq'), axis=0, tiled=True)  38 us
    convert_element_type x1, local copies, waits for them, and re-layouts, per_device(): down_grad[None].astype(jnp.bfloat16)  26.8 us
  transfers between devices with their start and end apart: 22, of which 12 were waited for; matrix products, arithmetic and copies ran while one was open for 51% of the time, Pallas kernels for 0%

commit v1 on v0

--- a/solution.py
+++ b/solution.py
@@ -294,10 +294,245 @@
         grads[5],
     )
 
+QUAD_MESH = (8, 4)
+FLAT = ("dp", "seq")
+
+
+def pairs_of(step):
+    found = []
+    for dp in range(8):
+        for seq in range(4):
+            place = (dp // 4, dp // 2 % 2, dp % 2, seq // 2, seq % 2)
+            target = step(*place)
+            if target is not None:
+                y, x, c, zh, zl = target
+                found.append((dp * 4 + seq, (4 * y + 2 * x + c) * 4 + 2 * zh + zl))
+    return found
+
+
+TO_X = pairs_of(lambda y, x, c, zh, zl: (y, 1 - x, c, zh, zl))
+TO_Y = pairs_of(lambda y, x, c, zh, zl: (1 - y, x, c, zh, zl))
+TO_XY = pairs_of(lambda y, x, c, zh, zl: (1 - y, 1 - x, c, zh, zl))
+TO_CORE = pairs_of(lambda y, x, c, zh, zl: (y, x, 1 - c, zh, zl))
+TO_ZH = pairs_of(lambda y, x, c, zh, zl: (y, x, c, 1 - zh, zl))
+TO_ZL = pairs_of(lambda y, x, c, zh, zl: (y, x, c, zh, 1 - zl))
+TO_HOME = pairs_of(lambda y, x, c, zh, zl: (y, x, zh, c, zl))
+ENTER = pairs_of(
+    lambda y, x, c, zh, zl: (y, x, c, zh, 1 - zl) if c == zh else (y, x, zh, c, zl)
+)
+ENTER_MOVED = pairs_of(lambda y, x, c, zh, zl: None if c == zh else (y, x, c, zh, 1 - zl))
+
+
+def send(array, pairs):
+    return lax.ppermute(array, FLAT, pairs)
+
+
+def pick(array, index, axis=0):
+    return lax.dynamic_index_in_dim(array, index, axis, keepdims=False)
+
+
+def in_order(bit, own, received, axis):
+    return jnp.where(
+        bit == 0, jnp.stack([own, received], axis), jnp.stack([received, own], axis)
+    )
+
+
+def enter_quad(block, place):
+    at_home = place["c"] == place["zh"]
+    first = send(block, ENTER)
+    second = send(first, ENTER_MOVED)
+    own = jnp.where(at_home, block, first)
+    other = jnp.where(at_home, first, second)
+    near = jnp.stack([own, other])
+    return jnp.concatenate([near, send(near, TO_CORE)])
+
+
+def quad_gather(block):
+    near = jnp.stack([block, send(block, TO_ZL)])
+    return jnp.concatenate([near, send(near, TO_CORE)])
+
+
+def quad_scatter(parts):
+    far = send(parts[2:].astype(jnp.bfloat16), TO_CORE)
+    near = parts[:2] + far.astype(jnp.float32)
+    return near[0] + send(near[1].astype(jnp.bfloat16), TO_ZL).astype(jnp.float32)
+
+
+def gather_columns(slices, place):
+    c, zl, zh, xy = place["c"], place["zl"], place["zh"], place["xy"]
+    both = in_order(c, pick(slices, c), send(pick(slices, 1 - c), TO_CORE), 0)
+    quad = in_order(zl, pick(both, zl, 1), send(pick(both, 1 - zl, 1), TO_ZL), 1)
+    line = in_order(zh, quad, send(quad, TO_ZH), 1)
+    pieces = jnp.stack([line, send(line, TO_X), send(line, TO_Y), send(line, TO_XY)])
+    return jnp.stack([pick(pieces, xy ^ i) for i in range(4)])
+
+
+def scatter_columns(grad, place):
+    c, zl, zh, xy = place["c"], place["zl"], place["zh"], place["xy"]
+    wide = jnp.float32
+    total = pick(grad, xy).astype(wide)
+    for i, pairs in ((1, TO_X), (2, TO_Y), (3, TO_XY)):
+        total = total + send(pick(grad, xy ^ i), pairs).astype(wide)
+    part = send(pick(total, 1 - zh, 1).astype(jnp.bfloat16), TO_ZH).astype(wide)
+    quad = (pick(total, zh, 1) + part).astype(jnp.bfloat16)
+    both = in_order(zl, pick(quad, zl, 1), send(pick(quad, 1 - zl, 1), TO_ZL), 0)
+    rows = in_order(c, pick(both, c, 1), send(pick(both, 1 - c, 1), TO_CORE), 0)
+    return rows.astype(wide)
+
+
+def quad_device(
+    inputs,
+    positions,
+    attn_gain,
+    qkv_weight,
+    attn_out_weight,
+    mlp_gain,
+    up_weight,
+    down_weight,
+    cotangent,
+):
+    dp, seq = lax.axis_index("dp"), lax.axis_index("seq")
+    place = {"c": dp % 2, "xy": dp // 2, "zl": seq % 2, "zh": seq // 2}
+    group = 2 * place["c"] + place["zl"]
+    low, wide = jnp.bfloat16, jnp.float32
+    rows, width = qkv_weight.shape[0], attn_out_weight.shape[1]
+    tokens = inputs.shape[1]
+    part, ff_part = width // 4, FF // 4
+    heads = HEADS // 4
+
+    pos = positions[0]
+    pos_row = jnp.concatenate([pos // 128, pos % 128]).astype(low)
+    pos_row = jnp.pad(pos_row[None], ((0, 15), (0, width - 2 * tokens)))
+    entered = enter_quad(jnp.concatenate([inputs[0], pos_row]), place)
+    all_in = entered[:, :tokens].reshape(4 * tokens, width)
+    pos_all = entered[:, tokens, : 2 * tokens].astype(wide)
+    pos_all = (pos_all[:, :tokens] * 128.0 + pos_all[:, tokens:]).reshape(4 * tokens)
+
+    gain_one, gain_two = attn_gain.astype(wide)[:, None], mlp_gain.astype(wide)[:, None]
+    qkv_scaled = (qkv_weight.astype(wide) * gain_one).astype(low)
+    qkv_slices = qkv_scaled.reshape(rows, 3, 4, part).transpose(2, 0, 1, 3)
+    w_qkv = gather_columns(qkv_slices.reshape(2, 2, rows, 3 * part), place)
+    w_qkv = w_qkv.reshape(width, 3 * part)
+    out_slices = attn_out_weight.reshape(rows, 4, part).transpose(1, 0, 2)
+    w_out = gather_columns(out_slices.reshape(2, 2, rows, part), place).reshape(width, part)
+    up_scaled = (up_weight.astype(wide) * gain_two).astype(low)
+    ff_all = jnp.concatenate([up_scaled, down_weight], axis=1)
+    ff_slices = ff_all.reshape(rows, 3, 4, ff_part).transpose(2, 1, 0, 3)
+    ff_slices = ff_slices.reshape(2, 2, 3 * rows, ff_part)
+    w_ff = gather_columns(ff_slices, place).reshape(32, 3, rows, ff_part)
+    w_inner = w_ff[:, 0].reshape(width, ff_part)
+    w_gate = w_ff[:, 1].reshape(width, ff_part)
+    w_down = w_ff[:, 2].reshape(width, ff_part)
+    w_cols = quad_gather(w_out)
+    w_cols = jnp.stack([pick(w_cols, group ^ i) for i in range(4)], axis=1)
+    w_rows = w_cols.reshape(4, part, width)
+    w_rows = jnp.concatenate([pick(w_rows, group ^ i) for i in range(4)])
+
+    cot = enter_quad(cotangent[0], place).reshape(4 * tokens, width)
+
+    cos_table, sin_table = rope_tables(pos_all)
+    normed_one, spread_one = normalize(all_in.astype(wide))
+    low_one = normed_one.astype(low)
+    mixed = jnp.dot(low_one, w_qkv, preferred_element_type=wide)
+    shaped = (4 * tokens, heads, HEAD_DIM)
+    queries = rotate(mixed[:, :part].reshape(shaped), cos_table, sin_table)
+    key_rows = rotate(mixed[:, part : 2 * part].reshape(shaped), cos_table, sin_table)
+    queries = queries.reshape(4 * tokens, part).astype(low)
+    key_rows = key_rows.reshape(4 * tokens, part).astype(low)
+    values = mixed[:, 2 * part :].astype(low)
+    attended, log_totals = attend_forward(queries, key_rows, values)
+
+    blocks = attended.reshape(2, 2, tokens, part)
+    side = send(blocks, TO_ZL)[:, ::-1]
+    near = jnp.stack([blocks, side])
+    far = send(near, TO_CORE)[:, ::-1]
+    every = jnp.concatenate([near, far]).reshape(4, 4 * tokens, part)
+    every = every.transpose(1, 0, 2).reshape(4 * tokens, width)
+    resid = all_in.astype(wide) + jnp.dot(every, w_rows, preferred_element_type=wide)
+    normed_two, spread_two = normalize(resid)
+    low_two = normed_two.astype(low)
+    inner_act = jnp.dot(low_two, w_inner, preferred_element_type=wide)
+    gate_act = jnp.dot(low_two, w_gate, preferred_element_type=wide)
+    gelu_val, gelu_slope = gelu_parts(inner_act)
+    hidden = (gelu_val * gate_act).astype(low)
+    d_hidden = jnp.dot(cot, w_down, preferred_element_type=wide)
+    d_inner = (d_hidden * gate_act * gelu_slope).astype(low)
+    d_gate = (d_hidden * gelu_val).astype(low)
+
+    def back(grad_rows, weight):
+        return jnp.einsum("tn,kn->tk", grad_rows, weight, preferred_element_type=wide)
+
+    def outer(left, right):
+        return jnp.einsum("tk,tn->kn", left, right, preferred_element_type=wide)
+
+    d_norm = back(d_inner, w_inner) + back(d_gate, w_gate)
+    scaled = quad_scatter(d_norm.reshape(4, tokens, width))
+    own_two, own_spread = normed_two[:tokens], spread_two[:tokens]
+
+    def norm_grad(scaled, normed, spread):
+        return spread * (
+            scaled
+            - jnp.mean(scaled, axis=-1, keepdims=True)
+            - normed * jnp.mean(scaled * normed, axis=-1, keepdims=True)
+        )
+
+    d_resid = cot[:tokens].astype(wide) + norm_grad(scaled, own_two, own_spread)
+    d_resid_all = quad_gather(d_resid.astype(low)).reshape(4 * tokens, width)
+    d_attended = back(d_resid_all, w_rows[:part]).astype(low)
+    d_q, d_k, d_v = attend_backward(queries, key_rows, values, d_attended, log_totals)
+
+    out_parts = back(hidden, w_down)
+    mlp_out = quad_scatter(out_parts.reshape(4, tokens, width))
+    output = send((resid[:tokens] + mlp_out).astype(low), TO_HOME)
+
+    ff_grad = jnp.stack(
+        [outer(low_two, d_inner), outer(low_two, d_gate), outer(cot, hidden)]
+    ).astype(low)
+    ff_grad = ff_grad.reshape(3, 32, rows, ff_part).transpose(1, 0, 2, 3)
+    ff_grad = scatter_columns(ff_grad.reshape(4, 2, 2, 2, 3 * rows, ff_part), place)
+    ff_grad = ff_grad.reshape(4, 3, rows, ff_part).transpose(2, 1, 0, 3).reshape(rows, 3, FF)
+
+    own_cols = lax.dynamic_slice(d_resid_all, (0, part * group), (4 * tokens, part))
+    out_grad = outer(every, own_cols).astype(low).reshape(4, part, part)
+    out_grad = jnp.stack([pick(out_grad, group ^ i) for i in range(4)])
+    out_grad = scatter_columns(out_grad.reshape(4, 2, 2, 2, rows, part), place)
+    out_grad = out_grad.reshape(4, rows, part).transpose(1, 0, 2).reshape(rows, width)
+
+    dq_pre = rotate_back(d_q.astype(wide).reshape(shaped), cos_table, sin_table)
+    dk_pre = rotate_back(d_k.astype(wide).reshape(shaped), cos_table, sin_table)
+    d_mixed = jnp.concatenate(
+        [
+            dq_pre.reshape(4 * tokens, part).astype(low),
+            dk_pre.reshape(4 * tokens, part).astype(low),
+            d_v,
+        ],
+        axis=1,
+    )
+    d_norm = back(d_mixed, w_qkv)
+    scaled = quad_scatter(d_norm.reshape(4, tokens, width))
+    d_first = norm_grad(scaled, normed_one[:tokens], spread_one[:tokens])
+    input_grad = send((d_resid + d_first).astype(low), TO_HOME)
+
+    qkv_grad = outer(low_one, d_mixed).astype(low)
+    qkv_grad = scatter_columns(qkv_grad.reshape(4, 2, 2, 2, rows, 3 * part), place)
+    qkv_grad = qkv_grad.reshape(4, rows, 3, part).transpose(1, 2, 0, 3).reshape(rows, 3 * width)
+
+    up_grad = ff_grad[:, :2].reshape(rows, 2 * FF)
+    return (
+        output[None],
+        input_grad[None],
+        jnp.sum(qkv_grad * qkv_weight.astype(wide), axis=1),
+        qkv_grad * gain_one,
+        out_grad,
+        jnp.sum(up_grad * up_weight.astype(wide), axis=1),
+        up_grad * gain_two,
+        ff_grad[:, 2],
+    )
+
 
 def solution(mesh):
     return jax.shard_map(
-        per_device,
+        quad_device if tuple(mesh.shape.values()) == QUAD_MESH else per_device,
         mesh=mesh,
         in_specs=(
             P("dp", "seq", None),

time: 999 us -> 495 us (0.50)
  local copies, waits for them, and re-layouts: 282 us -> 92.6 us
  other arithmetic: 204 us -> 63.3 us
  waiting for transfers between devices: 281 us -> 174 us
  blocking collectives: 51.9 us -> 0 us
  between operations: 15.9 us -> 2.75 us
  starting transfers between devices: 64.6 us -> 77.4 us
  matrix products: 86.5 us -> 75.2 us
    ppermute x0 -> x56, waiting for transfers between devices: none -> 174 us  [send(): return lax.ppermute(array, FLAT, pairs)]
    all_to_all x14 -> x0, waiting for transfers between devices: 157 us -> none  [the longest x1 52 us: per_device(): lax.all_to_all(up_grad[None].astype(jnp.bfloat16), 'dp', split_axis=1, co...]
    unnamed x6 -> x7, other arithmetic: 153 us -> 1.35 us
    all_gather x4 -> x0, waiting for transfers between devices: 121 us -> none  [the longest x1 58.5 us: per_device(): lax.all_gather(down_weight, ('dp', 'seq'), axis=0, tiled=True)]
    unnamed x87 -> x124, local copies, waits for them, and re-layouts: 128 us -> 17.8 us
    convert_element_type x6 -> x8, local copies, waits for them, and re-layouts: 109 us -> 2 us  [the longest x2 1.67 us: quad_device(): dq_pre = rotate_back(d_q.astype(wide).reshape(shaped), cos_table, sin_table)]
    ppermute x0 -> x56, starting transfers between devices: none -> 77.4 us  [send(): return lax.ppermute(array, FLAT, pairs)]
    all_to_all x14 -> x0, starting transfers between devices: 63.9 us -> none  [the longest x1 6.73 us: per_device(): lax.all_to_all(gain_two_grad[None].astype(jnp.bfloat16), 'dp', split_axis...]
  transfers between devices with their start and end apart: 22 -> 56, of which waited for: 12 -> 22; matrix products, arithmetic and copies ran while one was open for 51% -> 33% of each run, Pallas kernels for 0% -> 0%
where the time goes in v1:
time: 495 us; the launch traced here: 486 us
  waiting for transfers between devices  174 us (35%)
  local copies, waits for them, and re-layouts  92.6 us (19%)
  starting transfers between devices  77.4 us (16%)
  matrix products  75.2 us (15%)
  other arithmetic  63.3 us (13%)
    ppermute x56, waiting for transfers between devices, send(): return lax.ppermute(array, FLAT, pairs)  174 us
    ppermute x56, starting transfers between devices, send(): return lax.ppermute(array, FLAT, pairs)  77.4 us
    unnamed x124, local copies, waits for them, and re-layouts  17.8 us
    dot_general x5, matrix products, outer(): return jnp.einsum('tk,tn->kn', left, right, preferred_element_type=wide)  14.8 us
    dot_general x5, matrix products, back(): jnp.einsum('tn,kn->tk', grad_rows, weight, preferred_element_type=wide)  11.1 us
  transfers between devices with their start and end apart: 56, of which 22 were waited for; matrix products, arithmetic and copies ran while one was open for 33% of the time, Pallas kernels for 0%

profile of v1, /device:TPU:1, one launch (start us, length us, event | category | flops | bytes accessed | tf_op | source)
XLA Modules:
  0.0 485.7 jit_solution(11752861661531615874)
XLA Ops:
  7.3 3.7 collective-permute-start
  13.4 21.6 %collective-permute-done.12 = bf16[2,32,256]{2,1,0:T(8,128)(2,1)S(1)} collective-permute-done((bf16[2,32,256]{2,1,0:T(8,128)(2,1)S(1)}, bf16[2,32,256]{2,1,0:T(8,128)(2,1)S(1)}, u32[]{:S(2)}, u32[]{:S(2)}) %collective-permute-start.12) | collective-permute-done | bytes 32800 | tf_op jit(solution)/shard_map/ppermute | solution.py:327
  50.4 4.4 collective-permute-done.5
  56.8 5.3 %collective-permute-start.8 = (bf16[2,2,2,32,768]{4,3,2,0,1:T(8,128)(2,1)S(1)}, bf16[2,2,2,32,768]{4,3,2,0,1:T(8,128)(2,1)S(1)}, u32[]{:S(2)}, u32[]{:S(2)}) collective-permute-start(bf16[2,2,2,32,768]{4,3,2,0,1:T(8,128)(2,1)S(1)} %maximum_select_fusion.8), channel_id=1, source_target_pairs={{0,24},{1,25},{2,26},{3,27},{4,28},{5,29},{6,30},{7,31},{8,16},{9,... | collective-permute-start | bytes 1179656 | tf_op jit(solution)/shard_map/ppermute | solution.py:327
  62.4 6.0 %collective-permute-done.17 = bf16[1024,256]{1,0:T(8,128)(2,1)S(1)} collective-permute-done((bf16[1024,256]{1,0:T(8,128)(2,1)S(1)}, bf16[1024,256]{1,0:T(8,128)(2,1)S(1)}, u32[]{:S(2)}, u32[]{:S(2)}) %collective-permute-start.17) | collective-permute-done | bytes 524320 | tf_op jit(solution)/shard_map/ppermute | solution.py:327
  73.4 4.1 collective-permute-start.29
  83.9 13.8 %collective-permute-done.21 = bf16[2,2,96,656]{3,2,1,0:T(8,128)(2,1)S(1)} collective-permute-done((bf16[2,2,96,656]{3,2,1,0:T(8,128)(2,1)S(1)}, bf16[2,2,96,656]{3,2,1,0:T(8,128)(2,1)S(1)}, u32[]{:S(2)}, u32[]{:S(2)}) %collective-permute-start.21) | collective-permute-done | bytes 503840 | tf_op jit(solution)/shard_map/ppermute | solution.py:327
  100.3 4.9 %collective-permute-start.23 = (bf16[2,2,2,96,656]{4,3,2,0,1:T(8,128)(2,1)}, bf16[2,2,2,96,656]{4,3,2,0,1:T(8,128)(2,1)}, u32[]{:S(2)}, u32[]{:S(2)}) collective-permute-start(bf16[2,2,2,96,656]{4,3,2,0,1:T(8,128)(2,1)} %maximum_select_fusion.1), channel_id=1, source_target_pairs={{0,16},{1,17},{2,18},{3,19},{4,20},{5,21},{6,22},{7,23},{8,24},{9,... | collective-permute-start | bytes 3022856 | tf_op jit(solution)/shard_map/ppermute | solution.py:327
  128.2 12.0 %while.27 = (s32[]{:T(128)}, bf16[2,512,4,64]{1,3,2,0:T(8,128)(2,1)}, f32[2,4,512]{2,1,0:T(4,128)S(1)}, bf16[2,512,4,64]{1,3,2,0:T(8,128)(2,1)S(1)}, bf16[1024,4...) while((s32[]{:T(128)}, bf16[2,512,4,64]{1,3,2,0:T(8,128)(2,1)}, ...), condition=%wide.region_5.6_spmd, body=%wide.region_2.5_spmd.sunk | while | flops 555874304 | bytes 28902000 | solution.py:101
  145.3 9.2 %collective-permute-done.23 = bf16[2,2,2,96,656]{4,3,2,0,1:T(8,128)(2,1)} collective-permute-done((bf16[2,2,2,96,656]{4,3,2,0,1:T(8,128)(2,1)}, bf16[2,2,2,96,656]{4,3,2,0,1:T(8,128)(2,1)}, u32[]{:S(2)}, u32[]{:S(2)}) %collective-permute-start.23) | collective-permute-done | bytes 1007648 | tf_op jit(solution)/shard_map/ppermute | solution.py:327
  155.6 3.9 pad_maximum_fusion
  161.5 5.8 %rev.6 = bf16[2,2,256,256]{2,1,3,0:T(2,128)(2,1)} reverse(bf16[2,2,256,256]{2,1,3,0:T(2,128)(2,1)} %collective-permute-done.9), dimensions={1} | reverse | bytes 1048576 | tf_op jit(solution)/shard_map/rev | solution.py:446
  167.3 3.8 pad_maximum_fusion.11
  182.2 4.0 copy.125
  198.7 4.5 copy.105
  203.3 4.8 fusion.130
  216.8 4.1 multiply_convert_fusion.1
  223.5 3.9 fusion.135
  229.3 4.6 convolution_convert_fusion.1
  236.5 3.9 fusion.69
  257.5 11.9 %collective-permute-done.50 = bf16[2,2,2,96,656]{4,3,2,1,0:T(8,128)(2,1)S(1)} collective-permute-done((bf16[2,2,2,96,656]{4,3,2,1,0:T(8,128)(2,1)S(1)}, bf16[2,2,2,96,656]{4,3,2,1,0:T(8,128)(2,1)S(1)}, u32[]{:S(2)}, u32[]{:S(2)}) %collective-permute-start.50) | collective-permute-done | bytes 1007648 | tf_op jit(solution)/shard_map/ppermute | solution.py:327
  270.2 25.6 %collective-permute-done.52 = bf16[2,2,2,96,656]{4,3,2,1,0:T(8,128)(2,1)S(1)} collective-permute-done((bf16[2,2,2,96,656]{4,3,2,1,0:T(8,128)(2,1)S(1)}, bf16[2,2,2,96,656]{4,3,2,1,0:T(8,128)(2,1)S(1)}, u32[]{:S(2)}, u32[]{:S(2)}) %collective-permute-start.52) | collective-permute-done | bytes 1007648 | tf_op jit(solution)/shard_map/ppermute | solution.py:327
  300.1 23.7 %collective-permute-done.53 = bf16[2,2,96,656]{3,2,1,0:T(8,128)(2,1)S(1)} collective-permute-done((bf16[2,2,96,656]{3,2,1,0:T(8,128)(2,1)S(1)}, bf16[2,2,96,656]{3,2,1,0:T(8,128)(2,1)S(1)}, u32[]{:S(2)}, u32[]{:S(2)}) %collective-permute-start.53) | collective-permute-done | bytes 503840 | tf_op jit(solution)/shard_map/ppermute | solution.py:327
  327.3 13.5 %collective-permute-done.54 = bf16[2,96,656]{2,1,0:T(8,128)(2,1)S(1)} collective-permute-done((bf16[2,96,656]{2,1,0:T(8,128)(2,1)S(1)}, bf16[2,96,656]{2,1,0:T(8,128)(2,1)S(1)}, u32[]{:S(2)}, u32[]{:S(2)}) %collective-permute-start.54) | collective-permute-done | bytes 251936 | tf_op jit(solution)/shard_map/ppermute | solution.py:327
  372.8 36.5 %while.28 = (s32[]{:T(128)}, f32[1024,4,64]{0,2,1:T(8,128)S(1)}, f32[1024,4,64]{0,2,1:T(8,128)S(1)}, bf16[2,512,4,64]{1,3,2,0:T(8,128)(2,1)}, bf16[2,512,4,64]{1...) while((s32[]{:T(128)}, f32[1024,4,64]{0,2,1:T(8,128)S(1)}, ...), condition=%wide.region_12.13_spmd.clone, body=%wide.region_10.12_spmd.clone.sunk | while | flops 1368913920 | bytes 147644784 | solution.py:148
  384.0 4.1 fusion.203
  402.2 4.1 fusion.203
  435.3 7.5 %collective-permute-done.40 = bf16[2,2,2,32,768]{4,3,2,1,0:T(8,128)(2,1)S(1)} collective-permute-done((bf16[2,2,2,32,768]{4,3,2,1,0:T(8,128)(2,1)S(1)}, bf16[2,2,2,32,768]{4,3,2,1,0:T(8,128)(2,1)S(1)}, u32[]{:S(2)}, u32[]{:S(2)}) %collective-permute-start.40) | collective-permute-done | bytes 393248 | tf_op jit(solution)/shard_map/ppermute | solution.py:327
  446.2 4.7 collective-permute-done.41
  452.4 9.6 %collective-permute-done.42 = bf16[2,32,768]{2,1,0:T(8,128)(2,1)S(1)} collective-permute-done((bf16[2,32,768]{2,1,0:T(8,128)(2,1)S(1)}, bf16[2,32,768]{2,1,0:T(8,128)(2,1)S(1)}, u32[]{:S(2)}, u32[]{:S(2)}) %collective-permute-start.42) | collective-permute-done | bytes 98336 | tf_op jit(solution)/shard_map/ppermute | solution.py:327
  465.4 4.2 collective-permute-start.37
  472.5 10.1 %collective-permute-done.37 = bf16[256,1024]{1,0:T(8,128)(2,1)S(1)} collective-permute-done((bf16[256,1024]{1,0:T(8,128)(2,1)S(1)}, bf16[256,1024]{1,0:T(8,128)(2,1)S(1)}, u32[]{:S(2)}, u32[]{:S(2)}) %collective-permute-start.37) | collective-permute-done | bytes 524320 | tf_op jit(solution)/shard_map/ppermute | solution.py:327
  (466 shorter events, 247.0 us)
Async XLA Ops:
  5.8 37.5 %collective-permute-start.19 = (bf16[2,96,656]{2,1,0:T(8,128)(2,1)}, bf16[2,96,656]{2,1,0:T(8,128)(2,1)}, u32[]{:S(2)}, u32[]{:S(2)}) collective-permute-start(bf16[2,96,656]{2,1,0:T(8,128)(2,1)} %get-tuple-element.278), channel_id=1, source_target_pairs={{0,4},{1,5},{2,6},{3,7},{4,0},{5,1},{6,2},{7,3},{8,12},{9,13},{10,... | collective-permute-start | bytes 755720 | tf_op jit(solution)/shard_map/ppermute | solution.py:327
  7.0 30.4 %collective-permute-start.3 = (bf16[2,32,768]{2,1,0:T(8,128)(2,1)S(1)}, bf16[2,32,768]{2,1,0:T(8,128)(2,1)S(1)}, u32[]{:S(2)}, u32[]{:S(2)}) collective-permute-start(bf16[2,32,768]{2,1,0:T(8,128)(2,1)S(1)} %get-tuple-element.307), channel_id=1, source_target_pairs={{0,4},{1,5},{2,6},{3,7},{4,0},{5,1},{6,2},{7,3},{8,12},{9,13},{10,... | collective-permute-start | bytes 294920 | tf_op jit(solution)/shard_map/ppermute | solution.py:327
  7.3 49.6 %collective-permute-start = (bf16[272,1024]{1,0:T(8,128)(2,1)S(1)}, bf16[272,1024]{1,0:T(8,128)(2,1)S(1)}, u32[]{:S(2)}, u32[]{:S(2)}) collective-permute-start(bf16[272,1024]{1,0:T(8,128)(2,1)S(1)} %pad_maximum_fusion.18), channel_id=1, source_target_pairs={{0,1},{1,0},{2,4},{3,5},{4,2},{5,3},{6,7},{7,6},{8,9},{9,8},{10,12... | collective-permute-start | bytes 1671176 | tf_op jit(solution)/shard_map/ppermute | solution.py:327
  11.0 59.8 %collective-permute-start.28 = (bf16[256,1024]{1,0:T(8,128)(2,1)S(1)}, bf16[256,1024]{1,0:T(8,128)(2,1)S(1)}, u32[]{:S(2)}, u32[]{:S(2)}) collective-permute-start(bf16[256,1024]{1,0:T(8,128)(2,1)S(1)} %bitcast.482), channel_id=1, source_target_pairs={{0,1},{1,0},{2,4},{3,5},{4,2},{5,3},{6,7},{7,6},{8,9},{9,8},{10,12... | collective-permute-start | bytes 1572872 | tf_op jit(solution)/shard_map/ppermute | solution.py:327
  11.1 23.8 %collective-permute-start.12 = (bf16[2,32,256]{2,1,0:T(8,128)(2,1)S(1)}, bf16[2,32,256]{2,1,0:T(8,128)(2,1)S(1)}, u32[]{:S(2)}, u32[]{:S(2)}) collective-permute-start(bf16[2,32,256]{2,1,0:T(8,128)(2,1)S(1)} %get-tuple-element.315), channel_id=1, source_target_pairs={{0,1},{1,0},{2,3},{3,2},{4,5},{5,4},{6,7},{7,6},{8,9},{9,8},{10,11... | collective-permute-start | bytes 98312 | tf_op jit(solution)/shard_map/ppermute | solution.py:327
  49.6 18.7 %collective-permute-start.17 = (bf16[1024,256]{1,0:T(8,128)(2,1)S(1)}, bf16[1024,256]{1,0:T(8,128)(2,1)S(1)}, u32[]{:S(2)}, u32[]{:S(2)}) collective-permute-start(bf16[1024,256]{1,0:T(8,128)(2,1)S(1)} %bitcast.448), channel_id=1, source_target_pairs={{0,1},{1,0},{2,3},{3,2},{4,5},{5,4},{6,7},{7,6},{8,9},{9,8},{10,11... | collective-permute-start | bytes 1572872 | tf_op jit(solution)/shard_map/ppermute | solution.py:327
  54.9 18.5 %collective-permute-start.6 = (bf16[2,2,2,32,768]{4,3,2,0,1:T(8,128)(2,1)S(1)}, bf16[2,2,2,32,768]{4,3,2,0,1:T(8,128)(2,1)S(1)}, u32[]{:S(2)}, u32[]{:S(2)}) collective-permute-start(bf16[2,2,2,32,768]{4,3,2,0,1:T(8,128)(2,1)S(1)} %maximum_select_fusion.8), channel_id=1, source_target_pairs={{0,8},{1,9},{2,10},{3,11},{4,12},{5,13},{6,14},{7,15},{8,0},{9,1},... | collective-permute-start | bytes 1179656 | tf_op jit(solution)/shard_map/ppermute | solution.py:327
  55.7 21.8 %collective-permute-start.7 = (bf16[2,2,2,32,768]{4,3,2,0,1:T(8,128)(2,1)S(1)}, bf16[2,2,2,32,768]{4,3,2,0,1:T(8,128)(2,1)S(1)}, u32[]{:S(2)}, u32[]{:S(2)}) collective-permute-start(bf16[2,2,2,32,768]{4,3,2,0,1:T(8,128)(2,1)S(1)} %maximum_select_fusion.8), channel_id=1, source_target_pairs={{0,16},{1,17},{2,18},{3,19},{4,20},{5,21},{6,22},{7,23},{8,24},{9,... | collective-permute-start | bytes 1179656 | tf_op jit(solution)/shard_map/ppermute | solution.py:327
  56.8 22.9 %collective-permute-start.8 = (bf16[2,2,2,32,768]{4,3,2,0,1:T(8,128)(2,1)S(1)}, bf16[2,2,2,32,768]{4,3,2,0,1:T(8,128)(2,1)S(1)}, u32[]{:S(2)}, u32[]{:S(2)}) collective-permute-start(bf16[2,2,2,32,768]{4,3,2,0,1:T(8,128)(2,1)S(1)} %maximum_select_fusion.8), channel_id=1, source_target_pairs={{0,24},{1,25},{2,26},{3,27},{4,28},{5,29},{6,30},{7,31},{8,16},{9,... | collective-permute-start | bytes 1179656 | tf_op jit(solution)/shard_map/ppermute | solution.py:327
  70.8 26.8 %collective-permute-start.21 = (bf16[2,2,96,656]{3,2,1,0:T(8,128)(2,1)S(1)}, bf16[2,2,96,656]{3,2,1,0:T(8,128)(2,1)S(1)}, u32[]{:S(2)}, u32[]{:S(2)}) collective-permute-start(bf16[2,2,96,656]{3,2,1,0:T(8,128)(2,1)S(1)} %maximum_select_fusion.4), channel_id=1, source_target_pairs={{0,2},{1,3},{2,0},{3,1},{4,6},{5,7},{6,4},{7,5},{8,10},{9,11},{10,... | collective-permute-start | bytes 1511432 | tf_op jit(solution)/shard_map/ppermute | solution.py:327
  73.4 33.1 %collective-permute-start.29 = (bf16[256,1024]{1,0:T(8,128)(2,1)S(1)}, bf16[256,1024]{1,0:T(8,128)(2,1)S(1)}, u32[]{:S(2)}, u32[]{:S(2)}) collective-permute-start(bf16[256,1024]{1,0:T(8,128)(2,1)S(1)} %collective-permute-done.28), channel_id=1, source_target_pairs={{2,3},{3,2},{4,5},{5,4},{10,11},{11,10},{12,13},{13,12},{18,19},{1... | collective-permute-start | bytes 1572872 | tf_op jit(solution)/shard_map/ppermute | solution.py:327
  77.5 30.3 %collective-permute-start.18 = (bf16[2,1024,256]{2,1,0:T(8,128)(2,1)S(1)}, bf16[2,1024,256]{2,1,0:T(8,128)(2,1)S(1)}, u32[]{:S(2)}, u32[]{:S(2)}) collective-permute-start(bf16[2,1024,256]{2,1,0:T(8,128)(2,1)S(1)} %pad_maximum_fusion.12), channel_id=1, source_target_pairs={{0,4},{1,5},{2,6},{3,7},{4,0},{5,1},{6,2},{7,3},{8,12},{9,13},{10,... | collective-permute-start | bytes 3145736 | tf_op jit(solution)/shard_map/ppermute | solution.py:327
  83.9 31.0 %collective-permute-start.2 = (bf16[2,272,1024]{2,1,0:T(8,128)(2,1)}, bf16[2,272,1024]{2,1,0:T(8,128)(2,1)}, u32[]{:S(2)}, u32[]{:S(2)}) collective-permute-start(bf16[2,272,1024]{2,1,0:T(8,128)(2,1)} %pad_maximum_fusion.10), channel_id=1, source_target_pairs={{0,4},{1,5},{2,6},{3,7},{4,0},{5,1},{6,2},{7,3},{8,12},{9,13},{10,... | collective-permute-start | bytes 3342344 | tf_op jit(solution)/shard_map/ppermute | solution.py:327
  98.9 46.4 %collective-permute-start.22 = (bf16[2,2,2,96,656]{4,3,2,0,1:T(8,128)(2,1)}, bf16[2,2,2,96,656]{4,3,2,0,1:T(8,128)(2,1)}, u32[]{:S(2)}, u32[]{:S(2)}) collective-permute-start(bf16[2,2,2,96,656]{4,3,2,0,1:T(8,128)(2,1)} %maximum_select_fusion.1), channel_id=1, source_target_pairs={{0,8},{1,9},{2,10},{3,11},{4,12},{5,13},{6,14},{7,15},{8,0},{9,1},... | collective-permute-start | bytes 3022856 | tf_op jit(solution)/shard_map/ppermute | solution.py:327
  100.3 54.3 %collective-permute-start.23 = (bf16[2,2,2,96,656]{4,3,2,0,1:T(8,128)(2,1)}, bf16[2,2,2,96,656]{4,3,2,0,1:T(8,128)(2,1)}, u32[]{:S(2)}, u32[]{:S(2)}) collective-permute-start(bf16[2,2,2,96,656]{4,3,2,0,1:T(8,128)(2,1)} %maximum_select_fusion.1), channel_id=1, source_target_pairs={{0,16},{1,17},{2,18},{3,19},{4,20},{5,21},{6,22},{7,23},{8,24},{9,... | collective-permute-start | bytes 3022856 | tf_op jit(solution)/shard_map/ppermute | solution.py:327
  106.5 49.1 %collective-permute-start.24 = (bf16[2,2,2,96,656]{4,3,2,0,1:T(8,128)(2,1)}, bf16[2,2,2,96,656]{4,3,2,0,1:T(8,128)(2,1)}, u32[]{:S(2)}, u32[]{:S(2)}) collective-permute-start(bf16[2,2,2,96,656]{4,3,2,0,1:T(8,128)(2,1)} %maximum_select_fusion.1), channel_id=1, source_target_pairs={{0,24},{1,25},{2,26},{3,27},{4,28},{5,29},{6,30},{7,31},{8,16},{9,... | collective-permute-start | bytes 3022856 | tf_op jit(solution)/shard_map/ppermute | solution.py:327
  107.9 71.6 %collective-permute-start.30 = (bf16[2,256,1024]{2,1,0:T(8,128)(2,1)}, bf16[2,256,1024]{2,1,0:T(8,128)(2,1)}, u32[]{:S(2)}, u32[]{:S(2)}) collective-permute-start(bf16[2,256,1024]{2,1,0:T(8,128)(2,1)} %pad_maximum_fusion.13), channel_id=1, source_target_pairs={{0,4},{1,5},{2,6},{3,7},{4,0},{5,1},{6,2},{7,3},{8,12},{9,13},{10,... | collective-permute-start | bytes 3145736 | tf_op jit(solution)/shard_map/ppermute | solution.py:327
  142.2 19.3 %collective-permute-start.9 = (bf16[2,2,256,256]{2,1,3,0:T(2,128)(2,1)}, bf16[2,2,256,256]{2,1,3,0:T(2,128)(2,1)}, u32[]{:S(2)}, u32[]{:S(2)}) collective-permute-start(bf16[2,2,256,256]{2,1,3,0:T(2,128)(2,1)} %reshape_reshape.3), channel_id=1, source_target_pairs={{0,1},{1,0},{2,3},{3,2},{4,5},{5,4},{6,7},{7,6},{8,9},{9,8},{10,11... | collective-permute-start | bytes 1572872 | tf_op jit(solution)/shard_map/ppermute | solution.py:327
  171.1 22.1 %collective-permute-start.10 = (bf16[2,2,2,256,256]{3,2,4,1,0:T(2,128)(2,1)}, bf16[2,2,2,256,256]{3,2,4,1,0:T(2,128)(2,1)}, u32[]{:S(2)}, u32[]{:S(2)}) collective-permute-start(bf16[2,2,2,256,256]{3,2,4,1,0:T(2,128)(2,1)} %pad_maximum_fusion.11), channel_id=1, source_target_pairs={{0,4},{1,5},{2,6},{3,7},{4,0},{5,1},{6,2},{7,3},{8,12},{9,13},{10,... | collective-permute-start | bytes 3145736 | tf_op jit(solution)/shard_map/ppermute | solution.py:327
  241.7 27.7 %collective-permute-start.50 = (bf16[2,2,2,96,656]{4,3,2,1,0:T(8,128)(2,1)S(1)}, bf16[2,2,2,96,656]{4,3,2,1,0:T(8,128)(2,1)S(1)}, u32[]{:S(2)}, u32[]{:S(2)}) collective-permute-start(bf16[2,2,2,96,656]{4,3,2,1,0:T(8,128)(2,1)S(1)} %get-tuple-element.232), channel_id=1, source_target_pairs={{0,8},{1,9},{2,10},{3,11},{4,12},{5,13},{6,14},{7,15},{8,0},{9,1},... | collective-permute-start | bytes 3022856 | tf_op jit(solution)/shard_map/ppermute | solution.py:327
  242.9 27.3 %collective-permute-start.51 = (bf16[2,2,2,96,656]{4,3,2,1,0:T(8,128)(2,1)S(1)}, bf16[2,2,2,96,656]{4,3,2,1,0:T(8,128)(2,1)S(1)}, u32[]{:S(2)}, u32[]{:S(2)}) collective-permute-start(bf16[2,2,2,96,656]{4,3,2,1,0:T(8,128)(2,1)S(1)} %get-tuple-element.234), channel_id=1, source_target_pairs={{0,16},{1,17},{2,18},{3,19},{4,20},{5,21},{6,22},{7,23},{8,24},{9,... | collective-permute-start | bytes 3022856 | tf_op jit(solution)/shard_map/ppermute | solution.py:327
  243.3 52.5 %collective-permute-start.52 = (bf16[2,2,2,96,656]{4,3,2,1,0:T(8,128)(2,1)S(1)}, bf16[2,2,2,96,656]{4,3,2,1,0:T(8,128)(2,1)S(1)}, u32[]{:S(2)}, u32[]{:S(2)}) collective-permute-start(bf16[2,2,2,96,656]{4,3,2,1,0:T(8,128)(2,1)S(1)} %get-tuple-element.233), channel_id=1, source_target_pairs={{0,24},{1,25},{2,26},{3,27},{4,28},{5,29},{6,30},{7,31},{8,16},{9,... | collective-permute-start | bytes 3022856 | tf_op jit(solution)/shard_map/ppermute | solution.py:327
  246.5 50.0 %collective-permute-start.31 = (bf16[2,256,1024]{2,1,0:T(8,128)(2,1)S(1)}, bf16[2,256,1024]{2,1,0:T(8,128)(2,1)S(1)}, u32[]{:S(2)}, u32[]{:S(2)}) collective-permute-start(bf16[2,256,1024]{2,1,0:T(8,128)(2,1)S(1)} %bitcast.503), channel_id=1, source_target_pairs={{0,4},{1,5},{2,6},{3,7},{4,0},{5,1},{6,2},{7,3},{8,12},{9,13},{10,... | collective-permute-start | bytes 3145736 | tf_op jit(solution)/shard_map/ppermute | solution.py:327
  256.9 41.3 %collective-permute-start.25 = (bf16[2,256,1024]{2,1,0:T(8,128)(2,1)S(1)}, bf16[2,256,1024]{2,1,0:T(8,128)(2,1)S(1)}, u32[]{:S(2)}, u32[]{:S(2)}) collective-permute-start(bf16[2,256,1024]{2,1,0:T(8,128)(2,1)S(1)} %bitcast.504), channel_id=1, source_target_pairs={{0,4},{1,5},{2,6},{3,7},{4,0},{5,1},{6,2},{7,3},{8,12},{9,13},{10,... | collective-permute-start | bytes 3145736 | tf_op jit(solution)/shard_map/ppermute | solution.py:327
  296.4 27.4 %collective-permute-start.53 = (bf16[2,2,96,656]{3,2,1,0:T(8,128)(2,1)S(1)}, bf16[2,2,96,656]{3,2,1,0:T(8,128)(2,1)S(1)}, u32[]{:S(2)}, u32[]{:S(2)}) collective-permute-start(bf16[2,2,96,656]{3,2,1,0:T(8,128)(2,1)S(1)} %fusion.90), channel_id=1, source_target_pairs={{0,2},{1,3},{2,0},{3,1},{4,6},{5,7},{6,4},{7,5},{8,10},{9,11},{10,... | collective-permute-start | bytes 1511432 | tf_op jit(solution)/shard_map/ppermute | solution.py:327
  297.9 26.2 %collective-permute-start.32 = (bf16[256,1024]{1,0:T(8,128)(2,1)S(1)}, bf16[256,1024]{1,0:T(8,128)(2,1)S(1)}, u32[]{:S(2)}, u32[]{:S(2)}) collective-permute-start(bf16[256,1024]{1,0:T(8,128)(2,1)S(1)} %fusion.92), channel_id=1, source_target_pairs={{0,1},{1,0},{2,3},{3,2},{4,5},{5,4},{6,7},{7,6},{8,9},{9,8},{10,11... | collective-permute-start | bytes 1572872 | tf_op jit(solution)/shard_map/ppermute | solution.py:327
  299.5 44.4 %collective-permute-start.26 = (bf16[256,1024]{1,0:T(8,128)(2,1)S(1)}, bf16[256,1024]{1,0:T(8,128)(2,1)S(1)}, u32[]{:S(2)}, u32[]{:S(2)}) collective-permute-start(bf16[256,1024]{1,0:T(8,128)(2,1)S(1)} %fusion.91), channel_id=1, source_target_pairs={{0,1},{1,0},{2,3},{3,2},{4,5},{5,4},{6,7},{7,6},{8,9},{9,8},{10,11... | collective-permute-start | bytes 1572872 | tf_op jit(solution)/shard_map/ppermute | solution.py:327
  326.5 25.5 %collective-permute-start.33 = (bf16[256,1024]{1,0:T(8,128)(2,1)S(1)}, bf16[256,1024]{1,0:T(8,128)(2,1)S(1)}, u32[]{:S(2)}, u32[]{:S(2)}) collective-permute-start(bf16[256,1024]{1,0:T(8,128)(2,1)S(1)} %get-tuple-element.219), channel_id=1, source_target_pairs={{0,1},{1,0},{2,3},{3,2},{4,5},{5,4},{6,7},{7,6},{8,9},{9,8},{10,11... | collective-permute-start | bytes 1572872 | tf_op jit(solution)/shard_map/ppermute | solution.py:327
  346.2 84.9 %collective-permute-start.27 = (bf16[256,1024]{1,0:T(8,128)(2,1)}, bf16[256,1024]{1,0:T(8,128)(2,1)}, u32[]{:S(2)}, u32[]{:S(2)}) collective-permute-start(bf16[256,1024]{1,0:T(8,128)(2,1)} %fusion.84), channel_id=1, source_target_pairs={{0,0},{1,1},{2,4},{3,5},{4,2},{5,3},{6,6},{7,7},{8,8},{9,9},{10,12... | collective-permute-start | bytes 1572872 | tf_op jit(solution)/shard_map/ppermute | solution.py:327
  434.3 18.0 %collective-permute-start.49 = (bf16[2,32,256]{2,1,0:T(8,128)(2,1)S(1)}, bf16[2,32,256]{2,1,0:T(8,128)(2,1)S(1)}, u32[]{:S(2)}, u32[]{:S(2)}) collective-permute-start(bf16[2,32,256]{2,1,0:T(8,128)(2,1)S(1)} %get-tuple-element.311), channel_id=1, source_target_pairs={{0,4},{1,5},{2,6},{3,7},{4,0},{5,1},{6,2},{7,3},{8,12},{9,13},{10,... | collective-permute-start | bytes 98312 | tf_op jit(solution)/shard_map/ppermute | solution.py:327
  445.9 18.9 %collective-permute-start.36 = (bf16[256,1024]{1,0:T(8,128)(2,1)S(1)}, bf16[256,1024]{1,0:T(8,128)(2,1)S(1)}, u32[]{:S(2)}, u32[]{:S(2)}) collective-permute-start(bf16[256,1024]{1,0:T(8,128)(2,1)S(1)} %fusion.93), channel_id=1, source_target_pairs={{0,1},{1,0},{2,3},{3,2},{4,5},{5,4},{6,7},{7,6},{8,9},{9,8},{10,11... | collective-permute-start | bytes 1572872 | tf_op jit(solution)/shard_map/ppermute | solution.py:327
  465.4 17.1 %collective-permute-start.37 = (bf16[256,1024]{1,0:T(8,128)(2,1)S(1)}, bf16[256,1024]{1,0:T(8,128)(2,1)S(1)}, u32[]{:S(2)}, u32[]{:S(2)}) collective-permute-start(bf16[256,1024]{1,0:T(8,128)(2,1)S(1)} %add_convert_fusion), channel_id=1, source_target_pairs={{0,0},{1,1},{2,4},{3,5},{4,2},{5,3},{6,6},{7,7},{8,8},{9,9},{10,12... | collective-permute-start | bytes 1572872 | tf_op jit(solution)/shard_map/ppermute | solution.py:327
  (103 other events, 670.7 us)

commit v2 on v0

--- a/solution.py
+++ b/solution.py
@@ -1,6 +1,8 @@
 import jax
 import jax.numpy as jnp
 from jax import lax
+from jax.experimental import pallas as pl
+from jax.experimental.pallas import tpu as pltpu
 from jax.sharding import PartitionSpec as P
 
 HEADS = 16
@@ -295,9 +297,749 @@
     )
 
 
+QUAD_MESH = (8, 4)
+FLAT = ("dp", "seq")
+LOW, WIDE = jnp.bfloat16, jnp.float32
+
+
+def pairs_of(step):
+    found = []
+    for dp in range(8):
+        for seq in range(4):
+            place = (dp // 4, dp // 2 % 2, dp % 2, seq // 2, seq % 2)
+            target = step(*place)
+            if target is not None:
+                y, x, c, zh, zl = target
+                found.append((dp * 4 + seq, (4 * y + 2 * x + c) * 4 + 2 * zh + zl))
+    return found
+
+
+TO_X = pairs_of(lambda y, x, c, zh, zl: (y, 1 - x, c, zh, zl))
+TO_Y = pairs_of(lambda y, x, c, zh, zl: (1 - y, x, c, zh, zl))
+TO_XY = pairs_of(lambda y, x, c, zh, zl: (1 - y, 1 - x, c, zh, zl))
+TO_CORE = pairs_of(lambda y, x, c, zh, zl: (y, x, 1 - c, zh, zl))
+TO_ZH = pairs_of(lambda y, x, c, zh, zl: (y, x, c, 1 - zh, zl))
+TO_ZL = pairs_of(lambda y, x, c, zh, zl: (y, x, c, zh, 1 - zl))
+TO_FAR = pairs_of(lambda y, x, c, zh, zl: (y, x, 1 - c, zh, 1 - zl))
+TO_HOME = pairs_of(lambda y, x, c, zh, zl: (y, x, zh, c, zl))
+ENTER = pairs_of(
+    lambda y, x, c, zh, zl: (y, x, c, zh, 1 - zl) if c == zh else (y, x, zh, c, zl)
+)
+ENTER_MOVED = pairs_of(lambda y, x, c, zh, zl: None if c == zh else (y, x, c, zh, 1 - zl))
+
+
+def send(array, pairs):
+    return lax.ppermute(array, FLAT, pairs)
+
+
+def core_of(flat):
+    return flat >> 2 & 1
+
+
+def half_of(flat):
+    return flat >> 1 & 1
+
+
+def group_of(flat):
+    return 2 * core_of(flat) + (flat & 1)
+
+
+def square_of(flat):
+    return flat >> 3
+
+
+def mm(left, right):
+    return lax.dot_general(left, right, (((1,), (0,)), ((), ())), preferred_element_type=WIDE)
+
+
+def mm_t(left, right):
+    return lax.dot_general(left, right, (((1,), (1,)), ((), ())), preferred_element_type=WIDE)
+
+
+def t_mm(left, right):
+    return lax.dot_general(left, right, (((0,), (0,)), ((), ())), preferred_element_type=WIDE)
+
+
+def window(index, size):
+    return pl.ds(pl.multiple_of(index * size, size), size)
+
+
+def whole(array):
+    rank = len(array.shape)
+    return (array, array.shape, lambda *_: (0,) * rank)
+
+
+def by_rows(array, rows, step=lambda b: b):
+    return (array, (rows,) + array.shape[1:], lambda b, f: (step(b),) + (0,) * (len(array.shape) - 1))
+
+
+def run(body, flat, grid, ins, outs, scratch=(), flops=0):
+    moved = sum(a.size * a.dtype.itemsize for a, _, _ in ins)
+    moved += sum(a.size * a.dtype.itemsize for a, _, _ in outs)
+    return pl.pallas_call(
+        body,
+        grid_spec=pltpu.PrefetchScalarGridSpec(
+            num_scalar_prefetch=1,
+            grid=grid,
+            in_specs=[pl.BlockSpec(block, index) for _, block, index in ins],
+            out_specs=[pl.BlockSpec(block, index) for _, block, index in outs],
+            scratch_shapes=list(scratch),
+        ),
+        out_shape=[a for a, _, _ in outs],
+        cost_estimate=pl.CostEstimate(flops=flops, bytes_accessed=moved, transcendentals=0),
+    )(flat, *[a for a, _, _ in ins])
+
+
+def shape_of(*dims, dtype=LOW):
+    return jax.ShapeDtypeStruct(dims, dtype)
+
+
+def normed_of(x):
+    centred = x - jnp.mean(x, axis=-1, keepdims=True)
+    spread = lax.rsqrt(jnp.mean(centred * centred, axis=-1, keepdims=True) + norm_eps)
+    return centred * spread, spread
+
+
+def split_qkv(flat, weight, gain):
+    rows, part = weight.shape[0], weight.shape[1] // 12
+
+    def body(flat_ref, w_ref, gain_ref, *refs):
+        held = refs[4]
+        for s in range(4):
+            for t in range(3):
+                cols = w_ref[:, (4 * t + s) * part : (4 * t + s + 1) * part].astype(WIDE)
+                held[s, :, t * part : (t + 1) * part] = (cols * gain_ref[...]).astype(LOW)
+        for i in range(4):
+            refs[i][...] = held[group_of(flat_ref[0]) ^ i]
+
+    out = shape_of(rows, 3 * part)
+    return run(
+        body, flat, (1,), [whole(weight), whole(gain)], [whole(out)] * 4,
+        [pltpu.VMEM((4, rows, 3 * part), LOW)],
+    )
+
+
+def split_rest(flat, out_weight, up_weight, down_weight, gain):
+    rows, part, ff = out_weight.shape[0], out_weight.shape[1] // 4, down_weight.shape[1] // 4
+
+    def body(flat_ref, out_ref, up_ref, down_ref, gain_ref, *refs):
+        ups, downs = refs[8:]
+        for s in range(4):
+            for t in range(2):
+                cols = up_ref[:, (4 * t + s) * ff : (4 * t + s + 1) * ff].astype(WIDE)
+                ups[s, :, t * ff : (t + 1) * ff] = (cols * gain_ref[...]).astype(LOW)
+            downs[s, :, :part] = out_ref[:, s * part : (s + 1) * part]
+            downs[s, :, part:] = down_ref[:, s * ff : (s + 1) * ff]
+        for i in range(4):
+            refs[i][...] = ups[group_of(flat_ref[0]) ^ i]
+            refs[4 + i][...] = downs[group_of(flat_ref[0]) ^ i]
+
+    up, down = shape_of(rows, 2 * ff), shape_of(rows, part + ff)
+    made = run(
+        body, flat, (1,), [whole(a) for a in (out_weight, up_weight, down_weight, gain)],
+        [whole(up)] * 4 + [whole(down)] * 4,
+        [pltpu.VMEM((4, rows, 2 * ff), LOW), pltpu.VMEM((4, rows, part + ff), LOW)],
+    )
+    return made[:4], made[4:]
+
+
+def quad_rows(flat, slices):
+    rows, width = slices[0].shape
+    parts = [slices[0]] + [
+        send(slices[i], pairs) for i, pairs in ((1, TO_ZL), (2, TO_CORE), (3, TO_FAR))
+    ]
+
+    def body(flat_ref, *refs):
+        for i in range(4):
+            refs[4][group_of(flat_ref[0]) ^ i] = refs[i][...]
+
+    return run(body, flat, (1,), [whole(p) for p in parts], [whole(shape_of(4, rows, width))])[0]
+
+
+def line_rows(flat, quad):
+    _, rows, width = quad.shape
+    near = quad.reshape(2, 2 * rows, width)
+    far = send(quad, TO_ZH).reshape(2, 2 * rows, width)
+
+    def body(flat_ref, near_ref, far_ref, out_ref):
+        half = half_of(flat_ref[0])
+        for c in range(2):
+            out_ref[c, half] = near_ref[c]
+            out_ref[c, 1 - half] = far_ref[c]
+
+    out = run(
+        body, flat, (1,), [whole(near), whole(far)], [whole(shape_of(2, 2, 2 * rows, width))]
+    )[0]
+    return out.reshape(8 * rows, width)
+
+
+def square_pieces(line, x_first):
+    one, two = (TO_X, TO_Y) if x_first else (TO_Y, TO_X)
+    first = send(line, one)
+    second = send(line, two)
+    third = send(first, two)
+    return [line, first, second, third] if x_first else [line, second, first, third]
+
+
+def enter_quad(flat, block, rows):
+    height, width = block.shape
+    extra = height - rows
+    at_home = core_of(flat[0]) == half_of(flat[0])
+    first = send(block, ENTER)
+    near = send(first, TO_CORE)
+    second = send(first, ENTER_MOVED)
+    far = send(jnp.where(at_home, block, second), TO_CORE)
+
+    def body(flat_ref, block_ref, first_ref, second_ref, near_ref, far_ref, *outs):
+        home = core_of(flat_ref[0]) == half_of(flat_ref[0])
+        here = (block_ref, first_ref, near_ref, far_ref)
+        moved = (first_ref, second_ref, far_ref, near_ref)
+        for k in range(4):
+            for flag, source in ((home, here[k]), (jnp.logical_not(home), moved[k])):
+
+                @pl.when(jnp.logical_and(pl.program_id(0) == k, flag))
+                def _(source=source):
+                    def step(r, carry):
+                        outs[0][window(r, 32), :] = source[window(r, 32), :]
+                        return carry
+
+                    lax.fori_loop(0, rows // 32, step, 0)
+                    if extra:
+                        outs[1][...] = source[rows:, :]
+
+    made = [shape_of(4 * rows, width)] + ([shape_of(4 * extra, width)] if extra else [])
+    return run(
+        body, flat, (4,), [whole(a) for a in (block, first, second, near, far)],
+        [by_rows(m, m.shape[0] // 4) for m in made],
+    )
+
+
+def quad_gather(block):
+    side = send(block, TO_ZL)
+    return [block, side, send(block, TO_CORE), send(side, TO_CORE)]
+
+
+def rope_lanes(seq_pos):
+    exponent = jnp.arange(0, HEAD_DIM, 2).astype(WIDE) / HEAD_DIM
+    angles = seq_pos[:, None] * (rope_base ** (-exponent))[None, :]
+    cos_half, sin_half = jnp.cos(angles), jnp.sin(angles)
+    return (
+        jnp.concatenate([cos_half] * 4, axis=1),
+        jnp.concatenate([-sin_half, sin_half] * 2, axis=1),
+    )
+
+
+def turned(v):
+    half = HEAD_DIM // 2
+    lane = lax.broadcasted_iota(jnp.int32, v.shape, 1)
+    return jnp.where(
+        lane % HEAD_DIM < half, pltpu.roll(v, 2 * HEAD_DIM - half, 1), pltpu.roll(v, half, 1)
+    )
+
+
+def project(flat, x, pieces, cos_table, sin_table):
+    tokens, width = x.shape
+    piece, columns = pieces[0].shape
+    rows = tokens // 4
+
+    def body(flat_ref, x_ref, *refs):
+        weights, (cos_ref, sin_ref, n_ref, mix_ref) = refs[:4], refs[4:]
+        n_ref[...] = normed_of(x_ref[...].astype(WIDE))[0].astype(LOW)
+        square = square_of(flat_ref[0])
+        mixed = sum(mm(n_ref[:, window(square ^ i, piece)], weights[i][...]) for i in range(4))
+        turned_to = 2 * columns // 3
+        for t in range(0, turned_to, 128):
+            v = mixed[:, t : t + 128]
+            mix_ref[:, t : t + 128] = (v * cos_ref[...] + turned(v) * sin_ref[...]).astype(LOW)
+        mix_ref[:, turned_to:] = mixed[:, turned_to:].astype(LOW)
+
+    return run(
+        body, flat, (4,),
+        [by_rows(x, rows)] + [whole(p) for p in pieces]
+        + [by_rows(cos_table, rows), by_rows(sin_table, rows)],
+        [by_rows(shape_of(tokens, width), rows), by_rows(shape_of(tokens, columns), rows)],
+        flops=2 * tokens * width * columns,
+    )
+
+
+def attend(flat, mix):
+    tokens, columns = mix.shape
+    part = columns // 3
+    rows = tokens // 4
+    scale = HEAD_DIM ** (-0.5)
+
+    def body(flat_ref, q_ref, k_ref, v_ref, out_ref, log_ref):
+        lane = lax.broadcasted_iota(jnp.int32, (rows, part), 1) // HEAD_DIM
+        log_lane = lax.broadcasted_iota(jnp.int32, (rows, 128), 1)
+        total = jnp.zeros((rows, part), WIDE)
+        logs = jnp.zeros((rows, 128), WIDE)
+        queries = q_ref[...].astype(WIDE) * scale
+        for h in range(part // HEAD_DIM):
+            q_head = jnp.where(lane == h, queries, 0.0).astype(LOW)
+            scores = mm_t(q_head, k_ref[...])
+            peak = jnp.max(scores, axis=-1, keepdims=True)
+            powers = jnp.exp(scores - peak)
+            mass = jnp.sum(powers, axis=-1, keepdims=True)
+            probs = (powers * (1.0 / mass)).astype(LOW)
+            total = jnp.where(lane == h, mm(probs, v_ref[...]), total)
+            logs = jnp.where(log_lane == h, peak + jnp.log(mass), logs)
+        out_ref[...] = total.astype(LOW)
+        log_ref[...] = logs
+
+    return run(
+        body, flat, (4,),
+        [
+            (mix, (rows, part), lambda b, f: (b, 0)),
+            (mix, (tokens, part), lambda b, f: (0, 1)),
+            (mix, (tokens, part), lambda b, f: (0, 2)),
+        ],
+        [by_rows(shape_of(tokens, part), rows), by_rows(shape_of(tokens, 128, dtype=WIDE), rows)],
+        flops=16 * tokens * tokens * part,
+    )
+
+
+def token_parts(arrays, rows):
+    return [by_rows(a, rows, lambda b, i=i: b ^ i) for i, a in enumerate(arrays)]
+
+
+def join_heads(flat, x, heads, columns):
+    tokens, width = x.shape
+    rows, part = tokens // 4, width // 4
+
+    def body(flat_ref, x_ref, *refs):
+        parts, weights, (n_ref, own_ref, held) = refs[:4], refs[4:8], refs[8:]
+        group, square = group_of(flat_ref[0]), square_of(flat_ref[0])
+        for j in range(4):
+            cols = window(group ^ j, part)
+            held[:, cols] = x_ref[:, cols].astype(WIDE) + sum(
+                mm(parts[i][...], weights[j][window(group ^ i ^ square, part), :])
+                for i in range(4)
+            )
+        resid = held[...]
+        n_ref[...] = normed_of(resid)[0].astype(LOW)
+
+        @pl.when(pl.program_id(0) == 0)
+        def _():
+            own_ref[...] = held[...]
+
+    return run(
+        body, flat, (4,),
+        [by_rows(x, rows)] + token_parts(heads, rows) + [whole(w) for w in columns],
+        [by_rows(shape_of(tokens, width), rows), whole(shape_of(rows, width, dtype=WIDE))],
+        [pltpu.VMEM((rows, width), WIDE)],
+        flops=2 * tokens * width * width,
+    )
+
+
+def feed(flat, normed, cot, ups, downs):
+    tokens, width = normed.shape
+    piece, ff = ups[0].shape[0], ups[0].shape[1] // 2
+    skip = downs[0].shape[1] - ff
+    rows = tokens // 4
+
+    def body(flat_ref, n_ref, cot_ref, *refs):
+        up_refs, down_refs, (h_ref, d_ref) = refs[:4], refs[4:8], refs[8:]
+        square = square_of(flat_ref[0])
+        wide = sum(mm(n_ref[:, window(square ^ i, piece)], up_refs[i][...]) for i in range(4))
+        d_hidden = sum(
+            mm(cot_ref[:, window(square ^ i, piece)], down_refs[i][:, skip:]) for i in range(4)
+        )
+        inner, gate = wide[:, :ff], wide[:, ff:]
+        cdf = 0.5 * (1.0 + lax.erf(inner * inv_root_two))
+        slope = cdf + inner * jnp.exp(-0.5 * inner * inner) * inv_root_tau
+        bent = inner * cdf
+        h_ref[...] = (bent * gate).astype(LOW)
+        d_ref[:, :ff] = (d_hidden * gate * slope).astype(LOW)
+        d_ref[:, ff:] = (d_hidden * bent).astype(LOW)
+
+    return run(
+        body, flat, (4,),
+        [by_rows(normed, rows), by_rows(cot, rows)] + [whole(w) for w in (*ups, *downs)],
+        [by_rows(shape_of(tokens, ff), rows), by_rows(shape_of(tokens, 2 * ff), rows)],
+        flops=6 * tokens * width * ff,
+    )
+
+
+def back_pair(flat, grads, pieces, odd):
+    tokens = grads[0][0].shape[0]
+    piece = pieces[0].shape[0]
+    rows, width, count = tokens // 4, 4 * piece, len(grads)
+
+    def body(flat_ref, *refs):
+        arrays, weights, (near_ref, far_ref, held) = (
+            refs[:count], refs[count : count + 4], refs[count + 4 :],
+        )
+        square = square_of(flat_ref[0])
+        for i in range(4):
+            held[:, window(square ^ i, piece)] = sum(
+                mm_t(a[...], weights[i][:, at : at + a.shape[1]])
+                for a, (_, at) in zip(arrays, grads)
+            )
+
+        @pl.when(pl.program_id(0) == 0)
+        def _():
+            near_ref[...] = held[...]
+
+        @pl.when(pl.program_id(0) == 1)
+        def _():
+            far_ref[...] = held[...].astype(LOW)
+
+    return run(
+        body, flat, (2,),
+        [by_rows(a, rows, lambda b: 2 * b + odd) for a, _ in grads] + [whole(p) for p in pieces],
+        [whole(shape_of(rows, width, dtype=WIDE)), whole(shape_of(rows, width))],
+        [pltpu.VMEM((rows, width), WIDE)],
+        flops=tokens * width * sum(a.shape[1] for a, _ in grads),
+    )
+
+
+def quad_sum(flat, grads, pieces):
+    near, far = back_pair(flat, grads, pieces, 1)
+    side = send((near + send(far, TO_CORE).astype(WIDE)).astype(LOW), TO_ZL)
+    own, far = back_pair(flat, grads, pieces, 0)
+    return own, send(far, TO_CORE), side
+
+
+def norm_pull(flat, x, terms, base, keep):
+    rows, width = terms[0].shape
+    step = rows // 4
+
+    def body(flat_ref, x_ref, a_ref, b_ref, c_ref, base_ref, *outs):
+        normed, spread = normed_of(x_ref[...].astype(WIDE))
+        scaled = a_ref[...] + b_ref[...].astype(WIDE) + c_ref[...].astype(WIDE)
+        grad = base_ref[...].astype(WIDE) + spread * (
+            scaled
+            - jnp.mean(scaled, axis=-1, keepdims=True)
+            - normed * jnp.mean(scaled * normed, axis=-1, keepdims=True)
+        )
+        outs[0][...] = grad.astype(LOW)
+        if keep:
+            outs[1][...] = grad
+
+    outs = [shape_of(rows, width)] + ([shape_of(rows, width, dtype=WIDE)] if keep else [])
+    return run(
+        body, flat, (4,), [by_rows(a, step) for a in (x, *terms, base)],
+        [by_rows(o, step) for o in outs],
+    )
+
+
+def feed_grads(flat, normed, cot, d_up, hidden):
+    tokens, width = normed.shape
+    rows, piece = tokens // 4, width // 4
+    ff = hidden.shape[1]
+
+    def body(flat_ref, n_ref, cot_ref, d_ref, h_ref, *refs):
+        outs, held = refs[:4], refs[4]
+        square = square_of(flat_ref[0])
+
+        @pl.when(pl.program_id(0) == 0)
+        def _():
+            held[...] = jnp.zeros_like(held)
+
+        for i in range(4):
+            cols = window(square ^ i, piece)
+            held[i, :, : 2 * ff] += t_mm(n_ref[:, cols], d_ref[...])
+            held[i, :, 2 * ff :] += t_mm(cot_ref[:, cols], h_ref[...])
+
+        @pl.when(pl.program_id(0) == 3)
+        def _():
+            for i in range(4):
+                outs[i][...] = held[i].astype(LOW)
+
+    return run(
+        body, flat, (4,), [by_rows(a, rows) for a in (normed, cot, d_up, hidden)],
+        [whole(shape_of(piece, 3 * ff))] * 4, [pltpu.VMEM((4, piece, 3 * ff), WIDE)],
+        flops=6 * tokens * width * ff,
+    )
+
+
+def heads_back(flat, d_all, heads, columns):
+    rows, width = d_all[0].shape
+    part = width // 4
+
+    def body(flat_ref, *refs):
+        blocks, parts, weights = refs[:4], refs[4:8], refs[8:12]
+        d_ref, grad_ref, block, held, total = refs[12:]
+        group, square = group_of(flat_ref[0]), square_of(flat_ref[0])
+        at = pl.program_id(0)
+        for k in range(4):
+
+            @pl.when(at == k)
+            def _(source=blocks[k]):
+                def step(r, carry):
+                    block[window(r, 32), :] = source[window(r, 32), :]
+                    return carry
+
+                lax.fori_loop(0, rows // 32, step, 0)
+
+            held[k] = parts[k][...]
+
+        @pl.when(at == 0)
+        def _():
+            total[...] = jnp.zeros_like(total)
+
+        d_ref[...] = sum(
+            mm_t(block[:, window(group ^ j, part)], weights[j][window(group ^ square, part), :])
+            for j in range(4)
+        ).astype(LOW)
+        mine = block[:, window(group, part)]
+        for i in range(4):
+            total[i] += t_mm(held[group ^ square ^ i], mine)
+
+        @pl.when(at == 3)
+        def _():
+            grad_ref[...] = total[...].astype(LOW)
+
+    return run(
+        body, flat, (4,),
+        [whole(d) for d in d_all] + token_parts(heads, rows) + [whole(w) for w in columns],
+        [by_rows(shape_of(4 * rows, part), rows), whole(shape_of(4, part, part))],
+        [
+            pltpu.VMEM((rows, width), LOW),
+            pltpu.VMEM((4, rows, part), LOW),
+            pltpu.VMEM((4, part, part), WIDE),
+        ],
+        flops=4 * 4 * rows * width * part,
+    )
+
+
+def attend_back(flat, mix, attended, d_attended, logs, cos_table, sin_table):
+    tokens, columns = mix.shape
+    part = columns // 3
+    rows = tokens // 4
+    scale = HEAD_DIM ** (-0.5)
+    heads = part // HEAD_DIM
+
+    def rotated(grad, cos, sin):
+        halves = [grad[:, t : t + 128] for t in range(0, part, 128)]
+        return jnp.concatenate([v * cos - turned(v) * sin for v in halves], axis=1).astype(LOW)
+
+    def body(flat_ref, q_ref, k_ref, v_ref, o_ref, d_ref, log_ref, cos_ref, sin_ref, *refs):
+        dq_ref, dk_ref, dv_ref, k_total, v_total = refs
+        at = pl.program_id(0)
+
+        @pl.when(at == 0)
+        def _():
+            k_total[...] = jnp.zeros_like(k_total)
+            v_total[...] = jnp.zeros_like(v_total)
+
+        lane = lax.broadcasted_iota(jnp.int32, (rows, part), 1) // HEAD_DIM
+        queries = q_ref[...].astype(WIDE) * scale
+        grads = d_ref[...].astype(WIDE)
+        chosen = lax.broadcasted_iota(jnp.int32, (8, part), 0) == (
+            lax.broadcasted_iota(jnp.int32, (8, part), 1) // HEAD_DIM
+        )
+        deltas = lax.dot_general(
+            chosen.astype(WIDE), grads * o_ref[...].astype(WIDE), (((1,), (1,)), ((), ())),
+            precision=lax.Precision.HIGHEST, preferred_element_type=WIDE,
+        )
+        d_query = jnp.zeros((rows, part), WIDE)
+        for h in range(heads):
+            q_head = jnp.where(lane == h, queries, 0.0).astype(LOW)
+            d_head = jnp.where(lane == h, grads, 0.0).astype(LOW)
+            probs = jnp.exp(mm_t(k_ref[...], q_head) - log_ref[h : h + 1, :])
+            d_probs = mm_t(v_ref[...], d_head)
+            d_scores = (probs * (d_probs - deltas[h : h + 1, :])).astype(LOW)
+            v_total[...] += mm(probs.astype(LOW), d_head)
+            k_total[...] += mm(d_scores, q_head)
+            d_query = jnp.where(lane == h, t_mm(d_scores, k_ref[...]), d_query)
+        here = window(at, rows)
+        dq_ref[...] = rotated(d_query * scale, cos_ref[here, :], sin_ref[here, :])
+
+        @pl.when(at == 3)
+        def _():
+            dk_ref[...] = rotated(k_total[...], cos_ref[...], sin_ref[...])
+            dv_ref[...] = v_total[...].astype(LOW)
+
+    out = shape_of(tokens, part)
+    return run(
+        body, flat, (4,),
+        [
+            (mix, (rows, part), lambda b, f: (b, 0)),
+            (mix, (tokens, part), lambda b, f: (0, 1)),
+            (mix, (tokens, part), lambda b, f: (0, 2)),
+            by_rows(attended, rows),
+            by_rows(d_attended, rows),
+            (logs, (8, rows), lambda b, f: (0, b)),
+            whole(cos_table),
+            whole(sin_table),
+        ],
+        [by_rows(out, rows), whole(out), whole(out)],
+        [pltpu.VMEM((tokens, part), WIDE)] * 2,
+        flops=40 * tokens * tokens * part,
+    )
+
+
+def mixed_grads(flat, normed, d_mixed, out_grad):
+    tokens, width = normed.shape
+    rows, piece = tokens // 4, width // 4
+    part = d_mixed[0].shape[1]
+
+    def body(flat_ref, n_ref, *refs):
+        grads, out_ref, outs, held = refs[:3], refs[3], refs[4:8], refs[8]
+        square = square_of(flat_ref[0])
+
+        @pl.when(pl.program_id(0) == 0)
+        def _():
+            held[...] = jnp.zeros_like(held)
+
+        for i in range(4):
+            cols = n_ref[:, window(square ^ i, piece)]
+            for t in range(3):
+                held[i, :, t * part : (t + 1) * part] += t_mm(cols, grads[t][...])
+
+        @pl.when(pl.program_id(0) == 3)
+        def _():
+            for i in range(4):
+                outs[i][:, : 3 * part] = held[i].astype(LOW)
+                outs[i][:, 3 * part :] = out_ref[i]
+
+    return run(
+        body, flat, (4,),
+        [by_rows(normed, rows)] + [by_rows(d, rows) for d in d_mixed] + [whole(out_grad)],
+        [whole(shape_of(piece, 4 * part))] * 4, [pltpu.VMEM((4, piece, 3 * part), WIDE)],
+        flops=6 * tokens * width * part,
+    )
+
+
+def owned_slices(flat, pieces):
+    high, width = pieces[0].shape
+    rows = high // 8
+    terms = [pieces[0]] + [
+        send(pieces[i], pairs) for i, pairs in ((1, TO_X), (2, TO_Y), (3, TO_XY))
+    ]
+    terms = [t.reshape(2, 2, 2 * rows, width) for t in terms]
+
+    def fold(flat_ref, *refs):
+        half = half_of(flat_ref[0])
+        refs[4][0] = sum(refs[i][0, half].astype(WIDE) for i in range(4))
+        refs[5][0] = sum(refs[i][0, 1 - half].astype(WIDE) for i in range(4)).astype(LOW)
+
+    kept, sent = run(
+        fold, flat, (2,), [by_rows(t, 1) for t in terms],
+        [
+            by_rows(shape_of(2, 2 * rows, width, dtype=WIDE), 1),
+            by_rows(shape_of(2, 2 * rows, width), 1),
+        ],
+    )
+    kept = kept.reshape(4, rows, width)
+    sent = send(sent, TO_ZH).reshape(4, rows, width)
+
+    def share(flat_ref, kept_ref, sent_ref, *outs):
+        for i in range(4):
+            at = group_of(flat_ref[0]) ^ i
+            outs[i][...] = (kept_ref[at] + sent_ref[at].astype(WIDE)).astype(LOW)
+
+    slices = run(
+        share, flat, (1,), [whole(kept), whole(sent)], [whole(shape_of(rows, width))] * 4
+    )
+    return [slices[0]] + [
+        send(slices[i], pairs) for i, pairs in ((1, TO_ZL), (2, TO_CORE), (3, TO_FAR))
+    ]
+
+
+def finish(flat, slices, weight, gain, sizes):
+    rows, width = slices[0].shape
+    count, part, rest = sizes
+
+    def body(flat_ref, *refs):
+        w_ref, gain_ref, scaled_ref, gain_out, plain_ref, held = refs[4:]
+        for i in range(4):
+            held[group_of(flat_ref[0]) ^ i] = refs[i][...].astype(WIDE)
+        total = jnp.zeros((rows, 1), WIDE)
+        for s in range(4):
+            for t in range(count):
+                at = (4 * t + s) * part
+                grad = held[s, :, t * part : (t + 1) * part]
+                total += jnp.sum(
+                    grad * w_ref[:, at : at + part].astype(WIDE), axis=1, keepdims=True
+                )
+                scaled_ref[:, at : at + part] = grad * gain_ref[...]
+            plain_ref[:, s * rest : (s + 1) * rest] = held[s, :, count * part :]
+        gain_out[...] = total
+
+    return run(
+        body, flat, (1,), [whole(a) for a in (*slices, weight, gain)],
+        [
+            whole(shape_of(*weight.shape, dtype=WIDE)),
+            whole(shape_of(rows, 1, dtype=WIDE)),
+            whole(shape_of(rows, 4 * rest, dtype=WIDE)),
+        ],
+        [pltpu.VMEM((4, rows, width), WIDE)],
+    )
+
+
+def quad_device(
+    inputs,
+    positions,
+    attn_gain,
+    qkv_weight,
+    attn_out_weight,
+    mlp_gain,
+    up_weight,
+    down_weight,
+    cotangent,
+):
+    flat = lax.axis_index(FLAT).astype(jnp.int32).reshape(1)
+    tokens, width = inputs.shape[1:]
+    part, ff = width // 4, FF // 4
+    gain_one, gain_two = attn_gain.astype(WIDE)[:, None], mlp_gain.astype(WIDE)[:, None]
+
+    pos = positions[0]
+    pos_row = jnp.concatenate([pos // 128, pos % 128]).astype(LOW)
+    pos_row = jnp.pad(pos_row[None], ((0, 15), (0, width - 2 * tokens)))
+    x, pos_all = enter_quad(flat, jnp.concatenate([inputs[0], pos_row]), tokens)
+    w_qkv = split_qkv(flat, qkv_weight, gain_one)
+    w_qkv = square_pieces(line_rows(flat, quad_rows(flat, w_qkv)), True)
+    w_up, w_down = split_rest(flat, attn_out_weight, up_weight, down_weight, gain_two)
+    w_down = square_pieces(line_rows(flat, quad_rows(flat, w_down)), True)
+    w_up = square_pieces(line_rows(flat, quad_rows(flat, w_up)), False)
+    w_out = quad_gather(jnp.concatenate([p[:, :part] for p in w_down]))
+    (cot,) = enter_quad(flat, cotangent[0], tokens)
+
+    pos_all = pos_all.reshape(4, 16, width)[:, 0, : 2 * tokens].astype(WIDE)
+    pos_all = (pos_all[:, :tokens] * 128.0 + pos_all[:, tokens:]).reshape(4 * tokens)
+    cos_table, sin_table = rope_lanes(pos_all)
+    normed_one, mix = project(flat, x, w_qkv, cos_table, sin_table)
+    attended, logs = attend(flat, mix)
+    logs = logs[:, :8].T
+    heads = quad_gather(attended)
+    normed_two, resid = join_heads(flat, x, heads, w_out)
+    hidden, d_up = feed(flat, normed_two, cot, w_up, w_down)
+    terms = quad_sum(flat, [(d_up, 0)], w_up)
+    d_low, d_resid = norm_pull(flat, resid, terms, cot, True)
+    ff_pieces = feed_grads(flat, normed_two, cot, d_up, hidden)
+    d_all = quad_gather(d_low)
+    out_terms = quad_sum(flat, [(hidden, part)], w_down)
+    output = resid + out_terms[0] + out_terms[1].astype(WIDE) + out_terms[2].astype(WIDE)
+    output = send(output.astype(LOW), TO_HOME)
+    d_attended, out_grad = heads_back(flat, d_all, heads, w_out)
+    d_mixed = attend_back(flat, mix, attended, d_attended, logs, cos_table, sin_table)
+    mixed_pieces = mixed_grads(flat, normed_one, d_mixed, out_grad)
+    terms = quad_sum(flat, [(d, t * part) for t, d in enumerate(d_mixed)], w_qkv)
+    (input_grad,) = norm_pull(flat, x, terms, d_resid, False)
+    input_grad = send(input_grad, TO_HOME)
+    up_grad, gain_two_grad, down_grad = finish(
+        flat, owned_slices(flat, ff_pieces), up_weight, gain_two, (2, ff, ff)
+    )
+    qkv_grad, gain_one_grad, out_grad = finish(
+        flat, owned_slices(flat, mixed_pieces), qkv_weight, gain_one, (3, part, part)
+    )
+    return (
+        output[None],
+        input_grad[None],
+        gain_one_grad[:, 0],
+        qkv_grad,
+        out_grad,
+        gain_two_grad[:, 0],
+        up_grad,
+        down_grad,
+    )
+
+
 def solution(mesh):
     return jax.shard_map(
-        per_device,
+        quad_device if tuple(mesh.shape.values()) == QUAD_MESH else per_device,
         mesh=mesh,
         in_specs=(
             P("dp", "seq", None),

time: 999 us -> 414 us (0.41); the launches traced: 986 us -> 412 us
  local copies, waits for them, and re-layouts: 282 us -> 27.5 us
  other arithmetic: 204 us -> 19.3 us
  Pallas kernels: 0 us -> 151 us
  waiting for transfers between devices: 281 us -> 133 us
  matrix products: 86.5 us -> 0 us
  blocking collectives: 51.9 us -> 0 us
  starting transfers between devices: 64.6 us -> 80.5 us
  between operations: 15.9 us -> 1.11 us
    all_to_all x14 -> x0, waiting for transfers between devices: 157 us -> none  [the longest x1 52 us: per_device(): lax.all_to_all(up_grad[None].astype(jnp.bfloat16), 'dp', split_axis=1, co...]
    unnamed x6 -> x1, other arithmetic: 153 us -> 0.01 us
    pallas_call x0 -> x32, Pallas kernels: none -> 151 us  [run(): pl.pallas_call(body, grid_spec=pltpu.PrefetchScalarGridSpec(num_scalar_pr...]
    ppermute x0 -> x63, waiting for transfers between devices: none -> 133 us  [send(): return lax.ppermute(array, FLAT, pairs)]
    unnamed x87 -> x106, local copies, waits for them, and re-layouts: 128 us -> 6.69 us
    all_gather x4 -> x0, waiting for transfers between devices: 121 us -> none  [the longest x1 58.5 us: per_device(): lax.all_gather(down_weight, ('dp', 'seq'), axis=0, tiled=True)]
    convert_element_type x6 -> x0, local copies, waits for them, and re-layouts: 109 us -> none  [the longest x1 57.7 us: per_device(): qkv_grad[None].astype(jnp.bfloat16)]
    dot_general x26 -> x0, matrix products: 86.5 us -> none  [the longest x1 8.88 us: per_device(): up_rows = jnp.dot(mlp_in, w_up, preferred_element_type=jnp.float32)]
  transfers between devices with their start and end apart: 22 -> 63, of which waited for: 12 -> 17; matrix products, arithmetic and copies ran while one was open for 51% -> 9% of each run, Pallas kernels for 0% -> 30%
where the time goes in v2:
time: 414 us; the launch traced here: 412 us
  Pallas kernels  151 us (36%)
  waiting for transfers between devices  133 us (32%)
  starting transfers between devices  80.5 us (19%)
  local copies, waits for them, and re-layouts  27.5 us (7%)
  other arithmetic  19.3 us (5%)
    pallas_call x32, Pallas kernels, run(): pl.pallas_call(body, grid_spec=pltpu.PrefetchScalarGridSpec(num_scalar_pr...  151 us
    ppermute x63, waiting for transfers between devices, send(): return lax.ppermute(array, FLAT, pairs)  133 us
    ppermute x63, starting transfers between devices, send(): return lax.ppermute(array, FLAT, pairs)  80.5 us
    ppermute x6, local copies, waits for them, and re-layouts, send(): return lax.ppermute(array, FLAT, pairs)  9.67 us
  transfers between devices with their start and end apart: 63, of which 17 were waited for; matrix products, arithmetic and copies ran while one was open for 9% of the time, Pallas kernels for 30%

profile of v2, /device:TPU:1, one launch (start us, length us, event | category | flops | bytes accessed | tf_op | source)
XLA Modules:
  0.0 411.7 jit_solution(146878650590600474)
XLA Ops:
  2.5 3.8 collective-permute-start
  11.8 8.3 %collective-permute-done.14.refs_1_ = bf16[32,912]{1,0:T(8,128)(2,1)S(1)} collective-permute-done((bf16[32,912]{1,0:T(8,128)(2,1)}, bf16[32,912]{1,0:T(8,128)(2,1)S(1)}, u32[]{:S(2)}, u32[]{:S(2)}) %collective-permute-start.14) | collective-permute-done | bytes 58400 | tf_op jit(solution)/shard_map/ppermute | solution.py:332
  26.1 14.6 %collective-permute-done.17 = bf16[4,32,912]{2,1,0:T(8,128)(2,1)S(1)} collective-permute-done((bf16[4,32,912]{2,1,0:T(8,128)(2,1)}, bf16[4,32,912]{2,1,0:T(8,128)(2,1)S(1)}, u32[]{:S(2)}, u32[]{:S(2)}) %collective-permute-start.17) | collective-permute-done | bytes 233504 | tf_op jit(solution)/shard_map/ppermute | solution.py:332
  51.3 6.8 %collective-permute-done.4.refs_1_ = bf16[32,768]{1,0:T(8,128)(2,1)S(1)} collective-permute-done((bf16[32,768]{1,0:T(8,128)(2,1)}, bf16[32,768]{1,0:T(8,128)(2,1)S(1)}, u32[]{:S(2)}, u32[]{:S(2)}) %collective-permute-start.4) | collective-permute-done | bytes 49184 | tf_op jit(solution)/shard_map/ppermute | solution.py:332
  78.5 19.0 %collective-permute-done.7 = bf16[4,32,768]{2,1,0:T(8,128)(2,1)S(1)} collective-permute-done((bf16[4,32,768]{2,1,0:T(8,128)(2,1)}, bf16[4,32,768]{2,1,0:T(8,128)(2,1)S(1)}, u32[]{:S(2)}, u32[]{:S(2)}) %collective-permute-start.7) | collective-permute-done | bytes 196640 | tf_op jit(solution)/shard_map/ppermute | solution.py:332
  114.3 3.7 shard_map.152
  122.9 17.1 %collective-permute-done.10.refs_3_.refs_6_ = bf16[256,768]{1,0:T(8,128)(2,1)S(1)} collective-permute-done((bf16[256,768]{1,0:T(8,128)(2,1)S(1)}, bf16[256,768]{1,0:T(8,128)(2,1)S(1)}, u32[]{:S(2)}, u32[]{:S(2)}) %collective-permute-start.10) | collective-permute-done | bytes 393248 | tf_op jit(solution)/shard_map/ppermute | solution.py:332
  140.7 7.1 %shard_map.156 = (bf16[1024,1024]{1,0:T(8,128)(2,1)}, bf16[1024,768]{1,0:T(8,128)(2,1)}) custom-call(s32[1]{0:T(128)} %bitcast.flat_ref, bf16[1024,1024]{1,0:T(8,128)(2,1)} %get-tuple-element.75.x_ref, bf16[256,768]{1,0:T(8,128)(2,1)} %bitcast.56, bf16[256,768]{1,0:T(8,128)(2,1)} %copy-done.10, bf16[256,768]{1,0:T(8,128)(2,1)} %copy-done.11, ...), custom_call_target="tpu_custom_call" | custom-call | flops 1610612736 | bytes 8388608 | tf_op jit(solution)/shard_map/pallas_call | solution.py:379
  147.8 9.9 %shard_map.157 = (bf16[1024,256]{1,0:T(8,128)(2,1)}, f32[1024,128]{1,0:T(8,128)}) custom-call(s32[1]{0:T(128)} %bitcast.flat_ref, bf16[1024,768]{1,0:T(8,128)(2,1)} %get-tuple-element.81.q_ref.k_ref.v_ref, bf16[1024,768]{1,0:T(8,128)(2,1)} %get-tuple-element.81.q_ref.k_ref.v_ref, bf16[1024,768]{1,0:T(8,128)(2,1)} %get-tuple-element.81.q_ref.k_ref.v_ref), custom_call_target="tpu_custom_call" | custom-call | flops 4294967296 | bytes 5767168 | tf_op jit(solution)/shard_map/pallas_call | solution.py:379
  162.5 7.2 %collective-permute-done.11.refs_1_.refs_5_ = bf16[1024,256]{1,0:T(8,128)(2,1)S(1)} collective-permute-done((bf16[1024,256]{1,0:T(8,128)(2,1)}, bf16[1024,256]{1,0:T(8,128)(2,1)S(1)}, u32[]{:S(2)}, u32[]{:S(2)}) %collective-permute-start.11) | collective-permute-done | bytes 524320 | tf_op jit(solution)/shard_map/ppermute | solution.py:332
  175.7 3.6 shard_map.162.cot_ref.base_ref
  180.5 8.0 %shard_map.161 = (bf16[1024,1024]{1,0:T(8,128)(2,1)}, f32[256,1024]{1,0:T(8,128)}) custom-call(s32[1]{0:T(128)} %bitcast.flat_ref, bf16[1024,1024]{1,0:T(8,128)(2,1)} %get-tuple-element.75.x_ref, bf16[1024,256]{1,0:T(8,128)(2,1)} %get-tuple-element.82.refs_0_.refs_4_.o_ref, bf16[1024,256]{1,0:T(8,128)(2,1)} %copy-done.20, ...), custom_call_target="tpu_custom_call" | custom-call | flops 2147483648 | bytes 9437184 | tf_op jit(solution)/shard_map/pallas_call | solution.py:379
  188.5 9.9 %shard_map.165 = (bf16[1024,656]{1,0:T(8,128)(2,1)}, bf16[1024,1312]{1,0:T(8,128)(2,1)}) custom-call(s32[1]{0:T(128)} %bitcast.flat_ref, bf16[1024,1024]{1,0:T(8,128)(2,1)} %get-tuple-element.88.n_ref, bf16[1024,1024]{1,0:T(8,128)(2,1)} %shard_map.162.cot_ref.base_ref, bf16[256,1312]{1,0:T(8,128)(2,1)} %bitcast.43, bf16[256,1312]{1,0:T(8,128)(2,1)} %copy.54.refs_1_.refs_2_, ...), custom_call_target="tpu_custom_call" | custom-call | flops 4127195136 | bytes 12779520 | tf_op jit(solution)/shard_map/pallas_call | solution.py:379
  198.4 5.4 %shard_map.169 = (f32[256,1024]{1,0:T(8,128)}, bf16[256,1024]{1,0:T(8,128)(2,1)}) custom-call(s32[1]{0:T(128)} %bitcast.flat_ref, bf16[1024,1312]{1,0:T(8,128)(2,1)} %get-tuple-element.98.refs_0_.d_ref, bf16[256,1312]{1,0:T(8,128)(2,1)} %bitcast.44, bf16[256,1312]{1,0:T(8,128)(2,1)} %copy.54.refs_1_.refs_2_, bf16[256,1312]{1,0:T(8,128)(2,1)} %copy.55.refs_2_.refs_3_, ...), custom_call_target="tpu_custom_call" | custom-call | flops 1375731712 | bytes 6946816 | tf_op jit(solution)/shard_map/pallas_call | solution.py:379
  204.0 5.4 %shard_map.168 = (f32[256,1024]{1,0:T(8,128)}, bf16[256,1024]{1,0:T(8,128)(2,1)}) custom-call(s32[1]{0:T(128)} %bitcast.flat_ref, bf16[1024,1312]{1,0:T(8,128)(2,1)} %get-tuple-element.98.refs_0_.d_ref, bf16[256,1312]{1,0:T(8,128)(2,1)} %bitcast.45, bf16[256,1312]{1,0:T(8,128)(2,1)} %copy.54.refs_1_.refs_2_, bf16[256,1312]{1,0:T(8,128)(2,1)} %copy.55.refs_2_.refs_3_, ...), custom_call_target="tpu_custom_call" | custom-call | flops 1375731712 | bytes 6946816 | tf_op jit(solution)/shard_map/pallas_call | solution.py:379
  211.5 11.6 %collective-permute-done.41.c_ref = bf16[256,1024]{1,0:T(8,128)(2,1)S(1)} collective-permute-done((bf16[256,1024]{1,0:T(8,128)(2,1)S(1)}, bf16[256,1024]{1,0:T(8,128)(2,1)S(1)}, u32[]{:S(2)}, u32[]{:S(2)}) %collective-permute-start.41) | collective-permute-done | bytes 524320 | tf_op jit(solution)/shard_map/ppermute | solution.py:332
  224.0 4.6 %shard_map.170 = (bf16[256,1024]{1,0:T(8,128)(2,1)}, f32[256,1024]{1,0:T(8,128)}) custom-call(s32[1]{0:T(128)} %bitcast.flat_ref, f32[256,1024]{1,0:T(8,128)} %get-tuple-element.87.x_ref, f32[256,1024]{1,0:T(8,128)} %get-tuple-element.99.a_ref, bf16[256,1024]{1,0:T(8,128)(2,1)} %copy-done.26, bf16[256,1024]{1,0:T(8,128)(2,1)} %copy-done.27, ...), custom_call_target="tpu_custom_call" | custom-call | bytes 6815744 | tf_op jit(solution)/shard_map/pallas_call | solution.py:379
  230.9 10.2 %collective-permute-done.42.refs_1_ = bf16[256,1024]{1,0:T(8,128)(2,1)S(1)} collective-permute-done((bf16[256,1024]{1,0:T(8,128)(2,1)}, bf16[256,1024]{1,0:T(8,128)(2,1)S(1)}, u32[]{:S(2)}, u32[]{:S(2)}) %collective-permute-start.42) | collective-permute-done | bytes 524320 | tf_op jit(solution)/shard_map/ppermute | solution.py:332
  243.7 4.2 %shard_map.167 = (f32[256,1024]{1,0:T(8,128)}, bf16[256,1024]{1,0:T(8,128)(2,1)}) custom-call(s32[1]{0:T(128)} %bitcast.flat_ref, bf16[1024,656]{1,0:T(8,128)(2,1)} %get-tuple-element.93.refs_0_.h_ref, bf16[256,912]{1,0:T(8,128)(2,1)} %bitcast.50, bf16[256,912]{1,0:T(8,128)(2,1)} %copy-done.2, bf16[256,912]{1,0:T(8,128)(2,1)} %copy-done.3, ...), custom_call_target="tpu_custom_call" | custom-call | flops 687865856 | bytes 4784128 | tf_op jit(solution)/shard_map/pallas_call | solution.py:379
  248.0 4.2 %shard_map.166 = (f32[256,1024]{1,0:T(8,128)}, bf16[256,1024]{1,0:T(8,128)(2,1)}) custom-call(s32[1]{0:T(128)} %bitcast.flat_ref, bf16[1024,656]{1,0:T(8,128)(2,1)} %get-tuple-element.93.refs_0_.h_ref, bf16[256,912]{1,0:T(8,128)(2,1)} %bitcast.51, bf16[256,912]{1,0:T(8,128)(2,1)} %copy-done.2, bf16[256,912]{1,0:T(8,128)(2,1)} %copy-done.3, ...), custom_call_target="tpu_custom_call" | custom-call | flops 687865856 | bytes 4784128 | tf_op jit(solution)/shard_map/pallas_call | solution.py:379
  252.7 11.2 %shard_map.180 = (bf16[256,1968]{1,0:T(8,128)(2,1)}, bf16[256,1968]{1,0:T(8,128)(2,1)}, bf16[256,1968]{1,0:T(8,128)(2,1)}, bf16[256,1968]{1,0:T(8,128)(2,1)}) custom-call(s32[1]{0:T(128)} %bitcast.flat_ref, bf16[1024,1024]{1,0:T(8,128)(2,1)} %get-tuple-element.88.n_ref, bf16[1024,1024]{1,0:T(8,128)(2,1)} %shard_map.162.cot_ref.base_ref, ...), custom_call_target="tpu_custom_call" | custom-call | flops 4127195136 | bytes 12255232 | tf_op jit(solution)/shard_map/pallas_call | solution.py:379
  269.7 6.4 %shard_map.171 = (bf16[1024,256]{1,0:T(8,128)(2,1)}, bf16[4,256,256]{2,1,0:T(8,128)(2,1)}) custom-call(s32[1]{0:T(128)} %bitcast.flat_ref, bf16[256,1024]{1,0:T(8,128)(2,1)} %get-tuple-element.103.refs_0_, bf16[256,1024]{1,0:T(8,128)(2,1)} %copy-done.21, bf16[256,1024]{1,0:T(8,128)(2,1)} %copy-done.22, bf16[256,1024]{1,0:T(8,128)(2,1)} %collective-permute-done.44.refs_3_, ...), custom_call_target="tpu_custom_call" | custom-call | flops 1073741824 | bytes 7340032 | tf_op jit(solution)/shard_map/pallas_call | solution.py:379
  276.1 17.4 %shard_map.172 = (bf16[1024,256]{1,0:T(8,128)(2,1)}, bf16[1024,256]{1,0:T(8,128)(2,1)}, bf16[1024,256]{1,0:T(8,128)(2,1)}) custom-call(s32[1]{0:T(128)} %bitcast.flat_ref, bf16[1024,768]{1,0:T(8,128)(2,1)} %get-tuple-element.81.q_ref.k_ref.v_ref, bf16[1024,768]{1,0:T(8,128)(2,1)} %get-tuple-element.81.q_ref.k_ref.v_ref, ...), custom_call_target="tpu_custom_call" | custom-call | flops 10737418240 | bytes 8421376 | tf_op jit(solution)/shard_map/pallas_call | solution.py:379
  293.5 4.3 %shard_map.174 = (f32[256,1024]{1,0:T(8,128)}, bf16[256,1024]{1,0:T(8,128)(2,1)}) custom-call(s32[1]{0:T(128)} %bitcast.flat_ref, bf16[1024,256]{1,0:T(8,128)(2,1)} %get-tuple-element.106.refs_0_, bf16[1024,256]{1,0:T(8,128)(2,1)} %get-tuple-element.107.refs_1_, bf16[1024,256]{1,0:T(8,128)(2,1)} %get-tuple-element.108.refs_2_, bf16[256,768]{1,0:T(8,128)(2,1)} %bitcast.57, ...), custom_call_target="tpu_custom_call" | custom-call | flops 805306368 | bytes 4718592 | tf_op jit(solution)/shard_map/pallas_call | solution.py:379
  302.5 4.3 %shard_map.173 = (f32[256,1024]{1,0:T(8,128)}, bf16[256,1024]{1,0:T(8,128)(2,1)}) custom-call(s32[1]{0:T(128)} %bitcast.flat_ref, bf16[1024,256]{1,0:T(8,128)(2,1)} %get-tuple-element.106.refs_0_, bf16[1024,256]{1,0:T(8,128)(2,1)} %get-tuple-element.107.refs_1_, bf16[1024,256]{1,0:T(8,128)(2,1)} %get-tuple-element.108.refs_2_, bf16[256,768]{1,0:T(8,128)(2,1)} %bitcast.58, ...), custom_call_target="tpu_custom_call" | custom-call | flops 805306368 | bytes 4718592 | tf_op jit(solution)/shard_map/pallas_call | solution.py:379
  311.0 6.4 %shard_map.176 = (bf16[256,1024]{1,0:T(8,128)(2,1)}, bf16[256,1024]{1,0:T(8,128)(2,1)}, bf16[256,1024]{1,0:T(8,128)(2,1)}, bf16[256,1024]{1,0:T(8,128)(2,1)}) custom-call(s32[1]{0:T(128)} %bitcast.flat_ref, bf16[1024,1024]{1,0:T(8,128)(2,1)} %get-tuple-element.114.n_ref, bf16[1024,256]{1,0:T(8,128)(2,1)} %get-tuple-element.106.refs_0_, ...), custom_call_target="tpu_custom_call" | custom-call | flops 1610612736 | bytes 6291456 | tf_op jit(solution)/shard_map/pallas_call | solution.py:379
  318.4 6.3 %collective-permute-done.58 = bf16[256,1968]{0,1:T(8,128)(2,1)S(1)} collective-permute-done((bf16[256,1968]{0,1:T(8,128)(2,1)}, bf16[256,1968]{0,1:T(8,128)(2,1)S(1)}, u32[]{:S(2)}, u32[]{:S(2)}) %collective-permute-start.58) | collective-permute-done | bytes 1007648 | tf_op jit(solution)/shard_map/ppermute | solution.py:332
  338.9 3.8 collective-permute-start.38
  342.7 4.4 %shard_map.175 = bf16[256,1024]{1,0:T(8,128)(2,1)} custom-call(s32[1]{0:T(128)} %bitcast.flat_ref, bf16[1024,1024]{1,0:T(8,128)(2,1)} %get-tuple-element.75.x_ref, f32[256,1024]{1,0:T(8,128)} %get-tuple-element.109.a_ref, bf16[256,1024]{1,0:T(8,128)(2,1)} %collective-permute-done.45.b_ref, bf16[256,1024]{1,0:T(8,128)(2,1)} %collective-permute-done.47.c_ref, ...), custom_call_target="tpu_custom_call" | custom-call | bytes 5767168 | tf_op jit(solution)/shard_map/pallas_call | solution.py:379
  353.4 24.2 %collective-permute-done.59 = bf16[2,64,1968]{2,1,0:T(8,128)(2,1)S(1)} collective-permute-done((bf16[2,64,1968]{2,1,0:T(8,128)(2,1)}, bf16[2,64,1968]{2,1,0:T(8,128)(2,1)S(1)}, u32[]{:S(2)}, u32[]{:S(2)}) %collective-permute-start.59) | collective-permute-done | bytes 503840 | tf_op jit(solution)/shard_map/ppermute | solution.py:332
  386.6 12.1 %collective-permute-start.53 = (bf16[32,1024]{1,0:T(8,128)(2,1)}, bf16[32,1024]{1,0:T(8,128)(2,1)S(1)}, u32[]{:S(2)}, u32[]{:S(2)}) collective-permute-start(bf16[32,1024]{1,0:T(8,128)(2,1)} %get-tuple-element.123), channel_id=1, source_target_pairs={{0,1},{1,0},{2,3},{3,2},{4,5},{5,4},{6,7},{7,6},{8,9},{9,8},{10,11... | collective-permute-start | bytes 196616 | tf_op jit(solution)/shard_map/ppermute | solution.py:332
  400.7 3.9 shard_map.183
  (271 shorter events, 141.5 us)
Async XLA Ops:
  2.5 42.9 %collective-permute-start = (bf16[272,1024]{1,0:T(8,128)(2,1)S(1)}, bf16[272,1024]{1,0:T(8,128)(2,1)}, u32[]{:S(2)}, u32[]{:S(2)}) collective-permute-start(bf16[272,1024]{1,0:T(8,128)(2,1)S(1)} %pad_maximum_fusion.block_ref), channel_id=1, source_target_pairs={{0,1},{1,0},{2,4},{3,5},{4,2},{5,3},{6,7},{7,6},{8,9},{9,8},{10,12... | collective-permute-start | bytes 1671176 | tf_op jit(solution)/shard_map/ppermute | solution.py:332
  25.2 39.5 %collective-permute-start.24 = (bf16[256,1024]{1,0:T(8,128)(2,1)S(1)}, bf16[256,1024]{1,0:T(8,128)(2,1)}, u32[]{:S(2)}, u32[]{:S(2)}) collective-permute-start(bf16[256,1024]{1,0:T(8,128)(2,1)S(1)} %bitcast.61), channel_id=1, source_target_pairs={{0,1},{1,0},{2,4},{3,5},{4,2},{5,3},{6,7},{7,6},{8,9},{9,8},{10,12... | collective-permute-start | bytes 1572872 | tf_op jit(solution)/shard_map/ppermute | solution.py:332
  43.3 31.4 %collective-permute-start.18 = (bf16[256,912]{1,0:T(8,128)(2,1)}, bf16[256,912]{1,0:T(8,128)(2,1)S(1)}, u32[]{:S(2)}, u32[]{:S(2)}) collective-permute-start(bf16[256,912]{1,0:T(8,128)(2,1)} %bitcast.46), channel_id=1, source_target_pairs={{0,8},{1,9},{2,10},{3,11},{4,12},{5,13},{6,14},{7,15},{8,0},{9,1},... | collective-permute-start | bytes 1400840 | tf_op jit(solution)/shard_map/ppermute | solution.py:332
  45.4 29.9 %collective-permute-start.1 = (bf16[272,1024]{1,0:T(8,128)(2,1)}, bf16[272,1024]{1,0:T(8,128)(2,1)S(1)}, u32[]{:S(2)}, u32[]{:S(2)}) collective-permute-start(bf16[272,1024]{1,0:T(8,128)(2,1)} %collective-permute-done.first_ref), channel_id=1, source_target_pairs={{2,3},{3,2},{4,5},{5,4},{10,11},{11,10},{12,13},{13,12},{18,19},{1... | collective-permute-start | bytes 1671176 | tf_op jit(solution)/shard_map/ppermute | solution.py:332
  60.8 40.0 %collective-permute-start.19 = (bf16[256,912]{1,0:T(8,128)(2,1)}, bf16[256,912]{1,0:T(8,128)(2,1)S(1)}, u32[]{:S(2)}, u32[]{:S(2)}) collective-permute-start(bf16[256,912]{1,0:T(8,128)(2,1)} %bitcast.47), channel_id=1, source_target_pairs={{0,16},{1,17},{2,18},{3,19},{4,20},{5,21},{6,22},{7,23},{8,24},{9,... | collective-permute-start | bytes 1400840 | tf_op jit(solution)/shard_map/ppermute | solution.py:332
  64.6 42.6 %collective-permute-start.25 = (bf16[256,1024]{1,0:T(8,128)(2,1)}, bf16[256,1024]{1,0:T(8,128)(2,1)}, u32[]{:S(2)}, u32[]{:S(2)}) collective-permute-start(bf16[256,1024]{1,0:T(8,128)(2,1)} %collective-permute-done.24.first_ref), channel_id=1, source_target_pairs={{2,3},{3,2},{4,5},{5,4},{10,11},{11,10},{12,13},{13,12},{18,19},{1... | collective-permute-start | bytes 1572872 | tf_op jit(solution)/shard_map/ppermute | solution.py:332
  69.8 29.1 %collective-permute-start.31 = (bf16[4,32,1312]{2,1,0:T(8,128)(2,1)}, bf16[4,32,1312]{2,1,0:T(8,128)(2,1)S(1)}, u32[]{:S(2)}, u32[]{:S(2)}) collective-permute-start(bf16[4,32,1312]{2,1,0:T(8,128)(2,1)} %shard_map.163), channel_id=1, source_target_pairs={{0,2},{1,3},{2,0},{3,1},{4,6},{5,7},{6,4},{7,5},{8,10},{9,11},{10,... | collective-permute-start | bytes 1007624 | tf_op jit(solution)/shard_map/ppermute | solution.py:332
  74.7 22.9 %collective-permute-start.7 = (bf16[4,32,768]{2,1,0:T(8,128)(2,1)}, bf16[4,32,768]{2,1,0:T(8,128)(2,1)S(1)}, u32[]{:S(2)}, u32[]{:S(2)}) collective-permute-start(bf16[4,32,768]{2,1,0:T(8,128)(2,1)} %shard_map.154), channel_id=1, source_target_pairs={{0,2},{1,3},{2,0},{3,1},{4,6},{5,7},{6,4},{7,5},{8,10},{9,11},{10,... | collective-permute-start | bytes 589832 | tf_op jit(solution)/shard_map/ppermute | solution.py:332
  75.2 35.3 %collective-permute-start.20 = (bf16[256,912]{1,0:T(8,128)(2,1)S(1)}, bf16[256,912]{1,0:T(8,128)(2,1)S(1)}, u32[]{:S(2)}, u32[]{:S(2)}) collective-permute-start(bf16[256,912]{1,0:T(8,128)(2,1)S(1)} %collective-permute-done.18.refs_5_.refs_2_), channel_id=1, source_target_pairs={{0,16},{1,17},{2,18},{3,19},{4,20},{5,21},{6,22},{7,23},{8,24},{9,... | collective-permute-start | bytes 1400840 | tf_op jit(solution)/shard_map/ppermute | solution.py:332
  110.5 49.0 %collective-permute-start.32 = (bf16[256,1312]{0,1:T(8,128)(2,1)}, bf16[256,1312]{0,1:T(8,128)(2,1)S(1)}, u32[]{:S(2)}, u32[]{:S(2)}) collective-permute-start(bf16[256,1312]{0,1:T(8,128)(2,1)} %copy.52), channel_id=1, source_target_pairs={{0,8},{1,9},{2,10},{3,11},{4,12},{5,13},{6,14},{7,15},{8,0},{9,1},... | collective-permute-start | bytes 2015240 | tf_op jit(solution)/shard_map/ppermute | solution.py:332
  111.6 46.9 %collective-permute-start.33 = (bf16[256,1312]{0,1:T(8,128)(2,1)}, bf16[256,1312]{0,1:T(8,128)(2,1)}, u32[]{:S(2)}, u32[]{:S(2)}) collective-permute-start(bf16[256,1312]{0,1:T(8,128)(2,1)} %copy.52), channel_id=1, source_target_pairs={{0,16},{1,17},{2,18},{3,19},{4,20},{5,21},{6,22},{7,23},{8,24},{9,... | collective-permute-start | bytes 2015240 | tf_op jit(solution)/shard_map/ppermute | solution.py:332
  112.4 45.3 %collective-permute-start.26 = (bf16[256,1024]{1,0:T(8,128)(2,1)}, bf16[256,1024]{1,0:T(8,128)(2,1)}, u32[]{:S(2)}, u32[]{:S(2)}) collective-permute-start(bf16[256,1024]{1,0:T(8,128)(2,1)} %collective-permute-done.24.first_ref), channel_id=1, source_target_pairs={{0,4},{1,5},{2,6},{3,7},{4,0},{5,1},{6,2},{7,3},{8,12},{9,13},{10,... | collective-permute-start | bytes 1572872 | tf_op jit(solution)/shard_map/ppermute | solution.py:332
  114.1 25.9 %collective-permute-start.10 = (bf16[256,768]{1,0:T(8,128)(2,1)S(1)}, bf16[256,768]{1,0:T(8,128)(2,1)S(1)}, u32[]{:S(2)}, u32[]{:S(2)}) collective-permute-start(bf16[256,768]{1,0:T(8,128)(2,1)S(1)} %collective-permute-done.8.refs_1_.refs_4_), channel_id=1, source_target_pairs={{0,16},{1,17},{2,18},{3,19},{4,20},{5,21},{6,22},{7,23},{8,24},{9,... | collective-permute-start | bytes 1179656 | tf_op jit(solution)/shard_map/ppermute | solution.py:332
  122.5 39.5 %collective-permute-start.27 = (bf16[256,1024]{1,0:T(8,128)(2,1)}, bf16[256,1024]{1,0:T(8,128)(2,1)}, u32[]{:S(2)}, u32[]{:S(2)}) collective-permute-start(bf16[256,1024]{1,0:T(8,128)(2,1)} %broadcast_select_fusion.1), channel_id=1, source_target_pairs={{0,4},{1,5},{2,6},{3,7},{4,0},{5,1},{6,2},{7,3},{8,12},{9,13},{10,... | collective-permute-start | bytes 1572872 | tf_op jit(solution)/shard_map/ppermute | solution.py:332
  140.0 22.1 %collective-permute-start.21 = (bf16[1024,256]{1,0:T(8,128)(2,1)S(1)}, bf16[1024,256]{1,0:T(8,128)(2,1)S(1)}, u32[]{:S(2)}, u32[]{:S(2)}) collective-permute-start(bf16[1024,256]{1,0:T(8,128)(2,1)S(1)} %pad_maximum_fusion.3.refs_4_.refs_8_), channel_id=1, source_target_pairs={{0,1},{1,0},{2,3},{3,2},{4,5},{5,4},{6,7},{7,6},{8,9},{9,8},{10,11... | collective-permute-start | bytes 1572872 | tf_op jit(solution)/shard_map/ppermute | solution.py:332
  159.5 21.0 %collective-permute-start.22 = (bf16[1024,256]{1,0:T(8,128)(2,1)S(1)}, bf16[1024,256]{1,0:T(8,128)(2,1)}, u32[]{:S(2)}, u32[]{:S(2)}) collective-permute-start(bf16[1024,256]{1,0:T(8,128)(2,1)S(1)} %pad_maximum_fusion.3.refs_4_.refs_8_), channel_id=1, source_target_pairs={{0,4},{1,5},{2,6},{3,7},{4,0},{5,1},{6,2},{7,3},{8,12},{9,13},{10,... | collective-permute-start | bytes 1572872 | tf_op jit(solution)/shard_map/ppermute | solution.py:332
  229.5 39.1 %collective-permute-start.43 = (bf16[256,1024]{1,0:T(8,128)(2,1)}, bf16[256,1024]{1,0:T(8,128)(2,1)S(1)}, u32[]{:S(2)}, u32[]{:S(2)}) collective-permute-start(bf16[256,1024]{1,0:T(8,128)(2,1)} %get-tuple-element.103.refs_0_), channel_id=1, source_target_pairs={{0,4},{1,5},{2,6},{3,7},{4,0},{5,1},{6,2},{7,3},{8,12},{9,13},{10,... | collective-permute-start | bytes 1572872 | tf_op jit(solution)/shard_map/ppermute | solution.py:332
  241.1 28.6 %collective-permute-start.44 = (bf16[256,1024]{1,0:T(8,128)(2,1)S(1)}, bf16[256,1024]{1,0:T(8,128)(2,1)}, u32[]{:S(2)}, u32[]{:S(2)}) collective-permute-start(bf16[256,1024]{1,0:T(8,128)(2,1)S(1)} %collective-permute-done.42.refs_1_), channel_id=1, source_target_pairs={{0,4},{1,5},{2,6},{3,7},{4,0},{5,1},{6,2},{7,3},{8,12},{9,13},{10,... | collective-permute-start | bytes 1572872 | tf_op jit(solution)/shard_map/ppermute | solution.py:332
  248.0 51.7 %collective-permute-start.36 = (bf16[256,1024]{1,0:T(8,128)(2,1)}, bf16[256,1024]{1,0:T(8,128)(2,1)}, u32[]{:S(2)}, u32[]{:S(2)}) collective-permute-start(bf16[256,1024]{1,0:T(8,128)(2,1)} %get-tuple-element.97), channel_id=1, source_target_pairs={{0,4},{1,5},{2,6},{3,7},{4,0},{5,1},{6,2},{7,3},{8,12},{9,13},{10,... | collective-permute-start | bytes 1572872 | tf_op jit(solution)/shard_map/ppermute | solution.py:332
  252.2 54.5 %collective-permute-start.35 = (bf16[256,1024]{1,0:T(8,128)(2,1)}, bf16[256,1024]{1,0:T(8,128)(2,1)}, u32[]{:S(2)}, u32[]{:S(2)}) collective-permute-start(bf16[256,1024]{1,0:T(8,128)(2,1)} %get-tuple-element.95), channel_id=1, source_target_pairs={{0,4},{1,5},{2,6},{3,7},{4,0},{5,1},{6,2},{7,3},{8,12},{9,13},{10,... | collective-permute-start | bytes 1572872 | tf_op jit(solution)/shard_map/ppermute | solution.py:332
  266.2 44.1 %collective-permute-start.56 = (bf16[256,1968]{0,1:T(8,128)(2,1)}, bf16[256,1968]{0,1:T(8,128)(2,1)S(1)}, u32[]{:S(2)}, u32[]{:S(2)}) collective-permute-start(bf16[256,1968]{0,1:T(8,128)(2,1)} %copy.65), channel_id=1, source_target_pairs={{0,8},{1,9},{2,10},{3,11},{4,12},{5,13},{6,14},{7,15},{8,0},{9,1},... | collective-permute-start | bytes 3022856 | tf_op jit(solution)/shard_map/ppermute | solution.py:332
  268.6 48.8 %collective-permute-start.57 = (bf16[256,1968]{0,1:T(8,128)(2,1)}, bf16[256,1968]{0,1:T(8,128)(2,1)}, u32[]{:S(2)}, u32[]{:S(2)}) collective-permute-start(bf16[256,1968]{0,1:T(8,128)(2,1)} %copy.67), channel_id=1, source_target_pairs={{0,16},{1,17},{2,18},{3,19},{4,20},{5,21},{6,22},{7,23},{8,24},{9,... | collective-permute-start | bytes 3022856 | tf_op jit(solution)/shard_map/ppermute | solution.py:332
  299.7 25.0 %collective-permute-start.58 = (bf16[256,1968]{0,1:T(8,128)(2,1)}, bf16[256,1968]{0,1:T(8,128)(2,1)S(1)}, u32[]{:S(2)}, u32[]{:S(2)}) collective-permute-start(bf16[256,1968]{0,1:T(8,128)(2,1)} %copy.69), channel_id=1, source_target_pairs={{0,24},{1,25},{2,26},{3,27},{4,28},{5,29},{6,30},{7,31},{8,16},{9,... | collective-permute-start | bytes 3022856 | tf_op jit(solution)/shard_map/ppermute | solution.py:332
  307.5 27.4 %collective-permute-start.45 = (bf16[256,1024]{1,0:T(8,128)(2,1)}, bf16[256,1024]{1,0:T(8,128)(2,1)}, u32[]{:S(2)}, u32[]{:S(2)}) collective-permute-start(bf16[256,1024]{1,0:T(8,128)(2,1)} %get-tuple-element.110), channel_id=1, source_target_pairs={{0,4},{1,5},{2,6},{3,7},{4,0},{5,1},{6,2},{7,3},{8,12},{9,13},{10,... | collective-permute-start | bytes 1572872 | tf_op jit(solution)/shard_map/ppermute | solution.py:332
  310.3 28.6 %collective-permute-start.47 = (bf16[256,1024]{1,0:T(8,128)(2,1)}, bf16[256,1024]{1,0:T(8,128)(2,1)}, u32[]{:S(2)}, u32[]{:S(2)}) collective-permute-start(bf16[256,1024]{1,0:T(8,128)(2,1)} %add_convert_fusion), channel_id=1, source_target_pairs={{0,1},{1,0},{2,3},{3,2},{4,5},{5,4},{6,7},{7,6},{8,9},{9,8},{10,11... | collective-permute-start | bytes 1572872 | tf_op jit(solution)/shard_map/ppermute | solution.py:332
  317.4 29.7 %collective-permute-start.49 = (bf16[256,1024]{1,0:T(8,128)(2,1)}, bf16[256,1024]{1,0:T(8,128)(2,1)}, u32[]{:S(2)}, u32[]{:S(2)}) collective-permute-start(bf16[256,1024]{1,0:T(8,128)(2,1)} %get-tuple-element.117), channel_id=1, source_target_pairs={{0,8},{1,9},{2,10},{3,11},{4,12},{5,13},{6,14},{7,15},{8,0},{9,1},... | collective-permute-start | bytes 1572872 | tf_op jit(solution)/shard_map/ppermute | solution.py:332
  324.7 25.1 %collective-permute-start.50 = (bf16[256,1024]{1,0:T(8,128)(2,1)}, bf16[256,1024]{1,0:T(8,128)(2,1)}, u32[]{:S(2)}, u32[]{:S(2)}) collective-permute-start(bf16[256,1024]{1,0:T(8,128)(2,1)} %get-tuple-element.118), channel_id=1, source_target_pairs={{0,16},{1,17},{2,18},{3,19},{4,20},{5,21},{6,22},{7,23},{8,24},{9,... | collective-permute-start | bytes 1572872 | tf_op jit(solution)/shard_map/ppermute | solution.py:332
  325.0 24.8 %collective-permute-start.51 = (bf16[256,1024]{1,0:T(8,128)(2,1)}, bf16[256,1024]{1,0:T(8,128)(2,1)}, u32[]{:S(2)}, u32[]{:S(2)}) collective-permute-start(bf16[256,1024]{1,0:T(8,128)(2,1)} %get-tuple-element.119), channel_id=1, source_target_pairs={{0,24},{1,25},{2,26},{3,27},{4,28},{5,29},{6,30},{7,31},{8,16},{9,... | collective-permute-start | bytes 1572872 | tf_op jit(solution)/shard_map/ppermute | solution.py:332
  334.9 42.6 %collective-permute-start.59 = (bf16[2,64,1968]{2,1,0:T(8,128)(2,1)}, bf16[2,64,1968]{2,1,0:T(8,128)(2,1)S(1)}, u32[]{:S(2)}, u32[]{:S(2)}) collective-permute-start(bf16[2,64,1968]{2,1,0:T(8,128)(2,1)} %get-tuple-element.134), channel_id=1, source_target_pairs={{0,2},{1,3},{2,0},{3,1},{4,6},{5,7},{6,4},{7,5},{8,10},{9,11},{10,... | collective-permute-start | bytes 1511432 | tf_op jit(solution)/shard_map/ppermute | solution.py:332
  338.9 47.7 %collective-permute-start.38 = (bf16[256,1024]{1,0:T(8,128)(2,1)S(1)}, bf16[256,1024]{1,0:T(8,128)(2,1)S(1)}, u32[]{:S(2)}, u32[]{:S(2)}) collective-permute-start(bf16[256,1024]{1,0:T(8,128)(2,1)S(1)} %add_convert_fusion.2), channel_id=1, source_target_pairs={{0,0},{1,1},{2,4},{3,5},{4,2},{5,3},{6,6},{7,7},{8,8},{9,9},{10,12... | collective-permute-start | bytes 1572872 | tf_op jit(solution)/shard_map/ppermute | solution.py:332
  347.1 63.0 %collective-permute-start.48 = (bf16[256,1024]{1,0:T(8,128)(2,1)}, bf16[256,1024]{1,0:T(8,128)(2,1)S(1)}, u32[]{:S(2)}, u32[]{:S(2)}) collective-permute-start(bf16[256,1024]{1,0:T(8,128)(2,1)} %shard_map.175), channel_id=1, source_target_pairs={{0,0},{1,1},{2,4},{3,5},{4,2},{5,3},{6,6},{7,7},{8,8},{9,9},{10,12... | collective-permute-start | bytes 1572872 | tf_op jit(solution)/shard_map/ppermute | solution.py:332
  352.1 30.7 %collective-permute-start.52 = (bf16[2,64,1024]{2,1,0:T(8,128)(2,1)}, bf16[2,64,1024]{2,1,0:T(8,128)(2,1)S(1)}, u32[]{:S(2)}, u32[]{:S(2)}) collective-permute-start(bf16[2,64,1024]{2,1,0:T(8,128)(2,1)} %get-tuple-element.121), channel_id=1, source_target_pairs={{0,2},{1,3},{2,0},{3,1},{4,6},{5,7},{6,4},{7,5},{8,10},{9,11},{10,... | collective-permute-start | bytes 786440 | tf_op jit(solution)/shard_map/ppermute | solution.py:332
  (83 other events, 966.8 us)

commit v3 on v2

--- a/solution.py
+++ b/solution.py
@@ -298,7 +298,7 @@
 
 
 QUAD_MESH = (8, 4)
-FLAT = ("dp", "seq")
+FLAT = ("y", "x", "c", "zh", "zl")
 LOW, WIDE = jnp.bfloat16, jnp.float32
 
 
@@ -328,8 +328,24 @@
 ENTER_MOVED = pairs_of(lambda y, x, c, zh, zl: None if c == zh else (y, x, c, zh, 1 - zl))
 
 
+class Order(list):
+    pass
+
+
 def send(array, pairs):
     return lax.ppermute(array, FLAT, pairs)
+
+
+def after(order, array):
+    return lax.optimization_barrier((array, order[0]))[0]
+
+
+def wait(order, *arrays):
+    order[0] = lax.optimization_barrier((order[0], *arrays))[0]
+
+
+def lanes(size):
+    return -(-size // 128) * 128
 
 
 def core_of(flat):
@@ -373,10 +389,10 @@
     return (array, (rows,) + array.shape[1:], lambda b, f: (step(b),) + (0,) * (len(array.shape) - 1))
 
 
-def run(body, flat, grid, ins, outs, scratch=(), flops=0):
+def run(body, order, grid, ins, outs, scratch=(), flops=0):
     moved = sum(a.size * a.dtype.itemsize for a, _, _ in ins)
     moved += sum(a.size * a.dtype.itemsize for a, _, _ in outs)
-    return pl.pallas_call(
+    made = pl.pallas_call(
         body,
         grid_spec=pltpu.PrefetchScalarGridSpec(
             num_scalar_prefetch=1,
@@ -386,12 +402,38 @@
             scratch_shapes=list(scratch),
         ),
         out_shape=[a for a, _, _ in outs],
-        cost_estimate=pl.CostEstimate(flops=flops, bytes_accessed=moved, transcendentals=0),
-    )(flat, *[a for a, _, _ in ins])
+        cost_estimate=pl.CostEstimate(flops=flops // 100, bytes_accessed=moved // 100, transcendentals=0),
+    )(order[0], *[a for a, _, _ in ins])
+    order[0], _ = lax.optimization_barrier((order[0], made[0]))
+    return made
+
+
+def spans(pieces):
+    rows = pieces[0].shape[0]
+    return [(0, 0, rows), (1, 0, rows), (2, 0, rows), (3, 0, rows // 2), (3, rows // 2, rows // 2)]
+
+
+def span_of(square, span, rows):
+    index, first, count = span
+    return pl.ds(pl.multiple_of((square ^ index) * rows + first, count), count)
 
 
 def shape_of(*dims, dtype=LOW):
     return jax.ShapeDtypeStruct(dims, dtype)
+
+
+def column_of(row):
+    size = row.shape[1]
+    down = lax.broadcasted_iota(jnp.int32, (size, size), 0)
+    across = lax.broadcasted_iota(jnp.int32, (size, size), 1)
+    return jnp.sum(jnp.where(down == across, row, 0.0), axis=1, keepdims=True)
+
+
+def row_of(column):
+    size = column.shape[0]
+    down = lax.broadcasted_iota(jnp.int32, (size, size), 0)
+    across = lax.broadcasted_iota(jnp.int32, (size, size), 1)
+    return jnp.sum(jnp.where(down == across, column, 0.0), axis=0, keepdims=True)
 
 
 def normed_of(x):
@@ -400,66 +442,48 @@
     return centred * spread, spread
 
 
-def split_qkv(flat, weight, gain):
-    rows, part = weight.shape[0], weight.shape[1] // 12
-
-    def body(flat_ref, w_ref, gain_ref, *refs):
+def split_slices(order, scaled, plain, gain, parts):
+    rows, part, rest = scaled.shape[0], scaled.shape[1] // (4 * parts), plain.shape[1] // 4
+    out = shape_of(rows, lanes(parts * part + rest))
+
+    def body(flat_ref, scaled_ref, plain_ref, gain_ref, *refs):
         held = refs[4]
+        scale = column_of(gain_ref[...].astype(WIDE))
         for s in range(4):
-            for t in range(3):
-                cols = w_ref[:, (4 * t + s) * part : (4 * t + s + 1) * part].astype(WIDE)
-                held[s, :, t * part : (t + 1) * part] = (cols * gain_ref[...]).astype(LOW)
+            for t in range(parts):
+                cols = scaled_ref[:, (4 * t + s) * part : (4 * t + s + 1) * part].astype(WIDE)
+                held[s, :, t * part : (t + 1) * part] = (cols * scale).astype(LOW)
+            held[s, :, parts * part : parts * part + rest] = plain_ref[
+                :, s * rest : (s + 1) * rest
+            ]
         for i in range(4):
             refs[i][...] = held[group_of(flat_ref[0]) ^ i]
 
-    out = shape_of(rows, 3 * part)
-    return run(
-        body, flat, (1,), [whole(weight), whole(gain)], [whole(out)] * 4,
-        [pltpu.VMEM((4, rows, 3 * part), LOW)],
-    )
-
-
-def split_rest(flat, out_weight, up_weight, down_weight, gain):
-    rows, part, ff = out_weight.shape[0], out_weight.shape[1] // 4, down_weight.shape[1] // 4
-
-    def body(flat_ref, out_ref, up_ref, down_ref, gain_ref, *refs):
-        ups, downs = refs[8:]
-        for s in range(4):
-            for t in range(2):
-                cols = up_ref[:, (4 * t + s) * ff : (4 * t + s + 1) * ff].astype(WIDE)
-                ups[s, :, t * ff : (t + 1) * ff] = (cols * gain_ref[...]).astype(LOW)
-            downs[s, :, :part] = out_ref[:, s * part : (s + 1) * part]
-            downs[s, :, part:] = down_ref[:, s * ff : (s + 1) * ff]
-        for i in range(4):
-            refs[i][...] = ups[group_of(flat_ref[0]) ^ i]
-            refs[4 + i][...] = downs[group_of(flat_ref[0]) ^ i]
-
-    up, down = shape_of(rows, 2 * ff), shape_of(rows, part + ff)
-    made = run(
-        body, flat, (1,), [whole(a) for a in (out_weight, up_weight, down_weight, gain)],
-        [whole(up)] * 4 + [whole(down)] * 4,
-        [pltpu.VMEM((4, rows, 2 * ff), LOW), pltpu.VMEM((4, rows, part + ff), LOW)],
-    )
-    return made[:4], made[4:]
-
-
-def quad_rows(flat, slices):
-    rows, width = slices[0].shape
-    parts = [slices[0]] + [
+    return run(
+        body, order, (1,), [whole(a) for a in (scaled, plain, gain)], [whole(out)] * 4,
+        [pltpu.VMEM((4, *out.shape), LOW)],
+    )
+
+
+def share_slices(slices):
+    return [slices[0]] + [
         send(slices[i], pairs) for i, pairs in ((1, TO_ZL), (2, TO_CORE), (3, TO_FAR))
     ]
 
+
+def quad_rows(order, parts):
     def body(flat_ref, *refs):
         for i in range(4):
             refs[4][group_of(flat_ref[0]) ^ i] = refs[i][...]
 
-    return run(body, flat, (1,), [whole(p) for p in parts], [whole(shape_of(4, rows, width))])[0]
-
-
-def line_rows(flat, quad):
-    _, rows, width = quad.shape
-    near = quad.reshape(2, 2 * rows, width)
-    far = send(quad, TO_ZH).reshape(2, 2 * rows, width)
+    out = shape_of(4, *parts[0].shape)
+    return run(body, order, (1,), [whole(p) for p in parts], [whole(out)])[0]
+
+
+def line_rows(order, near, far):
+    _, rows, width = near.shape
+    near = near.reshape(2, 2 * rows, width)
+    far = far.reshape(2, 2 * rows, width)
 
     def body(flat_ref, near_ref, far_ref, out_ref):
         half = half_of(flat_ref[0])
@@ -468,32 +492,19 @@
             out_ref[c, 1 - half] = far_ref[c]
 
     out = run(
-        body, flat, (1,), [whole(near), whole(far)], [whole(shape_of(2, 2, 2 * rows, width))]
+        body, order, (1,), [whole(near), whole(far)], [whole(shape_of(2, 2, 2 * rows, width))]
     )[0]
     return out.reshape(8 * rows, width)
 
 
-def square_pieces(line, x_first):
-    one, two = (TO_X, TO_Y) if x_first else (TO_Y, TO_X)
-    first = send(line, one)
-    second = send(line, two)
-    third = send(first, two)
-    return [line, first, second, third] if x_first else [line, second, first, third]
-
-
-def enter_quad(flat, block, rows):
-    height, width = block.shape
+def join_tokens(order, parts, rows):
+    height, width = parts[0].shape
     extra = height - rows
-    at_home = core_of(flat[0]) == half_of(flat[0])
-    first = send(block, ENTER)
-    near = send(first, TO_CORE)
-    second = send(first, ENTER_MOVED)
-    far = send(jnp.where(at_home, block, second), TO_CORE)
-
-    def body(flat_ref, block_ref, first_ref, second_ref, near_ref, far_ref, *outs):
+
+    def body(flat_ref, block, first, second, core_block, core_first, core_second, *outs):
         home = core_of(flat_ref[0]) == half_of(flat_ref[0])
-        here = (block_ref, first_ref, near_ref, far_ref)
-        moved = (first_ref, second_ref, far_ref, near_ref)
+        here = (block, first, core_first, core_second)
+        moved = (first, second, core_block, core_first)
         for k in range(4):
             for flag, source in ((home, here[k]), (jnp.logical_not(home), moved[k])):
 
@@ -509,14 +520,9 @@
 
     made = [shape_of(4 * rows, width)] + ([shape_of(4 * extra, width)] if extra else [])
     return run(
-        body, flat, (4,), [whole(a) for a in (block, first, second, near, far)],
+        body, order, (4,), [whole(a) for a in parts],
         [by_rows(m, m.shape[0] // 4) for m in made],
     )
-
-
-def quad_gather(block):
-    side = send(block, TO_ZL)
-    return [block, side, send(block, TO_CORE), send(side, TO_CORE)]
 
 
 def rope_lanes(seq_pos):
@@ -537,16 +543,19 @@
     )
 
 
-def project(flat, x, pieces, cos_table, sin_table):
+def project(order, x, pieces, cos_table, sin_table):
     tokens, width = x.shape
-    piece, columns = pieces[0].shape
+    piece, columns = pieces[0].shape[0], 3 * width // 4
     rows = tokens // 4
 
     def body(flat_ref, x_ref, *refs):
-        weights, (cos_ref, sin_ref, n_ref, mix_ref) = refs[:4], refs[4:]
+        weights, (cos_ref, sin_ref, n_ref, mix_ref) = refs[:5], refs[5:]
         n_ref[...] = normed_of(x_ref[...].astype(WIDE))[0].astype(LOW)
         square = square_of(flat_ref[0])
-        mixed = sum(mm(n_ref[:, window(square ^ i, piece)], weights[i][...]) for i in range(4))
+        mixed = sum(
+            mm(n_ref[:, span_of(square, span, piece)], w[:, :columns])
+            for span, w in zip(spans(pieces), weights)
+        )
         turned_to = 2 * columns // 3
         for t in range(0, turned_to, 128):
             v = mixed[:, t : t + 128]
@@ -554,7 +563,7 @@
         mix_ref[:, turned_to:] = mixed[:, turned_to:].astype(LOW)
 
     return run(
-        body, flat, (4,),
+        body, order, (4,),
         [by_rows(x, rows)] + [whole(p) for p in pieces]
         + [by_rows(cos_table, rows), by_rows(sin_table, rows)],
         [by_rows(shape_of(tokens, width), rows), by_rows(shape_of(tokens, columns), rows)],
@@ -562,7 +571,7 @@
     )
 
 
-def attend(flat, mix):
+def attend(order, mix):
     tokens, columns = mix.shape
     part = columns // 3
     rows = tokens // 4
@@ -587,7 +596,7 @@
         log_ref[...] = logs
 
     return run(
-        body, flat, (4,),
+        body, order, (4,),
         [
             (mix, (rows, part), lambda b, f: (b, 0)),
             (mix, (tokens, part), lambda b, f: (0, 1)),
@@ -602,7 +611,7 @@
     return [by_rows(a, rows, lambda b, i=i: b ^ i) for i, a in enumerate(arrays)]
 
 
-def join_heads(flat, x, heads, columns):
+def join_heads(order, x, heads, columns):
     tokens, width = x.shape
     rows, part = tokens // 4, width // 4
 
@@ -623,7 +632,7 @@
             own_ref[...] = held[...]
 
     return run(
-        body, flat, (4,),
+        body, order, (4,),
         [by_rows(x, rows)] + token_parts(heads, rows) + [whole(w) for w in columns],
         [by_rows(shape_of(tokens, width), rows), whole(shape_of(rows, width, dtype=WIDE))],
         [pltpu.VMEM((rows, width), WIDE)],
@@ -631,19 +640,17 @@
     )
 
 
-def feed(flat, normed, cot, ups, downs):
+def feed(order, normed, cot, pieces):
     tokens, width = normed.shape
-    piece, ff = ups[0].shape[0], ups[0].shape[1] // 2
-    skip = downs[0].shape[1] - ff
+    piece, ff = pieces[0].shape[0], FF // 4
     rows = tokens // 4
 
     def body(flat_ref, n_ref, cot_ref, *refs):
-        up_refs, down_refs, (h_ref, d_ref) = refs[:4], refs[4:8], refs[8:]
+        weights, (h_ref, d_ref) = refs[:5], refs[5:]
         square = square_of(flat_ref[0])
-        wide = sum(mm(n_ref[:, window(square ^ i, piece)], up_refs[i][...]) for i in range(4))
-        d_hidden = sum(
-            mm(cot_ref[:, window(square ^ i, piece)], down_refs[i][:, skip:]) for i in range(4)
-        )
+        cols = [span_of(square, span, piece) for span in spans(pieces)]
+        wide = sum(mm(n_ref[:, at], w[:, : 2 * ff]) for at, w in zip(cols, weights))
+        d_hidden = sum(mm(cot_ref[:, at], w[:, 2 * ff : 3 * ff]) for at, w in zip(cols, weights))
         inner, gate = wide[:, :ff], wide[:, ff:]
         cdf = 0.5 * (1.0 + lax.erf(inner * inv_root_two))
         slope = cdf + inner * jnp.exp(-0.5 * inner * inner) * inv_root_tau
@@ -653,55 +660,37 @@
         d_ref[:, ff:] = (d_hidden * bent).astype(LOW)
 
     return run(
-        body, flat, (4,),
-        [by_rows(normed, rows), by_rows(cot, rows)] + [whole(w) for w in (*ups, *downs)],
+        body, order, (4,),
+        [by_rows(normed, rows), by_rows(cot, rows)] + [whole(w) for w in pieces],
         [by_rows(shape_of(tokens, ff), rows), by_rows(shape_of(tokens, 2 * ff), rows)],
         flops=6 * tokens * width * ff,
     )
 
 
-def back_pair(flat, grads, pieces, odd):
+def back_half(order, grads, pieces, far):
     tokens = grads[0][0].shape[0]
     piece = pieces[0].shape[0]
-    rows, width, count = tokens // 4, 4 * piece, len(grads)
+    rows, width, count = tokens // 2, 4 * piece, len(grads)
+    out = shape_of(rows, width, dtype=LOW if far else WIDE)
 
     def body(flat_ref, *refs):
-        arrays, weights, (near_ref, far_ref, held) = (
-            refs[:count], refs[count : count + 4], refs[count + 4 :],
-        )
+        arrays, weights, out_ref = refs[:count], refs[count : count + 5], refs[count + 5]
         square = square_of(flat_ref[0])
-        for i in range(4):
-            held[:, window(square ^ i, piece)] = sum(
-                mm_t(a[...], weights[i][:, at : at + a.shape[1]])
-                for a, (_, at) in zip(arrays, grads)
-            )
-
-        @pl.when(pl.program_id(0) == 0)
-        def _():
-            near_ref[...] = held[...]
-
-        @pl.when(pl.program_id(0) == 1)
-        def _():
-            far_ref[...] = held[...].astype(LOW)
-
-    return run(
-        body, flat, (2,),
-        [by_rows(a, rows, lambda b: 2 * b + odd) for a, _ in grads] + [whole(p) for p in pieces],
-        [whole(shape_of(rows, width, dtype=WIDE)), whole(shape_of(rows, width))],
-        [pltpu.VMEM((rows, width), WIDE)],
+        for span, w in zip(spans(pieces), weights):
+            out_ref[:, span_of(square, span, piece)] = sum(
+                mm_t(a[...], w[:, at : at + a.shape[1]]) for a, (_, at) in zip(arrays, grads)
+            ).astype(out.dtype)
+
+    return run(
+        body, order, (1,),
+        [by_rows(a, rows, lambda b: int(far)) for a, _ in grads] + [whole(p) for p in pieces],
+        [whole(out)],
         flops=tokens * width * sum(a.shape[1] for a, _ in grads),
-    )
-
-
-def quad_sum(flat, grads, pieces):
-    near, far = back_pair(flat, grads, pieces, 1)
-    side = send((near + send(far, TO_CORE).astype(WIDE)).astype(LOW), TO_ZL)
-    own, far = back_pair(flat, grads, pieces, 0)
-    return own, send(far, TO_CORE), side
-
-
-def norm_pull(flat, x, terms, base, keep):
-    rows, width = terms[0].shape
+    )[0]
+
+
+def norm_pull(order, x, terms, base, keep):
+    rows, width = base.shape[0] // (4 if keep else 1), base.shape[1]
     step = rows // 4
 
     def body(flat_ref, x_ref, a_ref, b_ref, c_ref, base_ref, *outs):
@@ -718,42 +707,39 @@
 
     outs = [shape_of(rows, width)] + ([shape_of(rows, width, dtype=WIDE)] if keep else [])
     return run(
-        body, flat, (4,), [by_rows(a, step) for a in (x, *terms, base)],
+        body, order, (4,), [by_rows(a, step) for a in (x, *terms, base)],
         [by_rows(o, step) for o in outs],
     )
 
 
-def feed_grads(flat, normed, cot, d_up, hidden):
+def feed_grads(order, normed, cot, d_up, hidden):
     tokens, width = normed.shape
     rows, piece = tokens // 4, width // 4
     ff = hidden.shape[1]
-
-    def body(flat_ref, n_ref, cot_ref, d_ref, h_ref, *refs):
-        outs, held = refs[:4], refs[4]
-        square = square_of(flat_ref[0])
-
+    out = shape_of(4, piece, lanes(3 * ff))
+
+    def body(flat_ref, n_ref, cot_ref, d_ref, h_ref, out_ref, held):
         @pl.when(pl.program_id(0) == 0)
         def _():
             held[...] = jnp.zeros_like(held)
 
         for i in range(4):
-            cols = window(square ^ i, piece)
+            cols = slice(i * piece, (i + 1) * piece)
             held[i, :, : 2 * ff] += t_mm(n_ref[:, cols], d_ref[...])
-            held[i, :, 2 * ff :] += t_mm(cot_ref[:, cols], h_ref[...])
+            held[i, :, 2 * ff : 3 * ff] += t_mm(cot_ref[:, cols], h_ref[...])
 
         @pl.when(pl.program_id(0) == 3)
         def _():
-            for i in range(4):
-                outs[i][...] = held[i].astype(LOW)
-
-    return run(
-        body, flat, (4,), [by_rows(a, rows) for a in (normed, cot, d_up, hidden)],
-        [whole(shape_of(piece, 3 * ff))] * 4, [pltpu.VMEM((4, piece, 3 * ff), WIDE)],
+            out_ref[...] = held[...].astype(LOW)
+
+    return run(
+        body, order, (4,), [by_rows(a, rows) for a in (normed, cot, d_up, hidden)],
+        [whole(out)], [pltpu.VMEM(out.shape, WIDE)],
         flops=6 * tokens * width * ff,
-    )
-
-
-def heads_back(flat, d_all, heads, columns):
+    )[0]
+
+
+def heads_back(order, d_all, heads, columns):
     rows, width = d_all[0].shape
     part = width // 4
 
@@ -791,7 +777,7 @@
             grad_ref[...] = total[...].astype(LOW)
 
     return run(
-        body, flat, (4,),
+        body, order, (4,),
         [whole(d) for d in d_all] + token_parts(heads, rows) + [whole(w) for w in columns],
         [by_rows(shape_of(4 * rows, part), rows), whole(shape_of(4, part, part))],
         [
@@ -803,7 +789,7 @@
     )
 
 
-def attend_back(flat, mix, attended, d_attended, logs, cos_table, sin_table):
+def attend_back(order, mix, attended, d_attended, logs, cos_table, sin_table):
     tokens, columns = mix.shape
     part = columns // 3
     rows = tokens // 4
@@ -853,7 +839,7 @@
 
     out = shape_of(tokens, part)
     return run(
-        body, flat, (4,),
+        body, order, (4,),
         [
             (mix, (rows, part), lambda b, f: (b, 0)),
             (mix, (tokens, part), lambda b, f: (0, 1)),
@@ -870,7 +856,7 @@
     )
 
 
-def mixed_grads(flat, normed, d_mixed, out_grad):
+def mixed_grads(order, normed, d_mixed, out_grad):
     tokens, width = normed.shape
     rows, piece = tokens // 4, width // 4
     part = d_mixed[0].shape[1]
@@ -895,50 +881,60 @@
                 outs[i][:, 3 * part :] = out_ref[i]
 
     return run(
-        body, flat, (4,),
+        body, order, (4,),
         [by_rows(normed, rows)] + [by_rows(d, rows) for d in d_mixed] + [whole(out_grad)],
         [whole(shape_of(piece, 4 * part))] * 4, [pltpu.VMEM((4, piece, 3 * part), WIDE)],
         flops=6 * tokens * width * part,
     )
 
 
-def owned_slices(flat, pieces):
-    high, width = pieces[0].shape
-    rows = high // 8
-    terms = [pieces[0]] + [
+def share_pieces(pieces):
+    return [pieces[0]] + [
         send(pieces[i], pairs) for i, pairs in ((1, TO_X), (2, TO_Y), (3, TO_XY))
     ]
-    terms = [t.reshape(2, 2, 2 * rows, width) for t in terms]
-
-    def fold(flat_ref, *refs):
+
+
+def fold(order, terms):
+    high, width = terms[0].shape[1:]
+    rows = high // 4
+    terms = [t.reshape(-1, 2, 2, rows, width) for t in terms]
+
+    def body(flat_ref, *refs):
+        ins, (kept_ref, sent_ref) = refs[:-2], refs[-2:]
         half = half_of(flat_ref[0])
-        refs[4][0] = sum(refs[i][0, half].astype(WIDE) for i in range(4))
-        refs[5][0] = sum(refs[i][0, 1 - half].astype(WIDE) for i in range(4)).astype(LOW)
-
-    kept, sent = run(
-        fold, flat, (2,), [by_rows(t, 1) for t in terms],
+
+        def total(at):
+            return sum(r[k, 0, at].astype(WIDE) for r in ins for k in range(r.shape[0]))
+
+        kept_ref[0] = total(half)
+        sent_ref[0] = total(1 - half).astype(LOW)
+
+    return run(
+        body, order, (2,),
         [
-            by_rows(shape_of(2, 2 * rows, width, dtype=WIDE), 1),
-            by_rows(shape_of(2, 2 * rows, width), 1),
+            (t, (t.shape[0], 1) + t.shape[2:], lambda b, f: (0, b, 0, 0, 0))
+            for t in terms
         ],
-    )
-    kept = kept.reshape(4, rows, width)
-    sent = send(sent, TO_ZH).reshape(4, rows, width)
-
-    def share(flat_ref, kept_ref, sent_ref, *outs):
+        [by_rows(shape_of(2, rows, width, dtype=WIDE), 1), by_rows(shape_of(2, rows, width), 1)],
+    )
+
+
+def split_rows(order, kept, received):
+    _, high, width = kept.shape
+    rows = high // 2
+    kept, received = kept.reshape(4, rows, width), received.reshape(4, rows, width)
+
+    def body(flat_ref, kept_ref, received_ref, *outs):
         for i in range(4):
             at = group_of(flat_ref[0]) ^ i
-            outs[i][...] = (kept_ref[at] + sent_ref[at].astype(WIDE)).astype(LOW)
-
-    slices = run(
-        share, flat, (1,), [whole(kept), whole(sent)], [whole(shape_of(rows, width))] * 4
-    )
-    return [slices[0]] + [
-        send(slices[i], pairs) for i, pairs in ((1, TO_ZL), (2, TO_CORE), (3, TO_FAR))
-    ]
-
-
-def finish(flat, slices, weight, gain, sizes):
+            outs[i][...] = (kept_ref[at] + received_ref[at].astype(WIDE)).astype(LOW)
+
+    return run(
+        body, order, (1,), [whole(kept), whole(received)], [whole(shape_of(rows, width))] * 4
+    )
+
+
+def finish(order, slices, weight, gain, sizes):
     rows, width = slices[0].shape
     count, part, rest = sizes
 
@@ -947,6 +943,7 @@
         for i in range(4):
             held[group_of(flat_ref[0]) ^ i] = refs[i][...].astype(WIDE)
         total = jnp.zeros((rows, 1), WIDE)
+        scale = column_of(gain_ref[...].astype(WIDE))
         for s in range(4):
             for t in range(count):
                 at = (4 * t + s) * part
@@ -954,15 +951,15 @@
                 total += jnp.sum(
                     grad * w_ref[:, at : at + part].astype(WIDE), axis=1, keepdims=True
                 )
-                scaled_ref[:, at : at + part] = grad * gain_ref[...]
-            plain_ref[:, s * rest : (s + 1) * rest] = held[s, :, count * part :]
-        gain_out[...] = total
-
-    return run(
-        body, flat, (1,), [whole(a) for a in (*slices, weight, gain)],
+                scaled_ref[:, at : at + part] = grad * scale
+            plain_ref[:, s * rest : (s + 1) * rest] = held[s, :, count * part : count * part + rest]
+        gain_out[...] = row_of(total)
+
+    return run(
+        body, order, (1,), [whole(a) for a in (*slices, weight, gain)],
         [
             whole(shape_of(*weight.shape, dtype=WIDE)),
-            whole(shape_of(rows, 1, dtype=WIDE)),
+            whole(shape_of(1, rows, dtype=WIDE)),
             whole(shape_of(rows, 4 * rest, dtype=WIDE)),
         ],
         [pltpu.VMEM((4, rows, width), WIDE)],
@@ -980,87 +977,167 @@
     down_weight,
     cotangent,
 ):
-    flat = lax.axis_index(FLAT).astype(jnp.int32).reshape(1)
+    order = Order([lax.axis_index(FLAT).astype(jnp.int32).reshape(1)])
     tokens, width = inputs.shape[1:]
     part, ff = width // 4, FF // 4
-    gain_one, gain_two = attn_gain.astype(WIDE)[:, None], mlp_gain.astype(WIDE)[:, None]
-
+    gain_one, gain_two = attn_gain[None], mlp_gain[None]
+
+    one = share_slices(split_slices(order, qkv_weight, attn_out_weight, gain_one, 3))
     pos = positions[0]
     pos_row = jnp.concatenate([pos // 128, pos % 128]).astype(LOW)
     pos_row = jnp.pad(pos_row[None], ((0, 15), (0, width - 2 * tokens)))
-    x, pos_all = enter_quad(flat, jnp.concatenate([inputs[0], pos_row]), tokens)
-    w_qkv = split_qkv(flat, qkv_weight, gain_one)
-    w_qkv = square_pieces(line_rows(flat, quad_rows(flat, w_qkv)), True)
-    w_up, w_down = split_rest(flat, attn_out_weight, up_weight, down_weight, gain_two)
-    w_down = square_pieces(line_rows(flat, quad_rows(flat, w_down)), True)
-    w_up = square_pieces(line_rows(flat, quad_rows(flat, w_up)), False)
-    w_out = quad_gather(jnp.concatenate([p[:, :part] for p in w_down]))
-    (cot,) = enter_quad(flat, cotangent[0], tokens)
-
+    block = jnp.concatenate([inputs[0], pos_row])
+    two = split_slices(order, up_weight, down_weight, gain_two, 2)
+    first = send(after(order, block), ENTER)
+    one = quad_rows(order, one)
+    one_far = send(one, TO_ZH)
+    two = share_slices([after(order, t) for t in two])
+    one = line_rows(order, one, one_far)
+    half = one.shape[0] // 2
+    one_x, one_y = send(one, TO_X), send(one, TO_Y)
+    two = quad_rows(order, two)
+    two_far = send(two, TO_ZH)
+    second = send(after(order, first), ENTER_MOVED)
+    core_first = send(after(order, first), TO_CORE)
+    wait(order, core_first, second)
+    core_block = send(after(order, block), TO_CORE)
+    core_second = send(after(order, second), TO_CORE)
+    x, pos_all = join_tokens(
+        order, [block, first, second, core_block, core_first, core_second], tokens
+    )
+    cot_first = send(after(order, cotangent[0]), ENTER)
+    one_top = send(one_x[:half], TO_Y)
+    one_low = send(one_y[half:], TO_X)
     pos_all = pos_all.reshape(4, 16, width)[:, 0, : 2 * tokens].astype(WIDE)
     pos_all = (pos_all[:, :tokens] * 128.0 + pos_all[:, tokens:]).reshape(4 * tokens)
     cos_table, sin_table = rope_lanes(pos_all)
-    normed_one, mix = project(flat, x, w_qkv, cos_table, sin_table)
-    attended, logs = attend(flat, mix)
+    one = [one, one_x, one_y, one_top, one_low]
+
+    normed_one, mix = project(order, x, one, cos_table, sin_table)
+    w_out = after(order, jnp.concatenate([p[:, 3 * part :] for p in one]))
+    w_side = send(w_out, TO_ZL)
+    w_core = send(w_out, TO_CORE)
+    two = line_rows(order, two, two_far)
+    two_x, two_y = send(two, TO_X), send(two, TO_Y)
+    attended, logs = attend(order, mix)
+    att_side = send(attended, TO_ZL)
+    att_core = send(attended, TO_CORE)
+    w_far = send(after(order, w_side), TO_CORE)
+    w_out = [w_out, w_side, w_core, w_far]
+    wait(order, w_far, cot_first)
+    cot_second = send(after(order, cot_first), ENTER_MOVED)
     logs = logs[:, :8].T
-    heads = quad_gather(attended)
-    normed_two, resid = join_heads(flat, x, heads, w_out)
-    hidden, d_up = feed(flat, normed_two, cot, w_up, w_down)
-    terms = quad_sum(flat, [(d_up, 0)], w_up)
-    d_low, d_resid = norm_pull(flat, resid, terms, cot, True)
-    ff_pieces = feed_grads(flat, normed_two, cot, d_up, hidden)
-    d_all = quad_gather(d_low)
-    out_terms = quad_sum(flat, [(hidden, part)], w_down)
-    output = resid + out_terms[0] + out_terms[1].astype(WIDE) + out_terms[2].astype(WIDE)
-    output = send(output.astype(LOW), TO_HOME)
-    d_attended, out_grad = heads_back(flat, d_all, heads, w_out)
-    d_mixed = attend_back(flat, mix, attended, d_attended, logs, cos_table, sin_table)
-    mixed_pieces = mixed_grads(flat, normed_one, d_mixed, out_grad)
-    terms = quad_sum(flat, [(d, t * part) for t, d in enumerate(d_mixed)], w_qkv)
-    (input_grad,) = norm_pull(flat, x, terms, d_resid, False)
+    wait(order, att_side, logs)
+    heads = [attended, att_side, att_core, send(att_side, TO_CORE)]
+    normed_two, resid = join_heads(order, x, heads, w_out)
+
+    two_top = send(two_x[:half], TO_Y)
+    two_low = send(two_y[half:], TO_X)
+    core_block = send(after(order, cotangent[0]), TO_CORE)
+    core_first = send(after(order, cot_first), TO_CORE)
+    core_second = send(after(order, cot_second), TO_CORE)
+    (cot,) = join_tokens(
+        order,
+        [cotangent[0], cot_first, cot_second, core_block, core_first, core_second],
+        tokens,
+    )
+    two = [two, two_x, two_y, two_top, two_low]
+    hidden, d_up = feed(order, normed_two, cot, two)
+
+    def crossed(far):
+        return send(far, TO_CORE)
+
+    def side_of(near, far):
+        return send((near[tokens:] + far[tokens:].astype(WIDE)).astype(LOW), TO_ZL)
+
+    grads = [(d_up, 0)]
+    far = crossed(back_half(order, grads, two, True))
+    near = back_half(order, grads, two, False)
+    side = side_of(near, far)
+    ff_terms = feed_grads(order, normed_two, cot, d_up, hidden)
+    d_low, d_resid = norm_pull(order, resid, (near, far, side), cot, True)
+    ff_terms = lax.all_to_all(
+        after(order, ff_terms), ("y", "x"), split_axis=0, concat_axis=0, tiled=True
+    )
+    d_side = send(d_low, TO_ZL)
+    d_core = send(d_low, TO_CORE)
+    grads = [(hidden, 2 * ff)]
+    out_far = back_half(order, grads, two, True)
+    out_near = back_half(order, grads, two, False)
+    d_all = [d_low, d_side, d_core, send(after(order, d_side), TO_CORE)]
+    d_attended, out_grad = heads_back(order, d_all, heads, w_out)
+    out_far = crossed(after(order, out_far))
+    out_side = side_of(out_near, out_far)
+    d_mixed = attend_back(order, mix, attended, d_attended, logs, cos_table, sin_table)
+    output = resid + out_near[:tokens] + out_far[:tokens].astype(WIDE) + out_side.astype(WIDE)
+    output = output.astype(LOW)
+    wait(order, output)
+    output = send(output, TO_HOME)
+    mixed_terms = share_pieces(mixed_grads(order, normed_one, d_mixed, out_grad))
+    grads = [(d, t * part) for t, d in enumerate(d_mixed)]
+    far = crossed(back_half(order, grads, one, True))
+    near = back_half(order, grads, one, False)
+    side = side_of(near, far)
+    ff_kept, ff_sent = fold(order, [ff_terms])
+    wait(order, output)
+    ff_sent = send(after(order, ff_sent), TO_ZH)
+    (input_grad,) = norm_pull(order, x, (near, far, side), d_resid, False)
     input_grad = send(input_grad, TO_HOME)
+    mixed_kept, mixed_sent = fold(order, [t[None] for t in mixed_terms])
+    mixed_sent = send(mixed_sent, TO_ZH)
+    ff_slices = share_slices(split_rows(order, ff_kept, ff_sent))
+    mixed_slices = share_slices(split_rows(order, mixed_kept, mixed_sent))
     up_grad, gain_two_grad, down_grad = finish(
-        flat, owned_slices(flat, ff_pieces), up_weight, gain_two, (2, ff, ff)
+        order, ff_slices, up_weight, gain_two, (2, ff, ff)
     )
     qkv_grad, gain_one_grad, out_grad = finish(
-        flat, owned_slices(flat, mixed_pieces), qkv_weight, gain_one, (3, part, part)
+        order, mixed_slices, qkv_weight, gain_one, (3, part, part)
     )
     return (
         output[None],
         input_grad[None],
-        gain_one_grad[:, 0],
+        gain_one_grad[0],
         qkv_grad,
         out_grad,
-        gain_two_grad[:, 0],
+        gain_two_grad[0],
         up_grad,
         down_grad,
     )
 
 
 def solution(mesh):
+    dp, seq = "dp", "seq"
+    step = per_device
+    if tuple(mesh.shape.values()) == QUAD_MESH:
+        dp, seq, step = ("y", "x", "c"), ("zh", "zl"), quad_device
+        mesh = jax.sharding.Mesh(mesh.devices.reshape(2, 2, 2, 2, 2), FLAT)
+        every = FLAT
+    else:
+        every = (dp, seq)
+    rows = P(every, None)
     return jax.shard_map(
-        quad_device if tuple(mesh.shape.values()) == QUAD_MESH else per_device,
+        step,
         mesh=mesh,
         in_specs=(
-            P("dp", "seq", None),
-            P("dp", "seq"),
-            P(("dp", "seq")),
-            P(("dp", "seq"), None),
-            P(("dp", "seq"), None),
-            P(("dp", "seq")),
-            P(("dp", "seq"), None),
-            P(("dp", "seq"), None),
-            P("dp", "seq", None),
+            P(dp, seq, None),
+            P(dp, seq),
+            P(every),
+            rows,
+            rows,
+            P(every),
+            rows,
+            rows,
+            P(dp, seq, None),
         ),
         out_specs=(
-            P("dp", "seq", None),
-            P("dp", "seq", None),
-            P(("dp", "seq")),
-            P(("dp", "seq"), None),
-            P(("dp", "seq"), None),
-            P(("dp", "seq")),
-            P(("dp", "seq"), None),
-            P(("dp", "seq"), None),
+            P(dp, seq, None),
+            P(dp, seq, None),
+            P(every),
+            rows,
+            rows,
+            P(every),
+            rows,
+            rows,
         ),
         check_vma=False,
     )

time: 414 us -> 350 us (0.85)
  waiting for transfers between devices: 133 us -> 95.3 us
  starting transfers between devices: 80.5 us -> 64.4 us
  local copies, waits for them, and re-layouts: 27.5 us -> 22.1 us
  other arithmetic: 19.3 us -> 14 us
    ppermute x63 -> x54, waiting for transfers between devices: 133 us -> 95.3 us  [send(): return lax.ppermute(array, FLAT, pairs)]
    ppermute x63 -> x54, starting transfers between devices: 80.5 us -> 59.4 us  [send(): return lax.ppermute(array, FLAT, pairs)]
    unnamed x106 -> x96, local copies, waits for them, and re-layouts: 6.69 us -> 17.1 us
    ppermute x6 -> x0, local copies, waits for them, and re-layouts: 9.67 us -> none  [send(): return lax.ppermute(array, FLAT, pairs)]
    all_to_all x0 -> x1, starting transfers between devices: none -> 4.98 us  [quad_device(): lax.all_to_all(after(order, ff_terms), ('y', 'x'), split_axis=0, concat_a...]
    pallas_call x32 -> x30, Pallas kernels: 151 us -> 151 us  [run(): pl.pallas_call(body, grid_spec=pltpu.PrefetchScalarGridSpec(num_scalar_pr...]
  transfers between devices with their start and end apart: 63 -> 55, of which waited for: 17 -> 22; matrix products, arithmetic and copies ran while one was open for 9% -> 5% of each run, Pallas kernels for 30% -> 34%
where the time goes in v3:
time: 350 us; the launch traced here: 348 us
  Pallas kernels  151 us (43%)
  waiting for transfers between devices  95.3 us (27%)
  starting transfers between devices  64.4 us (18%)
  local copies, waits for them, and re-layouts  22.1 us (6%)
  other arithmetic  14 us (4%)
    pallas_call x30, Pallas kernels, run(): pl.pallas_call(body, grid_spec=pltpu.PrefetchScalarGridSpec(num_scalar_pr...  151 us
    ppermute x54, waiting for transfers between devices, send(): return lax.ppermute(array, FLAT, pairs)  95.3 us
    ppermute x54, starting transfers between devices, send(): return lax.ppermute(array, FLAT, pairs)  59.4 us
    unnamed x96, local copies, waits for them, and re-layouts  17.1 us
  transfers between devices with their start and end apart: 55, of which 22 were waited for; matrix products, arithmetic and copies ran while one was open for 5% of the time, Pallas kernels for 34%

profile of v3, /device:TPU:1, one launch (start us, length us, event | category | flops | bytes accessed | tf_op | source)
XLA Modules:
  0.0 348.0 jit_solution(5792226745221122512)
XLA Ops:
  6.4 3.8 %collective-permute-start.7 = (bf16[272,1024]{1,0:T(8,128)(2,1)S(1)}, bf16[272,1024]{1,0:T(8,128)(2,1)S(1)}, u32[]{:S(2)}, u32[]{:S(2)}) collective-permute-start(bf16[272,1024]{1,0:T(8,128)(2,1)S(1)} %pad_maximum_fusion.block), channel_id=1, source_target_pairs={{0,1},{1,0},{2,4},{3,5},{4,2},{5,3},{6,7},{7,6},{8,9},{9,8},{10,12... | collective-permute-start | bytes 1671176 | tf_op jit(solution)/shard_map/ppermute | solution.py:336
  12.1 12.0 %collective-permute-done.refs_1_ = bf16[32,1024]{1,0:T(8,128)(2,1)S(1)} collective-permute-done((bf16[32,1024]{1,0:T(8,128)(2,1)}, bf16[32,1024]{1,0:T(8,128)(2,1)S(1)}, u32[]{:S(2)}, u32[]{:S(2)}) %collective-permute-start) | collective-permute-done | bytes 65568 | tf_op jit(solution)/shard_map/ppermute | solution.py:336
  30.3 11.1 %collective-permute-done.3 = bf16[4,32,1024]{2,1,0:T(8,128)(2,1)S(1)} collective-permute-done((bf16[4,32,1024]{2,1,0:T(8,128)(2,1)}, bf16[4,32,1024]{2,1,0:T(8,128)(2,1)S(1)}, u32[]{:S(2)}, u32[]{:S(2)}) %collective-permute-start.3) | collective-permute-done | bytes 262176 | tf_op jit(solution)/shard_map/ppermute | solution.py:336
  49.9 4.5 %collective-permute-done.6.refs_3_ = bf16[32,2048]{1,0:T(8,128)(2,1)S(1)} collective-permute-done((bf16[32,2048]{1,0:T(8,128)(2,1)S(1)}, bf16[32,2048]{1,0:T(8,128)(2,1)S(1)}, u32[]{:S(2)}, u32[]{:S(2)}) %collective-permute-start.6) | collective-permute-done | bytes 131104 | tf_op jit(solution)/shard_map/ppermute | solution.py:336
  64.3 9.0 %collective-permute-done.9.second = bf16[272,1024]{1,0:T(8,128)(2,1)S(1)} collective-permute-done((bf16[272,1024]{1,0:T(8,128)(2,1)S(1)}, bf16[272,1024]{1,0:T(8,128)(2,1)S(1)}, u32[]{:S(2)}, u32[]{:S(2)}) %collective-permute-start.9) | collective-permute-done | bytes 557088 | tf_op jit(solution)/shard_map/ppermute | solution.py:336
  76.7 3.9 %shard_map.157 = (bf16[1024,1024]{1,0:T(8,128)(2,1)}, bf16[64,1024]{1,0:T(8,128)(2,1)}) custom-call(s32[1]{0:T(128)} %bitcast.flat_ref, bf16[272,1024]{1,0:T(8,128)(2,1)} %copy-done.12, bf16[272,1024]{1,0:T(8,128)(2,1)} %copy-done.14, bf16[272,1024]{1,0:T(8,128)(2,1)} %copy-done.15, bf16[272,1024]{1,0:T(8,128)(2,1)} %copy-done.17, ...), custom_call_target="tpu_custom_call" | custom-call | bytes 55705 | tf_op jit(solution)/shard_map/pallas_call | solution.py:395
  85.2 7.6 %shard_map.158 = (bf16[1024,1024]{1,0:T(8,128)(2,1)}, bf16[1024,768]{1,0:T(8,128)(2,1)}) custom-call(s32[1]{0:T(128)} %bitcast.flat_ref, bf16[1024,1024]{1,0:T(8,128)(2,1)} %get-tuple-element.130.x_ref, bf16[256,1024]{1,0:T(8,128)(2,1)} %bitcast.43, bf16[256,1024]{1,0:T(8,128)(2,1)} %copy-done.6, bf16[256,1024]{1,0:T(8,128)(2,1)} %copy-done.5, ...), custom_call_target="tpu_custom_call" | custom-call | flops 16106127 | bytes 89128 | tf_op jit(solution)/shard_map/pallas_call | solution.py:395
  96.6 9.9 %shard_map.160 = (bf16[1024,256]{1,0:T(8,128)(2,1)}, f32[1024,128]{1,0:T(8,128)}) custom-call(s32[1]{0:T(128)} %bitcast.flat_ref, bf16[1024,768]{1,0:T(8,128)(2,1)} %get-tuple-element.136.q_ref.k_ref.v_ref, bf16[1024,768]{1,0:T(8,128)(2,1)} %get-tuple-element.136.q_ref.k_ref.v_ref, bf16[1024,768]{1,0:T(8,128)(2,1)} %get-tuple-element.136.q_ref.k_ref.v_ref), custom_call_target="tpu_custom_call" | custom-call | flops 42949672 | bytes 57671 | tf_op jit(solution)/shard_map/pallas_call | solution.py:395
  107.8 4.4 %collective-permute-done.17.refs_5_.refs_9_ = bf16[1024,256]{1,0:T(8,128)(2,1)} collective-permute-done((bf16[1024,256]{1,0:T(8,128)(2,1)}, bf16[1024,256]{1,0:T(8,128)(2,1)}, u32[]{:S(2)}, u32[]{:S(2)}) %collective-permute-start.17) | collective-permute-done | bytes 524320 | tf_op jit(solution)/shard_map/ppermute | solution.py:336
  116.0 11.1 %collective-permute-done.20.refs_1_.refs_5_ = bf16[1024,256]{1,0:T(8,128)(2,1)} collective-permute-done((bf16[1024,256]{1,0:T(8,128)(2,1)}, bf16[1024,256]{1,0:T(8,128)(2,1)}, u32[]{:S(2)}, u32[]{:S(2)}) %collective-permute-start.20) | collective-permute-done | bytes 524320 | tf_op jit(solution)/shard_map/ppermute | solution.py:336
  135.3 8.1 %shard_map.161 = (bf16[1024,1024]{1,0:T(8,128)(2,1)}, f32[256,1024]{1,0:T(8,128)}) custom-call(s32[1]{0:T(128)} %bitcast.flat_ref, bf16[1024,1024]{1,0:T(8,128)(2,1)} %get-tuple-element.130.x_ref, bf16[1024,256]{1,0:T(8,128)(2,1)} %get-tuple-element.137.refs_0_.refs_4_.o_ref, bf16[1024,256]{1,0:T(8,128)(2,1)} %collective-permute-done.20.refs_1_.refs_5_, ...), custom_call_target="tpu_custom_call" | custom-call | flops 21474836 | bytes 94371 | tf_op jit(solution)/shard_map/pallas_call | solution.py:395
  147.2 3.8 %shard_map.162.cot_ref.base_ref = bf16[1024,1024]{1,0:T(8,128)(2,1)} custom-call(s32[1]{0:T(128)} %bitcast.flat_ref, bf16[256,1024]{1,0:T(8,128)(2,1)} %bitcast.58, bf16[256,1024]{1,0:T(8,128)(2,1)} %collective-permute-done.19.first, bf16[256,1024]{1,0:T(8,128)(2,1)} %collective-permute-done.24.second, bf16[256,1024]{1,0:T(8,128)(2,1)} %collective-permute-done.25.core_block, ...), custom_call_target="tpu_custom_call" | custom-call | bytes 52428 | tf_op jit(solution)/shard_map/pallas_call | solution.py:395
  151.0 7.4 %collective-permute-done.31.refs_4_.refs_5_ = bf16[128,2048]{1,0:T(8,128)(2,1)} collective-permute-done((bf16[128,2048]{1,0:T(8,128)(2,1)}, bf16[128,2048]{1,0:T(8,128)(2,1)}, u32[]{:S(2)}, u32[]{:S(2)}) %collective-permute-start.31) | collective-permute-done | bytes 524320 | tf_op jit(solution)/shard_map/ppermute | solution.py:336
  159.2 10.7 %shard_map.163 = (bf16[1024,656]{1,0:T(8,128)(2,1)}, bf16[1024,1312]{1,0:T(8,128)(2,1)}) custom-call(s32[1]{0:T(128)} %bitcast.flat_ref, bf16[1024,1024]{1,0:T(8,128)(2,1)} %get-tuple-element.146.n_ref, bf16[1024,1024]{1,0:T(8,128)(2,1)} %shard_map.162.cot_ref.base_ref, bf16[256,2048]{1,0:T(8,128)(2,1)} %bitcast.33, bf16[256,2048]{1,0:T(8,128)(2,1)} %copy-done.2, ...), custom_call_target="tpu_custom_call" | custom-call | flops 41271952 | bytes 124190 | tf_op jit(solution)/shard_map/pallas_call | solution.py:395
  169.9 5.8 %shard_map.164 = bf16[512,1024]{1,0:T(8,128)(2,1)} custom-call(s32[1]{0:T(128)} %bitcast.flat_ref, bf16[1024,1312]{1,0:T(8,128)(2,1)} %get-tuple-element.155.refs_0_.d_ref, bf16[256,2048]{1,0:T(8,128)(2,1)} %bitcast.34, bf16[256,2048]{1,0:T(8,128)(2,1)} %copy-done.2, bf16[256,2048]{1,0:T(8,128)(2,1)} %copy-done.1, bf16[128,2048]{1,0:T(8,128)(2,1)} %copy-done.3, ...), custom_call_target="tpu_custom_call" | custom-call | flops 13757317 | bytes 79298 | tf_op jit(solution)/shard_map/pallas_call | solution.py:395
  177.0 6.1 %shard_map.165.a_ref = f32[512,1024]{1,0:T(8,128)} custom-call(s32[1]{0:T(128)} %bitcast.flat_ref, bf16[1024,1312]{1,0:T(8,128)(2,1)} %get-tuple-element.155.refs_0_.d_ref, bf16[256,2048]{1,0:T(8,128)(2,1)} %bitcast.35, bf16[256,2048]{1,0:T(8,128)(2,1)} %copy-done.2, bf16[256,2048]{1,0:T(8,128)(2,1)} %copy-done.1, bf16[128,2048]{1,0:T(8,128)(2,1)} %copy-done.3, ...), custom_call_target="tpu_custom_call" | custom-call | flops 13757317 | bytes 89784 | tf_op jit(solution)/shard_map/pallas_call | solution.py:395
  186.4 11.0 %shard_map.166 = bf16[4,256,2048]{2,1,0:T(8,128)(2,1)} custom-call(s32[1]{0:T(128)} %bitcast.flat_ref, bf16[1024,1024]{1,0:T(8,128)(2,1)} %get-tuple-element.146.n_ref, bf16[1024,1024]{1,0:T(8,128)(2,1)} %shard_map.162.cot_ref.base_ref, bf16[1024,1312]{1,0:T(8,128)(2,1)} %get-tuple-element.155.refs_0_.d_ref, bf16[1024,656]{1,0:T(8,128)(2,1)} %get-tuple-element.153.h_ref.refs_0_), custom_call_target="tpu_custom_call" | custom-call | flops 41271952 | bytes 124190 | tf_op jit(solution)/shard_map/pallas_call | solution.py:395
  199.3 4.6 %shard_map.167 = (bf16[256,1024]{1,0:T(8,128)(2,1)}, f32[256,1024]{1,0:T(8,128)}) custom-call(s32[1]{0:T(128)} %bitcast.flat_ref, f32[256,1024]{1,0:T(8,128)} %get-tuple-element.145.x_ref, f32[512,1024]{1,0:T(8,128)} %shard_map.165.a_ref, bf16[512,1024]{1,0:T(8,128)(2,1)} %copy-done.10, bf16[256,1024]{1,0:T(8,128)(2,1)} %copy-done.27, ...), custom_call_target="tpu_custom_call" | custom-call | bytes 83886 | tf_op jit(solution)/shard_map/pallas_call | solution.py:395
  206.4 4.8 %shard_map.168 = bf16[512,1024]{1,0:T(8,128)(2,1)} custom-call(s32[1]{0:T(128)} %bitcast.flat_ref, bf16[1024,656]{1,0:T(8,128)(2,1)} %get-tuple-element.153.h_ref.refs_0_, bf16[256,2048]{1,0:T(8,128)(2,1)} %bitcast.36, bf16[256,2048]{1,0:T(8,128)(2,1)} %copy-done.2, bf16[256,2048]{1,0:T(8,128)(2,1)} %copy-done.1, bf16[128,2048]{1,0:T(8,128)(2,1)} %copy-done.3, ...), custom_call_target="tpu_custom_call" | custom-call | flops 6878658 | bytes 65863 | tf_op jit(solution)/shard_map/pallas_call | solution.py:395
  211.1 5.1 %shard_map.169 = f32[512,1024]{1,0:T(8,128)} custom-call(s32[1]{0:T(128)} %bitcast.flat_ref, bf16[1024,656]{1,0:T(8,128)(2,1)} %get-tuple-element.153.h_ref.refs_0_, bf16[256,2048]{1,0:T(8,128)(2,1)} %bitcast.37, bf16[256,2048]{1,0:T(8,128)(2,1)} %copy-done.2, bf16[256,2048]{1,0:T(8,128)(2,1)} %copy-done.1, bf16[128,2048]{1,0:T(8,128)(2,1)} %copy-done.3, ...), custom_call_target="tpu_custom_call" | custom-call | flops 6878658 | bytes 76349 | tf_op jit(solution)/shard_map/pallas_call | solution.py:395
  220.7 6.4 %shard_map.170 = (bf16[1024,256]{1,0:T(8,128)(2,1)}, bf16[4,256,256]{2,1,0:T(8,128)(2,1)}) custom-call(s32[1]{0:T(128)} %bitcast.flat_ref, bf16[256,1024]{1,0:T(8,128)(2,1)} %get-tuple-element.159.refs_0_, bf16[256,1024]{1,0:T(8,128)(2,1)} %copy-done.22, bf16[256,1024]{1,0:T(8,128)(2,1)} %copy-done.23, bf16[256,1024]{1,0:T(8,128)(2,1)} %copy-done.24, ...), custom_call_target="tpu_custom_call" | custom-call | flops 10737418 | bytes 73400 | tf_op jit(solution)/shard_map/pallas_call | solution.py:395
  227.5 5.0 %all-to-all-start = ((bf16[4,256,2048]{2,1,0:T(8,128)(2,1)}), bf16[4,256,2048]{2,1,0:T(8,128)(2,1)}, u32[]{:S(2)}, u32[]{:S(2)}) async-start(bf16[4,256,2048]{2,1,0:T(8,128)(2,1)} %shard_map.166), calls=%async_computation | async-start | bytes 8388608 | tf_op jit(solution)/shard_map/all_to_all | solution.py:1059
  235.9 17.4 %shard_map.171 = (bf16[1024,256]{1,0:T(8,128)(2,1)}, bf16[1024,256]{1,0:T(8,128)(2,1)}, bf16[1024,256]{1,0:T(8,128)(2,1)}) custom-call(s32[1]{0:T(128)} %bitcast.flat_ref, bf16[1024,768]{1,0:T(8,128)(2,1)} %get-tuple-element.136.q_ref.k_ref.v_ref, bf16[1024,768]{1,0:T(8,128)(2,1)} %get-tuple-element.136.q_ref.k_ref.v_ref, ...), custom_call_target="tpu_custom_call" | custom-call | flops 107374184 | bytes 84213 | tf_op jit(solution)/shard_map/pallas_call | solution.py:395
  255.6 6.5 %shard_map.172 = (bf16[256,1024]{1,0:T(8,128)(2,1)}, bf16[256,1024]{1,0:T(8,128)(2,1)}, bf16[256,1024]{1,0:T(8,128)(2,1)}, bf16[256,1024]{1,0:T(8,128)(2,1)}) custom-call(s32[1]{0:T(128)} %bitcast.flat_ref, bf16[1024,1024]{1,0:T(8,128)(2,1)} %get-tuple-element.133.n_ref, bf16[1024,256]{1,0:T(8,128)(2,1)} %get-tuple-element.167.refs_0_, ...), custom_call_target="tpu_custom_call" | custom-call | flops 16106127 | bytes 62914 | tf_op jit(solution)/shard_map/pallas_call | solution.py:395
  262.1 4.1 %shard_map.173 = bf16[512,1024]{1,0:T(8,128)(2,1)} custom-call(s32[1]{0:T(128)} %bitcast.flat_ref, bf16[1024,256]{1,0:T(8,128)(2,1)} %get-tuple-element.167.refs_0_, bf16[1024,256]{1,0:T(8,128)(2,1)} %get-tuple-element.170.refs_1_, bf16[1024,256]{1,0:T(8,128)(2,1)} %get-tuple-element.171.refs_2_, bf16[256,1024]{1,0:T(8,128)(2,1)} %bitcast.44, ...), custom_call_target="tpu_custom_call" | custom-call | flops 8053063 | bytes 47185 | tf_op jit(solution)/shard_map/pallas_call | solution.py:395
  269.9 4.4 %shard_map.174.a_ref = f32[512,1024]{1,0:T(8,128)} custom-call(s32[1]{0:T(128)} %bitcast.flat_ref, bf16[1024,256]{1,0:T(8,128)(2,1)} %get-tuple-element.167.refs_0_, bf16[1024,256]{1,0:T(8,128)(2,1)} %get-tuple-element.170.refs_1_, bf16[1024,256]{1,0:T(8,128)(2,1)} %get-tuple-element.171.refs_2_, bf16[256,1024]{1,0:T(8,128)(2,1)} %bitcast.45, ...), custom_call_target="tpu_custom_call" | custom-call | flops 8053063 | bytes 57671 | tf_op jit(solution)/shard_map/pallas_call | solution.py:395
  284.9 13.0 %collective-permute-done.41.c_ref = bf16[256,1024]{1,0:T(8,128)(2,1)} collective-permute-done((bf16[256,1024]{1,0:T(8,128)(2,1)}, bf16[256,1024]{1,0:T(8,128)(2,1)}, u32[]{:S(2)}, u32[]{:S(2)}) %collective-permute-start.41) | collective-permute-done | bytes 524320 | tf_op jit(solution)/shard_map/ppermute | solution.py:336
  297.9 4.4 %shard_map.176 = bf16[256,1024]{1,0:T(8,128)(2,1)} custom-call(s32[1]{0:T(128)} %bitcast.flat_ref, bf16[1024,1024]{1,0:T(8,128)(2,1)} %get-tuple-element.130.x_ref, f32[512,1024]{1,0:T(8,128)} %shard_map.174.a_ref, bf16[512,1024]{1,0:T(8,128)(2,1)} %copy-done.11, bf16[256,1024]{1,0:T(8,128)(2,1)} %collective-permute-done.41.c_ref, ...), custom_call_target="tpu_custom_call" | custom-call | bytes 73400 | tf_op jit(solution)/shard_map/pallas_call | solution.py:395
  307.9 12.1 %collective-permute-done.46 = bf16[2,64,2048]{2,1,0:T(8,128)(2,1)S(1)} collective-permute-done((bf16[2,64,2048]{2,1,0:T(8,128)(2,1)}, bf16[2,64,2048]{2,1,0:T(8,128)(2,1)S(1)}, u32[]{:S(2)}, u32[]{:S(2)}) %collective-permute-start.46) | collective-permute-done | bytes 524320 | tf_op jit(solution)/shard_map/ppermute | solution.py:336
  323.0 3.4 collective-permute-start.49
  329.9 4.6 %collective-permute-start.51 = (bf16[32,1024]{1,0:T(8,128)(2,1)}, bf16[32,1024]{1,0:T(8,128)(2,1)S(1)}, u32[]{:S(2)}, u32[]{:S(2)}) collective-permute-start(bf16[32,1024]{1,0:T(8,128)(2,1)} %get-tuple-element.200), channel_id=1, source_target_pairs={{0,1},{1,0},{2,3},{3,2},{4,5},{5,4},{6,7},{7,6},{8,9},{9,8},{10,11... | collective-permute-start | bytes 196616 | tf_op jit(solution)/shard_map/ppermute | solution.py:336
  338.6 3.5 %shard_map.180 = (f32[32,5248]{1,0:T(8,128)}, f32[1,32]{1,0:T(1,128)}, f32[32,2624]{1,0:T(8,128)}) custom-call(s32[1]{0:T(128)} %bitcast.flat_ref, bf16[32,2048]{1,0:T(8,128)(2,1)} %get-tuple-element.190.refs_0_, bf16[32,2048]{1,0:T(8,128)(2,1)} %copy-done.30, bf16[32,2048]{1,0:T(8,128)(2,1)} %copy-done.31, bf16[32,2048]{1,0:T(8,128)(2,1)} %copy-done.32, ...), custom_call_target="tpu_custom_call" | custom-call | bytes 18679 | tf_op jit(solution)/shard_map/pallas_call | solution.py:395
  (224 shorter events, 117.8 us)
Async XLA Ops:
  6.4 50.6 %collective-permute-start.7 = (bf16[272,1024]{1,0:T(8,128)(2,1)S(1)}, bf16[272,1024]{1,0:T(8,128)(2,1)S(1)}, u32[]{:S(2)}, u32[]{:S(2)}) collective-permute-start(bf16[272,1024]{1,0:T(8,128)(2,1)S(1)} %pad_maximum_fusion.block), channel_id=1, source_target_pairs={{0,1},{1,0},{2,4},{3,5},{4,2},{5,3},{6,7},{7,6},{8,9},{9,8},{10,12... | collective-permute-start | bytes 1671176 | tf_op jit(solution)/shard_map/ppermute | solution.py:336
  10.2 13.9 %collective-permute-start = (bf16[32,1024]{1,0:T(8,128)(2,1)}, bf16[32,1024]{1,0:T(8,128)(2,1)S(1)}, u32[]{:S(2)}, u32[]{:S(2)}) collective-permute-start(bf16[32,1024]{1,0:T(8,128)(2,1)} %get-tuple-element.112), channel_id=1, source_target_pairs={{0,1},{1,0},{2,3},{3,2},{4,5},{5,4},{6,7},{7,6},{8,9},{9,8},{10,11... | collective-permute-start | bytes 196616 | tf_op jit(solution)/shard_map/ppermute | solution.py:336
  11.5 13.7 %collective-permute-start.2 = (bf16[32,1024]{1,0:T(8,128)(2,1)}, bf16[32,1024]{1,0:T(8,128)(2,1)S(1)}, u32[]{:S(2)}, u32[]{:S(2)}) collective-permute-start(bf16[32,1024]{1,0:T(8,128)(2,1)} %get-tuple-element.114), channel_id=1, source_target_pairs={{0,5},{1,4},{2,7},{3,6},{4,1},{5,0},{6,3},{7,2},{8,13},{9,12},{10,... | collective-permute-start | bytes 196616 | tf_op jit(solution)/shard_map/ppermute | solution.py:336
  27.5 14.0 %collective-permute-start.3 = (bf16[4,32,1024]{2,1,0:T(8,128)(2,1)}, bf16[4,32,1024]{2,1,0:T(8,128)(2,1)S(1)}, u32[]{:S(2)}, u32[]{:S(2)}) collective-permute-start(bf16[4,32,1024]{2,1,0:T(8,128)(2,1)} %shard_map.154), channel_id=1, source_target_pairs={{0,2},{1,3},{2,0},{3,1},{4,6},{5,7},{6,4},{7,5},{8,10},{9,11},{10,... | collective-permute-start | bytes 786440 | tf_op jit(solution)/shard_map/ppermute | solution.py:336
  29.1 19.9 %collective-permute-start.4 = (bf16[32,2048]{1,0:T(8,128)(2,1)}, bf16[32,2048]{1,0:T(8,128)(2,1)S(1)}, u32[]{:S(2)}, u32[]{:S(2)}) collective-permute-start(bf16[32,2048]{1,0:T(8,128)(2,1)} %get-tuple-element.119), channel_id=1, source_target_pairs={{0,1},{1,0},{2,3},{3,2},{4,5},{5,4},{6,7},{7,6},{8,9},{9,8},{10,11... | collective-permute-start | bytes 393224 | tf_op jit(solution)/shard_map/ppermute | solution.py:336
  44.0 19.0 %collective-permute-start.13 = (bf16[256,1024]{1,0:T(8,128)(2,1)}, bf16[256,1024]{1,0:T(8,128)(2,1)S(1)}, u32[]{:S(2)}, u32[]{:S(2)}) collective-permute-start(bf16[256,1024]{1,0:T(8,128)(2,1)} %bitcast.40), channel_id=1, source_target_pairs={{0,16},{1,17},{2,18},{3,19},{4,20},{5,21},{6,22},{7,23},{8,24},{9,... | collective-permute-start | bytes 1572872 | tf_op jit(solution)/shard_map/ppermute | solution.py:336
  45.7 17.6 %collective-permute-start.12 = (bf16[256,1024]{1,0:T(8,128)(2,1)}, bf16[256,1024]{1,0:T(8,128)(2,1)S(1)}, u32[]{:S(2)}, u32[]{:S(2)}) collective-permute-start(bf16[256,1024]{1,0:T(8,128)(2,1)} %bitcast.41), channel_id=1, source_target_pairs={{0,8},{1,9},{2,10},{3,11},{4,12},{5,13},{6,14},{7,15},{8,0},{9,1},... | collective-permute-start | bytes 1572872 | tf_op jit(solution)/shard_map/ppermute | solution.py:336
  57.0 16.3 %collective-permute-start.9 = (bf16[272,1024]{1,0:T(8,128)(2,1)S(1)}, bf16[272,1024]{1,0:T(8,128)(2,1)S(1)}, u32[]{:S(2)}, u32[]{:S(2)}) collective-permute-start(bf16[272,1024]{1,0:T(8,128)(2,1)S(1)} %collective-permute-done.7.first), channel_id=1, source_target_pairs={{2,3},{3,2},{4,5},{5,4},{10,11},{11,10},{12,13},{13,12},{18,19},{1... | collective-permute-start | bytes 1671176 | tf_op jit(solution)/shard_map/ppermute | solution.py:336
  59.0 14.3 %collective-permute-start.8 = (bf16[272,1024]{1,0:T(8,128)(2,1)S(1)}, bf16[272,1024]{1,0:T(8,128)(2,1)S(1)}, u32[]{:S(2)}, u32[]{:S(2)}) collective-permute-start(bf16[272,1024]{1,0:T(8,128)(2,1)S(1)} %collective-permute-done.7.first), channel_id=1, source_target_pairs={{0,4},{1,5},{2,6},{3,7},{4,0},{5,1},{6,2},{7,3},{8,12},{9,13},{10,... | collective-permute-start | bytes 1671176 | tf_op jit(solution)/shard_map/ppermute | solution.py:336
  59.1 35.2 %collective-permute-start.16 = (bf16[4,32,2048]{2,1,0:T(8,128)(2,1)}, bf16[4,32,2048]{2,1,0:T(8,128)(2,1)}, u32[]{:S(2)}, u32[]{:S(2)}) collective-permute-start(bf16[4,32,2048]{2,1,0:T(8,128)(2,1)} %shard_map.156), channel_id=1, source_target_pairs={{0,2},{1,3},{2,0},{3,1},{4,6},{5,7},{6,4},{7,5},{8,10},{9,11},{10,... | collective-permute-start | bytes 1572872 | tf_op jit(solution)/shard_map/ppermute | solution.py:336
  92.8 19.4 %collective-permute-start.17 = (bf16[1024,256]{1,0:T(8,128)(2,1)}, bf16[1024,256]{1,0:T(8,128)(2,1)}, u32[]{:S(2)}, u32[]{:S(2)}) collective-permute-start(bf16[1024,256]{1,0:T(8,128)(2,1)} %slice_dynamic-update-slice_fusion.3.refs_4_.refs_8_), channel_id=1, source_target_pairs={{0,1},{1,0},{2,3},{3,2},{4,5},{5,4},{6,7},{7,6},{8,9},{9,8},{10,11... | collective-permute-start | bytes 1572872 | tf_op jit(solution)/shard_map/ppermute | solution.py:336
  92.8 22.9 %collective-permute-start.19 = (bf16[256,1024]{1,0:T(8,128)(2,1)S(1)}, bf16[256,1024]{1,0:T(8,128)(2,1)}, u32[]{:S(2)}, u32[]{:S(2)}) collective-permute-start(bf16[256,1024]{1,0:T(8,128)(2,1)S(1)} %bitcast.59), channel_id=1, source_target_pairs={{0,1},{1,0},{2,4},{3,5},{4,2},{5,3},{6,7},{7,6},{8,9},{9,8},{10,12... | collective-permute-start | bytes 1572872 | tf_op jit(solution)/shard_map/ppermute | solution.py:336
  106.6 20.5 %collective-permute-start.20 = (bf16[1024,256]{1,0:T(8,128)(2,1)}, bf16[1024,256]{1,0:T(8,128)(2,1)}, u32[]{:S(2)}, u32[]{:S(2)}) collective-permute-start(bf16[1024,256]{1,0:T(8,128)(2,1)} %get-tuple-element.137.refs_0_.refs_4_.o_ref), channel_id=1, source_target_pairs={{0,1},{1,0},{2,3},{3,2},{4,5},{5,4},{6,7},{7,6},{8,9},{9,8},{10,11... | collective-permute-start | bytes 1572872 | tf_op jit(solution)/shard_map/ppermute | solution.py:336
  112.2 17.7 %collective-permute-start.18 = (bf16[1024,256]{1,0:T(8,128)(2,1)}, bf16[1024,256]{1,0:T(8,128)(2,1)}, u32[]{:S(2)}, u32[]{:S(2)}) collective-permute-start(bf16[1024,256]{1,0:T(8,128)(2,1)} %collective-permute-done.17.refs_5_.refs_9_), channel_id=1, source_target_pairs={{0,4},{1,5},{2,6},{3,7},{4,0},{5,1},{6,2},{7,3},{8,12},{9,13},{10,... | collective-permute-start | bytes 1572872 | tf_op jit(solution)/shard_map/ppermute | solution.py:336
  113.6 16.4 %collective-permute-start.23 = (bf16[1024,256]{1,0:T(8,128)(2,1)}, bf16[1024,256]{1,0:T(8,128)(2,1)}, u32[]{:S(2)}, u32[]{:S(2)}) collective-permute-start(bf16[1024,256]{1,0:T(8,128)(2,1)} %slice_dynamic-update-slice_fusion.3.refs_4_.refs_8_), channel_id=1, source_target_pairs={{0,4},{1,5},{2,6},{3,7},{4,0},{5,1},{6,2},{7,3},{8,12},{9,13},{10,... | collective-permute-start | bytes 1572872 | tf_op jit(solution)/shard_map/ppermute | solution.py:336
  113.6 30.5 %collective-permute-start.29 = (bf16[256,2048]{1,0:T(8,128)(2,1)S(1)}, bf16[256,2048]{1,0:T(8,128)(2,1)S(1)}, u32[]{:S(2)}, u32[]{:S(2)}) collective-permute-start(bf16[256,2048]{1,0:T(8,128)(2,1)S(1)} %bitcast.38), channel_id=1, source_target_pairs={{0,16},{1,17},{2,18},{3,19},{4,20},{5,21},{6,22},{7,23},{8,24},{9,... | collective-permute-start | bytes 3145736 | tf_op jit(solution)/shard_map/ppermute | solution.py:336
  115.7 29.4 %collective-permute-start.28 = (bf16[256,2048]{1,0:T(8,128)(2,1)S(1)}, bf16[256,2048]{1,0:T(8,128)(2,1)S(1)}, u32[]{:S(2)}, u32[]{:S(2)}) collective-permute-start(bf16[256,2048]{1,0:T(8,128)(2,1)S(1)} %bitcast.39), channel_id=1, source_target_pairs={{0,8},{1,9},{2,10},{3,11},{4,12},{5,13},{6,14},{7,15},{8,0},{9,1},... | collective-permute-start | bytes 3145736 | tf_op jit(solution)/shard_map/ppermute | solution.py:336
  130.0 14.0 %collective-permute-start.24 = (bf16[256,1024]{1,0:T(8,128)(2,1)}, bf16[256,1024]{1,0:T(8,128)(2,1)}, u32[]{:S(2)}, u32[]{:S(2)}) collective-permute-start(bf16[256,1024]{1,0:T(8,128)(2,1)} %collective-permute-done.19.first), channel_id=1, source_target_pairs={{2,3},{3,2},{4,5},{5,4},{10,11},{11,10},{12,13},{13,12},{18,19},{1... | collective-permute-start | bytes 1572872 | tf_op jit(solution)/shard_map/ppermute | solution.py:336
  144.9 13.4 %collective-permute-start.31 = (bf16[128,2048]{1,0:T(8,128)(2,1)}, bf16[128,2048]{1,0:T(8,128)(2,1)}, u32[]{:S(2)}, u32[]{:S(2)}) collective-permute-start(bf16[128,2048]{1,0:T(8,128)(2,1)} %slice.96), channel_id=1, source_target_pairs={{0,8},{1,9},{2,10},{3,11},{4,12},{5,13},{6,14},{7,15},{8,0},{9,1},... | collective-permute-start | bytes 1572872 | tf_op jit(solution)/shard_map/ppermute | solution.py:336
  145.2 13.1 %collective-permute-start.30 = (bf16[128,2048]{1,0:T(8,128)(2,1)S(1)}, bf16[128,2048]{1,0:T(8,128)(2,1)S(1)}, u32[]{:S(2)}, u32[]{:S(2)}) collective-permute-start(bf16[128,2048]{1,0:T(8,128)(2,1)S(1)} %slice.95), channel_id=1, source_target_pairs={{0,16},{1,17},{2,18},{3,19},{4,20},{5,21},{6,22},{7,23},{8,24},{9,... | collective-permute-start | bytes 1572872 | tf_op jit(solution)/shard_map/ppermute | solution.py:336
  184.8 13.6 %collective-permute-start.33 = (bf16[256,1024]{1,0:T(8,128)(2,1)S(1)}, bf16[256,1024]{1,0:T(8,128)(2,1)S(1)}, u32[]{:S(2)}, u32[]{:S(2)}) collective-permute-start(bf16[256,1024]{1,0:T(8,128)(2,1)S(1)} %fusion.5), channel_id=1, source_target_pairs={{0,1},{1,0},{2,3},{3,2},{4,5},{5,4},{6,7},{7,6},{8,9},{9,8},{10,11... | collective-permute-start | bytes 1572872 | tf_op jit(solution)/shard_map/ppermute | solution.py:336
  205.3 13.1 %collective-permute-start.35 = (bf16[256,1024]{1,0:T(8,128)(2,1)}, bf16[256,1024]{1,0:T(8,128)(2,1)S(1)}, u32[]{:S(2)}, u32[]{:S(2)}) collective-permute-start(bf16[256,1024]{1,0:T(8,128)(2,1)} %get-tuple-element.159.refs_0_), channel_id=1, source_target_pairs={{0,4},{1,5},{2,6},{3,7},{4,0},{5,1},{6,2},{7,3},{8,12},{9,13},{10,... | collective-permute-start | bytes 1572872 | tf_op jit(solution)/shard_map/ppermute | solution.py:336
  227.5 52.4 %all-to-all-start = ((bf16[4,256,2048]{2,1,0:T(8,128)(2,1)}), bf16[4,256,2048]{2,1,0:T(8,128)(2,1)}, u32[]{:S(2)}, u32[]{:S(2)}) async-start(bf16[4,256,2048]{2,1,0:T(8,128)(2,1)} %shard_map.166), calls=%async_computation | async-start | bytes 8388608 | tf_op jit(solution)/shard_map/all_to_all | solution.py:1059
  234.5 18.8 %collective-permute-start.38 = (bf16[256,1024]{1,0:T(8,128)(2,1)}, bf16[256,1024]{1,0:T(8,128)(2,1)}, u32[]{:S(2)}, u32[]{:S(2)}) collective-permute-start(bf16[256,1024]{1,0:T(8,128)(2,1)} %fusion.1), channel_id=1, source_target_pairs={{0,1},{1,0},{2,3},{3,2},{4,5},{5,4},{6,7},{7,6},{8,9},{9,8},{10,11... | collective-permute-start | bytes 1572872 | tf_op jit(solution)/shard_map/ppermute | solution.py:336
  266.7 17.0 %collective-permute-start.39 = (bf16[256,1024]{1,0:T(8,128)(2,1)S(1)}, bf16[256,1024]{1,0:T(8,128)(2,1)}, u32[]{:S(2)}, u32[]{:S(2)}) collective-permute-start(bf16[256,1024]{1,0:T(8,128)(2,1)S(1)} %copy-done.18), channel_id=1, source_target_pairs={{0,0},{1,1},{2,4},{3,5},{4,2},{5,3},{6,6},{7,7},{8,8},{9,9},{10,12... | collective-permute-start | bytes 1572872 | tf_op jit(solution)/shard_map/ppermute | solution.py:336
  276.8 21.1 %collective-permute-start.41 = (bf16[256,1024]{1,0:T(8,128)(2,1)}, bf16[256,1024]{1,0:T(8,128)(2,1)}, u32[]{:S(2)}, u32[]{:S(2)}) collective-permute-start(bf16[256,1024]{1,0:T(8,128)(2,1)} %fusion), channel_id=1, source_target_pairs={{0,1},{1,0},{2,3},{3,2},{4,5},{5,4},{6,7},{7,6},{8,9},{9,8},{10,11... | collective-permute-start | bytes 1572872 | tf_op jit(solution)/shard_map/ppermute | solution.py:336
  277.1 27.1 %collective-permute-start.43 = (bf16[256,1024]{1,0:T(8,128)(2,1)}, bf16[256,1024]{1,0:T(8,128)(2,1)S(1)}, u32[]{:S(2)}, u32[]{:S(2)}) collective-permute-start(bf16[256,1024]{1,0:T(8,128)(2,1)} %get-tuple-element.183), channel_id=1, source_target_pairs={{0,8},{1,9},{2,10},{3,11},{4,12},{5,13},{6,14},{7,15},{8,0},{9,1},... | collective-permute-start | bytes 1572872 | tf_op jit(solution)/shard_map/ppermute | solution.py:336
  278.7 25.5 %collective-permute-start.44 = (bf16[256,1024]{1,0:T(8,128)(2,1)}, bf16[256,1024]{1,0:T(8,128)(2,1)S(1)}, u32[]{:S(2)}, u32[]{:S(2)}) collective-permute-start(bf16[256,1024]{1,0:T(8,128)(2,1)} %get-tuple-element.184), channel_id=1, source_target_pairs={{0,16},{1,17},{2,18},{3,19},{4,20},{5,21},{6,22},{7,23},{8,24},{9,... | collective-permute-start | bytes 1572872 | tf_op jit(solution)/shard_map/ppermute | solution.py:336
  279.9 24.4 %collective-permute-start.45 = (bf16[256,1024]{1,0:T(8,128)(2,1)}, bf16[256,1024]{1,0:T(8,128)(2,1)S(1)}, u32[]{:S(2)}, u32[]{:S(2)}) collective-permute-start(bf16[256,1024]{1,0:T(8,128)(2,1)} %get-tuple-element.185), channel_id=1, source_target_pairs={{0,24},{1,25},{2,26},{3,27},{4,28},{5,29},{6,30},{7,31},{8,16},{9,... | collective-permute-start | bytes 1572872 | tf_op jit(solution)/shard_map/ppermute | solution.py:336
  283.6 36.4 %collective-permute-start.46 = (bf16[2,64,2048]{2,1,0:T(8,128)(2,1)}, bf16[2,64,2048]{2,1,0:T(8,128)(2,1)S(1)}, u32[]{:S(2)}, u32[]{:S(2)}) collective-permute-start(bf16[2,64,2048]{2,1,0:T(8,128)(2,1)} %get-tuple-element.189), channel_id=1, source_target_pairs={{0,2},{1,3},{2,0},{3,1},{4,6},{5,7},{6,4},{7,5},{8,10},{9,11},{10,... | collective-permute-start | bytes 1572872 | tf_op jit(solution)/shard_map/ppermute | solution.py:336
  302.2 43.1 %collective-permute-start.42 = (bf16[256,1024]{1,0:T(8,128)(2,1)}, bf16[256,1024]{1,0:T(8,128)(2,1)S(1)}, u32[]{:S(2)}, u32[]{:S(2)}) collective-permute-start(bf16[256,1024]{1,0:T(8,128)(2,1)} %shard_map.176), channel_id=1, source_target_pairs={{0,0},{1,1},{2,4},{3,5},{4,2},{5,3},{6,6},{7,7},{8,8},{9,9},{10,12... | collective-permute-start | bytes 1572872 | tf_op jit(solution)/shard_map/ppermute | solution.py:336
  307.7 19.6 %collective-permute-start.47 = (bf16[2,64,1024]{2,1,0:T(8,128)(2,1)}, bf16[2,64,1024]{2,1,0:T(8,128)(2,1)S(1)}, u32[]{:S(2)}, u32[]{:S(2)}) collective-permute-start(bf16[2,64,1024]{2,1,0:T(8,128)(2,1)} %get-tuple-element.192), channel_id=1, source_target_pairs={{0,2},{1,3},{2,0},{3,1},{4,6},{5,7},{6,4},{7,5},{8,10},{9,11},{10,... | collective-permute-start | bytes 786440 | tf_op jit(solution)/shard_map/ppermute | solution.py:336
  (67 other events, 526.3 us)

commit v4 on v3

--- a/solution.py
+++ b/solution.py
@@ -1,3 +1,5 @@
+import math
+
 import jax
 import jax.numpy as jnp
 from jax import lax
@@ -389,9 +391,15 @@
     return (array, (rows,) + array.shape[1:], lambda b, f: (step(b),) + (0,) * (len(array.shape) - 1))
 
 
-def run(body, order, grid, ins, outs, scratch=(), flops=0):
+def run(body, order, grid, ins, outs, scratch=(), flops=0, spare=6 * 2**20):
     moved = sum(a.size * a.dtype.itemsize for a, _, _ in ins)
     moved += sum(a.size * a.dtype.itemsize for a, _, _ in outs)
+    def held(block, dtype, count):
+        return count * math.prod(block) * jnp.dtype(dtype).itemsize
+
+    count = 1 if grid == (1,) else 2
+    grant = sum(held(block, a.dtype, count) for a, block, _ in (*ins, *outs))
+    grant += sum(held(m.shape, m.dtype, 1) for m in scratch) + spare
     made = pl.pallas_call(
         body,
         grid_spec=pltpu.PrefetchScalarGridSpec(
@@ -402,6 +410,7 @@
             scratch_shapes=list(scratch),
         ),
         out_shape=[a for a, _, _ in outs],
+        compiler_params=pltpu.CompilerParams(vmem_limit_bytes=grant),
         cost_estimate=pl.CostEstimate(flops=flops // 100, bytes_accessed=moved // 100, transcendentals=0),
     )(order[0], *[a for a, _, _ in ins])
     order[0], _ = lax.optimization_barrier((order[0], made[0]))
@@ -444,10 +453,9 @@
 
 def split_slices(order, scaled, plain, gain, parts):
     rows, part, rest = scaled.shape[0], scaled.shape[1] // (4 * parts), plain.shape[1] // 4
-    out = shape_of(rows, lanes(parts * part + rest))
-
-    def body(flat_ref, scaled_ref, plain_ref, gain_ref, *refs):
-        held = refs[4]
+    out = shape_of(2, rows, lanes(parts * part + rest))
+
+    def body(flat_ref, scaled_ref, plain_ref, gain_ref, own_ref, sent_ref, held):
         scale = column_of(gain_ref[...].astype(WIDE))
         for s in range(4):
             for t in range(parts):
@@ -456,28 +464,42 @@
             held[s, :, parts * part : parts * part + rest] = plain_ref[
                 :, s * rest : (s + 1) * rest
             ]
-        for i in range(4):
-            refs[i][...] = held[group_of(flat_ref[0]) ^ i]
-
-    return run(
-        body, order, (1,), [whole(a) for a in (scaled, plain, gain)], [whole(out)] * 4,
-        [pltpu.VMEM((4, *out.shape), LOW)],
-    )
-
-
-def share_slices(slices):
-    return [slices[0]] + [
-        send(slices[i], pairs) for i, pairs in ((1, TO_ZL), (2, TO_CORE), (3, TO_FAR))
-    ]
-
-
-def quad_rows(order, parts):
-    def body(flat_ref, *refs):
-        for i in range(4):
-            refs[4][group_of(flat_ref[0]) ^ i] = refs[i][...]
-
-    out = shape_of(4, *parts[0].shape)
-    return run(body, order, (1,), [whole(p) for p in parts], [whole(out)])[0]
+        core = core_of(flat_ref[0])
+        for zl in range(2):
+            own_ref[zl] = held[2 * core + zl]
+            sent_ref[zl] = held[2 * (1 - core) + zl]
+
+    return run(
+        body, order, (1,), [whole(a) for a in (scaled, plain, gain)], [whole(out)] * 2,
+        [pltpu.VMEM((4, *out.shape[1:]), LOW)],
+    )
+
+
+def chip_rows(order, own, received):
+    def body(flat_ref, own_ref, received_ref, kept_ref, sent_ref):
+        core, chip = core_of(flat_ref[0]), flat_ref[0] & 1
+        kept_ref[core] = own_ref[chip]
+        kept_ref[1 - core] = received_ref[chip]
+        sent_ref[core] = own_ref[1 - chip]
+        sent_ref[1 - core] = received_ref[1 - chip]
+
+    return run(
+        body, order, (1,), [whole(own), whole(received)], [whole(shape_of(*own.shape))] * 2
+    )
+
+
+def quad_rows(order, own, received):
+    _, rows, width = own.shape
+
+    def body(flat_ref, own_ref, received_ref, out_ref):
+        chip = flat_ref[0] & 1
+        for c in range(2):
+            out_ref[2 * c + chip] = own_ref[c]
+            out_ref[2 * c + 1 - chip] = received_ref[c]
+
+    return run(
+        body, order, (1,), [whole(own), whole(received)], [whole(shape_of(4, rows, width))]
+    )[0]
 
 
 def line_rows(order, near, far):
@@ -579,9 +601,7 @@
 
     def body(flat_ref, q_ref, k_ref, v_ref, out_ref, log_ref):
         lane = lax.broadcasted_iota(jnp.int32, (rows, part), 1) // HEAD_DIM
-        log_lane = lax.broadcasted_iota(jnp.int32, (rows, 128), 1)
         total = jnp.zeros((rows, part), WIDE)
-        logs = jnp.zeros((rows, 128), WIDE)
         queries = q_ref[...].astype(WIDE) * scale
         for h in range(part // HEAD_DIM):
             q_head = jnp.where(lane == h, queries, 0.0).astype(LOW)
@@ -591,9 +611,8 @@
             mass = jnp.sum(powers, axis=-1, keepdims=True)
             probs = (powers * (1.0 / mass)).astype(LOW)
             total = jnp.where(lane == h, mm(probs, v_ref[...]), total)
-            logs = jnp.where(log_lane == h, peak + jnp.log(mass), logs)
+            log_ref[h : h + 1, :] = row_of(peak + jnp.log(mass))
         out_ref[...] = total.astype(LOW)
-        log_ref[...] = logs
 
     return run(
         body, order, (4,),
@@ -602,7 +621,10 @@
             (mix, (tokens, part), lambda b, f: (0, 1)),
             (mix, (tokens, part), lambda b, f: (0, 2)),
         ],
-        [by_rows(shape_of(tokens, part), rows), by_rows(shape_of(tokens, 128, dtype=WIDE), rows)],
+        [
+            by_rows(shape_of(tokens, part), rows),
+            (shape_of(8, tokens, dtype=WIDE), (8, rows), lambda b, f: (0, b)),
+        ],
         flops=16 * tokens * tokens * part,
     )
 
@@ -888,6 +910,12 @@
     )
 
 
+def share_slices(slices):
+    return [slices[0]] + [
+        send(slices[i], pairs) for i, pairs in ((1, TO_ZL), (2, TO_CORE), (3, TO_FAR))
+    ]
+
+
 def share_pieces(pieces):
     return [pieces[0]] + [
         send(pieces[i], pairs) for i, pairs in ((1, TO_X), (2, TO_Y), (3, TO_XY))
@@ -982,20 +1010,26 @@
     part, ff = width // 4, FF // 4
     gain_one, gain_two = attn_gain[None], mlp_gain[None]
 
-    one = share_slices(split_slices(order, qkv_weight, attn_out_weight, gain_one, 3))
+    own, sent = split_slices(order, qkv_weight, attn_out_weight, gain_one, 3)
+    received = send(sent, TO_CORE)
+    own_two, sent = split_slices(order, up_weight, down_weight, gain_two, 2)
+    received_two = send(sent, TO_CORE)
+    own, sent = chip_rows(order, own, received)
+    received = send(sent, TO_ZL)
+    own_two, sent = chip_rows(order, own_two, received_two)
     pos = positions[0]
     pos_row = jnp.concatenate([pos // 128, pos % 128]).astype(LOW)
     pos_row = jnp.pad(pos_row[None], ((0, 15), (0, width - 2 * tokens)))
     block = jnp.concatenate([inputs[0], pos_row])
-    two = split_slices(order, up_weight, down_weight, gain_two, 2)
+    wait(order, block)
+    one = quad_rows(order, own, received)
+    one_far = send(one, TO_ZH)
     first = send(after(order, block), ENTER)
-    one = quad_rows(order, one)
-    one_far = send(one, TO_ZH)
-    two = share_slices([after(order, t) for t in two])
+    received_two = send(after(order, sent), TO_ZL)
     one = line_rows(order, one, one_far)
     half = one.shape[0] // 2
     one_x, one_y = send(one, TO_X), send(one, TO_Y)
-    two = quad_rows(order, two)
+    two = quad_rows(order, own_two, received_two)
     two_far = send(two, TO_ZH)
     second = send(after(order, first), ENTER_MOVED)
     core_first = send(after(order, first), TO_CORE)
@@ -1013,21 +1047,21 @@
     cos_table, sin_table = rope_lanes(pos_all)
     one = [one, one_x, one_y, one_top, one_low]
 
+    w_out = jnp.concatenate([p[:, 3 * part :] for p in one])
+    wait(order, w_out, cos_table, sin_table)
+    w_side = send(after(order, w_out), TO_ZL)
+    w_core = send(after(order, w_out), TO_CORE)
     normed_one, mix = project(order, x, one, cos_table, sin_table)
-    w_out = after(order, jnp.concatenate([p[:, 3 * part :] for p in one]))
-    w_side = send(w_out, TO_ZL)
-    w_core = send(w_out, TO_CORE)
     two = line_rows(order, two, two_far)
     two_x, two_y = send(two, TO_X), send(two, TO_Y)
+    wait(order, w_core, cot_first)
     attended, logs = attend(order, mix)
     att_side = send(attended, TO_ZL)
     att_core = send(attended, TO_CORE)
+    wait(order, att_core, w_side)
     w_far = send(after(order, w_side), TO_CORE)
+    cot_second = send(after(order, cot_first), ENTER_MOVED)
     w_out = [w_out, w_side, w_core, w_far]
-    wait(order, w_far, cot_first)
-    cot_second = send(after(order, cot_first), ENTER_MOVED)
-    logs = logs[:, :8].T
-    wait(order, att_side, logs)
     heads = [attended, att_side, att_core, send(att_side, TO_CORE)]
     normed_two, resid = join_heads(order, x, heads, w_out)
 
@@ -1081,10 +1115,10 @@
     ff_kept, ff_sent = fold(order, [ff_terms])
     wait(order, output)
     ff_sent = send(after(order, ff_sent), TO_ZH)
+    mixed_kept, mixed_sent = fold(order, [t[None] for t in mixed_terms])
+    mixed_sent = send(mixed_sent, TO_ZH)
     (input_grad,) = norm_pull(order, x, (near, far, side), d_resid, False)
     input_grad = send(input_grad, TO_HOME)
-    mixed_kept, mixed_sent = fold(order, [t[None] for t in mixed_terms])
-    mixed_sent = send(mixed_sent, TO_ZH)
     ff_slices = share_slices(split_rows(order, ff_kept, ff_sent))
     mixed_slices = share_slices(split_rows(order, mixed_kept, mixed_sent))
     up_grad, gain_two_grad, down_grad = finish(

time: 350 us -> 300 us (0.86)
  Pallas kernels: 151 us -> 75.9 us
  waiting for transfers between devices: 95.3 us -> 134 us
  local copies, waits for them, and re-layouts: 22.1 us -> 11.6 us
  other arithmetic: 14 us -> 8.85 us
    pallas_call x30 -> x32, Pallas kernels: 151 us -> 75.9 us  [run(): pl.pallas_call(body, grid_spec=pltpu.PrefetchScalarGridSpec(num_scalar_pr...]
    ppermute x54 -> x52, waiting for transfers between devices: 95.3 us -> 122 us  [send(): return lax.ppermute(array, FLAT, pairs)]
    all_to_all x1, waiting for transfers between devices: 0.07 us -> 11.7 us  [quad_device(): lax.all_to_all(after(order, ff_terms), ('y', 'x'), split_axis=0, concat_a...]
    unnamed x96 -> x88, local copies, waits for them, and re-layouts: 17.1 us -> 11.5 us
    ppermute x54 -> x52, starting transfers between devices: 59.4 us -> 62.8 us  [send(): return lax.ppermute(array, FLAT, pairs)]
  transfers between devices with their start and end apart: 55 -> 53, of which waited for: 22 -> 24; matrix products, arithmetic and copies ran while one was open for 5% -> 3% of each run, Pallas kernels for 34% -> 21%
where the time goes in v4:
time: 300 us; the launch traced here: 299 us
  waiting for transfers between devices  134 us (45%)
  Pallas kernels  75.9 us (25%)
  starting transfers between devices  67.7 us (23%)
  local copies, waits for them, and re-layouts  11.6 us (4%)
  other arithmetic  8.85 us (3%)
    ppermute x52, waiting for transfers between devices, send(): return lax.ppermute(array, FLAT, pairs)  122 us
    pallas_call x32, Pallas kernels, run(): pl.pallas_call(body, grid_spec=pltpu.PrefetchScalarGridSpec(num_scalar_pr...  75.9 us
    ppermute x52, starting transfers between devices, send(): return lax.ppermute(array, FLAT, pairs)  62.8 us
    all_to_all x1, waiting for transfers between devices, quad_device(): lax.all_to_all(after(order, ff_terms), ('y', 'x'), split_axis=0, concat_a...  11.7 us
    unnamed x88, local copies, waits for them, and re-layouts  11.5 us
  transfers between devices with their start and end apart: 53, of which 24 were waited for; matrix products, arithmetic and copies ran while one was open for 3% of the time, Pallas kernels for 21%

profile of v4, /device:TPU:1, one launch (start us, length us, event | category | flops | bytes accessed | tf_op | source)
XLA Modules:
  0.0 299.1 jit_solution(2536476145278235791)
XLA Ops:
  7.5 2.4 collective-permute-start.2
  13.3 3.4 %collective-permute-start.5 = (bf16[272,1024]{1,0:T(8,128)(2,1)S(1)}, bf16[272,1024]{1,0:T(8,128)(2,1)S(1)}, u32[]{:S(2)}, u32[]{:S(2)}) collective-permute-start(bf16[272,1024]{1,0:T(8,128)(2,1)S(1)} %pad_maximum_fusion.block), channel_id=1, source_target_pairs={{0,1},{1,0},{2,4},{3,5},{4,2},{5,3},{6,7},{7,6},{8,9},{9,8},{10,12... | collective-permute-start | bytes 1671176 | tf_op jit(solution)/shard_map/ppermute | solution.py:338
  18.1 18.8 %collective-permute-done.3 = bf16[4,32,1024]{2,1,0:T(8,128)(2,1)S(1)} collective-permute-done((bf16[4,32,1024]{2,1,0:T(8,128)(2,1)S(1)}, bf16[4,32,1024]{2,1,0:T(8,128)(2,1)S(1)}, u32[]{:S(2)}, u32[]{:S(2)}) %collective-permute-start.3) | collective-permute-done | bytes 262176 | tf_op jit(solution)/shard_map/ppermute | solution.py:338
  40.1 6.1 %collective-permute-start.7 = (bf16[272,1024]{1,0:T(8,128)(2,1)S(1)}, bf16[272,1024]{1,0:T(8,128)(2,1)S(1)}, u32[]{:S(2)}, u32[]{:S(2)}) collective-permute-start(bf16[272,1024]{1,0:T(8,128)(2,1)S(1)} %collective-permute-done.5.first), channel_id=1, source_target_pairs={{2,3},{3,2},{4,5},{5,4},{10,11},{11,10},{12,13},{13,12},{18,19},{1... | collective-permute-start | bytes 1671176 | tf_op jit(solution)/shard_map/ppermute | solution.py:338
  47.9 9.9 %collective-permute-done.7.second = bf16[272,1024]{1,0:T(8,128)(2,1)S(1)} collective-permute-done((bf16[272,1024]{1,0:T(8,128)(2,1)S(1)}, bf16[272,1024]{1,0:T(8,128)(2,1)S(1)}, u32[]{:S(2)}, u32[]{:S(2)}) %collective-permute-start.7) | collective-permute-done | bytes 557088 | tf_op jit(solution)/shard_map/ppermute | solution.py:338
  61.1 3.4 %collective-permute-start.16 = (bf16[256,1024]{1,0:T(8,128)(2,1)S(1)}, bf16[256,1024]{1,0:T(8,128)(2,1)S(1)}, u32[]{:S(2)}, u32[]{:S(2)}) collective-permute-start(bf16[256,1024]{1,0:T(8,128)(2,1)S(1)} %bitcast.51), channel_id=1, source_target_pairs={{0,1},{1,0},{2,4},{3,5},{4,2},{5,3},{6,7},{7,6},{8,9},{9,8},{10,12... | collective-permute-start | bytes 1572872 | tf_op jit(solution)/shard_map/ppermute | solution.py:338
  67.5 4.9 %shard_map.160 = (bf16[1024,1024]{1,0:T(8,128)(2,1)S(1)}, bf16[1024,768]{1,0:T(8,128)(2,1)S(1)}) custom-call(s32[1]{0:T(128)} %bitcast.flat_ref, bf16[1024,1024]{1,0:T(8,128)(2,1)S(1)} %get-tuple-element.131.x_ref, bf16[256,1024]{1,0:T(8,128)(2,1)S(1)} %bitcast.41, bf16[256,1024]{1,0:T(8,128)(2,1)S(1)} %collective-permute-done.10.refs_1_.refs_4_, ...), custom_call_target="tpu_custom_call" | custom-call | flops 16106127 | bytes 89128 | tf_op jit(solution)/shard_map/pallas_call | solution.py:403
  72.4 4.2 %collective-permute-done.14 = bf16[4,32,2048]{2,1,0:T(8,128)(2,1)S(1)} collective-permute-done((bf16[4,32,2048]{2,1,0:T(8,128)(2,1)S(1)}, bf16[4,32,2048]{2,1,0:T(8,128)(2,1)S(1)}, u32[]{:S(2)}, u32[]{:S(2)}) %collective-permute-start.14) | collective-permute-done | bytes 524320 | tf_op jit(solution)/shard_map/ppermute | solution.py:338
  76.7 6.5 %collective-permute-done.16.first = bf16[256,1024]{1,0:T(8,128)(2,1)S(1)} collective-permute-done((bf16[256,1024]{1,0:T(8,128)(2,1)S(1)}, bf16[256,1024]{1,0:T(8,128)(2,1)S(1)}, u32[]{:S(2)}, u32[]{:S(2)}) %collective-permute-start.16) | collective-permute-done | bytes 524320 | tf_op jit(solution)/shard_map/ppermute | solution.py:338
  83.2 8.1 %shard_map.162 = (bf16[1024,256]{1,0:T(8,128)(2,1)S(1)}, f32[8,1024]{1,0:T(8,128)S(1)}) custom-call(s32[1]{0:T(128)} %bitcast.flat_ref, bf16[1024,768]{1,0:T(8,128)(2,1)S(1)} %get-tuple-element.141.q_ref.k_ref.v_ref, bf16[1024,768]{1,0:T(8,128)(2,1)S(1)} %get-tuple-element.141.q_ref.k_ref.v_ref, bf16[1024,768]{1,0:T(8,128)(2,1)S(1)} %get-tuple-element.141.q_ref.k_ref.v_ref), custom_call_target="tpu_custom_call" | custom-call | flops 42949672 | bytes 52756 | tf_op jit(solution)/shard_map/pallas_call | solution.py:403
  91.4 3.5 %collective-permute-start.17 = (bf16[1024,256]{1,0:T(8,128)(2,1)S(1)}, bf16[1024,256]{1,0:T(8,128)(2,1)S(1)}, u32[]{:S(2)}, u32[]{:S(2)}) collective-permute-start(bf16[1024,256]{1,0:T(8,128)(2,1)S(1)} %get-tuple-element.142.refs_0_.refs_4_.o_ref), channel_id=1, source_target_pairs={{0,4},{1,5},{2,6},{3,7},{4,0},{5,1},{6,2},{7,3},{8,12},{9,13},{10,... | collective-permute-start | bytes 1572872 | tf_op jit(solution)/shard_map/ppermute | solution.py:338
  96.5 11.9 %collective-permute-done.19.refs_1_.refs_5_ = bf16[1024,256]{1,0:T(8,128)(2,1)S(1)} collective-permute-done((bf16[1024,256]{1,0:T(8,128)(2,1)S(1)}, bf16[1024,256]{1,0:T(8,128)(2,1)S(1)}, u32[]{:S(2)}, u32[]{:S(2)}) %collective-permute-start.19) | collective-permute-done | bytes 524320 | tf_op jit(solution)/shard_map/ppermute | solution.py:338
  111.5 4.3 %shard_map.163 = (bf16[1024,1024]{1,0:T(8,128)(2,1)S(1)}, f32[256,1024]{1,0:T(8,128)S(1)}) custom-call(s32[1]{0:T(128)} %bitcast.flat_ref, bf16[1024,1024]{1,0:T(8,128)(2,1)S(1)} %get-tuple-element.131.x_ref, bf16[1024,256]{1,0:T(8,128)(2,1)S(1)} %get-tuple-element.142.refs_0_.refs_4_.o_ref, bf16[1024,256]{1,0:T(8,128)(2,1)S(1)} %collective-permute-done.19.refs_1_.refs_5_, ...), custom_call_target="tpu_custom_call" | custom-call | flops 21474836 | bytes 94371 | tf_op jit(solution)/shard_map/pallas_call | solution.py:403
  115.8 3.6 %collective-permute-done.22.second = bf16[256,1024]{1,0:T(8,128)(2,1)S(1)} collective-permute-done((bf16[256,1024]{1,0:T(8,128)(2,1)S(1)}, bf16[256,1024]{1,0:T(8,128)(2,1)S(1)}, u32[]{:S(2)}, u32[]{:S(2)}) %collective-permute-start.22) | collective-permute-done | bytes 524320 | tf_op jit(solution)/shard_map/ppermute | solution.py:338
  123.3 9.8 %collective-permute-done.29.refs_4_.refs_5_ = bf16[128,2048]{1,0:T(8,128)(2,1)S(1)} collective-permute-done((bf16[128,2048]{1,0:T(8,128)(2,1)S(1)}, bf16[128,2048]{1,0:T(8,128)(2,1)S(1)}, u32[]{:S(2)}, u32[]{:S(2)}) %collective-permute-start.29) | collective-permute-done | bytes 524320 | tf_op jit(solution)/shard_map/ppermute | solution.py:338
  134.3 7.3 %shard_map.165 = (bf16[1024,656]{1,0:T(8,128)(2,1)S(1)}, bf16[1024,1312]{1,0:T(8,128)(2,1)S(1)}) custom-call(s32[1]{0:T(128)} %bitcast.flat_ref, bf16[1024,1024]{1,0:T(8,128)(2,1)S(1)} %get-tuple-element.147.n_ref, bf16[1024,1024]{1,0:T(8,128)(2,1)S(1)} %shard_map.164.cot_ref.base_ref, bf16[256,2048]{1,0:T(8,128)(2,1)S(1)} %bitcast.33, ...), custom_call_target="tpu_custom_call" | custom-call | flops 41271952 | bytes 124190 | tf_op jit(solution)/shard_map/pallas_call | solution.py:403
  148.8 7.4 %shard_map.168 = bf16[4,256,2048]{2,1,0:T(8,128)(2,1)S(1)} custom-call(s32[1]{0:T(128)} %bitcast.flat_ref, bf16[1024,1024]{1,0:T(8,128)(2,1)S(1)} %get-tuple-element.147.n_ref, bf16[1024,1024]{1,0:T(8,128)(2,1)S(1)} %shard_map.164.cot_ref.base_ref, bf16[1024,1312]{1,0:T(8,128)(2,1)S(1)} %get-tuple-element.156.refs_0_.d_ref, ...), custom_call_target="tpu_custom_call" | custom-call | flops 41271952 | bytes 124190 | tf_op jit(solution)/shard_map/pallas_call | solution.py:403
  156.2 4.9 %collective-permute-done.31.c_ref = bf16[256,1024]{1,0:T(8,128)(2,1)S(1)} collective-permute-done((bf16[256,1024]{1,0:T(8,128)(2,1)S(1)}, bf16[256,1024]{1,0:T(8,128)(2,1)S(1)}, u32[]{:S(2)}, u32[]{:S(2)}) %collective-permute-start.31) | collective-permute-done | bytes 524320 | tf_op jit(solution)/shard_map/ppermute | solution.py:338
  164.8 2.4 shard_map.170
  168.6 6.2 %collective-permute-done.32.refs_1_ = bf16[256,1024]{1,0:T(8,128)(2,1)S(1)} collective-permute-done((bf16[256,1024]{1,0:T(8,128)(2,1)S(1)}, bf16[256,1024]{1,0:T(8,128)(2,1)S(1)}, u32[]{:S(2)}, u32[]{:S(2)}) %collective-permute-start.32) | collective-permute-done | bytes 524320 | tf_op jit(solution)/shard_map/ppermute | solution.py:338
  178.4 2.5 shard_map.172
  182.9 4.9 %all-to-all-start = ((bf16[4,256,2048]{2,1,0:T(8,128)(2,1)}), bf16[4,256,2048]{2,1,0:T(8,128)(2,1)}, u32[]{:S(2)}, u32[]{:S(2)}) async-start(bf16[4,256,2048]{2,1,0:T(8,128)(2,1)} %copy-done.2), calls=%async_computation | async-start | bytes 8388608 | tf_op jit(solution)/shard_map/all_to_all | solution.py:1093
  190.3 14.7 %shard_map.173 = (bf16[1024,256]{1,0:T(8,128)(2,1)S(1)}, bf16[1024,256]{1,0:T(8,128)(2,1)S(1)}, bf16[1024,256]{1,0:T(8,128)(2,1)S(1)}) custom-call(s32[1]{0:T(128)} %bitcast.flat_ref, bf16[1024,768]{1,0:T(8,128)(2,1)S(1)} %get-tuple-element.141.q_ref.k_ref.v_ref, bf16[1024,768]{1,0:T(8,128)(2,1)S(1)} %get-tuple-element.141.q_ref.k_ref.v_ref, ...), custom_call_target="tpu_custom_call" | custom-call | flops 107374184 | bytes 84213 | tf_op jit(solution)/shard_map/pallas_call | solution.py:403
  207.5 4.2 %shard_map.174 = (bf16[256,1024]{1,0:T(8,128)(2,1)S(1)}, bf16[256,1024]{1,0:T(8,128)(2,1)}, bf16[256,1024]{1,0:T(8,128)(2,1)}, bf16[256,1024]{1,0:T(8,128)(2,1)}) custom-call(s32[1]{0:T(128)} %bitcast.flat_ref, bf16[1024,1024]{1,0:T(8,128)(2,1)S(1)} %copy-done.20, bf16[1024,256]{1,0:T(8,128)(2,1)S(1)} %get-tuple-element.169.refs_0_, ...), custom_call_target="tpu_custom_call" | custom-call | flops 16106127 | bytes 62914 | tf_op jit(solution)/shard_map/pallas_call | solution.py:403
  213.4 3.5 %collective-permute-start.37 = (bf16[256,1024]{1,0:T(8,128)(2,1)}, bf16[256,1024]{1,0:T(8,128)(2,1)}, u32[]{:S(2)}, u32[]{:S(2)}) collective-permute-start(bf16[256,1024]{1,0:T(8,128)(2,1)} %fusion.4), channel_id=1, source_target_pairs={{0,0},{1,1},{2,4},{3,5},{4,2},{5,3},{6,6},{7,7},{8,8},{9,9},{10,12... | collective-permute-start | bytes 1572872 | tf_op jit(solution)/shard_map/ppermute | solution.py:338
  223.4 11.7 %all-to-all-done = bf16[4,256,2048]{2,1,0:T(8,128)(2,1)} async-done(((bf16[4,256,2048]{2,1,0:T(8,128)(2,1)}), bf16[4,256,2048]{2,1,0:T(8,128)(2,1)}, u32[]{:S(2)}, u32[]{:S(2)}) %all-to-all-start) | async-done | bytes 4194336 | tf_op jit(solution)/shard_map/all_to_all | solution.py:1093
  235.1 2.6 shard_map.177
  238.8 7.5 %collective-permute-done.38 = bf16[256,1024]{1,0:T(8,128)(2,1)} collective-permute-done((bf16[256,1024]{1,0:T(8,128)(2,1)}, bf16[256,1024]{1,0:T(8,128)(2,1)}, u32[]{:S(2)}, u32[]{:S(2)}) %collective-permute-start.38) | collective-permute-done | bytes 524320 | tf_op jit(solution)/shard_map/ppermute | solution.py:338
  246.4 12.1 %collective-permute-done.40 = bf16[256,1024]{1,0:T(8,128)(2,1)} collective-permute-done((bf16[256,1024]{1,0:T(8,128)(2,1)}, bf16[256,1024]{1,0:T(8,128)(2,1)}, u32[]{:S(2)}, u32[]{:S(2)}) %collective-permute-start.40) | collective-permute-done | bytes 524320 | tf_op jit(solution)/shard_map/ppermute | solution.py:338
  261.4 3.8 %collective-permute-start.43 = (bf16[256,1024]{1,0:T(8,128)(2,1)S(1)}, bf16[256,1024]{1,0:T(8,128)(2,1)S(1)}, u32[]{:S(2)}, u32[]{:S(2)}) collective-permute-start(bf16[256,1024]{1,0:T(8,128)(2,1)S(1)} %shard_map.179), channel_id=1, source_target_pairs={{0,0},{1,1},{2,4},{3,5},{4,2},{5,3},{6,6},{7,7},{8,8},{9,9},{10,12... | collective-permute-start | bytes 1572872 | tf_op jit(solution)/shard_map/ppermute | solution.py:338
  268.4 16.4 %collective-permute-done.45 = bf16[2,64,1024]{2,1,0:T(8,128)(2,1)S(1)} collective-permute-done((bf16[2,64,1024]{2,1,0:T(8,128)(2,1)S(1)}, bf16[2,64,1024]{2,1,0:T(8,128)(2,1)S(1)}, u32[]{:S(2)}, u32[]{:S(2)}) %collective-permute-start.45) | collective-permute-done | bytes 262176 | tf_op jit(solution)/shard_map/ppermute | solution.py:338
  284.9 4.6 %collective-permute-start.49 = (bf16[32,1024]{1,0:T(8,128)(2,1)S(1)}, bf16[32,1024]{1,0:T(8,128)(2,1)S(1)}, u32[]{:S(2)}, u32[]{:S(2)}) collective-permute-start(bf16[32,1024]{1,0:T(8,128)(2,1)S(1)} %get-tuple-element.202), channel_id=1, source_target_pairs={{0,1},{1,0},{2,3},{3,2},{4,5},{5,4},{6,7},{7,6},{8,9},{9,8},{10,11... | collective-permute-start | bytes 196616 | tf_op jit(solution)/shard_map/ppermute | solution.py:338
  (212 shorter events, 80.1 us)
Async XLA Ops:
  13.3 26.8 %collective-permute-start.5 = (bf16[272,1024]{1,0:T(8,128)(2,1)S(1)}, bf16[272,1024]{1,0:T(8,128)(2,1)S(1)}, u32[]{:S(2)}, u32[]{:S(2)}) collective-permute-start(bf16[272,1024]{1,0:T(8,128)(2,1)S(1)} %pad_maximum_fusion.block), channel_id=1, source_target_pairs={{0,1},{1,0},{2,4},{3,5},{4,2},{5,3},{6,7},{7,6},{8,9},{9,8},{10,12... | collective-permute-start | bytes 1671176 | tf_op jit(solution)/shard_map/ppermute | solution.py:338
  16.8 20.1 %collective-permute-start.3 = (bf16[4,32,1024]{2,1,0:T(8,128)(2,1)S(1)}, bf16[4,32,1024]{2,1,0:T(8,128)(2,1)S(1)}, u32[]{:S(2)}, u32[]{:S(2)}) collective-permute-start(bf16[4,32,1024]{2,1,0:T(8,128)(2,1)S(1)} %shard_map.156), channel_id=1, source_target_pairs={{0,2},{1,3},{2,0},{3,1},{4,6},{5,7},{6,4},{7,5},{8,10},{9,11},{10,... | collective-permute-start | bytes 786440 | tf_op jit(solution)/shard_map/ppermute | solution.py:338
  16.8 23.2 %collective-permute-start.4 = (bf16[2,32,2048]{2,1,0:T(8,128)(2,1)S(1)}, bf16[2,32,2048]{2,1,0:T(8,128)(2,1)S(1)}, u32[]{:S(2)}, u32[]{:S(2)}) collective-permute-start(bf16[2,32,2048]{2,1,0:T(8,128)(2,1)S(1)} %get-tuple-element.124), channel_id=1, source_target_pairs={{0,1},{1,0},{2,3},{3,2},{4,5},{5,4},{6,7},{7,6},{8,9},{9,8},{10,11... | collective-permute-start | bytes 786440 | tf_op jit(solution)/shard_map/ppermute | solution.py:338
  40.1 17.7 %collective-permute-start.7 = (bf16[272,1024]{1,0:T(8,128)(2,1)S(1)}, bf16[272,1024]{1,0:T(8,128)(2,1)S(1)}, u32[]{:S(2)}, u32[]{:S(2)}) collective-permute-start(bf16[272,1024]{1,0:T(8,128)(2,1)S(1)} %collective-permute-done.5.first), channel_id=1, source_target_pairs={{2,3},{3,2},{4,5},{5,4},{10,11},{11,10},{12,13},{13,12},{18,19},{1... | collective-permute-start | bytes 1671176 | tf_op jit(solution)/shard_map/ppermute | solution.py:338
  46.2 11.7 %collective-permute-start.6 = (bf16[272,1024]{1,0:T(8,128)(2,1)S(1)}, bf16[272,1024]{1,0:T(8,128)(2,1)S(1)}, u32[]{:S(2)}, u32[]{:S(2)}) collective-permute-start(bf16[272,1024]{1,0:T(8,128)(2,1)S(1)} %collective-permute-done.5.first), channel_id=1, source_target_pairs={{0,4},{1,5},{2,6},{3,7},{4,0},{5,1},{6,2},{7,3},{8,12},{9,13},{10,... | collective-permute-start | bytes 1671176 | tf_op jit(solution)/shard_map/ppermute | solution.py:338
  46.3 30.4 %collective-permute-start.14 = (bf16[4,32,2048]{2,1,0:T(8,128)(2,1)S(1)}, bf16[4,32,2048]{2,1,0:T(8,128)(2,1)S(1)}, u32[]{:S(2)}, u32[]{:S(2)}) collective-permute-start(bf16[4,32,2048]{2,1,0:T(8,128)(2,1)S(1)} %shard_map.158), channel_id=1, source_target_pairs={{0,2},{1,3},{2,0},{3,1},{4,6},{5,7},{6,4},{7,5},{8,10},{9,11},{10,... | collective-permute-start | bytes 1572872 | tf_op jit(solution)/shard_map/ppermute | solution.py:338
  46.4 12.0 %collective-permute-start.13 = (bf16[128,1024]{1,0:T(8,128)(2,1)S(1)}, bf16[128,1024]{1,0:T(8,128)(2,1)S(1)}, u32[]{:S(2)}, u32[]{:S(2)}) collective-permute-start(bf16[128,1024]{1,0:T(8,128)(2,1)S(1)} %slice.85), channel_id=1, source_target_pairs={{0,8},{1,9},{2,10},{3,11},{4,12},{5,13},{6,14},{7,15},{8,0},{9,1},... | collective-permute-start | bytes 786440 | tf_op jit(solution)/shard_map/ppermute | solution.py:338
  46.8 11.6 %collective-permute-start.12 = (bf16[128,1024]{1,0:T(8,128)(2,1)S(1)}, bf16[128,1024]{1,0:T(8,128)(2,1)S(1)}, u32[]{:S(2)}, u32[]{:S(2)}) collective-permute-start(bf16[128,1024]{1,0:T(8,128)(2,1)S(1)} %slice.83), channel_id=1, source_target_pairs={{0,16},{1,17},{2,18},{3,19},{4,20},{5,21},{6,22},{7,23},{8,24},{9,... | collective-permute-start | bytes 786440 | tf_op jit(solution)/shard_map/ppermute | solution.py:338
  61.1 22.1 %collective-permute-start.16 = (bf16[256,1024]{1,0:T(8,128)(2,1)S(1)}, bf16[256,1024]{1,0:T(8,128)(2,1)S(1)}, u32[]{:S(2)}, u32[]{:S(2)}) collective-permute-start(bf16[256,1024]{1,0:T(8,128)(2,1)S(1)} %bitcast.51), channel_id=1, source_target_pairs={{0,1},{1,0},{2,4},{3,5},{4,2},{5,3},{6,7},{7,6},{8,9},{9,8},{10,12... | collective-permute-start | bytes 1572872 | tf_op jit(solution)/shard_map/ppermute | solution.py:338
  67.3 15.9 %collective-permute-start.15 = (bf16[1024,256]{1,0:T(8,128)(2,1)S(1)}, bf16[1024,256]{1,0:T(8,128)(2,1)S(1)}, u32[]{:S(2)}, u32[]{:S(2)}) collective-permute-start(bf16[1024,256]{1,0:T(8,128)(2,1)S(1)} %slice_dynamic-update-slice_fusion.3.refs_4_.refs_8_), channel_id=1, source_target_pairs={{0,4},{1,5},{2,6},{3,7},{4,0},{5,1},{6,2},{7,3},{8,12},{9,13},{10,... | collective-permute-start | bytes 1572872 | tf_op jit(solution)/shard_map/ppermute | solution.py:338
  67.4 29.1 %collective-permute-start.18 = (bf16[1024,256]{1,0:T(8,128)(2,1)S(1)}, bf16[1024,256]{1,0:T(8,128)(2,1)S(1)}, u32[]{:S(2)}, u32[]{:S(2)}) collective-permute-start(bf16[1024,256]{1,0:T(8,128)(2,1)S(1)} %slice_dynamic-update-slice_fusion.3.refs_4_.refs_8_), channel_id=1, source_target_pairs={{0,1},{1,0},{2,3},{3,2},{4,5},{5,4},{6,7},{7,6},{8,9},{9,8},{10,11... | collective-permute-start | bytes 1572872 | tf_op jit(solution)/shard_map/ppermute | solution.py:338
  94.9 13.5 %collective-permute-start.19 = (bf16[1024,256]{1,0:T(8,128)(2,1)S(1)}, bf16[1024,256]{1,0:T(8,128)(2,1)S(1)}, u32[]{:S(2)}, u32[]{:S(2)}) collective-permute-start(bf16[1024,256]{1,0:T(8,128)(2,1)S(1)} %get-tuple-element.142.refs_0_.refs_4_.o_ref), channel_id=1, source_target_pairs={{0,1},{1,0},{2,3},{3,2},{4,5},{5,4},{6,7},{7,6},{8,9},{9,8},{10,11... | collective-permute-start | bytes 1572872 | tf_op jit(solution)/shard_map/ppermute | solution.py:338
  94.9 25.1 %collective-permute-start.27 = (bf16[256,2048]{1,0:T(8,128)(2,1)S(1)}, bf16[256,2048]{1,0:T(8,128)(2,1)S(1)}, u32[]{:S(2)}, u32[]{:S(2)}) collective-permute-start(bf16[256,2048]{1,0:T(8,128)(2,1)S(1)} %bitcast.31), channel_id=1, source_target_pairs={{0,16},{1,17},{2,18},{3,19},{4,20},{5,21},{6,22},{7,23},{8,24},{9,... | collective-permute-start | bytes 3145736 | tf_op jit(solution)/shard_map/ppermute | solution.py:338
  96.3 25.2 %collective-permute-start.26 = (bf16[256,2048]{1,0:T(8,128)(2,1)S(1)}, bf16[256,2048]{1,0:T(8,128)(2,1)S(1)}, u32[]{:S(2)}, u32[]{:S(2)}) collective-permute-start(bf16[256,2048]{1,0:T(8,128)(2,1)S(1)} %bitcast.32), channel_id=1, source_target_pairs={{0,8},{1,9},{2,10},{3,11},{4,12},{5,13},{6,14},{7,15},{8,0},{9,1},... | collective-permute-start | bytes 3145736 | tf_op jit(solution)/shard_map/ppermute | solution.py:338
  120.0 13.0 %collective-permute-start.29 = (bf16[128,2048]{1,0:T(8,128)(2,1)S(1)}, bf16[128,2048]{1,0:T(8,128)(2,1)S(1)}, u32[]{:S(2)}, u32[]{:S(2)}) collective-permute-start(bf16[128,2048]{1,0:T(8,128)(2,1)S(1)} %slice.91), channel_id=1, source_target_pairs={{0,8},{1,9},{2,10},{3,11},{4,12},{5,13},{6,14},{7,15},{8,0},{9,1},... | collective-permute-start | bytes 1572872 | tf_op jit(solution)/shard_map/ppermute | solution.py:338
  121.5 12.7 %collective-permute-start.28 = (bf16[128,2048]{1,0:T(8,128)(2,1)S(1)}, bf16[128,2048]{1,0:T(8,128)(2,1)S(1)}, u32[]{:S(2)}, u32[]{:S(2)}) collective-permute-start(bf16[128,2048]{1,0:T(8,128)(2,1)S(1)} %slice.90), channel_id=1, source_target_pairs={{0,16},{1,17},{2,18},{3,19},{4,20},{5,21},{6,22},{7,23},{8,24},{9,... | collective-permute-start | bytes 1572872 | tf_op jit(solution)/shard_map/ppermute | solution.py:338
  147.9 13.2 %collective-permute-start.31 = (bf16[256,1024]{1,0:T(8,128)(2,1)S(1)}, bf16[256,1024]{1,0:T(8,128)(2,1)S(1)}, u32[]{:S(2)}, u32[]{:S(2)}) collective-permute-start(bf16[256,1024]{1,0:T(8,128)(2,1)S(1)} %fusion.5), channel_id=1, source_target_pairs={{0,1},{1,0},{2,3},{3,2},{4,5},{5,4},{6,7},{7,6},{8,9},{9,8},{10,11... | collective-permute-start | bytes 1572872 | tf_op jit(solution)/shard_map/ppermute | solution.py:338
  162.5 12.3 %collective-permute-start.32 = (bf16[256,1024]{1,0:T(8,128)(2,1)S(1)}, bf16[256,1024]{1,0:T(8,128)(2,1)S(1)}, u32[]{:S(2)}, u32[]{:S(2)}) collective-permute-start(bf16[256,1024]{1,0:T(8,128)(2,1)S(1)} %get-tuple-element.160.refs_0_), channel_id=1, source_target_pairs={{0,1},{1,0},{2,3},{3,2},{4,5},{5,4},{6,7},{7,6},{8,9},{9,8},{10,11... | collective-permute-start | bytes 1572872 | tf_op jit(solution)/shard_map/ppermute | solution.py:338
  163.3 13.5 %collective-permute-start.33 = (bf16[256,1024]{1,0:T(8,128)(2,1)S(1)}, bf16[256,1024]{1,0:T(8,128)(2,1)S(1)}, u32[]{:S(2)}, u32[]{:S(2)}) collective-permute-start(bf16[256,1024]{1,0:T(8,128)(2,1)S(1)} %get-tuple-element.160.refs_0_), channel_id=1, source_target_pairs={{0,4},{1,5},{2,6},{3,7},{4,0},{5,1},{6,2},{7,3},{8,12},{9,13},{10,... | collective-permute-start | bytes 1572872 | tf_op jit(solution)/shard_map/ppermute | solution.py:338
  182.9 52.3 %all-to-all-start = ((bf16[4,256,2048]{2,1,0:T(8,128)(2,1)}), bf16[4,256,2048]{2,1,0:T(8,128)(2,1)}, u32[]{:S(2)}, u32[]{:S(2)}) async-start(bf16[4,256,2048]{2,1,0:T(8,128)(2,1)} %copy-done.2), calls=%async_computation | async-start | bytes 8388608 | tf_op jit(solution)/shard_map/all_to_all | solution.py:1093
  189.4 15.7 %collective-permute-start.36 = (bf16[256,1024]{1,0:T(8,128)(2,1)S(1)}, bf16[256,1024]{1,0:T(8,128)(2,1)S(1)}, u32[]{:S(2)}, u32[]{:S(2)}) collective-permute-start(bf16[256,1024]{1,0:T(8,128)(2,1)S(1)} %fusion.1), channel_id=1, source_target_pairs={{0,1},{1,0},{2,3},{3,2},{4,5},{5,4},{6,7},{7,6},{8,9},{9,8},{10,11... | collective-permute-start | bytes 1572872 | tf_op jit(solution)/shard_map/ppermute | solution.py:338
  213.4 24.4 %collective-permute-start.37 = (bf16[256,1024]{1,0:T(8,128)(2,1)}, bf16[256,1024]{1,0:T(8,128)(2,1)}, u32[]{:S(2)}, u32[]{:S(2)}) collective-permute-start(bf16[256,1024]{1,0:T(8,128)(2,1)} %fusion.4), channel_id=1, source_target_pairs={{0,0},{1,1},{2,4},{3,5},{4,2},{5,3},{6,6},{7,7},{8,8},{9,9},{10,12... | collective-permute-start | bytes 1572872 | tf_op jit(solution)/shard_map/ppermute | solution.py:338
  216.9 29.4 %collective-permute-start.38 = (bf16[256,1024]{1,0:T(8,128)(2,1)}, bf16[256,1024]{1,0:T(8,128)(2,1)}, u32[]{:S(2)}, u32[]{:S(2)}) collective-permute-start(bf16[256,1024]{1,0:T(8,128)(2,1)} %get-tuple-element.183), channel_id=1, source_target_pairs={{0,8},{1,9},{2,10},{3,11},{4,12},{5,13},{6,14},{7,15},{8,0},{9,1},... | collective-permute-start | bytes 1572872 | tf_op jit(solution)/shard_map/ppermute | solution.py:338
  218.6 27.7 %collective-permute-start.39 = (bf16[256,1024]{1,0:T(8,128)(2,1)}, bf16[256,1024]{1,0:T(8,128)(2,1)}, u32[]{:S(2)}, u32[]{:S(2)}) collective-permute-start(bf16[256,1024]{1,0:T(8,128)(2,1)} %get-tuple-element.184), channel_id=1, source_target_pairs={{0,16},{1,17},{2,18},{3,19},{4,20},{5,21},{6,22},{7,23},{8,24},{9,... | collective-permute-start | bytes 1572872 | tf_op jit(solution)/shard_map/ppermute | solution.py:338
  219.8 38.7 %collective-permute-start.40 = (bf16[256,1024]{1,0:T(8,128)(2,1)}, bf16[256,1024]{1,0:T(8,128)(2,1)}, u32[]{:S(2)}, u32[]{:S(2)}) collective-permute-start(bf16[256,1024]{1,0:T(8,128)(2,1)} %get-tuple-element.185), channel_id=1, source_target_pairs={{0,24},{1,25},{2,26},{3,27},{4,28},{5,29},{6,30},{7,31},{8,16},{9,... | collective-permute-start | bytes 1572872 | tf_op jit(solution)/shard_map/ppermute | solution.py:338
  223.4 36.6 %collective-permute-start.42 = (bf16[256,1024]{1,0:T(8,128)(2,1)S(1)}, bf16[256,1024]{1,0:T(8,128)(2,1)S(1)}, u32[]{:S(2)}, u32[]{:S(2)}) collective-permute-start(bf16[256,1024]{1,0:T(8,128)(2,1)S(1)} %fusion), channel_id=1, source_target_pairs={{0,1},{1,0},{2,3},{3,2},{4,5},{5,4},{6,7},{7,6},{8,9},{9,8},{10,11... | collective-permute-start | bytes 1572872 | tf_op jit(solution)/shard_map/ppermute | solution.py:338
  237.8 27.6 %collective-permute-start.44 = (bf16[2,64,2048]{2,1,0:T(8,128)(2,1)S(1)}, bf16[2,64,2048]{2,1,0:T(8,128)(2,1)S(1)}, u32[]{:S(2)}, u32[]{:S(2)}) collective-permute-start(bf16[2,64,2048]{2,1,0:T(8,128)(2,1)S(1)} %get-tuple-element.191), channel_id=1, source_target_pairs={{0,2},{1,3},{2,0},{3,1},{4,6},{5,7},{6,4},{7,5},{8,10},{9,11},{10,... | collective-permute-start | bytes 1572872 | tf_op jit(solution)/shard_map/ppermute | solution.py:338
  261.4 35.0 %collective-permute-start.43 = (bf16[256,1024]{1,0:T(8,128)(2,1)S(1)}, bf16[256,1024]{1,0:T(8,128)(2,1)S(1)}, u32[]{:S(2)}, u32[]{:S(2)}) collective-permute-start(bf16[256,1024]{1,0:T(8,128)(2,1)S(1)} %shard_map.179), channel_id=1, source_target_pairs={{0,0},{1,1},{2,4},{3,5},{4,2},{5,3},{6,6},{7,7},{8,8},{9,9},{10,12... | collective-permute-start | bytes 1572872 | tf_op jit(solution)/shard_map/ppermute | solution.py:338
  265.3 19.6 %collective-permute-start.45 = (bf16[2,64,1024]{2,1,0:T(8,128)(2,1)S(1)}, bf16[2,64,1024]{2,1,0:T(8,128)(2,1)S(1)}, u32[]{:S(2)}, u32[]{:S(2)}) collective-permute-start(bf16[2,64,1024]{2,1,0:T(8,128)(2,1)S(1)} %get-tuple-element.194), channel_id=1, source_target_pairs={{0,2},{1,3},{2,0},{3,1},{4,6},{5,7},{6,4},{7,5},{8,10},{9,11},{10,... | collective-permute-start | bytes 786440 | tf_op jit(solution)/shard_map/ppermute | solution.py:338
  265.5 24.0 %collective-permute-start.46 = (bf16[32,2048]{1,0:T(8,128)(2,1)S(1)}, bf16[32,2048]{1,0:T(8,128)(2,1)S(1)}, u32[]{:S(2)}, u32[]{:S(2)}) collective-permute-start(bf16[32,2048]{1,0:T(8,128)(2,1)S(1)} %get-tuple-element.197), channel_id=1, source_target_pairs={{0,1},{1,0},{2,3},{3,2},{4,5},{5,4},{6,7},{7,6},{8,9},{9,8},{10,11... | collective-permute-start | bytes 393224 | tf_op jit(solution)/shard_map/ppermute | solution.py:338
  267.0 23.7 %collective-permute-start.47 = (bf16[32,2048]{1,0:T(8,128)(2,1)S(1)}, bf16[32,2048]{1,0:T(8,128)(2,1)S(1)}, u32[]{:S(2)}, u32[]{:S(2)}) collective-permute-start(bf16[32,2048]{1,0:T(8,128)(2,1)S(1)} %get-tuple-element.198), channel_id=1, source_target_pairs={{0,4},{1,5},{2,6},{3,7},{4,0},{5,1},{6,2},{7,3},{8,12},{9,13},{10,... | collective-permute-start | bytes 393224 | tf_op jit(solution)/shard_map/ppermute | solution.py:338
  267.9 24.5 %collective-permute-start.48 = (bf16[32,2048]{1,0:T(8,128)(2,1)S(1)}, bf16[32,2048]{1,0:T(8,128)(2,1)S(1)}, u32[]{:S(2)}, u32[]{:S(2)}) collective-permute-start(bf16[32,2048]{1,0:T(8,128)(2,1)S(1)} %get-tuple-element.199), channel_id=1, source_target_pairs={{0,5},{1,4},{2,7},{3,6},{4,1},{5,0},{6,3},{7,2},{8,13},{9,12},{10,... | collective-permute-start | bytes 393224 | tf_op jit(solution)/shard_map/ppermute | solution.py:338
  (61 other events, 815.5 us)

commit v5 on v4

--- a/solution.py
+++ b/solution.py
@@ -397,8 +397,10 @@
     def held(block, dtype, count):
         return count * math.prod(block) * jnp.dtype(dtype).itemsize
 
-    count = 1 if grid == (1,) else 2
-    grant = sum(held(block, a.dtype, count) for a, block, _ in (*ins, *outs))
+    grant = sum(
+        held(block, a.dtype, 1 if tuple(block) == tuple(a.shape) else 2)
+        for a, block, _ in (*ins, *outs)
+    )
     grant += sum(held(m.shape, m.dtype, 1) for m in scratch) + spare
     made = pl.pallas_call(
         body,
@@ -422,6 +424,11 @@
     return [(0, 0, rows), (1, 0, rows), (2, 0, rows), (3, 0, rows // 2), (3, rows // 2, rows // 2)]
 
 
+def rows_of(ref, span):
+    count = span[2]
+    return slice(ref.shape[0] - count, None) if span[1] else slice(0, count)
+
+
 def span_of(square, span, rows):
     index, first, count = span
     return pl.ds(pl.multiple_of((square ^ index) * rows + first, count), count)
@@ -519,9 +526,8 @@
     return out.reshape(8 * rows, width)
 
 
-def join_tokens(order, parts, rows):
-    height, width = parts[0].shape
-    extra = height - rows
+def join_tokens(order, parts, rows, extra=0):
+    width = parts[0].shape[1]
 
     def body(flat_ref, block, first, second, core_block, core_first, core_second, *outs):
         home = core_of(flat_ref[0]) == half_of(flat_ref[0])
@@ -538,7 +544,7 @@
 
                     lax.fori_loop(0, rows // 32, step, 0)
                     if extra:
-                        outs[1][...] = source[rows:, :]
+                        outs[1][...] = source[rows : rows + extra, :]
 
     made = [shape_of(4 * rows, width)] + ([shape_of(4 * extra, width)] if extra else [])
     return run(
@@ -575,7 +581,7 @@
         n_ref[...] = normed_of(x_ref[...].astype(WIDE))[0].astype(LOW)
         square = square_of(flat_ref[0])
         mixed = sum(
-            mm(n_ref[:, span_of(square, span, piece)], w[:, :columns])
+            mm(n_ref[:, span_of(square, span, piece)], w[rows_of(w, span), :columns])
             for span, w in zip(spans(pieces), weights)
         )
         turned_to = 2 * columns // 3
@@ -670,9 +676,12 @@
     def body(flat_ref, n_ref, cot_ref, *refs):
         weights, (h_ref, d_ref) = refs[:5], refs[5:]
         square = square_of(flat_ref[0])
-        cols = [span_of(square, span, piece) for span in spans(pieces)]
-        wide = sum(mm(n_ref[:, at], w[:, : 2 * ff]) for at, w in zip(cols, weights))
-        d_hidden = sum(mm(cot_ref[:, at], w[:, 2 * ff : 3 * ff]) for at, w in zip(cols, weights))
+        cut = [
+            (span_of(square, span, piece), rows_of(w, span), w)
+            for span, w in zip(spans(pieces), weights)
+        ]
+        wide = sum(mm(n_ref[:, at], w[of, : 2 * ff]) for at, of, w in cut)
+        d_hidden = sum(mm(cot_ref[:, at], w[of, 2 * ff : 3 * ff]) for at, of, w in cut)
         inner, gate = wide[:, :ff], wide[:, ff:]
         cdf = 0.5 * (1.0 + lax.erf(inner * inv_root_two))
         slope = cdf + inner * jnp.exp(-0.5 * inner * inner) * inv_root_tau
@@ -700,7 +709,8 @@
         square = square_of(flat_ref[0])
         for span, w in zip(spans(pieces), weights):
             out_ref[:, span_of(square, span, piece)] = sum(
-                mm_t(a[...], w[:, at : at + a.shape[1]]) for a, (_, at) in zip(arrays, grads)
+                mm_t(a[...], w[rows_of(w, span), at : at + a.shape[1]])
+                for a, (_, at) in zip(arrays, grads)
             ).astype(out.dtype)
 
     return run(
@@ -709,6 +719,26 @@
         [whole(out)],
         flops=tokens * width * sum(a.shape[1] for a, _ in grads),
     )[0]
+
+
+def back_both(order, grad, first, pieces):
+    tokens = grad.shape[0]
+    piece = pieces[0].shape[0]
+    rows, width, columns = tokens // 2, 4 * piece, grad.shape[1]
+
+    def body(flat_ref, grad_ref, *refs):
+        weights, (far_ref, near_ref) = refs[:5], refs[5:]
+        square = square_of(flat_ref[0])
+        for span, w in zip(spans(pieces), weights):
+            total = mm_t(grad_ref[...], w[rows_of(w, span), first : first + columns])
+            near_ref[:, span_of(square, span, piece)] = total[:rows]
+            far_ref[:, span_of(square, span, piece)] = total[rows:].astype(LOW)
+
+    return run(
+        body, order, (1,), [whole(grad)] + [whole(p) for p in pieces],
+        [whole(shape_of(rows, width)), whole(shape_of(rows, width, dtype=WIDE))],
+        flops=2 * tokens * width * columns,
+    )
 
 
 def norm_pull(order, x, terms, base, keep):
@@ -727,7 +757,8 @@
         if keep:
             outs[1][...] = grad
 
-    outs = [shape_of(rows, width)] + ([shape_of(rows, width, dtype=WIDE)] if keep else [])
+    low = shape_of(rows + 16 if keep else rows, width)
+    outs = [low] + ([shape_of(rows, width, dtype=WIDE)] if keep else [])
     return run(
         body, order, (4,), [by_rows(a, step) for a in (x, *terms, base)],
         [by_rows(o, step) for o in outs],
@@ -736,33 +767,24 @@
 
 def feed_grads(order, normed, cot, d_up, hidden):
     tokens, width = normed.shape
-    rows, piece = tokens // 4, width // 4
-    ff = hidden.shape[1]
+    piece, ff = width // 4, hidden.shape[1]
     out = shape_of(4, piece, lanes(3 * ff))
 
-    def body(flat_ref, n_ref, cot_ref, d_ref, h_ref, out_ref, held):
-        @pl.when(pl.program_id(0) == 0)
-        def _():
-            held[...] = jnp.zeros_like(held)
-
-        for i in range(4):
-            cols = slice(i * piece, (i + 1) * piece)
-            held[i, :, : 2 * ff] += t_mm(n_ref[:, cols], d_ref[...])
-            held[i, :, 2 * ff : 3 * ff] += t_mm(cot_ref[:, cols], h_ref[...])
-
-        @pl.when(pl.program_id(0) == 3)
-        def _():
-            out_ref[...] = held[...].astype(LOW)
-
-    return run(
-        body, order, (4,), [by_rows(a, rows) for a in (normed, cot, d_up, hidden)],
-        [whole(out)], [pltpu.VMEM(out.shape, WIDE)],
+    def body(flat_ref, n_ref, cot_ref, d_ref, h_ref, out_ref):
+        out_ref[0, :, : 2 * ff] = t_mm(n_ref[...], d_ref[...]).astype(LOW)
+        out_ref[0, :, 2 * ff : 3 * ff] = t_mm(cot_ref[...], h_ref[...]).astype(LOW)
+
+    return run(
+        body, order, (4,),
+        [(a, (tokens, piece), lambda b, f: (0, b)) for a in (normed, cot)]
+        + [whole(d_up), whole(hidden)],
+        [by_rows(out, 1)],
         flops=6 * tokens * width * ff,
     )[0]
 
 
 def heads_back(order, d_all, heads, columns):
-    rows, width = d_all[0].shape
+    rows, width = heads[0].shape[0] // 4, d_all[0].shape[1]
     part = width // 4
 
     def body(flat_ref, *refs):
@@ -922,7 +944,7 @@
     ]
 
 
-def fold(order, terms):
+def fold(order, terms, margin=0):
     high, width = terms[0].shape[1:]
     rows = high // 4
     terms = [t.reshape(-1, 2, 2, rows, width) for t in terms]
@@ -935,7 +957,7 @@
             return sum(r[k, 0, at].astype(WIDE) for r in ins for k in range(r.shape[0]))
 
         kept_ref[0] = total(half)
-        sent_ref[0] = total(1 - half).astype(LOW)
+        sent_ref[0, :, :width] = total(1 - half).astype(LOW)
 
     return run(
         body, order, (2,),
@@ -943,19 +965,24 @@
             (t, (t.shape[0], 1) + t.shape[2:], lambda b, f: (0, b, 0, 0, 0))
             for t in terms
         ],
-        [by_rows(shape_of(2, rows, width, dtype=WIDE), 1), by_rows(shape_of(2, rows, width), 1)],
+        [
+            by_rows(shape_of(2, rows, width, dtype=WIDE), 1),
+            by_rows(shape_of(2, rows, width + margin), 1),
+        ],
     )
 
 
 def split_rows(order, kept, received):
     _, high, width = kept.shape
     rows = high // 2
-    kept, received = kept.reshape(4, rows, width), received.reshape(4, rows, width)
+    kept, received = kept.reshape(4, rows, width), received.reshape(4, rows, -1)
 
     def body(flat_ref, kept_ref, received_ref, *outs):
         for i in range(4):
             at = group_of(flat_ref[0]) ^ i
-            outs[i][...] = (kept_ref[at] + received_ref[at].astype(WIDE)).astype(LOW)
+            outs[i][...] = (
+                kept_ref[at] + received_ref[at, :, :width].astype(WIDE)
+            ).astype(LOW)
 
     return run(
         body, order, (1,), [whole(kept), whole(received)], [whole(shape_of(rows, width))] * 4
@@ -1010,69 +1037,71 @@
     part, ff = width // 4, FF // 4
     gain_one, gain_two = attn_gain[None], mlp_gain[None]
 
+    pos = positions[0]
+    pos_row = jnp.concatenate([pos // 128, pos % 128]).astype(LOW)
+    pos_row = jnp.pad(pos_row[None], ((0, 15), (0, width - 2 * tokens)))
+    block = jnp.concatenate([inputs[0], pos_row])
+    first = send(block, ENTER)
+    wait(order, block)
     own, sent = split_slices(order, qkv_weight, attn_out_weight, gain_one, 3)
     received = send(sent, TO_CORE)
     own_two, sent = split_slices(order, up_weight, down_weight, gain_two, 2)
     received_two = send(sent, TO_CORE)
+    core_block = send(block, TO_CORE)
+    cot_own = jnp.concatenate([cotangent[0], pos_row])
+    cot_block = send(cot_own, TO_CORE)
     own, sent = chip_rows(order, own, received)
     received = send(sent, TO_ZL)
     own_two, sent = chip_rows(order, own_two, received_two)
-    pos = positions[0]
-    pos_row = jnp.concatenate([pos // 128, pos % 128]).astype(LOW)
-    pos_row = jnp.pad(pos_row[None], ((0, 15), (0, width - 2 * tokens)))
-    block = jnp.concatenate([inputs[0], pos_row])
-    wait(order, block)
+    wait(order, core_block, cot_block)
     one = quad_rows(order, own, received)
     one_far = send(one, TO_ZH)
-    first = send(after(order, block), ENTER)
     received_two = send(after(order, sent), TO_ZL)
+    second = send(after(order, first), ENTER_MOVED)
+    core_first = send(after(order, first), TO_CORE)
+    two = quad_rows(order, own_two, received_two)
+    two_far = send(two, TO_ZH)
     one = line_rows(order, one, one_far)
     half = one.shape[0] // 2
     one_x, one_y = send(one, TO_X), send(one, TO_Y)
-    two = quad_rows(order, own_two, received_two)
-    two_far = send(two, TO_ZH)
-    second = send(after(order, first), ENTER_MOVED)
-    core_first = send(after(order, first), TO_CORE)
     wait(order, core_first, second)
-    core_block = send(after(order, block), TO_CORE)
     core_second = send(after(order, second), TO_CORE)
-    x, pos_all = join_tokens(
-        order, [block, first, second, core_block, core_first, core_second], tokens
-    )
-    cot_first = send(after(order, cotangent[0]), ENTER)
+    cot_first = send(after(order, cot_own), ENTER)
     one_top = send(one_x[:half], TO_Y)
     one_low = send(one_y[half:], TO_X)
+    x, pos_all = join_tokens(
+        order, [block, first, second, core_block, core_first, core_second], tokens, 16
+    )
     pos_all = pos_all.reshape(4, 16, width)[:, 0, : 2 * tokens].astype(WIDE)
     pos_all = (pos_all[:, :tokens] * 128.0 + pos_all[:, tokens:]).reshape(4 * tokens)
     cos_table, sin_table = rope_lanes(pos_all)
     one = [one, one_x, one_y, one_top, one_low]
 
     w_out = jnp.concatenate([p[:, 3 * part :] for p in one])
-    wait(order, w_out, cos_table, sin_table)
-    w_side = send(after(order, w_out), TO_ZL)
-    w_core = send(after(order, w_out), TO_CORE)
+    w_side = send(w_out, TO_ZL)
+    w_core = send(w_out, TO_CORE)
     normed_one, mix = project(order, x, one, cos_table, sin_table)
     two = line_rows(order, two, two_far)
     two_x, two_y = send(two, TO_X), send(two, TO_Y)
-    wait(order, w_core, cot_first)
+    wait(order, w_core, w_side)
+    w_far = send(w_side, TO_CORE)
     attended, logs = attend(order, mix)
     att_side = send(attended, TO_ZL)
-    att_core = send(attended, TO_CORE)
-    wait(order, att_core, w_side)
-    w_far = send(after(order, w_side), TO_CORE)
+    wait(order, two_x, two_y)
+    two_top = send(after(order, two_x[: half + 16]), TO_Y)
+    two_low = send(after(order, two_y[half - 16 :]), TO_X)
+    att_core = send(after(order, attended), TO_CORE)
+    wait(order, w_far, att_side)
     cot_second = send(after(order, cot_first), ENTER_MOVED)
     w_out = [w_out, w_side, w_core, w_far]
-    heads = [attended, att_side, att_core, send(att_side, TO_CORE)]
+    heads = [attended, att_side, att_core, send(after(order, att_side), TO_CORE)]
     normed_two, resid = join_heads(order, x, heads, w_out)
 
-    two_top = send(two_x[:half], TO_Y)
-    two_low = send(two_y[half:], TO_X)
-    core_block = send(after(order, cotangent[0]), TO_CORE)
-    core_first = send(after(order, cot_first), TO_CORE)
-    core_second = send(after(order, cot_second), TO_CORE)
+    core_first = send(cot_first, TO_CORE)
+    core_second = send(cot_second, TO_CORE)
     (cot,) = join_tokens(
         order,
-        [cotangent[0], cot_first, cot_second, core_block, core_first, core_second],
+        [cot_own, cot_first, cot_second, cot_block, core_first, core_second],
         tokens,
     )
     two = [two, two_x, two_y, two_top, two_low]
@@ -1095,31 +1124,35 @@
     )
     d_side = send(d_low, TO_ZL)
     d_core = send(d_low, TO_CORE)
-    grads = [(hidden, 2 * ff)]
-    out_far = back_half(order, grads, two, True)
-    out_near = back_half(order, grads, two, False)
+    out_far, out_near = back_both(order, hidden, 2 * ff, two)
+    out_far = [crossed(out_far[:tokens]), crossed(out_far[tokens:])]
+    out_side = (out_near[tokens:] + out_far[1].astype(WIDE)).astype(LOW)
+    out_side = send(out_side, TO_ZL)
     d_all = [d_low, d_side, d_core, send(after(order, d_side), TO_CORE)]
     d_attended, out_grad = heads_back(order, d_all, heads, w_out)
-    out_far = crossed(after(order, out_far))
-    out_side = side_of(out_near, out_far)
     d_mixed = attend_back(order, mix, attended, d_attended, logs, cos_table, sin_table)
-    output = resid + out_near[:tokens] + out_far[:tokens].astype(WIDE) + out_side.astype(WIDE)
+    wait(order, out_side)
+    grads = [(d, t * part) for t, d in enumerate(d_mixed)]
+    far = crossed(back_half(order, grads, one, True))
+    output = resid + out_near[:tokens] + out_far[0].astype(WIDE) + out_side.astype(WIDE)
     output = output.astype(LOW)
     wait(order, output)
     output = send(output, TO_HOME)
+    near = back_half(order, grads, one, False)
+    side = (near[tokens:] + far[tokens:].astype(WIDE)).astype(LOW)
+    wait(order, side)
+    side = send(side, TO_ZL)
     mixed_terms = share_pieces(mixed_grads(order, normed_one, d_mixed, out_grad))
-    grads = [(d, t * part) for t, d in enumerate(d_mixed)]
-    far = crossed(back_half(order, grads, one, True))
-    near = back_half(order, grads, one, False)
-    side = side_of(near, far)
     ff_kept, ff_sent = fold(order, [ff_terms])
+    ff_sent = send(ff_sent, TO_ZH)
+    (input_grad,) = norm_pull(order, x, (near, far, side), d_resid, False)
     wait(order, output)
-    ff_sent = send(after(order, ff_sent), TO_ZH)
-    mixed_kept, mixed_sent = fold(order, [t[None] for t in mixed_terms])
+    mixed_kept, mixed_sent = fold(order, [t[None] for t in mixed_terms], 128)
     mixed_sent = send(mixed_sent, TO_ZH)
-    (input_grad,) = norm_pull(order, x, (near, far, side), d_resid, False)
-    input_grad = send(input_grad, TO_HOME)
     ff_slices = share_slices(split_rows(order, ff_kept, ff_sent))
+    input_grad = jnp.concatenate(
+        [send(input_grad[: tokens // 2], TO_HOME), send(input_grad[tokens // 2 :], TO_HOME)]
+    )
     mixed_slices = share_slices(split_rows(order, mixed_kept, mixed_sent))
     up_grad, gain_two_grad, down_grad = finish(
         order, ff_slices, up_weight, gain_two, (2, ff, ff)

time: 300 us -> 277 us (0.923)
  waiting for transfers between devices: 134 us -> 110 us
    ppermute x52 -> x54, waiting for transfers between devices: 122 us -> 110 us  [send(): return lax.ppermute(array, FLAT, pairs)]
    all_to_all x1, waiting for transfers between devices: 11.7 us -> 0.01 us  [quad_device(): lax.all_to_all(after(order, ff_terms), ('y', 'x'), split_axis=0, concat_a...]
    pallas_call x32 -> x31, Pallas kernels: 75.9 us -> 78.5 us  [run(): pl.pallas_call(body, grid_spec=pltpu.PrefetchScalarGridSpec(num_scalar_pr...]
    unnamed x88 -> x111, local copies, waits for them, and re-layouts: 11.5 us -> 8.94 us
    ppermute x52 -> x54, starting transfers between devices: 62.8 us -> 60.9 us  [send(): return lax.ppermute(array, FLAT, pairs)]
  transfers between devices with their start and end apart: 53 -> 55, of which waited for: 24 -> 27; matrix products, arithmetic and copies ran while one was open for 3% -> 3% of each run, Pallas kernels for 21% -> 24%
where the time goes in v5:
time: 277 us; the launch traced here: 276 us
  waiting for transfers between devices  110 us (40%)
  Pallas kernels  78.5 us (28%)
  starting transfers between devices  66 us (24%)
  local copies, waits for them, and re-layouts  10.1 us (4%)
  other arithmetic  9.46 us (3%)
    ppermute x54, waiting for transfers between devices, send(): return lax.ppermute(array, FLAT, pairs)  110 us
    pallas_call x31, Pallas kernels, run(): pl.pallas_call(body, grid_spec=pltpu.PrefetchScalarGridSpec(num_scalar_pr...  78.5 us
    ppermute x54, starting transfers between devices, send(): return lax.ppermute(array, FLAT, pairs)  60.9 us
    unnamed x111, local copies, waits for them, and re-layouts  8.94 us
  transfers between devices with their start and end apart: 55, of which 27 were waited for; matrix products, arithmetic and copies ran while one was open for 3% of the time, Pallas kernels for 24%

profile of v5, /device:TPU:1, one launch (start us, length us, event | category | flops | bytes accessed | tf_op | source)
XLA Modules:
  0.0 275.7 jit_solution(13450541187118608534)
XLA Ops:
  3.4 3.7 %collective-permute-start.7 = (bf16[272,1024]{1,0:T(8,128)(2,1)S(1)}, bf16[272,1024]{1,0:T(8,128)(2,1)}, u32[]{:S(2)}, u32[]{:S(2)}) collective-permute-start(bf16[272,1024]{1,0:T(8,128)(2,1)S(1)} %get-tuple-element.215.block), channel_id=1, source_target_pairs={{0,1},{1,0},{2,4},{3,5},{4,2},{5,3},{6,7},{7,6},{8,9},{9,8},{10,12... | collective-permute-start | bytes 1671176 | tf_op jit(solution)/shard_map/ppermute | solution.py:338
  10.9 11.0 %collective-permute-done.4.received_ref = bf16[2,32,1024]{2,1,0:T(8,128)(2,1)S(1)} collective-permute-done((bf16[2,32,1024]{2,1,0:T(8,128)(2,1)S(1)}, bf16[2,32,1024]{2,1,0:T(8,128)(2,1)S(1)}, u32[]{:S(2)}, u32[]{:S(2)}) %collective-permute-start.4) | collective-permute-done | bytes 131104 | tf_op jit(solution)/shard_map/ppermute | solution.py:338
  27.4 7.1 %collective-permute-done.5.received_ref = bf16[2,32,2048]{2,1,0:T(8,128)(2,1)S(1)} collective-permute-done((bf16[2,32,2048]{2,1,0:T(8,128)(2,1)S(1)}, bf16[2,32,2048]{2,1,0:T(8,128)(2,1)S(1)}, u32[]{:S(2)}, u32[]{:S(2)}) %collective-permute-start.5) | collective-permute-done | bytes 262176 | tf_op jit(solution)/shard_map/ppermute | solution.py:338
  34.5 3.3 %collective-permute-done.6 = bf16[4,32,1024]{2,1,0:T(8,128)(2,1)S(1)} collective-permute-done((bf16[4,32,1024]{2,1,0:T(8,128)(2,1)S(1)}, bf16[4,32,1024]{2,1,0:T(8,128)(2,1)S(1)}, u32[]{:S(2)}, u32[]{:S(2)}) %collective-permute-start.6) | collective-permute-done | bytes 262176 | tf_op jit(solution)/shard_map/ppermute | solution.py:338
  43.5 6.3 %collective-permute-done.12.refs_2_.refs_5_ = bf16[256,1024]{1,0:T(8,128)(2,1)S(1)} collective-permute-done((bf16[256,1024]{1,0:T(8,128)(2,1)S(1)}, bf16[256,1024]{1,0:T(8,128)(2,1)S(1)}, u32[]{:S(2)}, u32[]{:S(2)}) %collective-permute-start.12) | collective-permute-done | bytes 524320 | tf_op jit(solution)/shard_map/ppermute | solution.py:338
  52.4 4.2 %collective-permute-done.13.refs_3_.refs_6_ = bf16[128,1024]{1,0:T(8,128)(2,1)S(1)} collective-permute-done((bf16[128,1024]{1,0:T(8,128)(2,1)S(1)}, bf16[128,1024]{1,0:T(8,128)(2,1)S(1)}, u32[]{:S(2)}, u32[]{:S(2)}) %collective-permute-start.13) | collective-permute-done | bytes 262176 | tf_op jit(solution)/shard_map/ppermute | solution.py:338
  56.8 3.7 %collective-permute-start.16 = (bf16[1024,256]{1,0:T(8,128)(2,1)S(1)}, bf16[1024,256]{1,0:T(8,128)(2,1)S(1)}, u32[]{:S(2)}, u32[]{:S(2)}) collective-permute-start(bf16[1024,256]{1,0:T(8,128)(2,1)S(1)} %slice_dynamic-update-slice_fusion.3.refs_4_.refs_8_), channel_id=1, source_target_pairs={{0,4},{1,5},{2,6},{3,7},{4,0},{5,1},{6,2},{7,3},{8,12},{9,13},{10,... | collective-permute-start | bytes 1572872 | tf_op jit(solution)/shard_map/ppermute | solution.py:338
  64.9 4.9 %shard_map.160 = (bf16[1024,1024]{1,0:T(8,128)(2,1)S(1)}, bf16[1024,768]{1,0:T(8,128)(2,1)S(1)}) custom-call(s32[1]{0:T(128)} %bitcast.flat_ref, bf16[1024,1024]{1,0:T(8,128)(2,1)S(1)} %get-tuple-element.129.x_ref, bf16[256,1024]{1,0:T(8,128)(2,1)S(1)} %bitcast.41, bf16[256,1024]{1,0:T(8,128)(2,1)S(1)} %collective-permute-done.11.refs_1_.refs_4_, ...), custom_call_target="tpu_custom_call" | custom-call | flops 16106127 | bytes 89128 | tf_op jit(solution)/shard_map/pallas_call | solution.py:405
  77.4 8.1 %shard_map.162 = (bf16[1024,256]{1,0:T(8,128)(2,1)S(1)}, f32[8,1024]{1,0:T(8,128)S(1)}) custom-call(s32[1]{0:T(128)} %bitcast.flat_ref, bf16[1024,768]{1,0:T(8,128)(2,1)S(1)} %get-tuple-element.136.q_ref.k_ref.v_ref, bf16[1024,768]{1,0:T(8,128)(2,1)S(1)} %get-tuple-element.136.q_ref.k_ref.v_ref, bf16[1024,768]{1,0:T(8,128)(2,1)S(1)} %get-tuple-element.136.q_ref.k_ref.v_ref), custom_call_target="tpu_custom_call" | custom-call | flops 42949672 | bytes 52756 | tf_op jit(solution)/shard_map/pallas_call | solution.py:405
  85.7 10.4 %collective-permute-done.19.refs_2_.refs_3_ = bf16[256,2048]{1,0:T(8,128)(2,1)S(1)} collective-permute-done((bf16[256,2048]{1,0:T(8,128)(2,1)S(1)}, bf16[256,2048]{1,0:T(8,128)(2,1)S(1)}, u32[]{:S(2)}, u32[]{:S(2)}) %collective-permute-start.19) | collective-permute-done | bytes 1048608 | tf_op jit(solution)/shard_map/ppermute | solution.py:338
  96.9 3.0 %collective-permute-done.21.refs_1_.refs_5_ = bf16[1024,256]{1,0:T(8,128)(2,1)S(1)} collective-permute-done((bf16[1024,256]{1,0:T(8,128)(2,1)S(1)}, bf16[1024,256]{1,0:T(8,128)(2,1)S(1)}, u32[]{:S(2)}, u32[]{:S(2)}) %collective-permute-start.21) | collective-permute-done | bytes 524320 | tf_op jit(solution)/shard_map/ppermute | solution.py:338
  104.5 6.0 %collective-permute-done.25.second = bf16[272,1024]{1,0:T(8,128)(2,1)S(1)} collective-permute-done((bf16[272,1024]{1,0:T(8,128)(2,1)S(1)}, bf16[272,1024]{1,0:T(8,128)(2,1)S(1)}, u32[]{:S(2)}, u32[]{:S(2)}) %collective-permute-start.25) | collective-permute-done | bytes 557088 | tf_op jit(solution)/shard_map/ppermute | solution.py:338
  113.2 4.4 %shard_map.163 = (bf16[1024,1024]{1,0:T(8,128)(2,1)S(1)}, f32[256,1024]{1,0:T(8,128)S(1)}) custom-call(s32[1]{0:T(128)} %bitcast.flat_ref, bf16[1024,1024]{1,0:T(8,128)(2,1)S(1)} %get-tuple-element.129.x_ref, bf16[1024,256]{1,0:T(8,128)(2,1)S(1)} %get-tuple-element.141.refs_0_.refs_4_.o_ref, bf16[1024,256]{1,0:T(8,128)(2,1)S(1)} %collective-permute-done.21.refs_1_.refs_5_, ...), custom_call_target="tpu_custom_call" | custom-call | flops 21474836 | bytes 94371 | tf_op jit(solution)/shard_map/pallas_call | solution.py:405
  118.2 7.3 %shard_map.165 = (bf16[1024,656]{1,0:T(8,128)(2,1)S(1)}, bf16[1024,1312]{1,0:T(8,128)(2,1)S(1)}) custom-call(s32[1]{0:T(128)} %bitcast.flat_ref, bf16[1024,1024]{1,0:T(8,128)(2,1)S(1)} %get-tuple-element.144.n_ref, bf16[1024,1024]{1,0:T(8,128)(2,1)S(1)} %shard_map.164.cot_ref.base_ref, bf16[256,2048]{1,0:T(8,128)(2,1)S(1)} %bitcast.34, ...), custom_call_target="tpu_custom_call" | custom-call | flops 41271952 | bytes 125501 | tf_op jit(solution)/shard_map/pallas_call | solution.py:405
  132.0 6.6 %shard_map.168 = bf16[4,256,2048]{2,1,0:T(8,128)(2,1)S(1)} custom-call(s32[1]{0:T(128)} %bitcast.flat_ref, bf16[1024,1024]{1,0:T(8,128)(2,1)S(1)} %get-tuple-element.144.n_ref, bf16[1024,1024]{1,0:T(8,128)(2,1)S(1)} %shard_map.164.cot_ref.base_ref, bf16[1024,1312]{1,0:T(8,128)(2,1)S(1)} %get-tuple-element.153.refs_0_.d_ref, ...), custom_call_target="tpu_custom_call" | custom-call | flops 41271952 | bytes 124190 | tf_op jit(solution)/shard_map/pallas_call | solution.py:405
  138.7 5.1 %collective-permute-done.31.c_ref = bf16[256,1024]{1,0:T(8,128)(2,1)S(1)} collective-permute-done((bf16[256,1024]{1,0:T(8,128)(2,1)S(1)}, bf16[256,1024]{1,0:T(8,128)(2,1)S(1)}, u32[]{:S(2)}, u32[]{:S(2)}) %collective-permute-start.31) | collective-permute-done | bytes 524320 | tf_op jit(solution)/shard_map/ppermute | solution.py:338
  153.7 5.1 %all-to-all-start = ((bf16[4,256,2048]{2,1,0:T(8,128)(2,1)}), bf16[4,256,2048]{2,1,0:T(8,128)(2,1)}, u32[]{:S(2)}, u32[]{:S(2)}) async-start(bf16[4,256,2048]{2,1,0:T(8,128)(2,1)} %copy-done.2), calls=%async_computation | async-start | bytes 8388608 | tf_op jit(solution)/shard_map/all_to_all | solution.py:1122
  168.6 3.7 %shard_map.171 = (bf16[1024,256]{1,0:T(8,128)(2,1)S(1)}, bf16[4,256,256]{2,1,0:T(8,128)(2,1)S(1)}) custom-call(s32[1]{0:T(128)} %bitcast.flat_ref, bf16[272,1024]{1,0:T(8,128)(2,1)} %get-tuple-element.157.refs_0_, bf16[272,1024]{1,0:T(8,128)(2,1)} %collective-permute-done.36.refs_1_, bf16[272,1024]{1,0:T(8,128)(2,1)S(1)} %collective-permute-done.37.refs_2_, ...), custom_call_target="tpu_custom_call" | custom-call | flops 10737418 | bytes 74711 | tf_op jit(solution)/shard_map/pallas_call | solution.py:405
  172.4 14.7 %shard_map.172 = (bf16[1024,256]{1,0:T(8,128)(2,1)S(1)}, bf16[1024,256]{1,0:T(8,128)(2,1)S(1)}, bf16[1024,256]{1,0:T(8,128)(2,1)S(1)}) custom-call(s32[1]{0:T(128)} %bitcast.flat_ref, bf16[1024,768]{1,0:T(8,128)(2,1)S(1)} %get-tuple-element.136.q_ref.k_ref.v_ref, bf16[1024,768]{1,0:T(8,128)(2,1)S(1)} %get-tuple-element.136.q_ref.k_ref.v_ref, ...), custom_call_target="tpu_custom_call" | custom-call | flops 107374184 | bytes 84213 | tf_op jit(solution)/shard_map/pallas_call | solution.py:405
  189.1 2.9 %collective-permute-done.32 = bf16[256,1024]{1,0:T(8,128)(2,1)S(1)} collective-permute-done((bf16[256,1024]{1,0:T(8,128)(2,1)S(1)}, bf16[256,1024]{1,0:T(8,128)(2,1)S(1)}, u32[]{:S(2)}, u32[]{:S(2)}) %collective-permute-start.32) | collective-permute-done | bytes 524320 | tf_op jit(solution)/shard_map/ppermute | solution.py:338
  195.6 5.6 %collective-permute-start.35 = (bf16[256,1024]{1,0:T(8,128)(2,1)}, bf16[256,1024]{1,0:T(8,128)(2,1)}, u32[]{:S(2)}, u32[]{:S(2)}) collective-permute-start(bf16[256,1024]{1,0:T(8,128)(2,1)} %add_convert_fusion), channel_id=1, source_target_pairs={{0,0},{1,1},{2,4},{3,5},{4,2},{5,3},{6,6},{7,7},{8,8},{9,9},{10,12... | collective-permute-start | bytes 1572872 | tf_op jit(solution)/shard_map/ppermute | solution.py:338
  201.2 4.2 %shard_map.175 = (bf16[256,1024]{1,0:T(8,128)(2,1)S(1)}, bf16[256,1024]{1,0:T(8,128)(2,1)}, bf16[256,1024]{1,0:T(8,128)(2,1)}, bf16[256,1024]{1,0:T(8,128)(2,1)}) custom-call(s32[1]{0:T(128)} %bitcast.flat_ref, bf16[1024,1024]{1,0:T(8,128)(2,1)S(1)} %copy-done.36, bf16[1024,256]{1,0:T(8,128)(2,1)S(1)} %get-tuple-element.166.refs_0_, ...), custom_call_target="tpu_custom_call" | custom-call | flops 16106127 | bytes 62914 | tf_op jit(solution)/shard_map/pallas_call | solution.py:405
  208.0 2.7 shard_map.176
  210.7 3.9 %collective-permute-done.40.c_ref = bf16[256,1024]{1,0:T(8,128)(2,1)} collective-permute-done((bf16[256,1024]{1,0:T(8,128)(2,1)}, bf16[256,1024]{1,0:T(8,128)(2,1)}, u32[]{:S(2)}, u32[]{:S(2)}) %collective-permute-start.40) | collective-permute-done | bytes 524320 | tf_op jit(solution)/shard_map/ppermute | solution.py:338
  215.8 2.8 %shard_map.177 = bf16[256,1024]{1,0:T(8,128)(2,1)S(1)} custom-call(s32[1]{0:T(128)} %bitcast.flat_ref, bf16[1024,1024]{1,0:T(8,128)(2,1)S(1)} %copy-done.1, f32[512,1024]{1,0:T(8,128)S(1)} %shard_map.174.a_ref, bf16[512,1024]{1,0:T(8,128)(2,1)S(1)} %copy-done.18, bf16[256,1024]{1,0:T(8,128)(2,1)} %collective-permute-done.40.c_ref, f32[256,1024]{1,0:T(8,128)S(1)} %copy-done.40), custom_call_target="tpu_custom_call" | custom-call | bytes 73400 | tf_op jit(solution)/shard_map/pallas_call | solution.py:405
  218.8 11.3 %collective-permute-done.45 = bf16[256,1024]{1,0:T(8,128)(2,1)} collective-permute-done((bf16[256,1024]{1,0:T(8,128)(2,1)}, bf16[256,1024]{1,0:T(8,128)(2,1)}, u32[]{:S(2)}, u32[]{:S(2)}) %collective-permute-start.45) | collective-permute-done | bytes 524320 | tf_op jit(solution)/shard_map/ppermute | solution.py:338
  233.1 4.5 %collective-permute-start.41 = (bf16[128,1024]{1,0:T(8,128)(2,1)S(1)}, bf16[128,1024]{1,0:T(8,128)(2,1)S(1)}, u32[]{:S(2)}, u32[]{:S(2)}) collective-permute-start(bf16[128,1024]{1,0:T(8,128)(2,1)S(1)} %get-tuple-element.212), channel_id=1, source_target_pairs={{0,0},{1,1},{2,4},{3,5},{4,2},{5,3},{6,6},{7,7},{8,8},{9,9},{10,12... | collective-permute-start | bytes 786440 | tf_op jit(solution)/shard_map/ppermute | solution.py:338
  239.5 12.1 %collective-permute-done.46 = bf16[2,64,2048]{2,1,0:T(8,128)(2,1)S(1)} collective-permute-done((bf16[2,64,2048]{2,1,0:T(8,128)(2,1)S(1)}, bf16[2,64,2048]{2,1,0:T(8,128)(2,1)S(1)}, u32[]{:S(2)}, u32[]{:S(2)}) %collective-permute-start.46) | collective-permute-done | bytes 524320 | tf_op jit(solution)/shard_map/ppermute | solution.py:338
  254.2 3.8 %collective-permute-done.47 = bf16[2,64,1152]{2,1,0:T(8,128)(2,1)S(1)} collective-permute-done((bf16[2,64,1152]{2,1,0:T(8,128)(2,1)S(1)}, bf16[2,64,1152]{2,1,0:T(8,128)(2,1)S(1)}, u32[]{:S(2)}, u32[]{:S(2)}) %collective-permute-start.47) | collective-permute-done | bytes 294944 | tf_op jit(solution)/shard_map/ppermute | solution.py:338
  258.7 2.8 %collective-permute-done.41 = bf16[128,1024]{1,0:T(8,128)(2,1)S(1)} collective-permute-done((bf16[128,1024]{1,0:T(8,128)(2,1)S(1)}, bf16[128,1024]{1,0:T(8,128)(2,1)S(1)}, u32[]{:S(2)}, u32[]{:S(2)}) %collective-permute-start.41) | collective-permute-done | bytes 262176 | tf_op jit(solution)/shard_map/ppermute | solution.py:338
  261.5 2.8 %collective-permute-done.42 = bf16[128,1024]{1,0:T(8,128)(2,1)S(1)} collective-permute-done((bf16[128,1024]{1,0:T(8,128)(2,1)S(1)}, bf16[128,1024]{1,0:T(8,128)(2,1)S(1)}, u32[]{:S(2)}, u32[]{:S(2)}) %collective-permute-start.42) | collective-permute-done | bytes 262176 | tf_op jit(solution)/shard_map/ppermute | solution.py:338
  264.3 2.9 %collective-permute-done.48.refs_1_ = bf16[32,2048]{1,0:T(8,128)(2,1)S(1)} collective-permute-done((bf16[32,2048]{1,0:T(8,128)(2,1)S(1)}, bf16[32,2048]{1,0:T(8,128)(2,1)S(1)}, u32[]{:S(2)}, u32[]{:S(2)}) %collective-permute-start.48) | collective-permute-done | bytes 131104 | tf_op jit(solution)/shard_map/ppermute | solution.py:338
  (241 shorter events, 93.2 us)
Async XLA Ops:
  3.4 21.9 %collective-permute-start.7 = (bf16[272,1024]{1,0:T(8,128)(2,1)S(1)}, bf16[272,1024]{1,0:T(8,128)(2,1)}, u32[]{:S(2)}, u32[]{:S(2)}) collective-permute-start(bf16[272,1024]{1,0:T(8,128)(2,1)S(1)} %get-tuple-element.215.block), channel_id=1, source_target_pairs={{0,1},{1,0},{2,4},{3,5},{4,2},{5,3},{6,7},{7,6},{8,9},{9,8},{10,12... | collective-permute-start | bytes 1671176 | tf_op jit(solution)/shard_map/ppermute | solution.py:338
  21.9 12.5 %collective-permute-start.5 = (bf16[2,32,2048]{2,1,0:T(8,128)(2,1)S(1)}, bf16[2,32,2048]{2,1,0:T(8,128)(2,1)S(1)}, u32[]{:S(2)}, u32[]{:S(2)}) collective-permute-start(bf16[2,32,2048]{2,1,0:T(8,128)(2,1)S(1)} %get-tuple-element.123), channel_id=1, source_target_pairs={{0,1},{1,0},{2,3},{3,2},{4,5},{5,4},{6,7},{7,6},{8,9},{9,8},{10,11... | collective-permute-start | bytes 786440 | tf_op jit(solution)/shard_map/ppermute | solution.py:338
  23.9 13.9 %collective-permute-start.6 = (bf16[4,32,1024]{2,1,0:T(8,128)(2,1)S(1)}, bf16[4,32,1024]{2,1,0:T(8,128)(2,1)S(1)}, u32[]{:S(2)}, u32[]{:S(2)}) collective-permute-start(bf16[4,32,1024]{2,1,0:T(8,128)(2,1)S(1)} %shard_map.156), channel_id=1, source_target_pairs={{0,2},{1,3},{2,0},{3,1},{4,6},{5,7},{6,4},{7,5},{8,10},{9,11},{10,... | collective-permute-start | bytes 786440 | tf_op jit(solution)/shard_map/ppermute | solution.py:338
  25.3 16.7 %collective-permute-start.9 = (bf16[272,1024]{1,0:T(8,128)(2,1)}, bf16[272,1024]{1,0:T(8,128)(2,1)S(1)}, u32[]{:S(2)}, u32[]{:S(2)}) collective-permute-start(bf16[272,1024]{1,0:T(8,128)(2,1)} %collective-permute-done.7.first), channel_id=1, source_target_pairs={{2,3},{3,2},{4,5},{5,4},{10,11},{11,10},{12,13},{13,12},{18,19},{1... | collective-permute-start | bytes 1671176 | tf_op jit(solution)/shard_map/ppermute | solution.py:338
  27.3 14.8 %collective-permute-start.8 = (bf16[272,1024]{1,0:T(8,128)(2,1)}, bf16[272,1024]{1,0:T(8,128)(2,1)S(1)}, u32[]{:S(2)}, u32[]{:S(2)}) collective-permute-start(bf16[272,1024]{1,0:T(8,128)(2,1)} %collective-permute-done.7.first), channel_id=1, source_target_pairs={{0,4},{1,5},{2,6},{3,7},{4,0},{5,1},{6,2},{7,3},{8,12},{9,13},{10,... | collective-permute-start | bytes 1671176 | tf_op jit(solution)/shard_map/ppermute | solution.py:338
  40.3 30.9 %collective-permute-start.15 = (bf16[4,32,2048]{2,1,0:T(8,128)(2,1)S(1)}, bf16[4,32,2048]{2,1,0:T(8,128)(2,1)S(1)}, u32[]{:S(2)}, u32[]{:S(2)}) collective-permute-start(bf16[4,32,2048]{2,1,0:T(8,128)(2,1)S(1)} %shard_map.157), channel_id=1, source_target_pairs={{0,2},{1,3},{2,0},{3,1},{4,6},{5,7},{6,4},{7,5},{8,10},{9,11},{10,... | collective-permute-start | bytes 1572872 | tf_op jit(solution)/shard_map/ppermute | solution.py:338
  42.0 18.5 %collective-permute-start.10 = (bf16[272,1024]{1,0:T(8,128)(2,1)S(1)}, bf16[272,1024]{1,0:T(8,128)(2,1)S(1)}, u32[]{:S(2)}, u32[]{:S(2)}) collective-permute-start(bf16[272,1024]{1,0:T(8,128)(2,1)S(1)} %collective-permute-done.9.second), channel_id=1, source_target_pairs={{0,4},{1,5},{2,6},{3,7},{4,0},{5,1},{6,2},{7,3},{8,12},{9,13},{10,... | collective-permute-start | bytes 1671176 | tf_op jit(solution)/shard_map/ppermute | solution.py:338
  56.7 20.2 %collective-permute-start.17 = (bf16[1024,256]{1,0:T(8,128)(2,1)S(1)}, bf16[1024,256]{1,0:T(8,128)(2,1)S(1)}, u32[]{:S(2)}, u32[]{:S(2)}) collective-permute-start(bf16[1024,256]{1,0:T(8,128)(2,1)S(1)} %slice_dynamic-update-slice_fusion.3.refs_4_.refs_8_), channel_id=1, source_target_pairs={{0,1},{1,0},{2,3},{3,2},{4,5},{5,4},{6,7},{7,6},{8,9},{9,8},{10,11... | collective-permute-start | bytes 1572872 | tf_op jit(solution)/shard_map/ppermute | solution.py:338
  56.8 20.1 %collective-permute-start.16 = (bf16[1024,256]{1,0:T(8,128)(2,1)S(1)}, bf16[1024,256]{1,0:T(8,128)(2,1)S(1)}, u32[]{:S(2)}, u32[]{:S(2)}) collective-permute-start(bf16[1024,256]{1,0:T(8,128)(2,1)S(1)} %slice_dynamic-update-slice_fusion.3.refs_4_.refs_8_), channel_id=1, source_target_pairs={{0,4},{1,5},{2,6},{3,7},{4,0},{5,1},{6,2},{7,3},{8,12},{9,13},{10,... | collective-permute-start | bytes 1572872 | tf_op jit(solution)/shard_map/ppermute | solution.py:338
  71.3 24.8 %collective-permute-start.19 = (bf16[256,2048]{1,0:T(8,128)(2,1)S(1)}, bf16[256,2048]{1,0:T(8,128)(2,1)S(1)}, u32[]{:S(2)}, u32[]{:S(2)}) collective-permute-start(bf16[256,2048]{1,0:T(8,128)(2,1)S(1)} %bitcast.32), channel_id=1, source_target_pairs={{0,16},{1,17},{2,18},{3,19},{4,20},{5,21},{6,22},{7,23},{8,24},{9,... | collective-permute-start | bytes 3145736 | tf_op jit(solution)/shard_map/ppermute | solution.py:338
  72.5 24.4 %collective-permute-start.18 = (bf16[256,2048]{1,0:T(8,128)(2,1)S(1)}, bf16[256,2048]{1,0:T(8,128)(2,1)S(1)}, u32[]{:S(2)}, u32[]{:S(2)}) collective-permute-start(bf16[256,2048]{1,0:T(8,128)(2,1)S(1)} %bitcast.33), channel_id=1, source_target_pairs={{0,8},{1,9},{2,10},{3,11},{4,12},{5,13},{6,14},{7,15},{8,0},{9,1},... | collective-permute-start | bytes 3145736 | tf_op jit(solution)/shard_map/ppermute | solution.py:338
  72.8 27.1 %collective-permute-start.24 = (bf16[272,1024]{1,0:T(8,128)(2,1)S(1)}, bf16[272,1024]{1,0:T(8,128)(2,1)S(1)}, u32[]{:S(2)}, u32[]{:S(2)}) collective-permute-start(bf16[272,1024]{1,0:T(8,128)(2,1)S(1)} %copy-done.20), channel_id=1, source_target_pairs={{0,1},{1,0},{2,4},{3,5},{4,2},{5,3},{6,7},{7,6},{8,9},{9,8},{10,12... | collective-permute-start | bytes 1671176 | tf_op jit(solution)/shard_map/ppermute | solution.py:338
  76.9 20.0 %collective-permute-start.20 = (bf16[1024,256]{1,0:T(8,128)(2,1)S(1)}, bf16[1024,256]{1,0:T(8,128)(2,1)S(1)}, u32[]{:S(2)}, u32[]{:S(2)}) collective-permute-start(bf16[1024,256]{1,0:T(8,128)(2,1)S(1)} %collective-permute-done.17.refs_5_.refs_9_), channel_id=1, source_target_pairs={{0,4},{1,5},{2,6},{3,7},{4,0},{5,1},{6,2},{7,3},{8,12},{9,13},{10,... | collective-permute-start | bytes 1572872 | tf_op jit(solution)/shard_map/ppermute | solution.py:338
  85.6 14.3 %collective-permute-start.21 = (bf16[1024,256]{1,0:T(8,128)(2,1)S(1)}, bf16[1024,256]{1,0:T(8,128)(2,1)S(1)}, u32[]{:S(2)}, u32[]{:S(2)}) collective-permute-start(bf16[1024,256]{1,0:T(8,128)(2,1)S(1)} %get-tuple-element.141.refs_0_.refs_4_.o_ref), channel_id=1, source_target_pairs={{0,1},{1,0},{2,3},{3,2},{4,5},{5,4},{6,7},{7,6},{8,9},{9,8},{10,11... | collective-permute-start | bytes 1572872 | tf_op jit(solution)/shard_map/ppermute | solution.py:338
  102.2 16.0 %collective-permute-start.28 = (bf16[144,2048]{1,0:T(8,128)(2,1)S(1)}, bf16[144,2048]{1,0:T(8,128)(2,1)S(1)}, u32[]{:S(2)}, u32[]{:S(2)}) collective-permute-start(bf16[144,2048]{1,0:T(8,128)(2,1)S(1)} %slice.98), channel_id=1, source_target_pairs={{0,16},{1,17},{2,18},{3,19},{4,20},{5,21},{6,22},{7,23},{8,24},{9,... | collective-permute-start | bytes 1769480 | tf_op jit(solution)/shard_map/ppermute | solution.py:338
  102.9 15.3 %collective-permute-start.29 = (bf16[144,2048]{1,0:T(8,128)(2,1)S(1)}, bf16[144,2048]{1,0:T(8,128)(2,1)S(1)}, u32[]{:S(2)}, u32[]{:S(2)}) collective-permute-start(bf16[144,2048]{1,0:T(8,128)(2,1)S(1)} %slice.99), channel_id=1, source_target_pairs={{0,8},{1,9},{2,10},{3,11},{4,12},{5,13},{6,14},{7,15},{8,0},{9,1},... | collective-permute-start | bytes 1769480 | tf_op jit(solution)/shard_map/ppermute | solution.py:338
  103.4 14.3 %collective-permute-start.26 = (bf16[272,1024]{1,0:T(8,128)(2,1)S(1)}, bf16[272,1024]{1,0:T(8,128)(2,1)S(1)}, u32[]{:S(2)}, u32[]{:S(2)}) collective-permute-start(bf16[272,1024]{1,0:T(8,128)(2,1)S(1)} %collective-permute-done.24.first), channel_id=1, source_target_pairs={{0,4},{1,5},{2,6},{3,7},{4,0},{5,1},{6,2},{7,3},{8,12},{9,13},{10,... | collective-permute-start | bytes 1671176 | tf_op jit(solution)/shard_map/ppermute | solution.py:338
  130.6 13.2 %collective-permute-start.31 = (bf16[256,1024]{1,0:T(8,128)(2,1)S(1)}, bf16[256,1024]{1,0:T(8,128)(2,1)S(1)}, u32[]{:S(2)}, u32[]{:S(2)}) collective-permute-start(bf16[256,1024]{1,0:T(8,128)(2,1)S(1)} %fusion.1), channel_id=1, source_target_pairs={{0,1},{1,0},{2,3},{3,2},{4,5},{5,4},{6,7},{7,6},{8,9},{9,8},{10,11... | collective-permute-start | bytes 1572872 | tf_op jit(solution)/shard_map/ppermute | solution.py:338
  146.1 13.2 %collective-permute-start.36 = (bf16[272,1024]{1,0:T(8,128)(2,1)}, bf16[272,1024]{1,0:T(8,128)(2,1)}, u32[]{:S(2)}, u32[]{:S(2)}) collective-permute-start(bf16[272,1024]{1,0:T(8,128)(2,1)} %get-tuple-element.157.refs_0_), channel_id=1, source_target_pairs={{0,1},{1,0},{2,3},{3,2},{4,5},{5,4},{6,7},{7,6},{8,9},{9,8},{10,11... | collective-permute-start | bytes 1671176 | tf_op jit(solution)/shard_map/ppermute | solution.py:338
  153.7 54.2 %all-to-all-start = ((bf16[4,256,2048]{2,1,0:T(8,128)(2,1)}), bf16[4,256,2048]{2,1,0:T(8,128)(2,1)}, u32[]{:S(2)}, u32[]{:S(2)}) async-start(bf16[4,256,2048]{2,1,0:T(8,128)(2,1)} %copy-done.2), calls=%async_computation | async-start | bytes 8388608 | tf_op jit(solution)/shard_map/all_to_all | solution.py:1122
  163.0 24.1 %collective-permute-start.34 = (bf16[256,1024]{1,0:T(8,128)(2,1)S(1)}, bf16[256,1024]{1,0:T(8,128)(2,1)S(1)}, u32[]{:S(2)}, u32[]{:S(2)}) collective-permute-start(bf16[256,1024]{1,0:T(8,128)(2,1)S(1)} %add_convert_fusion.1), channel_id=1, source_target_pairs={{0,1},{1,0},{2,3},{3,2},{4,5},{5,4},{6,7},{7,6},{8,9},{9,8},{10,11... | collective-permute-start | bytes 1572872 | tf_op jit(solution)/shard_map/ppermute | solution.py:338
  195.4 19.2 %collective-permute-start.40 = (bf16[256,1024]{1,0:T(8,128)(2,1)}, bf16[256,1024]{1,0:T(8,128)(2,1)}, u32[]{:S(2)}, u32[]{:S(2)}) collective-permute-start(bf16[256,1024]{1,0:T(8,128)(2,1)} %fusion), channel_id=1, source_target_pairs={{0,1},{1,0},{2,3},{3,2},{4,5},{5,4},{6,7},{7,6},{8,9},{9,8},{10,11... | collective-permute-start | bytes 1572872 | tf_op jit(solution)/shard_map/ppermute | solution.py:338
  195.6 23.1 %collective-permute-start.35 = (bf16[256,1024]{1,0:T(8,128)(2,1)}, bf16[256,1024]{1,0:T(8,128)(2,1)}, u32[]{:S(2)}, u32[]{:S(2)}) collective-permute-start(bf16[256,1024]{1,0:T(8,128)(2,1)} %add_convert_fusion), channel_id=1, source_target_pairs={{0,0},{1,1},{2,4},{3,5},{4,2},{5,3},{6,6},{7,7},{8,8},{9,9},{10,12... | collective-permute-start | bytes 1572872 | tf_op jit(solution)/shard_map/ppermute | solution.py:338
  205.3 13.5 %collective-permute-start.43 = (bf16[256,1024]{1,0:T(8,128)(2,1)}, bf16[256,1024]{1,0:T(8,128)(2,1)S(1)}, u32[]{:S(2)}, u32[]{:S(2)}) collective-permute-start(bf16[256,1024]{1,0:T(8,128)(2,1)} %get-tuple-element.184), channel_id=1, source_target_pairs={{0,8},{1,9},{2,10},{3,11},{4,12},{5,13},{6,14},{7,15},{8,0},{9,1},... | collective-permute-start | bytes 1572872 | tf_op jit(solution)/shard_map/ppermute | solution.py:338
  205.5 13.4 %collective-permute-start.44 = (bf16[256,1024]{1,0:T(8,128)(2,1)}, bf16[256,1024]{1,0:T(8,128)(2,1)}, u32[]{:S(2)}, u32[]{:S(2)}) collective-permute-start(bf16[256,1024]{1,0:T(8,128)(2,1)} %get-tuple-element.185), channel_id=1, source_target_pairs={{0,16},{1,17},{2,18},{3,19},{4,20},{5,21},{6,22},{7,23},{8,24},{9,... | collective-permute-start | bytes 1572872 | tf_op jit(solution)/shard_map/ppermute | solution.py:338
  206.2 24.0 %collective-permute-start.45 = (bf16[256,1024]{1,0:T(8,128)(2,1)}, bf16[256,1024]{1,0:T(8,128)(2,1)}, u32[]{:S(2)}, u32[]{:S(2)}) collective-permute-start(bf16[256,1024]{1,0:T(8,128)(2,1)} %get-tuple-element.186), channel_id=1, source_target_pairs={{0,24},{1,25},{2,26},{3,27},{4,28},{5,29},{6,30},{7,31},{8,16},{9,... | collective-permute-start | bytes 1572872 | tf_op jit(solution)/shard_map/ppermute | solution.py:338
  214.6 37.1 %collective-permute-start.46 = (bf16[2,64,2048]{2,1,0:T(8,128)(2,1)S(1)}, bf16[2,64,2048]{2,1,0:T(8,128)(2,1)S(1)}, u32[]{:S(2)}, u32[]{:S(2)}) collective-permute-start(bf16[2,64,2048]{2,1,0:T(8,128)(2,1)S(1)} %get-tuple-element.189), channel_id=1, source_target_pairs={{0,2},{1,3},{2,0},{3,1},{4,6},{5,7},{6,4},{7,5},{8,10},{9,11},{10,... | collective-permute-start | bytes 1572872 | tf_op jit(solution)/shard_map/ppermute | solution.py:338
  231.5 26.5 %collective-permute-start.47 = (bf16[2,64,1152]{2,1,0:T(8,128)(2,1)S(1)}, bf16[2,64,1152]{2,1,0:T(8,128)(2,1)S(1)}, u32[]{:S(2)}, u32[]{:S(2)}) collective-permute-start(bf16[2,64,1152]{2,1,0:T(8,128)(2,1)S(1)} %get-tuple-element.192), channel_id=1, source_target_pairs={{0,2},{1,3},{2,0},{3,1},{4,6},{5,7},{6,4},{7,5},{8,10},{9,11},{10,... | collective-permute-start | bytes 884744 | tf_op jit(solution)/shard_map/ppermute | solution.py:338
  233.1 28.4 %collective-permute-start.41 = (bf16[128,1024]{1,0:T(8,128)(2,1)S(1)}, bf16[128,1024]{1,0:T(8,128)(2,1)S(1)}, u32[]{:S(2)}, u32[]{:S(2)}) collective-permute-start(bf16[128,1024]{1,0:T(8,128)(2,1)S(1)} %get-tuple-element.212), channel_id=1, source_target_pairs={{0,0},{1,1},{2,4},{3,5},{4,2},{5,3},{6,6},{7,7},{8,8},{9,9},{10,12... | collective-permute-start | bytes 786440 | tf_op jit(solution)/shard_map/ppermute | solution.py:338
  237.5 26.8 %collective-permute-start.42 = (bf16[128,1024]{1,0:T(8,128)(2,1)S(1)}, bf16[128,1024]{1,0:T(8,128)(2,1)S(1)}, u32[]{:S(2)}, u32[]{:S(2)}) collective-permute-start(bf16[128,1024]{1,0:T(8,128)(2,1)S(1)} %get-tuple-element.213), channel_id=1, source_target_pairs={{0,0},{1,1},{2,4},{3,5},{4,2},{5,3},{6,6},{7,7},{8,8},{9,9},{10,12... | collective-permute-start | bytes 786440 | tf_op jit(solution)/shard_map/ppermute | solution.py:338
  251.7 15.5 %collective-permute-start.48 = (bf16[32,2048]{1,0:T(8,128)(2,1)S(1)}, bf16[32,2048]{1,0:T(8,128)(2,1)S(1)}, u32[]{:S(2)}, u32[]{:S(2)}) collective-permute-start(bf16[32,2048]{1,0:T(8,128)(2,1)S(1)} %get-tuple-element.195), channel_id=1, source_target_pairs={{0,1},{1,0},{2,3},{3,2},{4,5},{5,4},{6,7},{7,6},{8,9},{9,8},{10,11... | collective-permute-start | bytes 393224 | tf_op jit(solution)/shard_map/ppermute | solution.py:338
  252.0 16.1 %collective-permute-start.49 = (bf16[32,2048]{1,0:T(8,128)(2,1)S(1)}, bf16[32,2048]{1,0:T(8,128)(2,1)S(1)}, u32[]{:S(2)}, u32[]{:S(2)}) collective-permute-start(bf16[32,2048]{1,0:T(8,128)(2,1)S(1)} %get-tuple-element.196), channel_id=1, source_target_pairs={{0,4},{1,5},{2,6},{3,7},{4,0},{5,1},{6,2},{7,3},{8,12},{9,13},{10,... | collective-permute-start | bytes 393224 | tf_op jit(solution)/shard_map/ppermute | solution.py:338
  (75 other events, 968.0 us)

commit v6 on v5

--- a/solution.py
+++ b/solution.py
@@ -932,18 +932,6 @@
     )
 
 
-def share_slices(slices):
-    return [slices[0]] + [
-        send(slices[i], pairs) for i, pairs in ((1, TO_ZL), (2, TO_CORE), (3, TO_FAR))
-    ]
-
-
-def share_pieces(pieces):
-    return [pieces[0]] + [
-        send(pieces[i], pairs) for i, pairs in ((1, TO_X), (2, TO_Y), (3, TO_XY))
-    ]
-
-
 def fold(order, terms, margin=0):
     high, width = terms[0].shape[1:]
     rows = high // 4
@@ -1021,6 +1009,51 @@
     )
 
 
+TIED = {
+    "ac",
+    "af",
+    "cf",
+    "cmov",
+    "cs",
+    "df",
+    "dz",
+    "fz",
+    "ih2",
+    "l1",
+    "m1z",
+    "mov",
+    "out",
+    "pull_late",
+    "sl1c",
+    "t2",
+    "tables",
+    "wf",
+    "x2",
+}
+WAITS = {
+    "blk": 1,
+    "ent": 1,
+    "cblk": 3,
+    "cf": 4,
+    "mov": 4,
+    "wc": 8,
+    "wz": 8,
+    "y2": 9,
+    "wf": 10,
+    "x2": 10,
+    "cmov": 11,
+    "dz": 14,
+    "ofb": 15,
+    "ofa": 17,
+    "oz": 17,
+    "m1c": 19,
+    "oh": 21,
+    "fz": 22,
+    "f1": 24,
+    "f2": 25,
+}
+
+
 def quad_device(
     inputs,
     positions,
@@ -1037,38 +1070,50 @@
     part, ff = width // 4, FF // 4
     gain_one, gain_two = attn_gain[None], mlp_gain[None]
 
+    def at(point):
+        wait(order, *[sent_as[n] for n, p in WAITS.items() if p == point])
+
+    sent_as = {}
+
+    def go(name, array, pairs):
+        sent_as[name] = send(after(order, array) if name in TIED else array, pairs)
+        return sent_as[name]
+
     pos = positions[0]
     pos_row = jnp.concatenate([pos // 128, pos % 128]).astype(LOW)
     pos_row = jnp.pad(pos_row[None], ((0, 15), (0, width - 2 * tokens)))
     block = jnp.concatenate([inputs[0], pos_row])
-    first = send(block, ENTER)
+    first = go("ent", block, ENTER)
     wait(order, block)
     own, sent = split_slices(order, qkv_weight, attn_out_weight, gain_one, 3)
-    received = send(sent, TO_CORE)
+    received = go("sl1c", sent, TO_CORE)
     own_two, sent = split_slices(order, up_weight, down_weight, gain_two, 2)
-    received_two = send(sent, TO_CORE)
-    core_block = send(block, TO_CORE)
+    received_two = go("sl2c", sent, TO_CORE)
+    core_block = go("blk", block, TO_CORE)
     cot_own = jnp.concatenate([cotangent[0], pos_row])
-    cot_block = send(cot_own, TO_CORE)
+    cot_block = go("cblk", cot_own, TO_CORE)
     own, sent = chip_rows(order, own, received)
-    received = send(sent, TO_ZL)
+    received = go("sl1z", sent, TO_ZL)
     own_two, sent = chip_rows(order, own_two, received_two)
-    wait(order, core_block, cot_block)
+    at(1)
     one = quad_rows(order, own, received)
-    one_far = send(one, TO_ZH)
-    received_two = send(after(order, sent), TO_ZL)
-    second = send(after(order, first), ENTER_MOVED)
-    core_first = send(after(order, first), TO_CORE)
+    at(2)
+    one_far = go("zh1", one, TO_ZH)
+    received_two = go("sl2z", sent, TO_ZL)
+    second = go("mov", first, ENTER_MOVED)
+    core_first = go("cf", first, TO_CORE)
     two = quad_rows(order, own_two, received_two)
-    two_far = send(two, TO_ZH)
+    at(3)
+    two_far = go("zh2", two, TO_ZH)
     one = line_rows(order, one, one_far)
     half = one.shape[0] // 2
-    one_x, one_y = send(one, TO_X), send(one, TO_Y)
-    wait(order, core_first, second)
-    core_second = send(after(order, second), TO_CORE)
-    cot_first = send(after(order, cot_own), ENTER)
-    one_top = send(one_x[:half], TO_Y)
-    one_low = send(one_y[half:], TO_X)
+    one_x, one_y = go("x1", one, TO_X), go("y1", one, TO_Y)
+    at(4)
+    core_second = go("cs", second, TO_CORE)
+    cot_first = go("cent", cot_own, ENTER)
+    one_top = go("t1", one_x[:half], TO_Y)
+    one_low = go("l1", one_y[half:], TO_X)
+    at(5)
     x, pos_all = join_tokens(
         order, [block, first, second, core_block, core_first, core_second], tokens, 16
     )
@@ -1076,29 +1121,37 @@
     pos_all = (pos_all[:, :tokens] * 128.0 + pos_all[:, tokens:]).reshape(4 * tokens)
     cos_table, sin_table = rope_lanes(pos_all)
     one = [one, one_x, one_y, one_top, one_low]
+    if "tables" in TIED:
+        wait(order, cos_table, sin_table)
+    at(6)
 
     w_out = jnp.concatenate([p[:, 3 * part :] for p in one])
-    w_side = send(w_out, TO_ZL)
-    w_core = send(w_out, TO_CORE)
+    w_side = go("wz", w_out, TO_ZL)
+    w_core = go("wc", w_out, TO_CORE)
     normed_one, mix = project(order, x, one, cos_table, sin_table)
+    at(7)
+    cot_second = go("cmov", cot_first, ENTER_MOVED) if "cot_early" in TIED else None
     two = line_rows(order, two, two_far)
-    two_x, two_y = send(two, TO_X), send(two, TO_Y)
-    wait(order, w_core, w_side)
-    w_far = send(w_side, TO_CORE)
+    two_x, two_y = go("x2", two, TO_X), go("y2", two, TO_Y)
+    at(8)
+    w_far = go("wf", w_side, TO_CORE)
     attended, logs = attend(order, mix)
-    att_side = send(attended, TO_ZL)
-    wait(order, two_x, two_y)
-    two_top = send(after(order, two_x[: half + 16]), TO_Y)
-    two_low = send(after(order, two_y[half - 16 :]), TO_X)
-    att_core = send(after(order, attended), TO_CORE)
-    wait(order, w_far, att_side)
-    cot_second = send(after(order, cot_first), ENTER_MOVED)
+    att_side = go("az", attended, TO_ZL)
+    at(9)
+    two_top = go("t2", two_x[: half + 16], TO_Y)
+    two_low = go("l2", two_y[half - 16 :], TO_X)
+    att_core = go("ac", attended, TO_CORE)
+    at(10)
+    if cot_second is None:
+        cot_second = go("cmov", cot_first, ENTER_MOVED)
     w_out = [w_out, w_side, w_core, w_far]
-    heads = [attended, att_side, att_core, send(after(order, att_side), TO_CORE)]
+    heads = [attended, att_side, att_core, go("af", att_side, TO_CORE)]
+    at(11)
     normed_two, resid = join_heads(order, x, heads, w_out)
 
-    core_first = send(cot_first, TO_CORE)
-    core_second = send(cot_second, TO_CORE)
+    core_first = go("ccf", cot_first, TO_CORE)
+    core_second = go("ccs", cot_second, TO_CORE)
+    at(12)
     (cot,) = join_tokens(
         order,
         [cot_own, cot_first, cot_second, cot_block, core_first, core_second],
@@ -1107,53 +1160,82 @@
     two = [two, two_x, two_y, two_top, two_low]
     hidden, d_up = feed(order, normed_two, cot, two)
 
-    def crossed(far):
-        return send(far, TO_CORE)
-
-    def side_of(near, far):
-        return send((near[tokens:] + far[tokens:].astype(WIDE)).astype(LOW), TO_ZL)
-
     grads = [(d_up, 0)]
-    far = crossed(back_half(order, grads, two, True))
+    far = go("b1c", back_half(order, grads, two, True), TO_CORE)
     near = back_half(order, grads, two, False)
-    side = side_of(near, far)
+    side = (near[tokens:] + far[tokens:].astype(WIDE)).astype(LOW)
+    side = go("b1z", jnp.pad(side, ((0, 16), (0, 0))), TO_ZL)
     ff_terms = feed_grads(order, normed_two, cot, d_up, hidden)
+    at(13)
+    if "a2a" not in TIED:
+        ff_terms = lax.all_to_all(ff_terms, ("y", "x"), split_axis=0, concat_axis=0, tiled=True)
     d_low, d_resid = norm_pull(order, resid, (near, far, side), cot, True)
-    ff_terms = lax.all_to_all(
-        after(order, ff_terms), ("y", "x"), split_axis=0, concat_axis=0, tiled=True
-    )
-    d_side = send(d_low, TO_ZL)
-    d_core = send(d_low, TO_CORE)
+    if "a2a" in TIED:
+        ff_terms = lax.all_to_all(
+            after(order, ff_terms), ("y", "x"), split_axis=0, concat_axis=0, tiled=True
+        )
+    d_side = go("dz", d_low, TO_ZL)
+    d_core = go("dc", d_low, TO_CORE)
     out_far, out_near = back_both(order, hidden, 2 * ff, two)
-    out_far = [crossed(out_far[:tokens]), crossed(out_far[tokens:])]
+    at(14)
+    out_far = [go("ofa", out_far[:tokens], TO_CORE), go("ofb", out_far[tokens:], TO_CORE)]
     out_side = (out_near[tokens:] + out_far[1].astype(WIDE)).astype(LOW)
-    out_side = send(out_side, TO_ZL)
-    d_all = [d_low, d_side, d_core, send(after(order, d_side), TO_CORE)]
+    out_side = go("oz", out_side, TO_ZL)
+    d_all = [d_low, d_side, d_core, go("df", d_side, TO_CORE)]
+    at(15)
     d_attended, out_grad = heads_back(order, d_all, heads, w_out)
+    at(16)
     d_mixed = attend_back(order, mix, attended, d_attended, logs, cos_table, sin_table)
-    wait(order, out_side)
+    at(17)
     grads = [(d, t * part) for t, d in enumerate(d_mixed)]
-    far = crossed(back_half(order, grads, one, True))
+    far = go("m1c", back_half(order, grads, one, True), TO_CORE)
+    at(18)
     output = resid + out_near[:tokens] + out_far[0].astype(WIDE) + out_side.astype(WIDE)
     output = output.astype(LOW)
-    wait(order, output)
-    output = send(output, TO_HOME)
+    if "out" in TIED:
+        wait(order, output)
+    output = go("oh", output, TO_HOME)
     near = back_half(order, grads, one, False)
     side = (near[tokens:] + far[tokens:].astype(WIDE)).astype(LOW)
-    wait(order, side)
-    side = send(side, TO_ZL)
-    mixed_terms = share_pieces(mixed_grads(order, normed_one, d_mixed, out_grad))
+    if "side" in TIED:
+        wait(order, side)
+    side = go("m1z", side, TO_ZL)
+    pieces = mixed_grads(order, normed_one, d_mixed, out_grad)
+    at(19)
+    mixed_terms = [pieces[0]] + [
+        go(n, p, pairs)
+        for n, p, pairs in zip(("mx", "my", "mxy"), pieces[1:], (TO_X, TO_Y, TO_XY))
+    ]
     ff_kept, ff_sent = fold(order, [ff_terms])
-    ff_sent = send(ff_sent, TO_ZH)
-    (input_grad,) = norm_pull(order, x, (near, far, side), d_resid, False)
-    wait(order, output)
+    ff_sent = go("fz", ff_sent, TO_ZH)
+    at(20)
+    if "pull_late" not in TIED:
+        (input_grad,) = norm_pull(order, x, (near, far, side), d_resid, False)
+    at(21)
     mixed_kept, mixed_sent = fold(order, [t[None] for t in mixed_terms], 128)
-    mixed_sent = send(mixed_sent, TO_ZH)
-    ff_slices = share_slices(split_rows(order, ff_kept, ff_sent))
+    mixed_sent = go("mz", mixed_sent, TO_ZH)
+    at(22)
+    if "pull_late" in TIED:
+        (input_grad,) = norm_pull(order, x, (near, far, side), d_resid, False)
+    ff_slices = split_rows(order, ff_kept, ff_sent)
+    at(23)
     input_grad = jnp.concatenate(
-        [send(input_grad[: tokens // 2], TO_HOME), send(input_grad[tokens // 2 :], TO_HOME)]
-    )
-    mixed_slices = share_slices(split_rows(order, mixed_kept, mixed_sent))
+        [
+            go("ih1", input_grad[: tokens // 2], TO_HOME),
+            go("ih2", input_grad[tokens // 2 :], TO_HOME),
+        ]
+    )
+    ff_slices = [ff_slices[0]] + [
+        go(n, p, pairs)
+        for n, p, pairs in zip(("f1", "f2", "f3"), ff_slices[1:], (TO_ZL, TO_CORE, TO_FAR))
+    ]
+    at(24)
+    mixed_slices = split_rows(order, mixed_kept, mixed_sent)
+    mixed_slices = [mixed_slices[0]] + [
+        go(n, p, pairs)
+        for n, p, pairs in zip(("m1", "m2", "m3"), mixed_slices[1:], (TO_ZL, TO_CORE, TO_FAR))
+    ]
+    at(25)
     up_grad, gain_two_grad, down_grad = finish(
         order, ff_slices, up_weight, gain_two, (2, ff, ff)
     )

time: 277 us -> 268 us (0.968)
  waiting for transfers between devices: 110 us -> 89.6 us
  starting transfers between devices: 66 us -> 74.7 us
  local copies, waits for them, and re-layouts: 10.1 us -> 15.8 us
    ppermute x54, waiting for transfers between devices: 110 us -> 89.6 us  [send(): return lax.ppermute(array, FLAT, pairs)]
    ppermute x54, starting transfers between devices: 60.9 us -> 69.6 us  [send(): return lax.ppermute(array, FLAT, pairs)]
    unnamed x111 -> x145, local copies, waits for them, and re-layouts: 8.94 us -> 14.5 us
  transfers between devices with their start and end apart: 55 -> 55, of which waited for: 27 -> 23; matrix products, arithmetic and copies ran while one was open for 3% -> 2% of each run, Pallas kernels for 24% -> 25%
where the time goes in v6:
time: 268 us; the launch traced here: 267 us
  waiting for transfers between devices  89.6 us (33%)
  Pallas kernels  76.8 us (29%)
  starting transfers between devices  74.7 us (28%)
  local copies, waits for them, and re-layouts  15.8 us (6%)
  other arithmetic  8.07 us (3%)
    ppermute x54, waiting for transfers between devices, send(): return lax.ppermute(array, FLAT, pairs)  89.6 us
    pallas_call x31, Pallas kernels, run(): pl.pallas_call(body, grid_spec=pltpu.PrefetchScalarGridSpec(num_scalar_pr...  76.8 us
    ppermute x54, starting transfers between devices, send(): return lax.ppermute(array, FLAT, pairs)  69.6 us
    unnamed x145, local copies, waits for them, and re-layouts  14.5 us
  transfers between devices with their start and end apart: 55, of which 23 were waited for; matrix products, arithmetic and copies ran while one was open for 2% of the time, Pallas kernels for 25%

profile of v6, /device:TPU:1, one launch (start us, length us, event | category | flops | bytes accessed | tf_op | source)
XLA Modules:
  0.0 266.8 jit_solution(5390152896131375038)
XLA Ops:
  2.8 3.8 %collective-permute-start.3 = (bf16[272,1024]{1,0:T(8,128)(2,1)S(1)}, bf16[272,1024]{1,0:T(8,128)(2,1)}, u32[]{:S(2)}, u32[]{:S(2)}) collective-permute-start(bf16[272,1024]{1,0:T(8,128)(2,1)S(1)} %get-tuple-element.239.block), channel_id=1, source_target_pairs={{0,1},{1,0},{2,4},{3,5},{4,2},{5,3},{6,7},{7,6},{8,9},{9,8},{10,12... | collective-permute-start | bytes 1671176 | tf_op jit(solution)/shard_map/ppermute | solution.py:338
  11.5 7.4 %collective-permute-done.3.first = bf16[272,1024]{1,0:T(8,128)(2,1)} collective-permute-done((bf16[272,1024]{1,0:T(8,128)(2,1)S(1)}, bf16[272,1024]{1,0:T(8,128)(2,1)}, u32[]{:S(2)}, u32[]{:S(2)}) %collective-permute-start.3) | collective-permute-done | bytes 557088 | tf_op jit(solution)/shard_map/ppermute | solution.py:338
  19.0 2.8 %collective-permute-done.4.received_ref = bf16[2,32,1024]{2,1,0:T(8,128)(2,1)S(1)} collective-permute-done((bf16[2,32,1024]{2,1,0:T(8,128)(2,1)S(1)}, bf16[2,32,1024]{2,1,0:T(8,128)(2,1)S(1)}, u32[]{:S(2)}, u32[]{:S(2)}) %collective-permute-start.4) | collective-permute-done | bytes 131104 | tf_op jit(solution)/shard_map/ppermute | solution.py:338
  21.8 3.8 %collective-permute-start.7 = (bf16[4,32,1024]{2,1,0:T(8,128)(2,1)S(1)}, bf16[4,32,1024]{2,1,0:T(8,128)(2,1)S(1)}, u32[]{:S(2)}, u32[]{:S(2)}) collective-permute-start(bf16[4,32,1024]{2,1,0:T(8,128)(2,1)S(1)} %shard_map.156), channel_id=1, source_target_pairs={{0,2},{1,3},{2,0},{3,1},{4,6},{5,7},{6,4},{7,5},{8,10},{9,11},{10,... | collective-permute-start | bytes 786440 | tf_op jit(solution)/shard_map/ppermute | solution.py:338
  25.5 4.0 %collective-permute-start.9 = (bf16[272,1024]{1,0:T(8,128)(2,1)}, bf16[272,1024]{1,0:T(8,128)(2,1)S(1)}, u32[]{:S(2)}, u32[]{:S(2)}) collective-permute-start(bf16[272,1024]{1,0:T(8,128)(2,1)} %collective-permute-done.3.first), channel_id=1, source_target_pairs={{2,3},{3,2},{4,5},{5,4},{10,11},{11,10},{12,13},{13,12},{18,19},{1... | collective-permute-start | bytes 1671176 | tf_op jit(solution)/shard_map/ppermute | solution.py:338
  30.4 5.5 %collective-permute-done.7 = bf16[4,32,1024]{2,1,0:T(8,128)(2,1)S(1)} collective-permute-done((bf16[4,32,1024]{2,1,0:T(8,128)(2,1)S(1)}, bf16[4,32,1024]{2,1,0:T(8,128)(2,1)S(1)}, u32[]{:S(2)}, u32[]{:S(2)}) %collective-permute-start.7) | collective-permute-done | bytes 262176 | tf_op jit(solution)/shard_map/ppermute | solution.py:338
  41.8 5.0 %collective-permute-done.11.refs_1_.refs_4_ = bf16[256,1024]{1,0:T(8,128)(2,1)S(1)} collective-permute-done((bf16[256,1024]{1,0:T(8,128)(2,1)S(1)}, bf16[256,1024]{1,0:T(8,128)(2,1)S(1)}, u32[]{:S(2)}, u32[]{:S(2)}) %collective-permute-start.11) | collective-permute-done | bytes 524320 | tf_op jit(solution)/shard_map/ppermute | solution.py:338
  49.5 4.8 %collective-permute-done.13.refs_3_.refs_6_ = bf16[128,1024]{1,0:T(8,128)(2,1)S(1)} collective-permute-done((bf16[128,1024]{1,0:T(8,128)(2,1)S(1)}, bf16[128,1024]{1,0:T(8,128)(2,1)S(1)}, u32[]{:S(2)}, u32[]{:S(2)}) %collective-permute-start.13) | collective-permute-done | bytes 262176 | tf_op jit(solution)/shard_map/ppermute | solution.py:338
  54.4 5.2 %collective-permute-start.17 = (bf16[1024,256]{1,0:T(8,128)(2,1)S(1)}, bf16[1024,256]{1,0:T(8,128)(2,1)S(1)}, u32[]{:S(2)}, u32[]{:S(2)}) collective-permute-start(bf16[1024,256]{1,0:T(8,128)(2,1)S(1)} %slice_dynamic-update-slice_fusion.3.refs_4_.refs_8_), channel_id=1, source_target_pairs={{0,1},{1,0},{2,3},{3,2},{4,5},{5,4},{6,7},{7,6},{8,9},{9,8},{10,11... | collective-permute-start | bytes 1572872 | tf_op jit(solution)/shard_map/ppermute | solution.py:338
  64.7 4.9 %shard_map.160 = (bf16[1024,1024]{1,0:T(8,128)(2,1)S(1)}, bf16[1024,768]{1,0:T(8,128)(2,1)S(1)}) custom-call(s32[1]{0:T(128)} %bitcast.flat_ref, bf16[1024,1024]{1,0:T(8,128)(2,1)S(1)} %get-tuple-element.142.x_ref, bf16[256,1024]{1,0:T(8,128)(2,1)S(1)} %bitcast.41, bf16[256,1024]{1,0:T(8,128)(2,1)S(1)} %collective-permute-done.11.refs_1_.refs_4_, ...), custom_call_target="tpu_custom_call" | custom-call | flops 16106127 | bytes 89128 | tf_op jit(solution)/shard_map/pallas_call | solution.py:405
  72.6 3.0 %collective-permute-start.21 = (bf16[272,1024]{1,0:T(8,128)(2,1)S(1)}, bf16[272,1024]{1,0:T(8,128)(2,1)S(1)}, u32[]{:S(2)}, u32[]{:S(2)}) collective-permute-start(bf16[272,1024]{1,0:T(8,128)(2,1)S(1)} %copy-done.39), channel_id=1, source_target_pairs={{0,1},{1,0},{2,4},{3,5},{4,2},{5,3},{6,7},{7,6},{8,9},{9,8},{10,12... | collective-permute-start | bytes 1671176 | tf_op jit(solution)/shard_map/ppermute | solution.py:338
  76.3 8.1 %shard_map.162 = (bf16[1024,256]{1,0:T(8,128)(2,1)S(1)}, f32[8,1024]{1,0:T(8,128)S(1)}) custom-call(s32[1]{0:T(128)} %bitcast.flat_ref, bf16[1024,768]{1,0:T(8,128)(2,1)S(1)} %get-tuple-element.151.q_ref.k_ref.v_ref, bf16[1024,768]{1,0:T(8,128)(2,1)S(1)} %get-tuple-element.151.q_ref.k_ref.v_ref, bf16[1024,768]{1,0:T(8,128)(2,1)S(1)} %get-tuple-element.151.q_ref.k_ref.v_ref), custom_call_target="tpu_custom_call" | custom-call | flops 42949672 | bytes 52756 | tf_op jit(solution)/shard_map/pallas_call | solution.py:405
  84.5 11.4 %collective-permute-done.18.refs_2_.refs_3_ = bf16[256,2048]{1,0:T(8,128)(2,1)S(1)} collective-permute-done((bf16[256,2048]{1,0:T(8,128)(2,1)S(1)}, bf16[256,2048]{1,0:T(8,128)(2,1)S(1)}, u32[]{:S(2)}, u32[]{:S(2)}) %collective-permute-start.18) | collective-permute-done | bytes 1048608 | tf_op jit(solution)/shard_map/ppermute | solution.py:338
  96.8 3.2 %collective-permute-start.22 = (bf16[272,1024]{1,0:T(8,128)(2,1)S(1)}, bf16[272,1024]{1,0:T(8,128)(2,1)S(1)}, u32[]{:S(2)}, u32[]{:S(2)}) collective-permute-start(bf16[272,1024]{1,0:T(8,128)(2,1)S(1)} %collective-permute-done.21.first), channel_id=1, source_target_pairs={{2,3},{3,2},{4,5},{5,4},{10,11},{11,10},{12,13},{13,12},{18,19},{1... | collective-permute-start | bytes 1671176 | tf_op jit(solution)/shard_map/ppermute | solution.py:338
  102.1 5.2 %collective-permute-done.22.second = bf16[272,1024]{1,0:T(8,128)(2,1)S(1)} collective-permute-done((bf16[272,1024]{1,0:T(8,128)(2,1)S(1)}, bf16[272,1024]{1,0:T(8,128)(2,1)S(1)}, u32[]{:S(2)}, u32[]{:S(2)}) %collective-permute-start.22) | collective-permute-done | bytes 557088 | tf_op jit(solution)/shard_map/ppermute | solution.py:338
  110.1 4.3 %shard_map.163 = (bf16[1024,1024]{1,0:T(8,128)(2,1)S(1)}, f32[256,1024]{1,0:T(8,128)S(1)}) custom-call(s32[1]{0:T(128)} %bitcast.flat_ref, bf16[1024,1024]{1,0:T(8,128)(2,1)S(1)} %get-tuple-element.142.x_ref, bf16[1024,256]{1,0:T(8,128)(2,1)S(1)} %get-tuple-element.160.refs_0_.refs_4_.o_ref, bf16[1024,256]{1,0:T(8,128)(2,1)S(1)} %collective-permute-done.23.refs_1_.refs_5_, ...), custom_call_target="tpu_custom_call" | custom-call | flops 21474836 | bytes 94371 | tf_op jit(solution)/shard_map/pallas_call | solution.py:405
  116.0 7.3 %shard_map.165 = (bf16[1024,656]{1,0:T(8,128)(2,1)S(1)}, bf16[1024,1312]{1,0:T(8,128)(2,1)S(1)}) custom-call(s32[1]{0:T(128)} %bitcast.flat_ref, bf16[1024,1024]{1,0:T(8,128)(2,1)S(1)} %get-tuple-element.163.n_ref, bf16[1024,1024]{1,0:T(8,128)(2,1)S(1)} %shard_map.164.cot_ref.base_ref, bf16[256,2048]{1,0:T(8,128)(2,1)S(1)} %bitcast.34, ...), custom_call_target="tpu_custom_call" | custom-call | flops 41271952 | bytes 125501 | tf_op jit(solution)/shard_map/pallas_call | solution.py:405
  131.1 6.6 %shard_map.168 = bf16[4,256,2048]{2,1,0:T(8,128)(2,1)S(1)} custom-call(s32[1]{0:T(128)} %bitcast.flat_ref, bf16[1024,1024]{1,0:T(8,128)(2,1)S(1)} %get-tuple-element.163.n_ref, bf16[1024,1024]{1,0:T(8,128)(2,1)S(1)} %shard_map.164.cot_ref.base_ref, bf16[1024,1312]{1,0:T(8,128)(2,1)S(1)} %get-tuple-element.169.refs_0_.d_ref, ...), custom_call_target="tpu_custom_call" | custom-call | flops 41271952 | bytes 124190 | tf_op jit(solution)/shard_map/pallas_call | solution.py:405
  139.8 5.1 %all-to-all-start = ((bf16[4,256,2048]{2,1,0:T(8,128)(2,1)}), bf16[4,256,2048]{2,1,0:T(8,128)(2,1)}, u32[]{:S(2)}, u32[]{:S(2)}) async-start(bf16[4,256,2048]{2,1,0:T(8,128)(2,1)} %copy-done.8), calls=%async_computation | async-start | bytes 8388608 | tf_op jit(solution)/shard_map/all_to_all | solution.py:1171
  150.8 3.2 %shard_map.169 = (bf16[272,1024]{1,0:T(8,128)(2,1)S(1)}, f32[256,1024]{1,0:T(8,128)S(1)}) custom-call(s32[1]{0:T(128)} %bitcast.flat_ref, f32[256,1024]{1,0:T(8,128)S(1)} %copy-done.28, f32[512,1024]{1,0:T(8,128)S(1)} %copy-done.10, bf16[512,1024]{1,0:T(8,128)(2,1)S(1)} %copy-done.35, bf16[272,1024]{1,0:T(8,128)(2,1)} %collective-permute-done.31.c_ref, ...), custom_call_target="tpu_custom_call" | custom-call | bytes 84541 | tf_op jit(solution)/shard_map/pallas_call | solution.py:405
  158.9 8.6 %collective-permute-done.36.refs_1_ = bf16[272,1024]{1,0:T(8,128)(2,1)S(1)} collective-permute-done((bf16[272,1024]{1,0:T(8,128)(2,1)S(1)}, bf16[272,1024]{1,0:T(8,128)(2,1)S(1)}, u32[]{:S(2)}, u32[]{:S(2)}) %collective-permute-start.36) | collective-permute-done | bytes 557088 | tf_op jit(solution)/shard_map/ppermute | solution.py:338
  173.3 14.7 %shard_map.172 = (bf16[1024,256]{1,0:T(8,128)(2,1)S(1)}, bf16[1024,256]{1,0:T(8,128)(2,1)S(1)}, bf16[1024,256]{1,0:T(8,128)(2,1)S(1)}) custom-call(s32[1]{0:T(128)} %bitcast.flat_ref, bf16[1024,768]{1,0:T(8,128)(2,1)S(1)} %get-tuple-element.151.q_ref.k_ref.v_ref, bf16[1024,768]{1,0:T(8,128)(2,1)S(1)} %get-tuple-element.151.q_ref.k_ref.v_ref, ...), custom_call_target="tpu_custom_call" | custom-call | flops 107374184 | bytes 84213 | tf_op jit(solution)/shard_map/pallas_call | solution.py:405
  191.0 5.7 %collective-permute-start.35 = (bf16[256,1024]{1,0:T(8,128)(2,1)}, bf16[256,1024]{1,0:T(8,128)(2,1)}, u32[]{:S(2)}, u32[]{:S(2)}) collective-permute-start(bf16[256,1024]{1,0:T(8,128)(2,1)} %add_convert_fusion), channel_id=1, source_target_pairs={{0,0},{1,1},{2,4},{3,5},{4,2},{5,3},{6,6},{7,7},{8,8},{9,9},{10,12... | collective-permute-start | bytes 1572872 | tf_op jit(solution)/shard_map/ppermute | solution.py:338
  198.0 4.2 %shard_map.175 = (bf16[256,1024]{1,0:T(8,128)(2,1)S(1)}, bf16[256,1024]{1,0:T(8,128)(2,1)}, bf16[256,1024]{1,0:T(8,128)(2,1)}, bf16[256,1024]{1,0:T(8,128)(2,1)}) custom-call(s32[1]{0:T(128)} %bitcast.flat_ref, bf16[1024,1024]{1,0:T(8,128)(2,1)S(1)} %copy-done.53, bf16[1024,256]{1,0:T(8,128)(2,1)S(1)} %get-tuple-element.185.refs_0_, ...), custom_call_target="tpu_custom_call" | custom-call | flops 16106127 | bytes 62914 | tf_op jit(solution)/shard_map/pallas_call | solution.py:405
  206.9 2.7 shard_map.176
  209.5 3.2 %collective-permute-start.43 = (bf16[2,64,2048]{2,1,0:T(8,128)(2,1)S(1)}, bf16[2,64,2048]{2,1,0:T(8,128)(2,1)S(1)}, u32[]{:S(2)}, u32[]{:S(2)}) collective-permute-start(bf16[2,64,2048]{2,1,0:T(8,128)(2,1)S(1)} %get-tuple-element.206), channel_id=1, source_target_pairs={{0,2},{1,3},{2,0},{3,1},{4,6},{5,7},{6,4},{7,5},{8,10},{9,11},{10,... | collective-permute-start | bytes 1572872 | tf_op jit(solution)/shard_map/ppermute | solution.py:338
  213.6 2.6 collective-permute-done.40
  216.4 11.3 %collective-permute-done.42 = bf16[256,1024]{1,0:T(8,128)(2,1)} collective-permute-done((bf16[256,1024]{1,0:T(8,128)(2,1)}, bf16[256,1024]{1,0:T(8,128)(2,1)}, u32[]{:S(2)}, u32[]{:S(2)}) %collective-permute-start.42) | collective-permute-done | bytes 524320 | tf_op jit(solution)/shard_map/ppermute | solution.py:338
  230.6 5.6 %collective-permute-done.43 = bf16[2,64,2048]{2,1,0:T(8,128)(2,1)S(1)} collective-permute-done((bf16[2,64,2048]{2,1,0:T(8,128)(2,1)S(1)}, bf16[2,64,2048]{2,1,0:T(8,128)(2,1)S(1)}, u32[]{:S(2)}, u32[]{:S(2)}) %collective-permute-start.43) | collective-permute-done | bytes 524320 | tf_op jit(solution)/shard_map/ppermute | solution.py:338
  239.6 2.9 %collective-permute-start.46 = (bf16[128,1024]{1,0:T(8,128)(2,1)S(1)}, bf16[128,1024]{1,0:T(8,128)(2,1)S(1)}, u32[]{:S(2)}, u32[]{:S(2)}) collective-permute-start(bf16[128,1024]{1,0:T(8,128)(2,1)S(1)} %get-tuple-element.213), channel_id=1, source_target_pairs={{0,0},{1,1},{2,4},{3,5},{4,2},{5,3},{6,6},{7,7},{8,8},{9,9},{10,12... | collective-permute-start | bytes 786440 | tf_op jit(solution)/shard_map/ppermute | solution.py:338
  242.5 3.6 %collective-permute-start.45 = (bf16[128,1024]{1,0:T(8,128)(2,1)S(1)}, bf16[128,1024]{1,0:T(8,128)(2,1)S(1)}, u32[]{:S(2)}, u32[]{:S(2)}) collective-permute-start(bf16[128,1024]{1,0:T(8,128)(2,1)S(1)} %get-tuple-element.236), channel_id=1, source_target_pairs={{0,0},{1,1},{2,4},{3,5},{4,2},{5,3},{6,6},{7,7},{8,8},{9,9},{10,12... | collective-permute-start | bytes 786440 | tf_op jit(solution)/shard_map/ppermute | solution.py:338
  246.5 7.9 %collective-permute-done.48 = bf16[2,64,1152]{2,1,0:T(8,128)(2,1)S(1)} collective-permute-done((bf16[2,64,1152]{2,1,0:T(8,128)(2,1)S(1)}, bf16[2,64,1152]{2,1,0:T(8,128)(2,1)S(1)}, u32[]{:S(2)}, u32[]{:S(2)}) %collective-permute-start.48) | collective-permute-done | bytes 294944 | tf_op jit(solution)/shard_map/ppermute | solution.py:338
  (276 shorter events, 87.5 us)
Async XLA Ops:
  2.8 16.2 %collective-permute-start.3 = (bf16[272,1024]{1,0:T(8,128)(2,1)S(1)}, bf16[272,1024]{1,0:T(8,128)(2,1)}, u32[]{:S(2)}, u32[]{:S(2)}) collective-permute-start(bf16[272,1024]{1,0:T(8,128)(2,1)S(1)} %get-tuple-element.239.block), channel_id=1, source_target_pairs={{0,1},{1,0},{2,4},{3,5},{4,2},{5,3},{6,7},{7,6},{8,9},{9,8},{10,12... | collective-permute-start | bytes 1671176 | tf_op jit(solution)/shard_map/ppermute | solution.py:338
  6.6 23.1 %collective-permute-start.6 = (bf16[272,1024]{1,0:T(8,128)(2,1)S(1)}, bf16[272,1024]{1,0:T(8,128)(2,1)S(1)}, u32[]{:S(2)}, u32[]{:S(2)}) collective-permute-start(bf16[272,1024]{1,0:T(8,128)(2,1)S(1)} %get-tuple-element.238.block), channel_id=1, source_target_pairs={{0,4},{1,5},{2,6},{3,7},{4,0},{5,1},{6,2},{7,3},{8,12},{9,13},{10,... | collective-permute-start | bytes 1671176 | tf_op jit(solution)/shard_map/ppermute | solution.py:338
  11.3 18.3 %collective-permute-start.5 = (bf16[2,32,2048]{2,1,0:T(8,128)(2,1)S(1)}, bf16[2,32,2048]{2,1,0:T(8,128)(2,1)S(1)}, u32[]{:S(2)}, u32[]{:S(2)}) collective-permute-start(bf16[2,32,2048]{2,1,0:T(8,128)(2,1)S(1)} %get-tuple-element.135), channel_id=1, source_target_pairs={{0,1},{1,0},{2,3},{3,2},{4,5},{5,4},{6,7},{7,6},{8,9},{9,8},{10,11... | collective-permute-start | bytes 786440 | tf_op jit(solution)/shard_map/ppermute | solution.py:338
  21.8 14.2 %collective-permute-start.7 = (bf16[4,32,1024]{2,1,0:T(8,128)(2,1)S(1)}, bf16[4,32,1024]{2,1,0:T(8,128)(2,1)S(1)}, u32[]{:S(2)}, u32[]{:S(2)}) collective-permute-start(bf16[4,32,1024]{2,1,0:T(8,128)(2,1)S(1)} %shard_map.156), channel_id=1, source_target_pairs={{0,2},{1,3},{2,0},{3,1},{4,6},{5,7},{6,4},{7,5},{8,10},{9,11},{10,... | collective-permute-start | bytes 786440 | tf_op jit(solution)/shard_map/ppermute | solution.py:338
  25.5 14.6 %collective-permute-start.9 = (bf16[272,1024]{1,0:T(8,128)(2,1)}, bf16[272,1024]{1,0:T(8,128)(2,1)S(1)}, u32[]{:S(2)}, u32[]{:S(2)}) collective-permute-start(bf16[272,1024]{1,0:T(8,128)(2,1)} %collective-permute-done.3.first), channel_id=1, source_target_pairs={{2,3},{3,2},{4,5},{5,4},{10,11},{11,10},{12,13},{13,12},{18,19},{1... | collective-permute-start | bytes 1671176 | tf_op jit(solution)/shard_map/ppermute | solution.py:338
  38.5 32.5 %collective-permute-start.15 = (bf16[4,32,2048]{2,1,0:T(8,128)(2,1)S(1)}, bf16[4,32,2048]{2,1,0:T(8,128)(2,1)S(1)}, u32[]{:S(2)}, u32[]{:S(2)}) collective-permute-start(bf16[4,32,2048]{2,1,0:T(8,128)(2,1)S(1)} %shard_map.157), channel_id=1, source_target_pairs={{0,2},{1,3},{2,0},{3,1},{4,6},{5,7},{6,4},{7,5},{8,10},{9,11},{10,... | collective-permute-start | bytes 1572872 | tf_op jit(solution)/shard_map/ppermute | solution.py:338
  40.1 20.1 %collective-permute-start.10 = (bf16[272,1024]{1,0:T(8,128)(2,1)S(1)}, bf16[272,1024]{1,0:T(8,128)(2,1)S(1)}, u32[]{:S(2)}, u32[]{:S(2)}) collective-permute-start(bf16[272,1024]{1,0:T(8,128)(2,1)S(1)} %collective-permute-done.9.second), channel_id=1, source_target_pairs={{0,4},{1,5},{2,6},{3,7},{4,0},{5,1},{6,2},{7,3},{8,12},{9,13},{10,... | collective-permute-start | bytes 1671176 | tf_op jit(solution)/shard_map/ppermute | solution.py:338
  54.4 21.4 %collective-permute-start.17 = (bf16[1024,256]{1,0:T(8,128)(2,1)S(1)}, bf16[1024,256]{1,0:T(8,128)(2,1)S(1)}, u32[]{:S(2)}, u32[]{:S(2)}) collective-permute-start(bf16[1024,256]{1,0:T(8,128)(2,1)S(1)} %slice_dynamic-update-slice_fusion.3.refs_4_.refs_8_), channel_id=1, source_target_pairs={{0,1},{1,0},{2,3},{3,2},{4,5},{5,4},{6,7},{7,6},{8,9},{9,8},{10,11... | collective-permute-start | bytes 1572872 | tf_op jit(solution)/shard_map/ppermute | solution.py:338
  59.6 16.1 %collective-permute-start.16 = (bf16[1024,256]{1,0:T(8,128)(2,1)S(1)}, bf16[1024,256]{1,0:T(8,128)(2,1)S(1)}, u32[]{:S(2)}, u32[]{:S(2)}) collective-permute-start(bf16[1024,256]{1,0:T(8,128)(2,1)S(1)} %slice_dynamic-update-slice_fusion.3.refs_4_.refs_8_), channel_id=1, source_target_pairs={{0,4},{1,5},{2,6},{3,7},{4,0},{5,1},{6,2},{7,3},{8,12},{9,13},{10,... | collective-permute-start | bytes 1572872 | tf_op jit(solution)/shard_map/ppermute | solution.py:338
  71.0 24.8 %collective-permute-start.18 = (bf16[256,2048]{1,0:T(8,128)(2,1)S(1)}, bf16[256,2048]{1,0:T(8,128)(2,1)S(1)}, u32[]{:S(2)}, u32[]{:S(2)}) collective-permute-start(bf16[256,2048]{1,0:T(8,128)(2,1)S(1)} %bitcast.32), channel_id=1, source_target_pairs={{0,16},{1,17},{2,18},{3,19},{4,20},{5,21},{6,22},{7,23},{8,24},{9,... | collective-permute-start | bytes 3145736 | tf_op jit(solution)/shard_map/ppermute | solution.py:338
  72.4 24.4 %collective-permute-start.20 = (bf16[256,2048]{1,0:T(8,128)(2,1)S(1)}, bf16[256,2048]{1,0:T(8,128)(2,1)S(1)}, u32[]{:S(2)}, u32[]{:S(2)}) collective-permute-start(bf16[256,2048]{1,0:T(8,128)(2,1)S(1)} %bitcast.33), channel_id=1, source_target_pairs={{0,8},{1,9},{2,10},{3,11},{4,12},{5,13},{6,14},{7,15},{8,0},{9,1},... | collective-permute-start | bytes 3145736 | tf_op jit(solution)/shard_map/ppermute | solution.py:338
  72.6 24.2 %collective-permute-start.21 = (bf16[272,1024]{1,0:T(8,128)(2,1)S(1)}, bf16[272,1024]{1,0:T(8,128)(2,1)S(1)}, u32[]{:S(2)}, u32[]{:S(2)}) collective-permute-start(bf16[272,1024]{1,0:T(8,128)(2,1)S(1)} %copy-done.39), channel_id=1, source_target_pairs={{0,1},{1,0},{2,4},{3,5},{4,2},{5,3},{6,7},{7,6},{8,9},{9,8},{10,12... | collective-permute-start | bytes 1671176 | tf_op jit(solution)/shard_map/ppermute | solution.py:338
  75.7 20.1 %collective-permute-start.19 = (bf16[1024,256]{1,0:T(8,128)(2,1)S(1)}, bf16[1024,256]{1,0:T(8,128)(2,1)S(1)}, u32[]{:S(2)}, u32[]{:S(2)}) collective-permute-start(bf16[1024,256]{1,0:T(8,128)(2,1)S(1)} %collective-permute-done.17.refs_5_.refs_9_), channel_id=1, source_target_pairs={{0,4},{1,5},{2,6},{3,7},{4,0},{5,1},{6,2},{7,3},{8,12},{9,13},{10,... | collective-permute-start | bytes 1572872 | tf_op jit(solution)/shard_map/ppermute | solution.py:338
  84.4 15.6 %collective-permute-start.23 = (bf16[1024,256]{1,0:T(8,128)(2,1)S(1)}, bf16[1024,256]{1,0:T(8,128)(2,1)S(1)}, u32[]{:S(2)}, u32[]{:S(2)}) collective-permute-start(bf16[1024,256]{1,0:T(8,128)(2,1)S(1)} %get-tuple-element.160.refs_0_.refs_4_.o_ref), channel_id=1, source_target_pairs={{0,1},{1,0},{2,3},{3,2},{4,5},{5,4},{6,7},{7,6},{8,9},{9,8},{10,11... | collective-permute-start | bytes 1572872 | tf_op jit(solution)/shard_map/ppermute | solution.py:338
  100.2 15.7 %collective-permute-start.29 = (bf16[144,2048]{1,0:T(8,128)(2,1)S(1)}, bf16[144,2048]{1,0:T(8,128)(2,1)S(1)}, u32[]{:S(2)}, u32[]{:S(2)}) collective-permute-start(bf16[144,2048]{1,0:T(8,128)(2,1)S(1)} %slice.99), channel_id=1, source_target_pairs={{0,8},{1,9},{2,10},{3,11},{4,12},{5,13},{6,14},{7,15},{8,0},{9,1},... | collective-permute-start | bytes 1769480 | tf_op jit(solution)/shard_map/ppermute | solution.py:338
  101.3 14.6 %collective-permute-start.28 = (bf16[144,2048]{1,0:T(8,128)(2,1)S(1)}, bf16[144,2048]{1,0:T(8,128)(2,1)S(1)}, u32[]{:S(2)}, u32[]{:S(2)}) collective-permute-start(bf16[144,2048]{1,0:T(8,128)(2,1)S(1)} %slice.98), channel_id=1, source_target_pairs={{0,16},{1,17},{2,18},{3,19},{4,20},{5,21},{6,22},{7,23},{8,24},{9,... | collective-permute-start | bytes 1769480 | tf_op jit(solution)/shard_map/ppermute | solution.py:338
  101.5 13.9 %collective-permute-start.26 = (bf16[272,1024]{1,0:T(8,128)(2,1)S(1)}, bf16[272,1024]{1,0:T(8,128)(2,1)S(1)}, u32[]{:S(2)}, u32[]{:S(2)}) collective-permute-start(bf16[272,1024]{1,0:T(8,128)(2,1)S(1)} %collective-permute-done.21.first), channel_id=1, source_target_pairs={{0,4},{1,5},{2,6},{3,7},{4,0},{5,1},{6,2},{7,3},{8,12},{9,13},{10,... | collective-permute-start | bytes 1671176 | tf_op jit(solution)/shard_map/ppermute | solution.py:338
  130.7 14.5 %collective-permute-start.31 = (bf16[272,1024]{1,0:T(8,128)(2,1)}, bf16[272,1024]{1,0:T(8,128)(2,1)}, u32[]{:S(2)}, u32[]{:S(2)}) collective-permute-start(bf16[272,1024]{1,0:T(8,128)(2,1)} %pad.9), channel_id=1, source_target_pairs={{0,1},{1,0},{2,3},{3,2},{4,5},{5,4},{6,7},{7,6},{8,9},{9,8},{10,11... | collective-permute-start | bytes 1671176 | tf_op jit(solution)/shard_map/ppermute | solution.py:338
  139.8 67.1 %all-to-all-start = ((bf16[4,256,2048]{2,1,0:T(8,128)(2,1)}), bf16[4,256,2048]{2,1,0:T(8,128)(2,1)}, u32[]{:S(2)}, u32[]{:S(2)}) async-start(bf16[4,256,2048]{2,1,0:T(8,128)(2,1)} %copy-done.8), calls=%async_computation | async-start | bytes 8388608 | tf_op jit(solution)/shard_map/all_to_all | solution.py:1171
  154.0 13.5 %collective-permute-start.36 = (bf16[272,1024]{1,0:T(8,128)(2,1)S(1)}, bf16[272,1024]{1,0:T(8,128)(2,1)S(1)}, u32[]{:S(2)}, u32[]{:S(2)}) collective-permute-start(bf16[272,1024]{1,0:T(8,128)(2,1)S(1)} %get-tuple-element.178.refs_0_), channel_id=1, source_target_pairs={{0,1},{1,0},{2,3},{3,2},{4,5},{5,4},{6,7},{7,6},{8,9},{9,8},{10,11... | collective-permute-start | bytes 1671176 | tf_op jit(solution)/shard_map/ppermute | solution.py:338
  158.5 29.6 %collective-permute-start.32 = (bf16[256,1024]{1,0:T(8,128)(2,1)S(1)}, bf16[256,1024]{1,0:T(8,128)(2,1)S(1)}, u32[]{:S(2)}, u32[]{:S(2)}) collective-permute-start(bf16[256,1024]{1,0:T(8,128)(2,1)S(1)} %get-tuple-element.234), channel_id=1, source_target_pairs={{0,4},{1,5},{2,6},{3,7},{4,0},{5,1},{6,2},{7,3},{8,12},{9,13},{10,... | collective-permute-start | bytes 1572872 | tf_op jit(solution)/shard_map/ppermute | solution.py:338
  169.3 18.7 %collective-permute-start.34 = (bf16[256,1024]{1,0:T(8,128)(2,1)S(1)}, bf16[256,1024]{1,0:T(8,128)(2,1)S(1)}, u32[]{:S(2)}, u32[]{:S(2)}) collective-permute-start(bf16[256,1024]{1,0:T(8,128)(2,1)S(1)} %add_convert_fusion.1), channel_id=1, source_target_pairs={{0,1},{1,0},{2,3},{3,2},{4,5},{5,4},{6,7},{7,6},{8,9},{9,8},{10,11... | collective-permute-start | bytes 1572872 | tf_op jit(solution)/shard_map/ppermute | solution.py:338
  189.4 15.4 %collective-permute-start.39 = (bf16[512,1024]{1,0:T(8,128)(2,1)S(1)}, bf16[512,1024]{1,0:T(8,128)(2,1)S(1)}, u32[]{:S(2)}, u32[]{:S(2)}) collective-permute-start(bf16[512,1024]{1,0:T(8,128)(2,1)S(1)} %shard_map.173), channel_id=1, source_target_pairs={{0,4},{1,5},{2,6},{3,7},{4,0},{5,1},{6,2},{7,3},{8,12},{9,13},{10,... | collective-permute-start | bytes 3145736 | tf_op jit(solution)/shard_map/ppermute | solution.py:338
  191.0 21.8 %collective-permute-start.35 = (bf16[256,1024]{1,0:T(8,128)(2,1)}, bf16[256,1024]{1,0:T(8,128)(2,1)}, u32[]{:S(2)}, u32[]{:S(2)}) collective-permute-start(bf16[256,1024]{1,0:T(8,128)(2,1)} %add_convert_fusion), channel_id=1, source_target_pairs={{0,0},{1,1},{2,4},{3,5},{4,2},{5,3},{6,6},{7,7},{8,8},{9,9},{10,12... | collective-permute-start | bytes 1572872 | tf_op jit(solution)/shard_map/ppermute | solution.py:338
  202.2 14.0 %collective-permute-start.40 = (bf16[256,1024]{1,0:T(8,128)(2,1)}, bf16[256,1024]{1,0:T(8,128)(2,1)S(1)}, u32[]{:S(2)}, u32[]{:S(2)}) collective-permute-start(bf16[256,1024]{1,0:T(8,128)(2,1)} %get-tuple-element.200), channel_id=1, source_target_pairs={{0,8},{1,9},{2,10},{3,11},{4,12},{5,13},{6,14},{7,15},{8,0},{9,1},... | collective-permute-start | bytes 1572872 | tf_op jit(solution)/shard_map/ppermute | solution.py:338
  202.9 13.5 %collective-permute-start.41 = (bf16[256,1024]{1,0:T(8,128)(2,1)}, bf16[256,1024]{1,0:T(8,128)(2,1)}, u32[]{:S(2)}, u32[]{:S(2)}) collective-permute-start(bf16[256,1024]{1,0:T(8,128)(2,1)} %get-tuple-element.201), channel_id=1, source_target_pairs={{0,16},{1,17},{2,18},{3,19},{4,20},{5,21},{6,22},{7,23},{8,24},{9,... | collective-permute-start | bytes 1572872 | tf_op jit(solution)/shard_map/ppermute | solution.py:338
  204.1 23.6 %collective-permute-start.42 = (bf16[256,1024]{1,0:T(8,128)(2,1)}, bf16[256,1024]{1,0:T(8,128)(2,1)}, u32[]{:S(2)}, u32[]{:S(2)}) collective-permute-start(bf16[256,1024]{1,0:T(8,128)(2,1)} %get-tuple-element.202), channel_id=1, source_target_pairs={{0,24},{1,25},{2,26},{3,27},{4,28},{5,29},{6,30},{7,31},{8,16},{9,... | collective-permute-start | bytes 1572872 | tf_op jit(solution)/shard_map/ppermute | solution.py:338
  209.5 26.6 %collective-permute-start.43 = (bf16[2,64,2048]{2,1,0:T(8,128)(2,1)S(1)}, bf16[2,64,2048]{2,1,0:T(8,128)(2,1)S(1)}, u32[]{:S(2)}, u32[]{:S(2)}) collective-permute-start(bf16[2,64,2048]{2,1,0:T(8,128)(2,1)S(1)} %get-tuple-element.206), channel_id=1, source_target_pairs={{0,2},{1,3},{2,0},{3,1},{4,6},{5,7},{6,4},{7,5},{8,10},{9,11},{10,... | collective-permute-start | bytes 1572872 | tf_op jit(solution)/shard_map/ppermute | solution.py:338
  212.8 23.4 %collective-permute-start.44 = (bf16[256,1024]{1,0:T(8,128)(2,1)S(1)}, bf16[256,1024]{1,0:T(8,128)(2,1)S(1)}, u32[]{:S(2)}, u32[]{:S(2)}) collective-permute-start(bf16[256,1024]{1,0:T(8,128)(2,1)S(1)} %copy-done.68), channel_id=1, source_target_pairs={{0,1},{1,0},{2,3},{3,2},{4,5},{5,4},{6,7},{7,6},{8,9},{9,8},{10,11... | collective-permute-start | bytes 1572872 | tf_op jit(solution)/shard_map/ppermute | solution.py:338
  229.0 25.4 %collective-permute-start.48 = (bf16[2,64,1152]{2,1,0:T(8,128)(2,1)S(1)}, bf16[2,64,1152]{2,1,0:T(8,128)(2,1)S(1)}, u32[]{:S(2)}, u32[]{:S(2)}) collective-permute-start(bf16[2,64,1152]{2,1,0:T(8,128)(2,1)S(1)} %get-tuple-element.216), channel_id=1, source_target_pairs={{0,2},{1,3},{2,0},{3,1},{4,6},{5,7},{6,4},{7,5},{8,10},{9,11},{10,... | collective-permute-start | bytes 884744 | tf_op jit(solution)/shard_map/ppermute | solution.py:338
  239.6 24.5 %collective-permute-start.46 = (bf16[128,1024]{1,0:T(8,128)(2,1)S(1)}, bf16[128,1024]{1,0:T(8,128)(2,1)S(1)}, u32[]{:S(2)}, u32[]{:S(2)}) collective-permute-start(bf16[128,1024]{1,0:T(8,128)(2,1)S(1)} %get-tuple-element.213), channel_id=1, source_target_pairs={{0,0},{1,1},{2,4},{3,5},{4,2},{5,3},{6,6},{7,7},{8,8},{9,9},{10,12... | collective-permute-start | bytes 786440 | tf_op jit(solution)/shard_map/ppermute | solution.py:338
  242.5 21.6 %collective-permute-start.45 = (bf16[128,1024]{1,0:T(8,128)(2,1)S(1)}, bf16[128,1024]{1,0:T(8,128)(2,1)S(1)}, u32[]{:S(2)}, u32[]{:S(2)}) collective-permute-start(bf16[128,1024]{1,0:T(8,128)(2,1)S(1)} %get-tuple-element.236), channel_id=1, source_target_pairs={{0,0},{1,1},{2,4},{3,5},{4,2},{5,3},{6,6},{7,7},{8,8},{9,9},{10,12... | collective-permute-start | bytes 786440 | tf_op jit(solution)/shard_map/ppermute | solution.py:338
  (92 other events, 1062.6 us)

commit v7 on v6

--- a/solution.py
+++ b/solution.py
@@ -391,7 +391,7 @@
     return (array, (rows,) + array.shape[1:], lambda b, f: (step(b),) + (0,) * (len(array.shape) - 1))
 
 
-def run(body, order, grid, ins, outs, scratch=(), flops=0, spare=6 * 2**20):
+def run(body, order, grid, ins, outs, scratch=(), flops=0, spare=6 * 2**20, far=()):
     moved = sum(a.size * a.dtype.itemsize for a, _, _ in ins)
     moved += sum(a.size * a.dtype.itemsize for a, _, _ in outs)
     def held(block, dtype, count):
@@ -411,7 +411,9 @@
             out_specs=[pl.BlockSpec(block, index) for _, block, index in outs],
             scratch_shapes=list(scratch),
         ),
-        out_shape=[a for a, _, _ in outs],
+        out_shape=[
+            pltpu.HBM(a.shape, a.dtype) if i in far else a for i, (a, _, _) in enumerate(outs)
+        ],
         compiler_params=pltpu.CompilerParams(vmem_limit_bytes=grant),
         cost_estimate=pl.CostEstimate(flops=flops // 100, bytes_accessed=moved // 100, transcendentals=0),
     )(order[0], *[a for a, _, _ in ins])
@@ -596,6 +598,7 @@
         + [by_rows(cos_table, rows), by_rows(sin_table, rows)],
         [by_rows(shape_of(tokens, width), rows), by_rows(shape_of(tokens, columns), rows)],
         flops=2 * tokens * width * columns,
+        far=(0,),
     )
 
 
@@ -702,23 +705,26 @@
     tokens = grads[0][0].shape[0]
     piece = pieces[0].shape[0]
     rows, width, count = tokens // 2, 4 * piece, len(grads)
-    out = shape_of(rows, width, dtype=LOW if far else WIDE)
+    outs = [shape_of(rows, width)] if far else [shape_of(rows // 2, width, dtype=WIDE)] * 2
 
     def body(flat_ref, *refs):
-        arrays, weights, out_ref = refs[:count], refs[count : count + 5], refs[count + 5]
+        arrays, weights, out_refs = refs[:count], refs[count : count + 5], refs[count + 5 :]
         square = square_of(flat_ref[0])
         for span, w in zip(spans(pieces), weights):
-            out_ref[:, span_of(square, span, piece)] = sum(
+            total = sum(
                 mm_t(a[...], w[rows_of(w, span), at : at + a.shape[1]])
                 for a, (_, at) in zip(arrays, grads)
-            ).astype(out.dtype)
+            )
+            for k, ref in enumerate(out_refs):
+                part = total[k * ref.shape[0] : (k + 1) * ref.shape[0]]
+                ref[:, span_of(square, span, piece)] = part.astype(ref.dtype)
 
     return run(
         body, order, (1,),
         [by_rows(a, rows, lambda b: int(far)) for a, _ in grads] + [whole(p) for p in pieces],
-        [whole(out)],
+        [whole(out) for out in outs],
         flops=tokens * width * sum(a.shape[1] for a, _ in grads),
-    )[0]
+    )
 
 
 def back_both(order, grad, first, pieces):
@@ -742,7 +748,7 @@
 
 
 def norm_pull(order, x, terms, base, keep):
-    rows, width = base.shape[0] // (4 if keep else 1), base.shape[1]
+    rows, width = base.shape
     step = rows // 4
 
     def body(flat_ref, x_ref, a_ref, b_ref, c_ref, base_ref, *outs):
@@ -780,6 +786,7 @@
         + [whole(d_up), whole(hidden)],
         [by_rows(out, 1)],
         flops=6 * tokens * width * ff,
+        far=(0,),
     )[0]
 
 
@@ -1158,18 +1165,19 @@
         tokens,
     )
     two = [two, two_x, two_y, two_top, two_low]
+    cot_base = cot[:tokens]
     hidden, d_up = feed(order, normed_two, cot, two)
 
     grads = [(d_up, 0)]
-    far = go("b1c", back_half(order, grads, two, True), TO_CORE)
-    near = back_half(order, grads, two, False)
-    side = (near[tokens:] + far[tokens:].astype(WIDE)).astype(LOW)
+    far = go("b1c", back_half(order, grads, two, True)[0], TO_CORE)
+    near, other = back_half(order, grads, two, False)
+    side = (other + far[tokens:].astype(WIDE)).astype(LOW)
     side = go("b1z", jnp.pad(side, ((0, 16), (0, 0))), TO_ZL)
     ff_terms = feed_grads(order, normed_two, cot, d_up, hidden)
     at(13)
     if "a2a" not in TIED:
         ff_terms = lax.all_to_all(ff_terms, ("y", "x"), split_axis=0, concat_axis=0, tiled=True)
-    d_low, d_resid = norm_pull(order, resid, (near, far, side), cot, True)
+    d_low, d_resid = norm_pull(order, resid, (near, far, side), cot_base, True)
     if "a2a" in TIED:
         ff_terms = lax.all_to_all(
             after(order, ff_terms), ("y", "x"), split_axis=0, concat_axis=0, tiled=True
@@ -1188,15 +1196,15 @@
     d_mixed = attend_back(order, mix, attended, d_attended, logs, cos_table, sin_table)
     at(17)
     grads = [(d, t * part) for t, d in enumerate(d_mixed)]
-    far = go("m1c", back_half(order, grads, one, True), TO_CORE)
+    far = go("m1c", back_half(order, grads, one, True)[0], TO_CORE)
     at(18)
     output = resid + out_near[:tokens] + out_far[0].astype(WIDE) + out_side.astype(WIDE)
     output = output.astype(LOW)
     if "out" in TIED:
         wait(order, output)
     output = go("oh", output, TO_HOME)
-    near = back_half(order, grads, one, False)
-    side = (near[tokens:] + far[tokens:].astype(WIDE)).astype(LOW)
+    near, other = back_half(order, grads, one, False)
+    side = (other + far[tokens:].astype(WIDE)).astype(LOW)
     if "side" in TIED:
         wait(order, side)
     side = go("m1z", side, TO_ZL)

time: 268 us -> 267 us (level)
  local copies, waits for them, and re-layouts: 15.8 us -> 13.1 us
    unnamed x145 -> x139, local copies, waits for them, and re-layouts: 14.5 us -> 10.8 us
  transfers between devices with their start and end apart: 55 -> 55, of which waited for: 23 -> 27; matrix products, arithmetic and copies ran while one was open for 2% -> 2% of each run, Pallas kernels for 25% -> 25%
where the time goes in v7:
time: 267 us; the launch traced here: 265 us
  waiting for transfers between devices  90.2 us (34%)
  Pallas kernels  77.1 us (29%)
  starting transfers between devices  74.9 us (28%)
  local copies, waits for them, and re-layouts  13.1 us (5%)
  other arithmetic  8.07 us (3%)
    ppermute x54, waiting for transfers between devices, send(): return lax.ppermute(array, FLAT, pairs)  90.1 us
    pallas_call x31, Pallas kernels, run(): pl.pallas_call(body, grid_spec=pltpu.PrefetchScalarGridSpec(num_scalar_pr...  77.1 us
    ppermute x54, starting transfers between devices, send(): return lax.ppermute(array, FLAT, pairs)  69.8 us
    unnamed x139, local copies, waits for them, and re-layouts  10.8 us
  transfers between devices with their start and end apart: 55, of which 27 were waited for; matrix products, arithmetic and copies ran while one was open for 2% of the time, Pallas kernels for 25%

profile of v7, /device:TPU:1, one launch (start us, length us, event | category | flops | bytes accessed | tf_op | source)
XLA Modules:
  0.0 265.1 jit_solution(6445637261303844683)
XLA Ops:
  2.8 3.8 %collective-permute-start.3 = (bf16[272,1024]{1,0:T(8,128)(2,1)S(1)}, bf16[272,1024]{1,0:T(8,128)(2,1)}, u32[]{:S(2)}, u32[]{:S(2)}) collective-permute-start(bf16[272,1024]{1,0:T(8,128)(2,1)S(1)} %get-tuple-element.247.block), channel_id=1, source_target_pairs={{0,1},{1,0},{2,4},{3,5},{4,2},{5,3},{6,7},{7,6},{8,9},{9,8},{10,12... | collective-permute-start | bytes 1671176 | tf_op jit(solution)/shard_map/ppermute | solution.py:338
  11.5 7.4 %collective-permute-done.3.first = bf16[272,1024]{1,0:T(8,128)(2,1)} collective-permute-done((bf16[272,1024]{1,0:T(8,128)(2,1)S(1)}, bf16[272,1024]{1,0:T(8,128)(2,1)}, u32[]{:S(2)}, u32[]{:S(2)}) %collective-permute-start.3) | collective-permute-done | bytes 557088 | tf_op jit(solution)/shard_map/ppermute | solution.py:338
  19.0 2.8 %collective-permute-done.4.received_ref = bf16[2,32,1024]{2,1,0:T(8,128)(2,1)S(1)} collective-permute-done((bf16[2,32,1024]{2,1,0:T(8,128)(2,1)S(1)}, bf16[2,32,1024]{2,1,0:T(8,128)(2,1)S(1)}, u32[]{:S(2)}, u32[]{:S(2)}) %collective-permute-start.4) | collective-permute-done | bytes 131104 | tf_op jit(solution)/shard_map/ppermute | solution.py:338
  21.7 3.8 %collective-permute-start.7 = (bf16[4,32,1024]{2,1,0:T(8,128)(2,1)S(1)}, bf16[4,32,1024]{2,1,0:T(8,128)(2,1)S(1)}, u32[]{:S(2)}, u32[]{:S(2)}) collective-permute-start(bf16[4,32,1024]{2,1,0:T(8,128)(2,1)S(1)} %shard_map.156), channel_id=1, source_target_pairs={{0,2},{1,3},{2,0},{3,1},{4,6},{5,7},{6,4},{7,5},{8,10},{9,11},{10,... | collective-permute-start | bytes 786440 | tf_op jit(solution)/shard_map/ppermute | solution.py:338
  25.5 4.0 %collective-permute-start.9 = (bf16[272,1024]{1,0:T(8,128)(2,1)}, bf16[272,1024]{1,0:T(8,128)(2,1)S(1)}, u32[]{:S(2)}, u32[]{:S(2)}) collective-permute-start(bf16[272,1024]{1,0:T(8,128)(2,1)} %collective-permute-done.3.first), channel_id=1, source_target_pairs={{2,3},{3,2},{4,5},{5,4},{10,11},{11,10},{12,13},{13,12},{18,19},{1... | collective-permute-start | bytes 1671176 | tf_op jit(solution)/shard_map/ppermute | solution.py:338
  30.4 5.5 %collective-permute-done.7 = bf16[4,32,1024]{2,1,0:T(8,128)(2,1)S(1)} collective-permute-done((bf16[4,32,1024]{2,1,0:T(8,128)(2,1)S(1)}, bf16[4,32,1024]{2,1,0:T(8,128)(2,1)S(1)}, u32[]{:S(2)}, u32[]{:S(2)}) %collective-permute-start.7) | collective-permute-done | bytes 262176 | tf_op jit(solution)/shard_map/ppermute | solution.py:338
  41.8 5.1 %collective-permute-done.12.refs_2_.refs_5_ = bf16[256,1024]{1,0:T(8,128)(2,1)S(1)} collective-permute-done((bf16[256,1024]{1,0:T(8,128)(2,1)S(1)}, bf16[256,1024]{1,0:T(8,128)(2,1)S(1)}, u32[]{:S(2)}, u32[]{:S(2)}) %collective-permute-start.12) | collective-permute-done | bytes 524320 | tf_op jit(solution)/shard_map/ppermute | solution.py:338
  49.5 4.2 %collective-permute-done.13.refs_3_.refs_6_ = bf16[128,1024]{1,0:T(8,128)(2,1)S(1)} collective-permute-done((bf16[128,1024]{1,0:T(8,128)(2,1)S(1)}, bf16[128,1024]{1,0:T(8,128)(2,1)S(1)}, u32[]{:S(2)}, u32[]{:S(2)}) %collective-permute-start.13) | collective-permute-done | bytes 262176 | tf_op jit(solution)/shard_map/ppermute | solution.py:338
  54.4 5.3 %collective-permute-start.16 = (bf16[1024,256]{1,0:T(8,128)(2,1)S(1)}, bf16[1024,256]{1,0:T(8,128)(2,1)S(1)}, u32[]{:S(2)}, u32[]{:S(2)}) collective-permute-start(bf16[1024,256]{1,0:T(8,128)(2,1)S(1)} %slice_dynamic-update-slice_fusion.3.refs_4_.refs_8_), channel_id=1, source_target_pairs={{0,4},{1,5},{2,6},{3,7},{4,0},{5,1},{6,2},{7,3},{8,12},{9,13},{10,... | collective-permute-start | bytes 1572872 | tf_op jit(solution)/shard_map/ppermute | solution.py:338
  64.4 5.2 %shard_map.160 = (bf16[1024,1024]{1,0:T(8,128)(2,1)}, bf16[1024,768]{1,0:T(8,128)(2,1)S(1)}) custom-call(s32[1]{0:T(128)} %bitcast.flat_ref, bf16[1024,1024]{1,0:T(8,128)(2,1)S(1)} %get-tuple-element.146.x_ref, bf16[256,1024]{1,0:T(8,128)(2,1)S(1)} %bitcast.41, bf16[256,1024]{1,0:T(8,128)(2,1)S(1)} %collective-permute-done.11.refs_1_.refs_4_, ...), custom_call_target="tpu_custom_call" | custom-call | flops 16106127 | bytes 89128 | tf_op jit(solution)/shard_map/pallas_call | solution.py:405
  71.3 3.6 %collective-permute-start.21 = (bf16[272,1024]{1,0:T(8,128)(2,1)S(1)}, bf16[272,1024]{1,0:T(8,128)(2,1)S(1)}, u32[]{:S(2)}, u32[]{:S(2)}) collective-permute-start(bf16[272,1024]{1,0:T(8,128)(2,1)S(1)} %copy-done.33), channel_id=1, source_target_pairs={{0,1},{1,0},{2,4},{3,5},{4,2},{5,3},{6,7},{7,6},{8,9},{9,8},{10,12... | collective-permute-start | bytes 1671176 | tf_op jit(solution)/shard_map/ppermute | solution.py:338
  76.2 8.1 %shard_map.162 = (bf16[1024,256]{1,0:T(8,128)(2,1)S(1)}, f32[8,1024]{1,0:T(8,128)S(1)}) custom-call(s32[1]{0:T(128)} %bitcast.flat_ref, bf16[1024,768]{1,0:T(8,128)(2,1)S(1)} %get-tuple-element.155.q_ref.k_ref.v_ref, bf16[1024,768]{1,0:T(8,128)(2,1)S(1)} %get-tuple-element.155.q_ref.k_ref.v_ref, bf16[1024,768]{1,0:T(8,128)(2,1)S(1)} %get-tuple-element.155.q_ref.k_ref.v_ref), custom_call_target="tpu_custom_call" | custom-call | flops 42949672 | bytes 52756 | tf_op jit(solution)/shard_map/pallas_call | solution.py:405
  84.4 9.7 %collective-permute-done.18.refs_2_.refs_3_ = bf16[256,2048]{1,0:T(8,128)(2,1)S(1)} collective-permute-done((bf16[256,2048]{1,0:T(8,128)(2,1)S(1)}, bf16[256,2048]{1,0:T(8,128)(2,1)S(1)}, u32[]{:S(2)}, u32[]{:S(2)}) %collective-permute-start.18) | collective-permute-done | bytes 1048608 | tf_op jit(solution)/shard_map/ppermute | solution.py:338
  94.8 2.7 %collective-permute-start.22 = (bf16[272,1024]{1,0:T(8,128)(2,1)S(1)}, bf16[272,1024]{1,0:T(8,128)(2,1)S(1)}, u32[]{:S(2)}, u32[]{:S(2)}) collective-permute-start(bf16[272,1024]{1,0:T(8,128)(2,1)S(1)} %collective-permute-done.21.first), channel_id=1, source_target_pairs={{2,3},{3,2},{4,5},{5,4},{10,11},{11,10},{12,13},{13,12},{18,19},{1... | collective-permute-start | bytes 1671176 | tf_op jit(solution)/shard_map/ppermute | solution.py:338
  101.3 4.1 %collective-permute-done.22.second = bf16[272,1024]{1,0:T(8,128)(2,1)S(1)} collective-permute-done((bf16[272,1024]{1,0:T(8,128)(2,1)S(1)}, bf16[272,1024]{1,0:T(8,128)(2,1)S(1)}, u32[]{:S(2)}, u32[]{:S(2)}) %collective-permute-start.22) | collective-permute-done | bytes 557088 | tf_op jit(solution)/shard_map/ppermute | solution.py:338
  108.1 4.4 %shard_map.163 = (bf16[1024,1024]{1,0:T(8,128)(2,1)S(1)}, f32[256,1024]{1,0:T(8,128)S(1)}) custom-call(s32[1]{0:T(128)} %bitcast.flat_ref, bf16[1024,1024]{1,0:T(8,128)(2,1)S(1)} %get-tuple-element.146.x_ref, bf16[1024,256]{1,0:T(8,128)(2,1)S(1)} %get-tuple-element.164.refs_0_.refs_4_.o_ref, bf16[1024,256]{1,0:T(8,128)(2,1)S(1)} %collective-permute-done.23.refs_1_.refs_5_, ...), custom_call_target="tpu_custom_call" | custom-call | flops 21474836 | bytes 94371 | tf_op jit(solution)/shard_map/pallas_call | solution.py:405
  115.1 7.4 %shard_map.165 = (bf16[1024,656]{1,0:T(8,128)(2,1)S(1)}, bf16[1024,1312]{1,0:T(8,128)(2,1)S(1)}) custom-call(s32[1]{0:T(128)} %bitcast.flat_ref, bf16[1024,1024]{1,0:T(8,128)(2,1)S(1)} %get-tuple-element.167.n_ref, bf16[1024,1024]{1,0:T(8,128)(2,1)S(1)} %shard_map.164.cot_ref, bf16[256,2048]{1,0:T(8,128)(2,1)S(1)} %bitcast.34, ...), custom_call_target="tpu_custom_call" | custom-call | flops 41271952 | bytes 125501 | tf_op jit(solution)/shard_map/pallas_call | solution.py:405
  131.4 7.7 %shard_map.168 = bf16[4,256,2048]{2,1,0:T(8,128)(2,1)} custom-call(s32[1]{0:T(128)} %bitcast.flat_ref, bf16[1024,1024]{1,0:T(8,128)(2,1)S(1)} %get-tuple-element.167.n_ref, bf16[1024,1024]{1,0:T(8,128)(2,1)S(1)} %shard_map.164.cot_ref, bf16[1024,1312]{1,0:T(8,128)(2,1)S(1)} %get-tuple-element.173.refs_0_.d_ref, ...), custom_call_target="tpu_custom_call" | custom-call | flops 41271952 | bytes 124190 | tf_op jit(solution)/shard_map/pallas_call | solution.py:405
  139.1 5.1 %all-to-all-start = ((bf16[4,256,2048]{2,1,0:T(8,128)(2,1)}), bf16[4,256,2048]{2,1,0:T(8,128)(2,1)}, u32[]{:S(2)}, u32[]{:S(2)}) async-start(bf16[4,256,2048]{2,1,0:T(8,128)(2,1)} %shard_map.168), calls=%async_computation | async-start | bytes 8388608 | tf_op jit(solution)/shard_map/all_to_all | solution.py:1179
  149.2 3.1 %shard_map.169 = (bf16[272,1024]{1,0:T(8,128)(2,1)S(1)}, f32[256,1024]{1,0:T(8,128)S(1)}) custom-call(s32[1]{0:T(128)} %bitcast.flat_ref, f32[256,1024]{1,0:T(8,128)S(1)} %copy-done.24, f32[256,1024]{1,0:T(8,128)S(1)} %copy-done.54, bf16[512,1024]{1,0:T(8,128)(2,1)S(1)} %copy-done.31, bf16[272,1024]{1,0:T(8,128)(2,1)} %collective-permute-done.31.c_ref, ...), custom_call_target="tpu_custom_call" | custom-call | bytes 58327 | tf_op jit(solution)/shard_map/pallas_call | solution.py:405
  158.0 8.6 %collective-permute-done.36.refs_1_ = bf16[272,1024]{1,0:T(8,128)(2,1)S(1)} collective-permute-done((bf16[272,1024]{1,0:T(8,128)(2,1)S(1)}, bf16[272,1024]{1,0:T(8,128)(2,1)S(1)}, u32[]{:S(2)}, u32[]{:S(2)}) %collective-permute-start.36) | collective-permute-done | bytes 557088 | tf_op jit(solution)/shard_map/ppermute | solution.py:338
  172.5 14.8 %shard_map.172 = (bf16[1024,256]{1,0:T(8,128)(2,1)S(1)}, bf16[1024,256]{1,0:T(8,128)(2,1)S(1)}, bf16[1024,256]{1,0:T(8,128)(2,1)S(1)}) custom-call(s32[1]{0:T(128)} %bitcast.flat_ref, bf16[1024,768]{1,0:T(8,128)(2,1)S(1)} %get-tuple-element.155.q_ref.k_ref.v_ref, bf16[1024,768]{1,0:T(8,128)(2,1)S(1)} %get-tuple-element.155.q_ref.k_ref.v_ref, ...), custom_call_target="tpu_custom_call" | custom-call | flops 107374184 | bytes 84213 | tf_op jit(solution)/shard_map/pallas_call | solution.py:405
  190.2 5.0 %collective-permute-start.35 = (bf16[256,1024]{1,0:T(8,128)(2,1)}, bf16[256,1024]{1,0:T(8,128)(2,1)}, u32[]{:S(2)}, u32[]{:S(2)}) collective-permute-start(bf16[256,1024]{1,0:T(8,128)(2,1)} %add_convert_fusion.1), channel_id=1, source_target_pairs={{0,0},{1,1},{2,4},{3,5},{4,2},{5,3},{6,6},{7,7},{8,8},{9,9},{10,12... | collective-permute-start | bytes 1572872 | tf_op jit(solution)/shard_map/ppermute | solution.py:338
  197.4 4.2 %shard_map.175 = (bf16[256,1024]{1,0:T(8,128)(2,1)S(1)}, bf16[256,1024]{1,0:T(8,128)(2,1)}, bf16[256,1024]{1,0:T(8,128)(2,1)}, bf16[256,1024]{1,0:T(8,128)(2,1)}) custom-call(s32[1]{0:T(128)} %bitcast.flat_ref, bf16[1024,1024]{1,0:T(8,128)(2,1)S(1)} %copy-done.46, bf16[1024,256]{1,0:T(8,128)(2,1)S(1)} %get-tuple-element.191.refs_0_, ...), custom_call_target="tpu_custom_call" | custom-call | flops 16106127 | bytes 62914 | tf_op jit(solution)/shard_map/pallas_call | solution.py:405
  205.1 2.7 %shard_map.176 = (f32[2,64,2048]{2,1,0:T(8,128)S(1)}, bf16[2,64,2048]{2,1,0:T(8,128)(2,1)S(1)}) custom-call(s32[1]{0:T(128)} %bitcast.flat_ref, bf16[4,2,2,64,2048]{4,3,2,1,0:T(8,128)(2,1)} %bitcast.13.refs_0_), custom_call_target="tpu_custom_call" | custom-call | bytes 57671 | tf_op jit(solution)/shard_map/pallas_call | solution.py:405
  207.8 3.2 %collective-permute-start.43 = (bf16[2,64,2048]{2,1,0:T(8,128)(2,1)S(1)}, bf16[2,64,2048]{2,1,0:T(8,128)(2,1)S(1)}, u32[]{:S(2)}, u32[]{:S(2)}) collective-permute-start(bf16[2,64,2048]{2,1,0:T(8,128)(2,1)S(1)} %get-tuple-element.213), channel_id=1, source_target_pairs={{0,2},{1,3},{2,0},{3,1},{4,6},{5,7},{6,4},{7,5},{8,10},{9,11},{10,... | collective-permute-start | bytes 1572872 | tf_op jit(solution)/shard_map/ppermute | solution.py:338
  211.7 2.9 %collective-permute-done.40 = bf16[256,1024]{1,0:T(8,128)(2,1)S(1)} collective-permute-done((bf16[256,1024]{1,0:T(8,128)(2,1)}, bf16[256,1024]{1,0:T(8,128)(2,1)S(1)}, u32[]{:S(2)}, u32[]{:S(2)}) %collective-permute-start.40) | collective-permute-done | bytes 524320 | tf_op jit(solution)/shard_map/ppermute | solution.py:338
  215.6 11.3 %collective-permute-done.42 = bf16[256,1024]{1,0:T(8,128)(2,1)S(1)} collective-permute-done((bf16[256,1024]{1,0:T(8,128)(2,1)}, bf16[256,1024]{1,0:T(8,128)(2,1)S(1)}, u32[]{:S(2)}, u32[]{:S(2)}) %collective-permute-start.42) | collective-permute-done | bytes 524320 | tf_op jit(solution)/shard_map/ppermute | solution.py:338
  229.3 5.3 %collective-permute-done.43 = bf16[2,64,2048]{2,1,0:T(8,128)(2,1)S(1)} collective-permute-done((bf16[2,64,2048]{2,1,0:T(8,128)(2,1)S(1)}, bf16[2,64,2048]{2,1,0:T(8,128)(2,1)S(1)}, u32[]{:S(2)}, u32[]{:S(2)}) %collective-permute-start.43) | collective-permute-done | bytes 524320 | tf_op jit(solution)/shard_map/ppermute | solution.py:338
  237.6 3.5 %collective-permute-start.46 = (bf16[128,1024]{1,0:T(8,128)(2,1)S(1)}, bf16[128,1024]{1,0:T(8,128)(2,1)S(1)}, u32[]{:S(2)}, u32[]{:S(2)}) collective-permute-start(bf16[128,1024]{1,0:T(8,128)(2,1)S(1)} %get-tuple-element.221), channel_id=1, source_target_pairs={{0,0},{1,1},{2,4},{3,5},{4,2},{5,3},{6,6},{7,7},{8,8},{9,9},{10,12... | collective-permute-start | bytes 786440 | tf_op jit(solution)/shard_map/ppermute | solution.py:338
  241.1 3.0 %collective-permute-start.45 = (bf16[128,1024]{1,0:T(8,128)(2,1)S(1)}, bf16[128,1024]{1,0:T(8,128)(2,1)S(1)}, u32[]{:S(2)}, u32[]{:S(2)}) collective-permute-start(bf16[128,1024]{1,0:T(8,128)(2,1)S(1)} %get-tuple-element.244), channel_id=1, source_target_pairs={{0,0},{1,1},{2,4},{3,5},{4,2},{5,3},{6,6},{7,7},{8,8},{9,9},{10,12... | collective-permute-start | bytes 786440 | tf_op jit(solution)/shard_map/ppermute | solution.py:338
  245.3 7.2 %collective-permute-done.48 = bf16[2,64,1152]{2,1,0:T(8,128)(2,1)S(1)} collective-permute-done((bf16[2,64,1152]{2,1,0:T(8,128)(2,1)S(1)}, bf16[2,64,1152]{2,1,0:T(8,128)(2,1)S(1)}, u32[]{:S(2)}, u32[]{:S(2)}) %collective-permute-start.48) | collective-permute-done | bytes 294944 | tf_op jit(solution)/shard_map/ppermute | solution.py:338
  (271 shorter events, 88.9 us)
Async XLA Ops:
  2.8 16.2 %collective-permute-start.3 = (bf16[272,1024]{1,0:T(8,128)(2,1)S(1)}, bf16[272,1024]{1,0:T(8,128)(2,1)}, u32[]{:S(2)}, u32[]{:S(2)}) collective-permute-start(bf16[272,1024]{1,0:T(8,128)(2,1)S(1)} %get-tuple-element.247.block), channel_id=1, source_target_pairs={{0,1},{1,0},{2,4},{3,5},{4,2},{5,3},{6,7},{7,6},{8,9},{9,8},{10,12... | collective-permute-start | bytes 1671176 | tf_op jit(solution)/shard_map/ppermute | solution.py:338
  6.6 23.0 %collective-permute-start.6 = (bf16[272,1024]{1,0:T(8,128)(2,1)S(1)}, bf16[272,1024]{1,0:T(8,128)(2,1)S(1)}, u32[]{:S(2)}, u32[]{:S(2)}) collective-permute-start(bf16[272,1024]{1,0:T(8,128)(2,1)S(1)} %get-tuple-element.246.block), channel_id=1, source_target_pairs={{0,4},{1,5},{2,6},{3,7},{4,0},{5,1},{6,2},{7,3},{8,12},{9,13},{10,... | collective-permute-start | bytes 1671176 | tf_op jit(solution)/shard_map/ppermute | solution.py:338
  11.3 18.2 %collective-permute-start.5 = (bf16[2,32,2048]{2,1,0:T(8,128)(2,1)S(1)}, bf16[2,32,2048]{2,1,0:T(8,128)(2,1)S(1)}, u32[]{:S(2)}, u32[]{:S(2)}) collective-permute-start(bf16[2,32,2048]{2,1,0:T(8,128)(2,1)S(1)} %get-tuple-element.139), channel_id=1, source_target_pairs={{0,1},{1,0},{2,3},{3,2},{4,5},{5,4},{6,7},{7,6},{8,9},{9,8},{10,11... | collective-permute-start | bytes 786440 | tf_op jit(solution)/shard_map/ppermute | solution.py:338
  21.7 14.2 %collective-permute-start.7 = (bf16[4,32,1024]{2,1,0:T(8,128)(2,1)S(1)}, bf16[4,32,1024]{2,1,0:T(8,128)(2,1)S(1)}, u32[]{:S(2)}, u32[]{:S(2)}) collective-permute-start(bf16[4,32,1024]{2,1,0:T(8,128)(2,1)S(1)} %shard_map.156), channel_id=1, source_target_pairs={{0,2},{1,3},{2,0},{3,1},{4,6},{5,7},{6,4},{7,5},{8,10},{9,11},{10,... | collective-permute-start | bytes 786440 | tf_op jit(solution)/shard_map/ppermute | solution.py:338
  25.5 13.0 %collective-permute-start.8 = (bf16[272,1024]{1,0:T(8,128)(2,1)}, bf16[272,1024]{1,0:T(8,128)(2,1)S(1)}, u32[]{:S(2)}, u32[]{:S(2)}) collective-permute-start(bf16[272,1024]{1,0:T(8,128)(2,1)} %collective-permute-done.3.first), channel_id=1, source_target_pairs={{0,4},{1,5},{2,6},{3,7},{4,0},{5,1},{6,2},{7,3},{8,12},{9,13},{10,... | collective-permute-start | bytes 1671176 | tf_op jit(solution)/shard_map/ppermute | solution.py:338
  25.5 14.6 %collective-permute-start.9 = (bf16[272,1024]{1,0:T(8,128)(2,1)}, bf16[272,1024]{1,0:T(8,128)(2,1)S(1)}, u32[]{:S(2)}, u32[]{:S(2)}) collective-permute-start(bf16[272,1024]{1,0:T(8,128)(2,1)} %collective-permute-done.3.first), channel_id=1, source_target_pairs={{2,3},{3,2},{4,5},{5,4},{10,11},{11,10},{12,13},{13,12},{18,19},{1... | collective-permute-start | bytes 1671176 | tf_op jit(solution)/shard_map/ppermute | solution.py:338
  38.5 31.2 %collective-permute-start.15 = (bf16[4,32,2048]{2,1,0:T(8,128)(2,1)S(1)}, bf16[4,32,2048]{2,1,0:T(8,128)(2,1)S(1)}, u32[]{:S(2)}, u32[]{:S(2)}) collective-permute-start(bf16[4,32,2048]{2,1,0:T(8,128)(2,1)S(1)} %shard_map.157), channel_id=1, source_target_pairs={{0,2},{1,3},{2,0},{3,1},{4,6},{5,7},{6,4},{7,5},{8,10},{9,11},{10,... | collective-permute-start | bytes 1572872 | tf_op jit(solution)/shard_map/ppermute | solution.py:338
  40.1 19.9 %collective-permute-start.10 = (bf16[272,1024]{1,0:T(8,128)(2,1)S(1)}, bf16[272,1024]{1,0:T(8,128)(2,1)S(1)}, u32[]{:S(2)}, u32[]{:S(2)}) collective-permute-start(bf16[272,1024]{1,0:T(8,128)(2,1)S(1)} %collective-permute-done.9.second), channel_id=1, source_target_pairs={{0,4},{1,5},{2,6},{3,7},{4,0},{5,1},{6,2},{7,3},{8,12},{9,13},{10,... | collective-permute-start | bytes 1671176 | tf_op jit(solution)/shard_map/ppermute | solution.py:338
  54.4 20.5 %collective-permute-start.16 = (bf16[1024,256]{1,0:T(8,128)(2,1)S(1)}, bf16[1024,256]{1,0:T(8,128)(2,1)S(1)}, u32[]{:S(2)}, u32[]{:S(2)}) collective-permute-start(bf16[1024,256]{1,0:T(8,128)(2,1)S(1)} %slice_dynamic-update-slice_fusion.3.refs_4_.refs_8_), channel_id=1, source_target_pairs={{0,4},{1,5},{2,6},{3,7},{4,0},{5,1},{6,2},{7,3},{8,12},{9,13},{10,... | collective-permute-start | bytes 1572872 | tf_op jit(solution)/shard_map/ppermute | solution.py:338
  59.7 16.1 %collective-permute-start.17 = (bf16[1024,256]{1,0:T(8,128)(2,1)S(1)}, bf16[1024,256]{1,0:T(8,128)(2,1)S(1)}, u32[]{:S(2)}, u32[]{:S(2)}) collective-permute-start(bf16[1024,256]{1,0:T(8,128)(2,1)S(1)} %slice_dynamic-update-slice_fusion.3.refs_4_.refs_8_), channel_id=1, source_target_pairs={{0,1},{1,0},{2,3},{3,2},{4,5},{5,4},{6,7},{7,6},{8,9},{9,8},{10,11... | collective-permute-start | bytes 1572872 | tf_op jit(solution)/shard_map/ppermute | solution.py:338
  69.8 24.4 %collective-permute-start.18 = (bf16[256,2048]{1,0:T(8,128)(2,1)S(1)}, bf16[256,2048]{1,0:T(8,128)(2,1)S(1)}, u32[]{:S(2)}, u32[]{:S(2)}) collective-permute-start(bf16[256,2048]{1,0:T(8,128)(2,1)S(1)} %bitcast.32), channel_id=1, source_target_pairs={{0,16},{1,17},{2,18},{3,19},{4,20},{5,21},{6,22},{7,23},{8,24},{9,... | collective-permute-start | bytes 3145736 | tf_op jit(solution)/shard_map/ppermute | solution.py:338
  70.8 24.0 %collective-permute-start.20 = (bf16[256,2048]{1,0:T(8,128)(2,1)S(1)}, bf16[256,2048]{1,0:T(8,128)(2,1)S(1)}, u32[]{:S(2)}, u32[]{:S(2)}) collective-permute-start(bf16[256,2048]{1,0:T(8,128)(2,1)S(1)} %bitcast.33), channel_id=1, source_target_pairs={{0,8},{1,9},{2,10},{3,11},{4,12},{5,13},{6,14},{7,15},{8,0},{9,1},... | collective-permute-start | bytes 3145736 | tf_op jit(solution)/shard_map/ppermute | solution.py:338
  71.3 23.5 %collective-permute-start.21 = (bf16[272,1024]{1,0:T(8,128)(2,1)S(1)}, bf16[272,1024]{1,0:T(8,128)(2,1)S(1)}, u32[]{:S(2)}, u32[]{:S(2)}) collective-permute-start(bf16[272,1024]{1,0:T(8,128)(2,1)S(1)} %copy-done.33), channel_id=1, source_target_pairs={{0,1},{1,0},{2,4},{3,5},{4,2},{5,3},{6,7},{7,6},{8,9},{9,8},{10,12... | collective-permute-start | bytes 1671176 | tf_op jit(solution)/shard_map/ppermute | solution.py:338
  75.8 18.4 %collective-permute-start.19 = (bf16[1024,256]{1,0:T(8,128)(2,1)S(1)}, bf16[1024,256]{1,0:T(8,128)(2,1)S(1)}, u32[]{:S(2)}, u32[]{:S(2)}) collective-permute-start(bf16[1024,256]{1,0:T(8,128)(2,1)S(1)} %collective-permute-done.17.refs_5_.refs_9_), channel_id=1, source_target_pairs={{0,4},{1,5},{2,6},{3,7},{4,0},{5,1},{6,2},{7,3},{8,12},{9,13},{10,... | collective-permute-start | bytes 1572872 | tf_op jit(solution)/shard_map/ppermute | solution.py:338
  84.4 14.4 %collective-permute-start.23 = (bf16[1024,256]{1,0:T(8,128)(2,1)S(1)}, bf16[1024,256]{1,0:T(8,128)(2,1)S(1)}, u32[]{:S(2)}, u32[]{:S(2)}) collective-permute-start(bf16[1024,256]{1,0:T(8,128)(2,1)S(1)} %get-tuple-element.164.refs_0_.refs_4_.o_ref), channel_id=1, source_target_pairs={{0,1},{1,0},{2,3},{3,2},{4,5},{5,4},{6,7},{7,6},{8,9},{9,8},{10,11... | collective-permute-start | bytes 1572872 | tf_op jit(solution)/shard_map/ppermute | solution.py:338
  99.4 15.0 %collective-permute-start.28 = (bf16[144,2048]{1,0:T(8,128)(2,1)S(1)}, bf16[144,2048]{1,0:T(8,128)(2,1)S(1)}, u32[]{:S(2)}, u32[]{:S(2)}) collective-permute-start(bf16[144,2048]{1,0:T(8,128)(2,1)S(1)} %slice.94), channel_id=1, source_target_pairs={{0,16},{1,17},{2,18},{3,19},{4,20},{5,21},{6,22},{7,23},{8,24},{9,... | collective-permute-start | bytes 1769480 | tf_op jit(solution)/shard_map/ppermute | solution.py:338
  100.4 14.7 %collective-permute-start.29 = (bf16[144,2048]{1,0:T(8,128)(2,1)S(1)}, bf16[144,2048]{1,0:T(8,128)(2,1)S(1)}, u32[]{:S(2)}, u32[]{:S(2)}) collective-permute-start(bf16[144,2048]{1,0:T(8,128)(2,1)S(1)} %slice.95), channel_id=1, source_target_pairs={{0,8},{1,9},{2,10},{3,11},{4,12},{5,13},{6,14},{7,15},{8,0},{9,1},... | collective-permute-start | bytes 1769480 | tf_op jit(solution)/shard_map/ppermute | solution.py:338
  130.9 14.5 %collective-permute-start.31 = (bf16[272,1024]{1,0:T(8,128)(2,1)}, bf16[272,1024]{1,0:T(8,128)(2,1)}, u32[]{:S(2)}, u32[]{:S(2)}) collective-permute-start(bf16[272,1024]{1,0:T(8,128)(2,1)} %pad.9), channel_id=1, source_target_pairs={{0,1},{1,0},{2,3},{3,2},{4,5},{5,4},{6,7},{7,6},{8,9},{9,8},{10,11... | collective-permute-start | bytes 1671176 | tf_op jit(solution)/shard_map/ppermute | solution.py:338
  139.1 66.1 %all-to-all-start = ((bf16[4,256,2048]{2,1,0:T(8,128)(2,1)}), bf16[4,256,2048]{2,1,0:T(8,128)(2,1)}, u32[]{:S(2)}, u32[]{:S(2)}) async-start(bf16[4,256,2048]{2,1,0:T(8,128)(2,1)} %shard_map.168), calls=%async_computation | async-start | bytes 8388608 | tf_op jit(solution)/shard_map/all_to_all | solution.py:1179
  153.2 13.4 %collective-permute-start.36 = (bf16[272,1024]{1,0:T(8,128)(2,1)S(1)}, bf16[272,1024]{1,0:T(8,128)(2,1)S(1)}, u32[]{:S(2)}, u32[]{:S(2)}) collective-permute-start(bf16[272,1024]{1,0:T(8,128)(2,1)S(1)} %get-tuple-element.184.refs_0_), channel_id=1, source_target_pairs={{0,1},{1,0},{2,3},{3,2},{4,5},{5,4},{6,7},{7,6},{8,9},{9,8},{10,11... | collective-permute-start | bytes 1671176 | tf_op jit(solution)/shard_map/ppermute | solution.py:338
  157.6 29.7 %collective-permute-start.32 = (bf16[256,1024]{1,0:T(8,128)(2,1)S(1)}, bf16[256,1024]{1,0:T(8,128)(2,1)S(1)}, u32[]{:S(2)}, u32[]{:S(2)}) collective-permute-start(bf16[256,1024]{1,0:T(8,128)(2,1)S(1)} %get-tuple-element.242), channel_id=1, source_target_pairs={{0,4},{1,5},{2,6},{3,7},{4,0},{5,1},{6,2},{7,3},{8,12},{9,13},{10,... | collective-permute-start | bytes 1572872 | tf_op jit(solution)/shard_map/ppermute | solution.py:338
  168.4 18.8 %collective-permute-start.34 = (bf16[256,1024]{1,0:T(8,128)(2,1)S(1)}, bf16[256,1024]{1,0:T(8,128)(2,1)S(1)}, u32[]{:S(2)}, u32[]{:S(2)}) collective-permute-start(bf16[256,1024]{1,0:T(8,128)(2,1)S(1)} %add_convert_fusion.2), channel_id=1, source_target_pairs={{0,1},{1,0},{2,3},{3,2},{4,5},{5,4},{6,7},{7,6},{8,9},{9,8},{10,11... | collective-permute-start | bytes 1572872 | tf_op jit(solution)/shard_map/ppermute | solution.py:338
  188.6 15.5 %collective-permute-start.39 = (bf16[512,1024]{1,0:T(8,128)(2,1)S(1)}, bf16[512,1024]{1,0:T(8,128)(2,1)S(1)}, u32[]{:S(2)}, u32[]{:S(2)}) collective-permute-start(bf16[512,1024]{1,0:T(8,128)(2,1)S(1)} %shard_map.173), channel_id=1, source_target_pairs={{0,4},{1,5},{2,6},{3,7},{4,0},{5,1},{6,2},{7,3},{8,12},{9,13},{10,... | collective-permute-start | bytes 3145736 | tf_op jit(solution)/shard_map/ppermute | solution.py:338
  190.2 20.8 %collective-permute-start.35 = (bf16[256,1024]{1,0:T(8,128)(2,1)}, bf16[256,1024]{1,0:T(8,128)(2,1)}, u32[]{:S(2)}, u32[]{:S(2)}) collective-permute-start(bf16[256,1024]{1,0:T(8,128)(2,1)} %add_convert_fusion.1), channel_id=1, source_target_pairs={{0,0},{1,1},{2,4},{3,5},{4,2},{5,3},{6,6},{7,7},{8,8},{9,9},{10,12... | collective-permute-start | bytes 1572872 | tf_op jit(solution)/shard_map/ppermute | solution.py:338
  201.5 13.0 %collective-permute-start.40 = (bf16[256,1024]{1,0:T(8,128)(2,1)}, bf16[256,1024]{1,0:T(8,128)(2,1)S(1)}, u32[]{:S(2)}, u32[]{:S(2)}) collective-permute-start(bf16[256,1024]{1,0:T(8,128)(2,1)} %get-tuple-element.207), channel_id=1, source_target_pairs={{0,8},{1,9},{2,10},{3,11},{4,12},{5,13},{6,14},{7,15},{8,0},{9,1},... | collective-permute-start | bytes 1572872 | tf_op jit(solution)/shard_map/ppermute | solution.py:338
  202.7 12.8 %collective-permute-start.41 = (bf16[256,1024]{1,0:T(8,128)(2,1)}, bf16[256,1024]{1,0:T(8,128)(2,1)S(1)}, u32[]{:S(2)}, u32[]{:S(2)}) collective-permute-start(bf16[256,1024]{1,0:T(8,128)(2,1)} %get-tuple-element.208), channel_id=1, source_target_pairs={{0,16},{1,17},{2,18},{3,19},{4,20},{5,21},{6,22},{7,23},{8,24},{9,... | collective-permute-start | bytes 1572872 | tf_op jit(solution)/shard_map/ppermute | solution.py:338
  203.9 23.0 %collective-permute-start.42 = (bf16[256,1024]{1,0:T(8,128)(2,1)}, bf16[256,1024]{1,0:T(8,128)(2,1)S(1)}, u32[]{:S(2)}, u32[]{:S(2)}) collective-permute-start(bf16[256,1024]{1,0:T(8,128)(2,1)} %get-tuple-element.209), channel_id=1, source_target_pairs={{0,24},{1,25},{2,26},{3,27},{4,28},{5,29},{6,30},{7,31},{8,16},{9,... | collective-permute-start | bytes 1572872 | tf_op jit(solution)/shard_map/ppermute | solution.py:338
  207.8 26.9 %collective-permute-start.43 = (bf16[2,64,2048]{2,1,0:T(8,128)(2,1)S(1)}, bf16[2,64,2048]{2,1,0:T(8,128)(2,1)S(1)}, u32[]{:S(2)}, u32[]{:S(2)}) collective-permute-start(bf16[2,64,2048]{2,1,0:T(8,128)(2,1)S(1)} %get-tuple-element.213), channel_id=1, source_target_pairs={{0,2},{1,3},{2,0},{3,1},{4,6},{5,7},{6,4},{7,5},{8,10},{9,11},{10,... | collective-permute-start | bytes 1572872 | tf_op jit(solution)/shard_map/ppermute | solution.py:338
  211.0 23.7 %collective-permute-start.44 = (bf16[256,1024]{1,0:T(8,128)(2,1)S(1)}, bf16[256,1024]{1,0:T(8,128)(2,1)S(1)}, u32[]{:S(2)}, u32[]{:S(2)}) collective-permute-start(bf16[256,1024]{1,0:T(8,128)(2,1)S(1)} %copy-done.65), channel_id=1, source_target_pairs={{0,1},{1,0},{2,3},{3,2},{4,5},{5,4},{6,7},{7,6},{8,9},{9,8},{10,11... | collective-permute-start | bytes 1572872 | tf_op jit(solution)/shard_map/ppermute | solution.py:338
  227.2 25.3 %collective-permute-start.48 = (bf16[2,64,1152]{2,1,0:T(8,128)(2,1)S(1)}, bf16[2,64,1152]{2,1,0:T(8,128)(2,1)S(1)}, u32[]{:S(2)}, u32[]{:S(2)}) collective-permute-start(bf16[2,64,1152]{2,1,0:T(8,128)(2,1)S(1)} %get-tuple-element.224), channel_id=1, source_target_pairs={{0,2},{1,3},{2,0},{3,1},{4,6},{5,7},{6,4},{7,5},{8,10},{9,11},{10,... | collective-permute-start | bytes 884744 | tf_op jit(solution)/shard_map/ppermute | solution.py:338
  237.6 24.8 %collective-permute-start.46 = (bf16[128,1024]{1,0:T(8,128)(2,1)S(1)}, bf16[128,1024]{1,0:T(8,128)(2,1)S(1)}, u32[]{:S(2)}, u32[]{:S(2)}) collective-permute-start(bf16[128,1024]{1,0:T(8,128)(2,1)S(1)} %get-tuple-element.221), channel_id=1, source_target_pairs={{0,0},{1,1},{2,4},{3,5},{4,2},{5,3},{6,6},{7,7},{8,8},{9,9},{10,12... | collective-permute-start | bytes 786440 | tf_op jit(solution)/shard_map/ppermute | solution.py:338
  241.1 21.3 %collective-permute-start.45 = (bf16[128,1024]{1,0:T(8,128)(2,1)S(1)}, bf16[128,1024]{1,0:T(8,128)(2,1)S(1)}, u32[]{:S(2)}, u32[]{:S(2)}) collective-permute-start(bf16[128,1024]{1,0:T(8,128)(2,1)S(1)} %get-tuple-element.244), channel_id=1, source_target_pairs={{0,0},{1,1},{2,4},{3,5},{4,2},{5,3},{6,6},{7,7},{8,8},{9,9},{10,12... | collective-permute-start | bytes 786440 | tf_op jit(solution)/shard_map/ppermute | solution.py:338
  (89 other events, 1056.1 us)

commit v8 on v7

--- a/solution.py
+++ b/solution.py
@@ -733,16 +733,17 @@
     rows, width, columns = tokens // 2, 4 * piece, grad.shape[1]
 
     def body(flat_ref, grad_ref, *refs):
-        weights, (far_ref, near_ref) = refs[:5], refs[5:]
+        weights, (far_ref, own_ref, other_ref) = refs[:5], refs[5:]
         square = square_of(flat_ref[0])
         for span, w in zip(spans(pieces), weights):
             total = mm_t(grad_ref[...], w[rows_of(w, span), first : first + columns])
-            near_ref[:, span_of(square, span, piece)] = total[:rows]
+            own_ref[:, span_of(square, span, piece)] = total[: rows // 2]
+            other_ref[:, span_of(square, span, piece)] = total[rows // 2 : rows]
             far_ref[:, span_of(square, span, piece)] = total[rows:].astype(LOW)
 
     return run(
         body, order, (1,), [whole(grad)] + [whole(p) for p in pieces],
-        [whole(shape_of(rows, width)), whole(shape_of(rows, width, dtype=WIDE))],
+        [whole(shape_of(rows, width))] + [whole(shape_of(rows // 2, width, dtype=WIDE))] * 2,
         flops=2 * tokens * width * columns,
     )
 
@@ -1184,10 +1185,10 @@
         )
     d_side = go("dz", d_low, TO_ZL)
     d_core = go("dc", d_low, TO_CORE)
-    out_far, out_near = back_both(order, hidden, 2 * ff, two)
+    out_far, out_near, out_other = back_both(order, hidden, 2 * ff, two)
     at(14)
     out_far = [go("ofa", out_far[:tokens], TO_CORE), go("ofb", out_far[tokens:], TO_CORE)]
-    out_side = (out_near[tokens:] + out_far[1].astype(WIDE)).astype(LOW)
+    out_side = (out_other + out_far[1].astype(WIDE)).astype(LOW)
     out_side = go("oz", out_side, TO_ZL)
     d_all = [d_low, d_side, d_core, go("df", d_side, TO_CORE)]
     at(15)
@@ -1198,7 +1199,7 @@
     grads = [(d, t * part) for t, d in enumerate(d_mixed)]
     far = go("m1c", back_half(order, grads, one, True)[0], TO_CORE)
     at(18)
-    output = resid + out_near[:tokens] + out_far[0].astype(WIDE) + out_side.astype(WIDE)
+    output = resid + out_near + out_far[0].astype(WIDE) + out_side.astype(WIDE)
     output = output.astype(LOW)
     if "out" in TIED:
         wait(order, output)

time: 267 us -> 267 us (level)
  no operation moved by 1% of the time
where the time goes in v8:
time: 267 us; the launch traced here: 265 us
  waiting for transfers between devices  90.2 us (34%)
  Pallas kernels  77.1 us (29%)
  starting transfers between devices  74.9 us (28%)
  local copies, waits for them, and re-layouts  13.1 us (5%)
  other arithmetic  8.07 us (3%)
    ppermute x54, waiting for transfers between devices, send(): return lax.ppermute(array, FLAT, pairs)  90.2 us
    pallas_call x31, Pallas kernels, run(): pl.pallas_call(body, grid_spec=pltpu.PrefetchScalarGridSpec(num_scalar_pr...  77.1 us
    ppermute x54, starting transfers between devices, send(): return lax.ppermute(array, FLAT, pairs)  69.8 us
    unnamed x139, local copies, waits for them, and re-layouts  10.8 us
  transfers between devices with their start and end apart: 55, of which 27 were waited for; matrix products, arithmetic and copies ran while one was open for 2% of the time, Pallas kernels for 25%

profile of v8, /device:TPU:1, one launch (start us, length us, event | category | flops | bytes accessed | tf_op | source)
XLA Modules:
  0.0 265.1 jit_solution(454640272606112635)
XLA Ops:
  2.8 3.8 %collective-permute-start.3 = (bf16[272,1024]{1,0:T(8,128)(2,1)S(1)}, bf16[272,1024]{1,0:T(8,128)(2,1)}, u32[]{:S(2)}, u32[]{:S(2)}) collective-permute-start(bf16[272,1024]{1,0:T(8,128)(2,1)S(1)} %get-tuple-element.249.block), channel_id=1, source_target_pairs={{0,1},{1,0},{2,4},{3,5},{4,2},{5,3},{6,7},{7,6},{8,9},{9,8},{10,12... | collective-permute-start | bytes 1671176 | tf_op jit(solution)/shard_map/ppermute | solution.py:338
  11.5 7.4 %collective-permute-done.3.first = bf16[272,1024]{1,0:T(8,128)(2,1)} collective-permute-done((bf16[272,1024]{1,0:T(8,128)(2,1)S(1)}, bf16[272,1024]{1,0:T(8,128)(2,1)}, u32[]{:S(2)}, u32[]{:S(2)}) %collective-permute-start.3) | collective-permute-done | bytes 557088 | tf_op jit(solution)/shard_map/ppermute | solution.py:338
  19.0 2.8 %collective-permute-done.4.received_ref = bf16[2,32,1024]{2,1,0:T(8,128)(2,1)S(1)} collective-permute-done((bf16[2,32,1024]{2,1,0:T(8,128)(2,1)S(1)}, bf16[2,32,1024]{2,1,0:T(8,128)(2,1)S(1)}, u32[]{:S(2)}, u32[]{:S(2)}) %collective-permute-start.4) | collective-permute-done | bytes 131104 | tf_op jit(solution)/shard_map/ppermute | solution.py:338
  21.7 3.8 %collective-permute-start.7 = (bf16[4,32,1024]{2,1,0:T(8,128)(2,1)S(1)}, bf16[4,32,1024]{2,1,0:T(8,128)(2,1)S(1)}, u32[]{:S(2)}, u32[]{:S(2)}) collective-permute-start(bf16[4,32,1024]{2,1,0:T(8,128)(2,1)S(1)} %shard_map.156), channel_id=1, source_target_pairs={{0,2},{1,3},{2,0},{3,1},{4,6},{5,7},{6,4},{7,5},{8,10},{9,11},{10,... | collective-permute-start | bytes 786440 | tf_op jit(solution)/shard_map/ppermute | solution.py:338
  25.5 4.0 %collective-permute-start.9 = (bf16[272,1024]{1,0:T(8,128)(2,1)}, bf16[272,1024]{1,0:T(8,128)(2,1)S(1)}, u32[]{:S(2)}, u32[]{:S(2)}) collective-permute-start(bf16[272,1024]{1,0:T(8,128)(2,1)} %collective-permute-done.3.first), channel_id=1, source_target_pairs={{2,3},{3,2},{4,5},{5,4},{10,11},{11,10},{12,13},{13,12},{18,19},{1... | collective-permute-start | bytes 1671176 | tf_op jit(solution)/shard_map/ppermute | solution.py:338
  30.4 5.5 %collective-permute-done.7 = bf16[4,32,1024]{2,1,0:T(8,128)(2,1)S(1)} collective-permute-done((bf16[4,32,1024]{2,1,0:T(8,128)(2,1)S(1)}, bf16[4,32,1024]{2,1,0:T(8,128)(2,1)S(1)}, u32[]{:S(2)}, u32[]{:S(2)}) %collective-permute-start.7) | collective-permute-done | bytes 262176 | tf_op jit(solution)/shard_map/ppermute | solution.py:338
  41.8 5.1 %collective-permute-done.12.refs_2_.refs_5_ = bf16[256,1024]{1,0:T(8,128)(2,1)S(1)} collective-permute-done((bf16[256,1024]{1,0:T(8,128)(2,1)S(1)}, bf16[256,1024]{1,0:T(8,128)(2,1)S(1)}, u32[]{:S(2)}, u32[]{:S(2)}) %collective-permute-start.12) | collective-permute-done | bytes 524320 | tf_op jit(solution)/shard_map/ppermute | solution.py:338
  49.5 4.2 %collective-permute-done.13.refs_3_.refs_6_ = bf16[128,1024]{1,0:T(8,128)(2,1)S(1)} collective-permute-done((bf16[128,1024]{1,0:T(8,128)(2,1)S(1)}, bf16[128,1024]{1,0:T(8,128)(2,1)S(1)}, u32[]{:S(2)}, u32[]{:S(2)}) %collective-permute-start.13) | collective-permute-done | bytes 262176 | tf_op jit(solution)/shard_map/ppermute | solution.py:338
  54.4 5.3 %collective-permute-start.16 = (bf16[1024,256]{1,0:T(8,128)(2,1)S(1)}, bf16[1024,256]{1,0:T(8,128)(2,1)S(1)}, u32[]{:S(2)}, u32[]{:S(2)}) collective-permute-start(bf16[1024,256]{1,0:T(8,128)(2,1)S(1)} %slice_dynamic-update-slice_fusion.3.refs_4_.refs_8_), channel_id=1, source_target_pairs={{0,4},{1,5},{2,6},{3,7},{4,0},{5,1},{6,2},{7,3},{8,12},{9,13},{10,... | collective-permute-start | bytes 1572872 | tf_op jit(solution)/shard_map/ppermute | solution.py:338
  64.4 5.2 %shard_map.160 = (bf16[1024,1024]{1,0:T(8,128)(2,1)}, bf16[1024,768]{1,0:T(8,128)(2,1)S(1)}) custom-call(s32[1]{0:T(128)} %bitcast.flat_ref, bf16[1024,1024]{1,0:T(8,128)(2,1)S(1)} %get-tuple-element.147.x_ref, bf16[256,1024]{1,0:T(8,128)(2,1)S(1)} %bitcast.41, bf16[256,1024]{1,0:T(8,128)(2,1)S(1)} %collective-permute-done.11.refs_1_.refs_4_, ...), custom_call_target="tpu_custom_call" | custom-call | flops 16106127 | bytes 89128 | tf_op jit(solution)/shard_map/pallas_call | solution.py:405
  71.3 3.6 %collective-permute-start.21 = (bf16[272,1024]{1,0:T(8,128)(2,1)S(1)}, bf16[272,1024]{1,0:T(8,128)(2,1)S(1)}, u32[]{:S(2)}, u32[]{:S(2)}) collective-permute-start(bf16[272,1024]{1,0:T(8,128)(2,1)S(1)} %copy-done.33), channel_id=1, source_target_pairs={{0,1},{1,0},{2,4},{3,5},{4,2},{5,3},{6,7},{7,6},{8,9},{9,8},{10,12... | collective-permute-start | bytes 1671176 | tf_op jit(solution)/shard_map/ppermute | solution.py:338
  76.2 8.1 %shard_map.162 = (bf16[1024,256]{1,0:T(8,128)(2,1)S(1)}, f32[8,1024]{1,0:T(8,128)S(1)}) custom-call(s32[1]{0:T(128)} %bitcast.flat_ref, bf16[1024,768]{1,0:T(8,128)(2,1)S(1)} %get-tuple-element.156.q_ref.k_ref.v_ref, bf16[1024,768]{1,0:T(8,128)(2,1)S(1)} %get-tuple-element.156.q_ref.k_ref.v_ref, bf16[1024,768]{1,0:T(8,128)(2,1)S(1)} %get-tuple-element.156.q_ref.k_ref.v_ref), custom_call_target="tpu_custom_call" | custom-call | flops 42949672 | bytes 52756 | tf_op jit(solution)/shard_map/pallas_call | solution.py:405
  84.4 9.7 %collective-permute-done.18.refs_2_.refs_3_ = bf16[256,2048]{1,0:T(8,128)(2,1)S(1)} collective-permute-done((bf16[256,2048]{1,0:T(8,128)(2,1)S(1)}, bf16[256,2048]{1,0:T(8,128)(2,1)S(1)}, u32[]{:S(2)}, u32[]{:S(2)}) %collective-permute-start.18) | collective-permute-done | bytes 1048608 | tf_op jit(solution)/shard_map/ppermute | solution.py:338
  94.8 2.7 %collective-permute-start.22 = (bf16[272,1024]{1,0:T(8,128)(2,1)S(1)}, bf16[272,1024]{1,0:T(8,128)(2,1)S(1)}, u32[]{:S(2)}, u32[]{:S(2)}) collective-permute-start(bf16[272,1024]{1,0:T(8,128)(2,1)S(1)} %collective-permute-done.21.first), channel_id=1, source_target_pairs={{2,3},{3,2},{4,5},{5,4},{10,11},{11,10},{12,13},{13,12},{18,19},{1... | collective-permute-start | bytes 1671176 | tf_op jit(solution)/shard_map/ppermute | solution.py:338
  101.3 4.1 %collective-permute-done.22.second = bf16[272,1024]{1,0:T(8,128)(2,1)S(1)} collective-permute-done((bf16[272,1024]{1,0:T(8,128)(2,1)S(1)}, bf16[272,1024]{1,0:T(8,128)(2,1)S(1)}, u32[]{:S(2)}, u32[]{:S(2)}) %collective-permute-start.22) | collective-permute-done | bytes 557088 | tf_op jit(solution)/shard_map/ppermute | solution.py:338
  108.1 4.4 %shard_map.163 = (bf16[1024,1024]{1,0:T(8,128)(2,1)S(1)}, f32[256,1024]{1,0:T(8,128)S(1)}) custom-call(s32[1]{0:T(128)} %bitcast.flat_ref, bf16[1024,1024]{1,0:T(8,128)(2,1)S(1)} %get-tuple-element.147.x_ref, bf16[1024,256]{1,0:T(8,128)(2,1)S(1)} %get-tuple-element.165.refs_0_.refs_4_.o_ref, bf16[1024,256]{1,0:T(8,128)(2,1)S(1)} %collective-permute-done.23.refs_1_.refs_5_, ...), custom_call_target="tpu_custom_call" | custom-call | flops 21474836 | bytes 94371 | tf_op jit(solution)/shard_map/pallas_call | solution.py:405
  115.1 7.4 %shard_map.165 = (bf16[1024,656]{1,0:T(8,128)(2,1)S(1)}, bf16[1024,1312]{1,0:T(8,128)(2,1)S(1)}) custom-call(s32[1]{0:T(128)} %bitcast.flat_ref, bf16[1024,1024]{1,0:T(8,128)(2,1)S(1)} %get-tuple-element.168.n_ref, bf16[1024,1024]{1,0:T(8,128)(2,1)S(1)} %shard_map.164.cot_ref, bf16[256,2048]{1,0:T(8,128)(2,1)S(1)} %bitcast.34, ...), custom_call_target="tpu_custom_call" | custom-call | flops 41271952 | bytes 125501 | tf_op jit(solution)/shard_map/pallas_call | solution.py:405
  131.4 7.7 %shard_map.168 = bf16[4,256,2048]{2,1,0:T(8,128)(2,1)} custom-call(s32[1]{0:T(128)} %bitcast.flat_ref, bf16[1024,1024]{1,0:T(8,128)(2,1)S(1)} %get-tuple-element.168.n_ref, bf16[1024,1024]{1,0:T(8,128)(2,1)S(1)} %shard_map.164.cot_ref, bf16[1024,1312]{1,0:T(8,128)(2,1)S(1)} %get-tuple-element.174.refs_0_.d_ref, ...), custom_call_target="tpu_custom_call" | custom-call | flops 41271952 | bytes 124190 | tf_op jit(solution)/shard_map/pallas_call | solution.py:405
  139.1 5.1 %all-to-all-start = ((bf16[4,256,2048]{2,1,0:T(8,128)(2,1)}), bf16[4,256,2048]{2,1,0:T(8,128)(2,1)}, u32[]{:S(2)}, u32[]{:S(2)}) async-start(bf16[4,256,2048]{2,1,0:T(8,128)(2,1)} %shard_map.168), calls=%async_computation | async-start | bytes 8388608 | tf_op jit(solution)/shard_map/all_to_all | solution.py:1180
  149.2 3.1 %shard_map.169 = (bf16[272,1024]{1,0:T(8,128)(2,1)S(1)}, f32[256,1024]{1,0:T(8,128)S(1)}) custom-call(s32[1]{0:T(128)} %bitcast.flat_ref, f32[256,1024]{1,0:T(8,128)S(1)} %copy-done.24, f32[256,1024]{1,0:T(8,128)S(1)} %copy-done.54, bf16[512,1024]{1,0:T(8,128)(2,1)S(1)} %copy-done.31, bf16[272,1024]{1,0:T(8,128)(2,1)} %collective-permute-done.31.c_ref, ...), custom_call_target="tpu_custom_call" | custom-call | bytes 58327 | tf_op jit(solution)/shard_map/pallas_call | solution.py:405
  158.0 8.7 %collective-permute-done.36.refs_1_ = bf16[272,1024]{1,0:T(8,128)(2,1)S(1)} collective-permute-done((bf16[272,1024]{1,0:T(8,128)(2,1)S(1)}, bf16[272,1024]{1,0:T(8,128)(2,1)S(1)}, u32[]{:S(2)}, u32[]{:S(2)}) %collective-permute-start.36) | collective-permute-done | bytes 557088 | tf_op jit(solution)/shard_map/ppermute | solution.py:338
  172.5 14.8 %shard_map.172 = (bf16[1024,256]{1,0:T(8,128)(2,1)S(1)}, bf16[1024,256]{1,0:T(8,128)(2,1)S(1)}, bf16[1024,256]{1,0:T(8,128)(2,1)S(1)}) custom-call(s32[1]{0:T(128)} %bitcast.flat_ref, bf16[1024,768]{1,0:T(8,128)(2,1)S(1)} %get-tuple-element.156.q_ref.k_ref.v_ref, bf16[1024,768]{1,0:T(8,128)(2,1)S(1)} %get-tuple-element.156.q_ref.k_ref.v_ref, ...), custom_call_target="tpu_custom_call" | custom-call | flops 107374184 | bytes 84213 | tf_op jit(solution)/shard_map/pallas_call | solution.py:405
  190.2 5.0 %collective-permute-start.35 = (bf16[256,1024]{1,0:T(8,128)(2,1)}, bf16[256,1024]{1,0:T(8,128)(2,1)}, u32[]{:S(2)}, u32[]{:S(2)}) collective-permute-start(bf16[256,1024]{1,0:T(8,128)(2,1)} %add_convert_fusion.1), channel_id=1, source_target_pairs={{0,0},{1,1},{2,4},{3,5},{4,2},{5,3},{6,6},{7,7},{8,8},{9,9},{10,12... | collective-permute-start | bytes 1572872 | tf_op jit(solution)/shard_map/ppermute | solution.py:338
  197.4 4.2 %shard_map.175 = (bf16[256,1024]{1,0:T(8,128)(2,1)S(1)}, bf16[256,1024]{1,0:T(8,128)(2,1)}, bf16[256,1024]{1,0:T(8,128)(2,1)}, bf16[256,1024]{1,0:T(8,128)(2,1)}) custom-call(s32[1]{0:T(128)} %bitcast.flat_ref, bf16[1024,1024]{1,0:T(8,128)(2,1)S(1)} %copy-done.46, bf16[1024,256]{1,0:T(8,128)(2,1)S(1)} %get-tuple-element.193.refs_0_, ...), custom_call_target="tpu_custom_call" | custom-call | flops 16106127 | bytes 62914 | tf_op jit(solution)/shard_map/pallas_call | solution.py:405
  205.1 2.7 %shard_map.176 = (f32[2,64,2048]{2,1,0:T(8,128)S(1)}, bf16[2,64,2048]{2,1,0:T(8,128)(2,1)S(1)}) custom-call(s32[1]{0:T(128)} %bitcast.flat_ref, bf16[4,2,2,64,2048]{4,3,2,1,0:T(8,128)(2,1)} %bitcast.13.refs_0_), custom_call_target="tpu_custom_call" | custom-call | bytes 57671 | tf_op jit(solution)/shard_map/pallas_call | solution.py:405
  207.8 3.2 %collective-permute-start.43 = (bf16[2,64,2048]{2,1,0:T(8,128)(2,1)S(1)}, bf16[2,64,2048]{2,1,0:T(8,128)(2,1)S(1)}, u32[]{:S(2)}, u32[]{:S(2)}) collective-permute-start(bf16[2,64,2048]{2,1,0:T(8,128)(2,1)S(1)} %get-tuple-element.215), channel_id=1, source_target_pairs={{0,2},{1,3},{2,0},{3,1},{4,6},{5,7},{6,4},{7,5},{8,10},{9,11},{10,... | collective-permute-start | bytes 1572872 | tf_op jit(solution)/shard_map/ppermute | solution.py:338
  211.7 2.9 %collective-permute-done.40 = bf16[256,1024]{1,0:T(8,128)(2,1)S(1)} collective-permute-done((bf16[256,1024]{1,0:T(8,128)(2,1)}, bf16[256,1024]{1,0:T(8,128)(2,1)S(1)}, u32[]{:S(2)}, u32[]{:S(2)}) %collective-permute-start.40) | collective-permute-done | bytes 524320 | tf_op jit(solution)/shard_map/ppermute | solution.py:338
  215.6 11.3 %collective-permute-done.42 = bf16[256,1024]{1,0:T(8,128)(2,1)S(1)} collective-permute-done((bf16[256,1024]{1,0:T(8,128)(2,1)}, bf16[256,1024]{1,0:T(8,128)(2,1)S(1)}, u32[]{:S(2)}, u32[]{:S(2)}) %collective-permute-start.42) | collective-permute-done | bytes 524320 | tf_op jit(solution)/shard_map/ppermute | solution.py:338
  229.3 5.3 %collective-permute-done.43 = bf16[2,64,2048]{2,1,0:T(8,128)(2,1)S(1)} collective-permute-done((bf16[2,64,2048]{2,1,0:T(8,128)(2,1)S(1)}, bf16[2,64,2048]{2,1,0:T(8,128)(2,1)S(1)}, u32[]{:S(2)}, u32[]{:S(2)}) %collective-permute-start.43) | collective-permute-done | bytes 524320 | tf_op jit(solution)/shard_map/ppermute | solution.py:338
  237.6 3.5 %collective-permute-start.46 = (bf16[128,1024]{1,0:T(8,128)(2,1)S(1)}, bf16[128,1024]{1,0:T(8,128)(2,1)S(1)}, u32[]{:S(2)}, u32[]{:S(2)}) collective-permute-start(bf16[128,1024]{1,0:T(8,128)(2,1)S(1)} %get-tuple-element.223), channel_id=1, source_target_pairs={{0,0},{1,1},{2,4},{3,5},{4,2},{5,3},{6,6},{7,7},{8,8},{9,9},{10,12... | collective-permute-start | bytes 786440 | tf_op jit(solution)/shard_map/ppermute | solution.py:338
  241.1 3.0 %collective-permute-start.45 = (bf16[128,1024]{1,0:T(8,128)(2,1)S(1)}, bf16[128,1024]{1,0:T(8,128)(2,1)S(1)}, u32[]{:S(2)}, u32[]{:S(2)}) collective-permute-start(bf16[128,1024]{1,0:T(8,128)(2,1)S(1)} %get-tuple-element.246), channel_id=1, source_target_pairs={{0,0},{1,1},{2,4},{3,5},{4,2},{5,3},{6,6},{7,7},{8,8},{9,9},{10,12... | collective-permute-start | bytes 786440 | tf_op jit(solution)/shard_map/ppermute | solution.py:338
  245.3 7.2 %collective-permute-done.48 = bf16[2,64,1152]{2,1,0:T(8,128)(2,1)S(1)} collective-permute-done((bf16[2,64,1152]{2,1,0:T(8,128)(2,1)S(1)}, bf16[2,64,1152]{2,1,0:T(8,128)(2,1)S(1)}, u32[]{:S(2)}, u32[]{:S(2)}) %collective-permute-start.48) | collective-permute-done | bytes 294944 | tf_op jit(solution)/shard_map/ppermute | solution.py:338
  (271 shorter events, 88.9 us)
Async XLA Ops:
  2.8 16.2 %collective-permute-start.3 = (bf16[272,1024]{1,0:T(8,128)(2,1)S(1)}, bf16[272,1024]{1,0:T(8,128)(2,1)}, u32[]{:S(2)}, u32[]{:S(2)}) collective-permute-start(bf16[272,1024]{1,0:T(8,128)(2,1)S(1)} %get-tuple-element.249.block), channel_id=1, source_target_pairs={{0,1},{1,0},{2,4},{3,5},{4,2},{5,3},{6,7},{7,6},{8,9},{9,8},{10,12... | collective-permute-start | bytes 1671176 | tf_op jit(solution)/shard_map/ppermute | solution.py:338
  6.6 23.0 %collective-permute-start.6 = (bf16[272,1024]{1,0:T(8,128)(2,1)S(1)}, bf16[272,1024]{1,0:T(8,128)(2,1)S(1)}, u32[]{:S(2)}, u32[]{:S(2)}) collective-permute-start(bf16[272,1024]{1,0:T(8,128)(2,1)S(1)} %get-tuple-element.248.block), channel_id=1, source_target_pairs={{0,4},{1,5},{2,6},{3,7},{4,0},{5,1},{6,2},{7,3},{8,12},{9,13},{10,... | collective-permute-start | bytes 1671176 | tf_op jit(solution)/shard_map/ppermute | solution.py:338
  11.3 18.2 %collective-permute-start.5 = (bf16[2,32,2048]{2,1,0:T(8,128)(2,1)S(1)}, bf16[2,32,2048]{2,1,0:T(8,128)(2,1)S(1)}, u32[]{:S(2)}, u32[]{:S(2)}) collective-permute-start(bf16[2,32,2048]{2,1,0:T(8,128)(2,1)S(1)} %get-tuple-element.140), channel_id=1, source_target_pairs={{0,1},{1,0},{2,3},{3,2},{4,5},{5,4},{6,7},{7,6},{8,9},{9,8},{10,11... | collective-permute-start | bytes 786440 | tf_op jit(solution)/shard_map/ppermute | solution.py:338
  21.7 14.2 %collective-permute-start.7 = (bf16[4,32,1024]{2,1,0:T(8,128)(2,1)S(1)}, bf16[4,32,1024]{2,1,0:T(8,128)(2,1)S(1)}, u32[]{:S(2)}, u32[]{:S(2)}) collective-permute-start(bf16[4,32,1024]{2,1,0:T(8,128)(2,1)S(1)} %shard_map.156), channel_id=1, source_target_pairs={{0,2},{1,3},{2,0},{3,1},{4,6},{5,7},{6,4},{7,5},{8,10},{9,11},{10,... | collective-permute-start | bytes 786440 | tf_op jit(solution)/shard_map/ppermute | solution.py:338
  25.5 13.0 %collective-permute-start.8 = (bf16[272,1024]{1,0:T(8,128)(2,1)}, bf16[272,1024]{1,0:T(8,128)(2,1)S(1)}, u32[]{:S(2)}, u32[]{:S(2)}) collective-permute-start(bf16[272,1024]{1,0:T(8,128)(2,1)} %collective-permute-done.3.first), channel_id=1, source_target_pairs={{0,4},{1,5},{2,6},{3,7},{4,0},{5,1},{6,2},{7,3},{8,12},{9,13},{10,... | collective-permute-start | bytes 1671176 | tf_op jit(solution)/shard_map/ppermute | solution.py:338
  25.5 14.6 %collective-permute-start.9 = (bf16[272,1024]{1,0:T(8,128)(2,1)}, bf16[272,1024]{1,0:T(8,128)(2,1)S(1)}, u32[]{:S(2)}, u32[]{:S(2)}) collective-permute-start(bf16[272,1024]{1,0:T(8,128)(2,1)} %collective-permute-done.3.first), channel_id=1, source_target_pairs={{2,3},{3,2},{4,5},{5,4},{10,11},{11,10},{12,13},{13,12},{18,19},{1... | collective-permute-start | bytes 1671176 | tf_op jit(solution)/shard_map/ppermute | solution.py:338
  38.5 31.2 %collective-permute-start.15 = (bf16[4,32,2048]{2,1,0:T(8,128)(2,1)S(1)}, bf16[4,32,2048]{2,1,0:T(8,128)(2,1)S(1)}, u32[]{:S(2)}, u32[]{:S(2)}) collective-permute-start(bf16[4,32,2048]{2,1,0:T(8,128)(2,1)S(1)} %shard_map.157), channel_id=1, source_target_pairs={{0,2},{1,3},{2,0},{3,1},{4,6},{5,7},{6,4},{7,5},{8,10},{9,11},{10,... | collective-permute-start | bytes 1572872 | tf_op jit(solution)/shard_map/ppermute | solution.py:338
  40.1 19.9 %collective-permute-start.10 = (bf16[272,1024]{1,0:T(8,128)(2,1)S(1)}, bf16[272,1024]{1,0:T(8,128)(2,1)S(1)}, u32[]{:S(2)}, u32[]{:S(2)}) collective-permute-start(bf16[272,1024]{1,0:T(8,128)(2,1)S(1)} %collective-permute-done.9.second), channel_id=1, source_target_pairs={{0,4},{1,5},{2,6},{3,7},{4,0},{5,1},{6,2},{7,3},{8,12},{9,13},{10,... | collective-permute-start | bytes 1671176 | tf_op jit(solution)/shard_map/ppermute | solution.py:338
  54.4 20.5 %collective-permute-start.16 = (bf16[1024,256]{1,0:T(8,128)(2,1)S(1)}, bf16[1024,256]{1,0:T(8,128)(2,1)S(1)}, u32[]{:S(2)}, u32[]{:S(2)}) collective-permute-start(bf16[1024,256]{1,0:T(8,128)(2,1)S(1)} %slice_dynamic-update-slice_fusion.3.refs_4_.refs_8_), channel_id=1, source_target_pairs={{0,4},{1,5},{2,6},{3,7},{4,0},{5,1},{6,2},{7,3},{8,12},{9,13},{10,... | collective-permute-start | bytes 1572872 | tf_op jit(solution)/shard_map/ppermute | solution.py:338
  59.7 16.1 %collective-permute-start.17 = (bf16[1024,256]{1,0:T(8,128)(2,1)S(1)}, bf16[1024,256]{1,0:T(8,128)(2,1)S(1)}, u32[]{:S(2)}, u32[]{:S(2)}) collective-permute-start(bf16[1024,256]{1,0:T(8,128)(2,1)S(1)} %slice_dynamic-update-slice_fusion.3.refs_4_.refs_8_), channel_id=1, source_target_pairs={{0,1},{1,0},{2,3},{3,2},{4,5},{5,4},{6,7},{7,6},{8,9},{9,8},{10,11... | collective-permute-start | bytes 1572872 | tf_op jit(solution)/shard_map/ppermute | solution.py:338
  69.8 24.4 %collective-permute-start.18 = (bf16[256,2048]{1,0:T(8,128)(2,1)S(1)}, bf16[256,2048]{1,0:T(8,128)(2,1)S(1)}, u32[]{:S(2)}, u32[]{:S(2)}) collective-permute-start(bf16[256,2048]{1,0:T(8,128)(2,1)S(1)} %bitcast.32), channel_id=1, source_target_pairs={{0,16},{1,17},{2,18},{3,19},{4,20},{5,21},{6,22},{7,23},{8,24},{9,... | collective-permute-start | bytes 3145736 | tf_op jit(solution)/shard_map/ppermute | solution.py:338
  70.8 24.0 %collective-permute-start.20 = (bf16[256,2048]{1,0:T(8,128)(2,1)S(1)}, bf16[256,2048]{1,0:T(8,128)(2,1)S(1)}, u32[]{:S(2)}, u32[]{:S(2)}) collective-permute-start(bf16[256,2048]{1,0:T(8,128)(2,1)S(1)} %bitcast.33), channel_id=1, source_target_pairs={{0,8},{1,9},{2,10},{3,11},{4,12},{5,13},{6,14},{7,15},{8,0},{9,1},... | collective-permute-start | bytes 3145736 | tf_op jit(solution)/shard_map/ppermute | solution.py:338
  71.3 23.5 %collective-permute-start.21 = (bf16[272,1024]{1,0:T(8,128)(2,1)S(1)}, bf16[272,1024]{1,0:T(8,128)(2,1)S(1)}, u32[]{:S(2)}, u32[]{:S(2)}) collective-permute-start(bf16[272,1024]{1,0:T(8,128)(2,1)S(1)} %copy-done.33), channel_id=1, source_target_pairs={{0,1},{1,0},{2,4},{3,5},{4,2},{5,3},{6,7},{7,6},{8,9},{9,8},{10,12... | collective-permute-start | bytes 1671176 | tf_op jit(solution)/shard_map/ppermute | solution.py:338
  75.8 18.4 %collective-permute-start.19 = (bf16[1024,256]{1,0:T(8,128)(2,1)S(1)}, bf16[1024,256]{1,0:T(8,128)(2,1)S(1)}, u32[]{:S(2)}, u32[]{:S(2)}) collective-permute-start(bf16[1024,256]{1,0:T(8,128)(2,1)S(1)} %collective-permute-done.17.refs_5_.refs_9_), channel_id=1, source_target_pairs={{0,4},{1,5},{2,6},{3,7},{4,0},{5,1},{6,2},{7,3},{8,12},{9,13},{10,... | collective-permute-start | bytes 1572872 | tf_op jit(solution)/shard_map/ppermute | solution.py:338
  84.4 14.4 %collective-permute-start.23 = (bf16[1024,256]{1,0:T(8,128)(2,1)S(1)}, bf16[1024,256]{1,0:T(8,128)(2,1)S(1)}, u32[]{:S(2)}, u32[]{:S(2)}) collective-permute-start(bf16[1024,256]{1,0:T(8,128)(2,1)S(1)} %get-tuple-element.165.refs_0_.refs_4_.o_ref), channel_id=1, source_target_pairs={{0,1},{1,0},{2,3},{3,2},{4,5},{5,4},{6,7},{7,6},{8,9},{9,8},{10,11... | collective-permute-start | bytes 1572872 | tf_op jit(solution)/shard_map/ppermute | solution.py:338
  99.4 15.0 %collective-permute-start.28 = (bf16[144,2048]{1,0:T(8,128)(2,1)S(1)}, bf16[144,2048]{1,0:T(8,128)(2,1)S(1)}, u32[]{:S(2)}, u32[]{:S(2)}) collective-permute-start(bf16[144,2048]{1,0:T(8,128)(2,1)S(1)} %slice.86), channel_id=1, source_target_pairs={{0,16},{1,17},{2,18},{3,19},{4,20},{5,21},{6,22},{7,23},{8,24},{9,... | collective-permute-start | bytes 1769480 | tf_op jit(solution)/shard_map/ppermute | solution.py:338
  100.4 14.7 %collective-permute-start.29 = (bf16[144,2048]{1,0:T(8,128)(2,1)S(1)}, bf16[144,2048]{1,0:T(8,128)(2,1)S(1)}, u32[]{:S(2)}, u32[]{:S(2)}) collective-permute-start(bf16[144,2048]{1,0:T(8,128)(2,1)S(1)} %slice.87), channel_id=1, source_target_pairs={{0,8},{1,9},{2,10},{3,11},{4,12},{5,13},{6,14},{7,15},{8,0},{9,1},... | collective-permute-start | bytes 1769480 | tf_op jit(solution)/shard_map/ppermute | solution.py:338
  130.9 14.5 %collective-permute-start.31 = (bf16[272,1024]{1,0:T(8,128)(2,1)}, bf16[272,1024]{1,0:T(8,128)(2,1)}, u32[]{:S(2)}, u32[]{:S(2)}) collective-permute-start(bf16[272,1024]{1,0:T(8,128)(2,1)} %pad.9), channel_id=1, source_target_pairs={{0,1},{1,0},{2,3},{3,2},{4,5},{5,4},{6,7},{7,6},{8,9},{9,8},{10,11... | collective-permute-start | bytes 1671176 | tf_op jit(solution)/shard_map/ppermute | solution.py:338
  139.1 66.1 %all-to-all-start = ((bf16[4,256,2048]{2,1,0:T(8,128)(2,1)}), bf16[4,256,2048]{2,1,0:T(8,128)(2,1)}, u32[]{:S(2)}, u32[]{:S(2)}) async-start(bf16[4,256,2048]{2,1,0:T(8,128)(2,1)} %shard_map.168), calls=%async_computation | async-start | bytes 8388608 | tf_op jit(solution)/shard_map/all_to_all | solution.py:1180
  153.2 13.4 %collective-permute-start.36 = (bf16[272,1024]{1,0:T(8,128)(2,1)S(1)}, bf16[272,1024]{1,0:T(8,128)(2,1)S(1)}, u32[]{:S(2)}, u32[]{:S(2)}) collective-permute-start(bf16[272,1024]{1,0:T(8,128)(2,1)S(1)} %get-tuple-element.186.refs_0_), channel_id=1, source_target_pairs={{0,1},{1,0},{2,3},{3,2},{4,5},{5,4},{6,7},{7,6},{8,9},{9,8},{10,11... | collective-permute-start | bytes 1671176 | tf_op jit(solution)/shard_map/ppermute | solution.py:338
  157.5 29.7 %collective-permute-start.32 = (bf16[256,1024]{1,0:T(8,128)(2,1)S(1)}, bf16[256,1024]{1,0:T(8,128)(2,1)S(1)}, u32[]{:S(2)}, u32[]{:S(2)}) collective-permute-start(bf16[256,1024]{1,0:T(8,128)(2,1)S(1)} %get-tuple-element.244), channel_id=1, source_target_pairs={{0,4},{1,5},{2,6},{3,7},{4,0},{5,1},{6,2},{7,3},{8,12},{9,13},{10,... | collective-permute-start | bytes 1572872 | tf_op jit(solution)/shard_map/ppermute | solution.py:338
  168.4 18.8 %collective-permute-start.34 = (bf16[256,1024]{1,0:T(8,128)(2,1)S(1)}, bf16[256,1024]{1,0:T(8,128)(2,1)S(1)}, u32[]{:S(2)}, u32[]{:S(2)}) collective-permute-start(bf16[256,1024]{1,0:T(8,128)(2,1)S(1)} %add_convert_fusion.2), channel_id=1, source_target_pairs={{0,1},{1,0},{2,3},{3,2},{4,5},{5,4},{6,7},{7,6},{8,9},{9,8},{10,11... | collective-permute-start | bytes 1572872 | tf_op jit(solution)/shard_map/ppermute | solution.py:338
  188.6 15.5 %collective-permute-start.39 = (bf16[512,1024]{1,0:T(8,128)(2,1)S(1)}, bf16[512,1024]{1,0:T(8,128)(2,1)S(1)}, u32[]{:S(2)}, u32[]{:S(2)}) collective-permute-start(bf16[512,1024]{1,0:T(8,128)(2,1)S(1)} %shard_map.173), channel_id=1, source_target_pairs={{0,4},{1,5},{2,6},{3,7},{4,0},{5,1},{6,2},{7,3},{8,12},{9,13},{10,... | collective-permute-start | bytes 3145736 | tf_op jit(solution)/shard_map/ppermute | solution.py:338
  190.2 20.8 %collective-permute-start.35 = (bf16[256,1024]{1,0:T(8,128)(2,1)}, bf16[256,1024]{1,0:T(8,128)(2,1)}, u32[]{:S(2)}, u32[]{:S(2)}) collective-permute-start(bf16[256,1024]{1,0:T(8,128)(2,1)} %add_convert_fusion.1), channel_id=1, source_target_pairs={{0,0},{1,1},{2,4},{3,5},{4,2},{5,3},{6,6},{7,7},{8,8},{9,9},{10,12... | collective-permute-start | bytes 1572872 | tf_op jit(solution)/shard_map/ppermute | solution.py:338
  201.5 13.0 %collective-permute-start.40 = (bf16[256,1024]{1,0:T(8,128)(2,1)}, bf16[256,1024]{1,0:T(8,128)(2,1)S(1)}, u32[]{:S(2)}, u32[]{:S(2)}) collective-permute-start(bf16[256,1024]{1,0:T(8,128)(2,1)} %get-tuple-element.209), channel_id=1, source_target_pairs={{0,8},{1,9},{2,10},{3,11},{4,12},{5,13},{6,14},{7,15},{8,0},{9,1},... | collective-permute-start | bytes 1572872 | tf_op jit(solution)/shard_map/ppermute | solution.py:338
  202.7 12.8 %collective-permute-start.41 = (bf16[256,1024]{1,0:T(8,128)(2,1)}, bf16[256,1024]{1,0:T(8,128)(2,1)S(1)}, u32[]{:S(2)}, u32[]{:S(2)}) collective-permute-start(bf16[256,1024]{1,0:T(8,128)(2,1)} %get-tuple-element.210), channel_id=1, source_target_pairs={{0,16},{1,17},{2,18},{3,19},{4,20},{5,21},{6,22},{7,23},{8,24},{9,... | collective-permute-start | bytes 1572872 | tf_op jit(solution)/shard_map/ppermute | solution.py:338
  203.9 23.0 %collective-permute-start.42 = (bf16[256,1024]{1,0:T(8,128)(2,1)}, bf16[256,1024]{1,0:T(8,128)(2,1)S(1)}, u32[]{:S(2)}, u32[]{:S(2)}) collective-permute-start(bf16[256,1024]{1,0:T(8,128)(2,1)} %get-tuple-element.211), channel_id=1, source_target_pairs={{0,24},{1,25},{2,26},{3,27},{4,28},{5,29},{6,30},{7,31},{8,16},{9,... | collective-permute-start | bytes 1572872 | tf_op jit(solution)/shard_map/ppermute | solution.py:338
  207.8 26.9 %collective-permute-start.43 = (bf16[2,64,2048]{2,1,0:T(8,128)(2,1)S(1)}, bf16[2,64,2048]{2,1,0:T(8,128)(2,1)S(1)}, u32[]{:S(2)}, u32[]{:S(2)}) collective-permute-start(bf16[2,64,2048]{2,1,0:T(8,128)(2,1)S(1)} %get-tuple-element.215), channel_id=1, source_target_pairs={{0,2},{1,3},{2,0},{3,1},{4,6},{5,7},{6,4},{7,5},{8,10},{9,11},{10,... | collective-permute-start | bytes 1572872 | tf_op jit(solution)/shard_map/ppermute | solution.py:338
  211.0 23.7 %collective-permute-start.44 = (bf16[256,1024]{1,0:T(8,128)(2,1)S(1)}, bf16[256,1024]{1,0:T(8,128)(2,1)S(1)}, u32[]{:S(2)}, u32[]{:S(2)}) collective-permute-start(bf16[256,1024]{1,0:T(8,128)(2,1)S(1)} %copy-done.65), channel_id=1, source_target_pairs={{0,1},{1,0},{2,3},{3,2},{4,5},{5,4},{6,7},{7,6},{8,9},{9,8},{10,11... | collective-permute-start | bytes 1572872 | tf_op jit(solution)/shard_map/ppermute | solution.py:338
  227.2 25.3 %collective-permute-start.48 = (bf16[2,64,1152]{2,1,0:T(8,128)(2,1)S(1)}, bf16[2,64,1152]{2,1,0:T(8,128)(2,1)S(1)}, u32[]{:S(2)}, u32[]{:S(2)}) collective-permute-start(bf16[2,64,1152]{2,1,0:T(8,128)(2,1)S(1)} %get-tuple-element.226), channel_id=1, source_target_pairs={{0,2},{1,3},{2,0},{3,1},{4,6},{5,7},{6,4},{7,5},{8,10},{9,11},{10,... | collective-permute-start | bytes 884744 | tf_op jit(solution)/shard_map/ppermute | solution.py:338
  237.6 24.8 %collective-permute-start.46 = (bf16[128,1024]{1,0:T(8,128)(2,1)S(1)}, bf16[128,1024]{1,0:T(8,128)(2,1)S(1)}, u32[]{:S(2)}, u32[]{:S(2)}) collective-permute-start(bf16[128,1024]{1,0:T(8,128)(2,1)S(1)} %get-tuple-element.223), channel_id=1, source_target_pairs={{0,0},{1,1},{2,4},{3,5},{4,2},{5,3},{6,6},{7,7},{8,8},{9,9},{10,12... | collective-permute-start | bytes 786440 | tf_op jit(solution)/shard_map/ppermute | solution.py:338
  241.1 21.3 %collective-permute-start.45 = (bf16[128,1024]{1,0:T(8,128)(2,1)S(1)}, bf16[128,1024]{1,0:T(8,128)(2,1)S(1)}, u32[]{:S(2)}, u32[]{:S(2)}) collective-permute-start(bf16[128,1024]{1,0:T(8,128)(2,1)S(1)} %get-tuple-element.246), channel_id=1, source_target_pairs={{0,0},{1,1},{2,4},{3,5},{4,2},{5,3},{6,6},{7,7},{8,8},{9,9},{10,12... | collective-permute-start | bytes 786440 | tf_op jit(solution)/shard_map/ppermute | solution.py:338
  (89 other events, 1056.3 us)
